TPU v7x, 32 devices: a whole 2x2x4 slice. The times are simulated.
32 devices in a mesh: row: 8 (over z, x), col: 4 (over y, core).
Axes of the slice: x: 2, y: 2, z: 4, core: 2. Of those that a mesh axis runs over, the one named last changes fastest.
Arguments:
- features: bfloat16 [14336, 2048], P('row', 'col'), may hold values from -6 to 6
- neighbours: int32 [14336, 32], P('row'), may hold values from -1 to 127, as said below
- node_valid: int32 [14336], P('row'), may hold values from 0 to 1, as said below
- weight_one: bfloat16 [2048, 2048], P(None, 'col'), may hold values from -0.125 to 0.125
- gamma_one: float32 [2048], P('col'), may hold values from 0.25 to 1.75
- beta_one: float32 [2048], P('col'), may hold values from -0.5 to 0.5
- weight_two: bfloat16 [2048, 2048], P(None, 'col'), may hold values from -0.125 to 0.125
- gamma_two: float32 [2048], P('col'), may hold values from 0.25 to 1.75
- beta_two: float32 [2048], P('col'), may hold values from -0.5 to 0.5
- cotangent: bfloat16 [14336, 2048], P('row', 'col'), may hold values from -6 to 6
Outputs:
- output: float32 [14336, 2048], P('row', 'col')
- grad_features: float32 [14336, 2048], P('row', 'col')
- grad_weight_one: float32 [2048, 2048], P(None, 'col')
- grad_gamma_one: float32 [2048], P('col')
- grad_beta_one: float32 [2048], P('col')
- grad_weight_two: float32 [2048, 2048], P(None, 'col')
- grad_gamma_two: float32 [2048], P('col')
- grad_beta_two: float32 [2048], P('col')
Inputs may be any that keep to these rules, and one draw needn't show every extreme that they name: `neighbours`: entries >= 0 name valid nodes of the same slot; every valid node has 1 to 32 such entries, first in its list, the rest are -1; a padding row has only -1; some slot is full. `node_valid`: in each slot the valid nodes come first and number at least 40.
All inputs are finite; a program needn't handle non-finite values.
Results may differ from a plain program's by a relative error of at most 0.012.
Values may be sent and summed in bfloat16 or wider, within the bound.
No kernel may reach another device: no remote copies, remote signals or barrier semaphores. Data moves between devices by JAX's collectives and lax.ppermute only.
A program may use at most 128 MiB of HBM per device.

v0:
```python
import jax
import jax.numpy as jnp
from jax import lax
from jax.sharding import PartitionSpec as P

SLOT = 128
NBR = 32


EPSILON = 1e-05


def build_tiles(neighbours):
    entries_all = neighbours.reshape(-1, SLOT, NBR)

    def build(entries):
        columns = jnp.arange(SLOT, dtype=jnp.int32)
        hits = jnp.sum((entries[:, :, None] == columns[None, None, :]).astype(jnp.float32), axis=1)
        degree = jnp.sum((entries >= 0).astype(jnp.float32), axis=1)
        joined = hits + jnp.eye(SLOT, dtype=jnp.float32)
        return joined / (degree[:, None] + 1.0)

    tiles = lax.map(build, entries_all)
    return (tiles, jnp.diagonal(tiles, axis1=1, axis2=2))


def spread(values, tiles, self_weight):
    shaped = values.reshape(tiles.shape[0], SLOT, values.shape[1])
    summed = jnp.einsum("sij,sjd->sid", tiles, shaped, precision=lax.Precision.HIGHEST)
    return (summed + self_weight[:, :, None] * shaped).reshape(values.shape)


def spread_back(grads, tiles, self_weight):
    shaped = grads.reshape(tiles.shape[0], SLOT, grads.shape[1])
    summed = jnp.einsum("sji,sjd->sid", tiles, shaped, precision=lax.Precision.HIGHEST)
    return (summed + self_weight[:, :, None] * shaped).reshape(grads.shape)


def moments(linear, valid):
    total_valid, summed = lax.psum((jnp.sum(valid), jnp.sum(valid * linear, axis=0)), "row")
    mean = summed / total_valid
    centred = linear - mean
    variance = lax.psum(jnp.sum(valid * centred * centred, axis=0), "row") / total_valid
    return (total_valid, mean, variance)


def forward_layer(values, weight, gamma, beta, tiles, self_weight, valid):
    mixed = spread(values, tiles, self_weight).astype(jnp.bfloat16)
    gathered = lax.all_gather(mixed, "col", axis=1, tiled=True)
    linear = jnp.dot(gathered, weight, preferred_element_type=jnp.float32)
    total_valid, mean, variance = moments(linear, valid)
    inv_std = lax.rsqrt(variance + EPSILON)
    normed = (linear - mean) * inv_std
    before = gamma * normed + beta
    result = valid * jax.nn.silu(before)
    return (result, (gathered, normed, inv_std, before, total_valid))


def backward_layer(grad_result, weight, gamma, kept, tiles, self_weight, valid):
    gathered, normed, inv_std, before, total_valid = kept
    sigmoid_value = jax.nn.sigmoid(before)
    slope = sigmoid_value * (1.0 + before * (1.0 - sigmoid_value))
    grad_before = grad_result * valid * slope
    grad_beta, grad_gamma = lax.psum(
        (jnp.sum(grad_before, axis=0), jnp.sum(grad_before * normed, axis=0)), "row"
    )
    grad_normed = gamma * grad_before
    grad_linear = inv_std * (
        grad_normed - valid * (gamma * grad_beta + normed * gamma * grad_gamma) / total_valid
    )
    grad_low = grad_linear.astype(jnp.bfloat16)
    weight_terms = lax.dot_general(
        gathered, grad_low, (((0,), (0,)), ((), ())), preferred_element_type=jnp.float32
    )
    grad_weight = lax.psum(weight_terms, "row")
    partial_terms = lax.dot_general(
        grad_low, weight, (((1,), (1,)), ((), ())), preferred_element_type=jnp.float32
    )
    grad_mixed = lax.psum_scatter(partial_terms, "col", scatter_dimension=1, tiled=True)
    grad_values = spread_back(grad_mixed, tiles, self_weight)
    return (grad_values, grad_weight, grad_gamma, grad_beta)


def local(
    features,
    neighbours,
    node_valid,
    weight_one,
    gamma_one,
    beta_one,
    weight_two,
    gamma_two,
    beta_two,
    cotangent,
):
    tiles, self_weight = build_tiles(neighbours)
    valid = node_valid.astype(jnp.float32)[:, None]
    hidden, kept_one = forward_layer(
        features.astype(jnp.float32), weight_one, gamma_one, beta_one, tiles, self_weight, valid
    )
    output, kept_two = forward_layer(
        hidden, weight_two, gamma_two, beta_two, tiles, self_weight, valid
    )
    grad_hidden, grad_weight_two, grad_gamma_two, grad_beta_two = backward_layer(
        cotangent.astype(jnp.float32), weight_two, gamma_two, kept_two, tiles, self_weight, valid
    )
    grad_features, grad_weight_one, grad_gamma_one, grad_beta_one = backward_layer(
        grad_hidden, weight_one, gamma_one, kept_one, tiles, self_weight, valid
    )
    return (
        output,
        grad_features,
        grad_weight_one,
        grad_gamma_one,
        grad_beta_one,
        grad_weight_two,
        grad_gamma_two,
        grad_beta_two,
    )


def solution(mesh):
    placed = (
        P("row", "col"),
        P("row", None),
        P("row"),
        P(None, "col"),
        P("col"),
        P("col"),
        P(None, "col"),
        P("col"),
        P("col"),
        P("row", "col"),
    )
    return jax.shard_map(
        local,
        mesh=mesh,
        in_specs=placed,
        out_specs=(
            P("row", "col"),
            P("row", "col"),
            P(None, "col"),
            P("col"),
            P("col"),
            P(None, "col"),
            P("col"),
            P("col"),
        ),
        check_vma=False,
    )
```

profile of v0, /device:TPU:0, one launch (start us, length us, event | category | flops | bytes accessed | tf_op | source)
XLA Modules:
  0.0 855.5 jit_solution(2408295498759646820)
XLA Ops:
  7.3 2.3 copy.23
  9.6 27.6 %while.10 = (s32[]{:T(128)}, f32[14,128,128]{2,1,0:T(8,128)S(1)}, s32[14,128,32]{2,1,0:T(8,128)}, s32[]{:T(128)}) while((s32[]{:T(128)}, f32[14,128,128]{2,1,0:T(8,128)S(1)}, s32[14,128,32]{2,1,0:T(8,128)}, s32[]{:T(128)}) %tuple.47), condition=%wide.region_3.4_spmd, body=%wide.region_0.3_spmd.sunk | while | flops 1634306 | bytes 247877 | solution.py:23
  11.5 0.9 convert_reduce_fusion.5
  13.5 0.9 convert_reduce_fusion.5
  15.5 0.9 convert_reduce_fusion.5
  17.4 0.9 convert_reduce_fusion.5
  19.4 0.9 convert_reduce_fusion.5
  21.4 0.9 convert_reduce_fusion.5
  23.4 0.9 convert_reduce_fusion.5
  25.3 0.9 convert_reduce_fusion.5
  27.3 0.9 convert_reduce_fusion.5
  29.3 0.9 convert_reduce_fusion.5
  31.3 0.9 convert_reduce_fusion.5
  35.2 0.9 convert_reduce_fusion.5
  37.2 4.7 copy.24
  41.8 1.8 gather_fusion
  43.7 5.1 add_convert_fusion.1
  49.5 54.5 %all-gather.3.cloned.1.call-done = bf16[1792,2048]{1,0:T(8,128)(2,1)} async-done(((bf16[1792,512]{1,0:T(8,128)(2,1)}), bf16[1792,2048]{1,0:T(8,128)(2,1)}) %all-gather.3.cloned.1.call-update) | async-done | bytes 7340048 | tf_op jit(solution)/shard_map/all_gather | solution.py:49
  104.0 9.5 %multiply_reduce_fusion.3 = (f32[512]{0:T(512)S(1)}, f32[1792,512]{1,0:T(8,128)}) fusion(f32[1792]{0:T(1024)S(1)} %convert_element_type.41, bf16[1792,2048]{1,0:T(8,128)(2,1)} %all-gather.3.cloned.1.call-done, bf16[2048,512]{1,0:T(8,128)(2,1)} %param.15), kind=kOutput, calls=%fused_computation.29 | convolution fusion | flops 3759930880 | bytes 13116416 | tf_op jit(solution)/shard_map/dot_general | solution.py:50
  113.5 22.0 %all-reduce.2 = (f32[512]{0:T(512)S(1)}, f32[]{:T(128)}) all-reduce(f32[512]{0:T(512)S(1)} %get-tuple-element.49, f32[]{:T(128)} %convert_reduce_fusion.2), channel_id=1, replica_groups=mesh['row'=8,'col'=4] {'row'}, use_global_device_ids=true, to_apply=%region_5.6 | all-reduce | flops 513 | bytes 4104 | tf_op jit(solution)/shard_map/psum | solution.py:40
  136.0 2.6 fusion.2
  138.6 17.1 %psum.82 = f32[512]{0:T(512)S(1)} all-reduce(f32[512]{0:T(512)S(1)} %fusion.2), channel_id=1, replica_groups=mesh['row'=8,'col'=4] {'row'}, use_global_device_ids=true, to_apply=%region_9.10 | all-reduce | flops 512 | bytes 4096 | tf_op jit(solution)/shard_map/psum | solution.py:43
  156.3 3.0 multiply_multiply_fusion.4
  159.4 4.5 add_convert_fusion
  164.1 50.0 %all-gather.5.cloned.1.call-done = bf16[1792,2048]{1,0:T(8,128)(2,1)} async-done(((bf16[1792,512]{1,0:T(8,128)(2,1)}), bf16[1792,2048]{1,0:T(8,128)(2,1)}) %all-gather.5.cloned.1.call-update) | async-done | bytes 7340048 | tf_op jit(solution)/shard_map/all_gather | solution.py:49
  214.1 8.9 %multiply_reduce_fusion.2 = (f32[512]{0:T(512)S(1)}, f32[1792,512]{1,0:T(8,128)}) fusion(f32[1792]{0:T(1024)S(1)} %convert_element_type.41, bf16[1792,2048]{1,0:T(8,128)(2,1)} %all-gather.5.cloned.1.call-done, bf16[2048,512]{1,0:T(8,128)(2,1)S(1)} %copy-done), kind=kOutput, calls=%fused_computation.25 | convolution fusion | flops 3759930880 | bytes 13116416 | tf_op jit(solution)/shard_map/dot_general | solution.py:50
  223.0 21.5 %psum.83 = f32[512]{0:T(512)S(1)} all-reduce(f32[512]{0:T(512)S(1)} %get-tuple-element.51), channel_id=1, replica_groups=mesh['row'=8,'col'=4] {'row'}, use_global_device_ids=true, to_apply=%region_11.12 | all-reduce | flops 512 | bytes 4096 | tf_op jit(solution)/shard_map/psum | solution.py:40
  245.1 2.6 fusion.3
  247.7 17.1 %psum.84 = f32[512]{0:T(512)S(1)} all-reduce(f32[512]{0:T(512)S(1)} %fusion.3), channel_id=1, replica_groups=mesh['row'=8,'col'=4] {'row'}, use_global_device_ids=true, to_apply=%region_13.14 | all-reduce | flops 512 | bytes 4096 | tf_op jit(solution)/shard_map/psum | solution.py:43
  265.4 6.3 fusion.6
  271.7 19.1 %all-reduce.1 = (f32[512]{0:T(512)S(1)}, f32[512]{0:T(512)S(1)}) all-reduce(f32[512]{0:T(512)S(1)} %get-tuple-element.29, f32[512]{0:T(512)S(1)} %get-tuple-element.28), channel_id=1, replica_groups=mesh['row'=8,'col'=4] {'row'}, use_global_device_ids=true, to_apply=%region_17.18 | all-reduce | flops 1024 | bytes 8192 | tf_op jit(solution)/shard_map/psum | solution.py:64
  290.8 4.5 multiply_convert_fusion.1
  295.4 1.2 copy-done.4
  296.6 7.2 fusion.8
  304.1 109.0 %reduce-scatter.3.cloned.1.call-done = f32[1792,512]{1,0:T(8,128)} async-done(((f32[1792,2048]{1,0:T(8,128)}), f32[1792,512]{1,0:T(8,128)}) %reduce-scatter.3.cloned.1.call-update) | async-done | bytes 3670032 | tf_op jit(solution)/shard_map/reduce_scatter | solution.py:79
  413.1 6.8 multiply_add_fusion.1
  419.9 3.7 fusion.5
  423.7 21.3 %all-reduce = (f32[512]{0:T(512)S(1)}, f32[512]{0:T(512)S(1)}) all-reduce(f32[512]{0:T(512)S(1)} %get-tuple-element.27, f32[512]{0:T(512)S(1)} %get-tuple-element.26), channel_id=1, replica_groups=mesh['row'=8,'col'=4] {'row'}, use_global_device_ids=true, to_apply=%region_22.23 | all-reduce | flops 1024 | bytes 8192 | tf_op jit(solution)/shard_map/psum | solution.py:64
  445.0 4.7 multiply_convert_fusion
  449.8 7.3 fusion.9
  457.4 1.2 copy-done.5
  458.5 9.9 %fusion.11 = f32[2048,512]{1,0:T(8,128)} fusion(bf16[1792,2048]{1,0:T(8,128)(2,1)} %all-gather.5.cloned.1.call-done, bf16[1792,512]{1,0:T(8,128)(2,1)S(1)} %copy-done.5), kind=kOutput, calls=%fused_computation.44 | convolution fusion | flops 3758096384 | bytes 13369344 | tf_op jit(solution)/shard_map/dot_general | solution.py:72
  468.4 10.5 %fusion.10 = f32[2048,512]{1,0:T(8,128)} fusion(bf16[1792,2048]{1,0:T(8,128)(2,1)} %all-gather.3.cloned.1.call-done, bf16[1792,512]{1,0:T(8,128)(2,1)S(1)} %copy-done.7), kind=kOutput, calls=%fused_computation.43 | convolution fusion | flops 3758096384 | bytes 13369344 | tf_op jit(solution)/shard_map/dot_general | solution.py:72
  479.0 87.5 %reduce-scatter.5.cloned.1.call-done = f32[1792,512]{1,0:T(8,128)} async-done(((f32[1792,2048]{1,0:T(8,128)}), f32[1792,512]{1,0:T(8,128)}) %reduce-scatter.5.cloned.1.call-update) | async-done | bytes 3670032 | tf_op jit(solution)/shard_map/reduce_scatter | solution.py:79
  566.5 8.5 multiply_add_fusion
  575.0 267.1 %all-reduce.6.cloned.1.call-done = (f32[2048,512]{1,0:T(8,128)}, f32[2048,512]{1,0:T(8,128)}) async-done(((f32[2048,512]{1,0:T(8,128)}, f32[2048,512]{1,0:T(8,128)}), (f32[2048,512]{1,0:T(8,128)}, f32[2048,512]{1,0:T(8,128)})) %all-reduce.6.cloned.1.call-update) | async-done | bytes 8388624 | tf_op jit(solution)/shard_map/psum | solution.py:75
  842.1 4.8 copy.41
  846.9 2.0 copy.42
  (99 shorter events, 19.7 us)
Async XLA Ops:
  7.2 207.0 %copy-start = (bf16[2048,512]{1,0:T(8,128)(2,1)S(1)}, bf16[2048,512]{1,0:T(8,128)(2,1)}, u32[]{:S(2)}) copy-start(bf16[2048,512]{1,0:T(8,128)(2,1)} %param.18) | copy-start | bytes 6291460
  7.2 96.8 %all-gather.3.cloned.1.call-start = ((), (), s32[]{:S(2)}) async-start(), calls=%async_computation.2 | async-start | bytes 9175040 | tf_op jit(solution)/shard_map/all_gather | solution.py:49
  41.8 7.0 copy-start.8
  48.8 165.3 %all-gather.5.cloned.1.call-start = ((), (), s32[]{:S(2)}) async-start(), calls=%async_computation.3 | async-start | bytes 9175040 | tf_op jit(solution)/shard_map/all_gather | solution.py:49
  113.5 42.8 %copy-start.9 = (f32[512]{0:T(512)S(1)}, f32[512]{0:T(512)}, u32[]{:S(2)}) copy-start(f32[512]{0:T(512)} %param.16) | copy-start | bytes 6148
  113.5 42.8 %copy-start.11 = (f32[512]{0:T(512)S(1)}, f32[512]{0:T(512)}, u32[]{:S(2)}) copy-start(f32[512]{0:T(512)} %param.17) | copy-start | bytes 6148
  163.9 249.3 %reduce-scatter.3.cloned.1.call-start = ((), (), s32[]{:S(2)}) async-start(), calls=%async_computation.4 | async-start | bytes 18350080 | tf_op jit(solution)/shard_map/reduce_scatter | solution.py:79
  223.0 42.3 %copy-start.10 = (f32[512]{0:T(512)S(1)}, f32[512]{0:T(512)}, u32[]{:S(2)}) copy-start(f32[512]{0:T(512)} %param.19) | copy-start | bytes 6148
  223.0 42.3 %copy-start.12 = (f32[512]{0:T(512)S(1)}, f32[512]{0:T(512)}, u32[]{:S(2)}) copy-start(f32[512]{0:T(512)} %param.20) | copy-start | bytes 6148
  290.8 4.5 copy-start.13
  290.8 4.6 copy-start.15
  295.3 1.2 copy-start.4
  303.8 262.6 %reduce-scatter.5.cloned.1.call-start = ((), (), s32[]{:S(2)}) async-start(), calls=%async_computation.5 | async-start | bytes 18350080 | tf_op jit(solution)/shard_map/reduce_scatter | solution.py:79
  413.1 6.8 copy-start.2
  445.0 4.7 copy-start.14
  445.0 4.7 copy-start.16
  445.0 4.7 copy-start.17
  449.7 7.3 copy-start.6
  457.0 1.5 copy-start.5
  457.0 385.1 %all-reduce.6.cloned.1.call-start = ((), (), s32[]{:S(2)}) async-start(), calls=%async_computation.6 | async-start | bytes 16777216 | tf_op jit(solution)/shard_map/psum | solution.py:75
  458.5 9.9 %copy-start.7 = (bf16[1792,512]{1,0:T(8,128)(2,1)S(1)}, bf16[1792,512]{1,0:T(8,128)(2,1)}, u32[]{:S(2)}) copy-start(bf16[1792,512]{1,0:T(8,128)(2,1)} %copy-done.6) | copy-start | bytes 5505028
  842.1 4.8 copy-start.3
  842.1 6.8 copy-start.1
Sparse Core Ops, SparseCore 0:
  48.9 55.0 all-gather.2
  164.0 50.1 all-gather.4
  303.9 109.1 reduce-scatter.2
  457.2 109.2 reduce-scatter.4
  571.0 271.0 all-reduce.5
where the time goes:
time: 857 us; the launch traced here: 855 us
  waiting for transfers between devices  568 us (66%)
  blocking collectives  118 us (14%)
  matrix products  78.2 us (9%)
  other arithmetic  57.2 us (7%)
  local copies, waits for them, and re-layouts  18.1 us (2%)
  between operations  14 us (2%)
    psum x1, waiting for transfers between devices, backward_layer(): grad_weight = lax.psum(weight_terms, 'row')  267 us
    reduce_scatter x2, waiting for transfers between devices, backward_layer(): lax.psum_scatter(partial_terms, 'col', scatter_dimension=1, tiled=True)  197 us
    all_gather x2, waiting for transfers between devices, forward_layer(): gathered = lax.all_gather(mixed, 'col', axis=1, tiled=True)  105 us
    psum x2, blocking collectives, moments(): lax.psum((jnp.sum(valid), jnp.sum(valid * linear, axis=0)), 'row')  43.4 us
    psum x2, blocking collectives, backward_layer(): lax.psum((jnp.sum(grad_before, axis=0), jnp.sum(grad_before * normed, axi...  40.5 us
    psum x2, blocking collectives, moments(): lax.psum(jnp.sum(valid * centred * centred, axis=0), 'row') / total_valid  34.3 us
    dot_general x2, matrix products, backward_layer(): lax.dot_general(gathered, grad_low, (((0,), (0,)), ((), ())), preferred_e...  20.4 us
    dot_general x2, matrix products, forward_layer(): linear = jnp.dot(gathered, weight, preferred_element_type=jnp.float32)  18.4 us
  transfers between devices with their start and end apart: 5, of which 5 were waited for; matrix products, arithmetic and copies ran while one was open for 3% of the time, Pallas kernels for 0%

commit v1 on v0

v1 whole, which is shorter than its diff:
```python
import functools

import jax
import jax.numpy as jnp
from jax import lax
from jax.experimental import pallas as pl
from jax.experimental.pallas import tpu as pltpu
from jax.sharding import PartitionSpec as P

SLOT = 128
NBR = 32
LANES = 128
EPSILON = 1e-05
BF = jnp.bfloat16
F32 = jnp.float32
ANY = pl.BlockSpec(memory_space=pl.ANY)


def params(limit=48 << 20):
    return pltpu.CompilerParams(dimension_semantics=("arbitrary",), vmem_limit_bytes=limit)


def cost(flops, moved):
    return pl.CostEstimate(flops=int(flops), bytes_accessed=int(moved), transcendentals=0)


def dot(a, b):
    return jnp.dot(a, b, preferred_element_type=F32)


def dot_t(a, b):
    return lax.dot_general(a, b, (((1,), (1,)), ((), ())), preferred_element_type=F32)


def wide(v, columns):
    return jnp.concatenate([v] * (columns // LANES), axis=1)


def sigmoid(v):
    return 0.5 * jnp.tanh(0.5 * v) + 0.5


def tiles_kernel(nbr_ref, valid_ref, h_ref, ht_ref, inv_ref, val_ref):
    entries = nbr_ref[0]
    rows = lax.broadcasted_iota(jnp.int32, (SLOT, SLOT), 0)
    cols = lax.broadcasted_iota(jnp.int32, (SLOT, SLOT), 1)
    hits = jnp.zeros((SLOT, SLOT), F32)
    degree = jnp.zeros((1, SLOT), F32)
    for k in range(entries.shape[0]):
        one = entries[k : k + 1, :]
        hits += (one == rows).astype(F32)
        degree += (one >= 0).astype(F32)
    eye = (rows == cols).astype(F32)
    joined = hits + eye
    counts = joined + joined * eye
    ht_ref[0] = counts.astype(BF)
    h_ref[0] = counts.T.astype(BF)
    inv_ref[0] = jnp.broadcast_to(1.0 / (degree + 1.0), (SLOT, SLOT)).T
    val_ref[0] = jnp.broadcast_to(valid_ref[0].astype(F32), (SLOT, SLOT)).T


def build_tiles(neighbours, node_valid):
    slots = neighbours.shape[0] // SLOT
    turned = neighbours.reshape(slots, SLOT, NBR).transpose(0, 2, 1)
    square = pl.BlockSpec((1, SLOT, SLOT), lambda i: (i, 0, 0))
    return pl.pallas_call(
        tiles_kernel,
        grid=(slots,),
        in_specs=[
            pl.BlockSpec((1, NBR, SLOT), lambda i: (i, 0, 0)),
            pl.BlockSpec((1, 1, SLOT), lambda i: (i, 0, 0)),
        ],
        out_specs=[square] * 4,
        out_shape=[jax.ShapeDtypeStruct((slots, SLOT, SLOT), t) for t in (BF, BF, F32, F32)],
        compiler_params=params(),
        cost_estimate=cost(slots * SLOT * SLOT * NBR * 3, slots * SLOT * SLOT * 12),
        name="tiles",
    )(turned, node_valid.reshape(slots, 1, SLOT))


def combine(gathered):
    mref, first, second, count = (gathered[:, k, :] for k in range(4))
    shift = first / count
    mean_each = mref + shift
    spread_each = second - first * shift
    total = jnp.sum(count, axis=0, keepdims=True)
    mean = jnp.sum(count * mean_each, axis=0, keepdims=True) / total
    away = mean_each - mean
    variance = jnp.sum(spread_each + count * away * away, axis=0, keepdims=True) / total
    return total, mean, lax.rsqrt(variance + EPSILON)


def small_gather(block, axis):
    parts = lax.axis_size(axis)
    copies = jnp.broadcast_to(block[None], (parts,) + block.shape)
    return lax.all_to_all(copies, axis, split_axis=0, concat_axis=0, tiled=True)


def mix(tile_ref, value, step):
    out = []
    for s in range(step):
        part = value[s * SLOT : (s + 1) * SLOT]
        high = part.astype(BF)
        low = (part - high.astype(F32)).astype(BF)
        out.append(dot(tile_ref[s], high) + dot(tile_ref[s], low))
    return out[0] if step == 1 else jnp.concatenate(out, axis=0)


def flat(ref, columns):
    v = ref[...]
    return wide(v.reshape(v.shape[0] * v.shape[1], v.shape[2]), columns)


def forward_kernel(step, first, *refs):
    refs = refs[1:]
    xs, ws = refs[:4], refs[4:8]
    h_ref, inv_ref, val_ref = refs[8:11]
    if first:
        lin_ref, all_ref, st_ref = refs[11:]
    else:
        stin_ref, lin_ref, all_ref, st_ref = refs[11], *refs[14:]
    i = pl.program_id(0)
    columns = lin_ref.shape[1]
    total = None
    for b in range(4):
        x = xs[b][...]
        all_ref[b] = x
        term = dot(x, ws[b][...])
        total = term if total is None else total + term
    lin = mix(h_ref, total, step) * flat(inv_ref, columns)
    lin_ref[...] = lin
    v = flat(val_ref, columns)

    @pl.when(i == 0)
    def _():
        if first:
            st_ref[...] = jnp.zeros_like(st_ref)
            st_ref[0:1, :] = jnp.sum(v * lin, axis=0, keepdims=True) / jnp.sum(v, axis=0, keepdims=True)
        else:
            st_ref[...] = stin_ref[...]

    away = (lin - st_ref[0:1, :]) * v
    st_ref[1:2, :] += jnp.sum(away, axis=0, keepdims=True)
    st_ref[2:3, :] += jnp.sum(away * away, axis=0, keepdims=True)
    st_ref[3:4, :] += jnp.sum(v, axis=0, keepdims=True)


def forward_chunk(ids, plan, k, blocks, weight, tiles, carried):
    step, starts, sizes = plan
    base, steps = starts[k], sizes[k]
    rows = step * SLOT
    h, _, inv, val = tiles
    nodes, columns = h.shape[0] * SLOT, weight.shape[1]
    depth = weight.shape[0] // 4
    first = carried is None

    def block_spec(x):
        off = base if x.shape[0] == nodes else 0
        return pl.BlockSpec((rows, depth), lambda i, ids: (i + off, 0))

    tile = pl.BlockSpec((step, SLOT, SLOT), lambda i, ids: (i + base, 0, 0))
    ins = [block_spec(x) for x in blocks]
    ins += [pl.BlockSpec((depth, columns), lambda i, ids, b=b: (ids[b], 0)) for b in range(4)]
    ins += [tile] * 3
    args = [*blocks, *[weight] * 4, h, inv, val]
    aliases = {}
    small = pl.BlockSpec((8, columns), lambda i, ids: (0, 0))
    if not first:
        lin, everything, stats = carried
        ins += [small, ANY, ANY]
        args += [stats, lin, everything]
        aliases = {13: 0, 14: 1}
    return pl.pallas_call(
        functools.partial(forward_kernel, step, first),
        grid_spec=pltpu.PrefetchScalarGridSpec(
            num_scalar_prefetch=1,
            grid=(steps,),
            in_specs=ins,
            out_specs=[
                pl.BlockSpec((rows, columns), lambda i, ids: (i + base, 0)),
                pl.BlockSpec((4, rows, depth), lambda i, ids: (0, i + base, 0)),
                small,
            ],
        ),
        out_shape=[
            jax.ShapeDtypeStruct((nodes, columns), F32),
            jax.ShapeDtypeStruct((4, nodes, depth), BF),
            jax.ShapeDtypeStruct((8, columns), F32),
        ],
        input_output_aliases=aliases,
        compiler_params=params(),
        cost_estimate=cost(2 * steps * rows * 4 * depth * columns, steps * rows * (8 * depth + 4 * columns) + 8 * depth * columns),
        name=f"forward_{k}",
    )(ids, *args)


def coefficients(g_ref, gamma_ref, beta_ref):
    total, mean, inv_std = combine(g_ref[...])
    return total, mean, inv_std, gamma_ref[...], beta_ref[...]


def hidden_kernel(lin_ref, val_ref, g_ref, gamma_ref, beta_ref, out_ref):
    _, mean, inv_std, gamma, beta = coefficients(g_ref, gamma_ref, beta_ref)
    before = gamma * ((lin_ref[...] - mean) * inv_std) + beta
    out_ref[...] = (flat(val_ref, lin_ref.shape[1]) * (before * sigmoid(before))).astype(out_ref.dtype)


def slope_of(lin, mean, inv_std, gamma, beta):
    normed = (lin - mean) * inv_std
    before = gamma * normed + beta
    sig = sigmoid(before)
    return normed, sig * (1.0 + before * (1.0 - sig))


def sums_kernel(lin_ref, cot_ref, val_ref, g_ref, gamma_ref, beta_ref, st_ref):
    _, mean, inv_std, gamma, beta = coefficients(g_ref, gamma_ref, beta_ref)
    normed, slope = slope_of(lin_ref[...], mean, inv_std, gamma, beta)
    grad = cot_ref[...].astype(F32) * flat(val_ref, lin_ref.shape[1]) * slope

    @pl.when(pl.program_id(0) == 0)
    def _():
        st_ref[...] = jnp.zeros_like(st_ref)

    st_ref[0:1, :] += jnp.sum(grad, axis=0, keepdims=True)
    st_ref[1:2, :] += jnp.sum(grad * normed, axis=0, keepdims=True)


def turn_kernel(step, from_cot, lin_ref, grad_ref, val_ref, inv_ref, ht_ref, g_ref, sg_ref, gamma_ref, beta_ref, out_ref):
    total, mean, inv_std, gamma, beta = coefficients(g_ref, gamma_ref, beta_ref)
    sg = sg_ref[...]
    grad_beta = jnp.sum(sg[:, 0, :], axis=0, keepdims=True)
    grad_gamma = jnp.sum(sg[:, 1, :], axis=0, keepdims=True)
    columns = lin_ref.shape[1]
    v = flat(val_ref, columns)
    if from_cot:
        normed, slope = slope_of(lin_ref[...], mean, inv_std, gamma, beta)
        grad = grad_ref[...].astype(F32) * v * slope
    else:
        normed = (lin_ref[...] - mean) * inv_std
        grad = grad_ref[...]
    scale = inv_std * gamma
    lin_grad = scale * (grad - v * ((grad_beta + normed * grad_gamma) / total))
    out_ref[...] = mix(ht_ref, lin_grad * flat(inv_ref, columns), step).astype(BF)


def rows_call(kernel, plan, k, big, tiles, smalls, out_dtype, out_full, name, ops, extra=()):
    step, starts, sizes = plan
    base, steps = (0, sum(sizes)) if k is None else (starts[k], sizes[k])
    rows = step * SLOT
    nodes, columns = big[0].shape
    ins = [pl.BlockSpec((rows, columns), lambda i: (i + base, 0)) for _ in big]
    ins += [pl.BlockSpec((step, SLOT, SLOT), lambda i: (i + base, 0, 0)) for _ in tiles]
    ins += [pl.BlockSpec(s.shape, lambda i, n=s.ndim: (0,) * n) for s in smalls]
    if out_dtype is None:
        out_spec = pl.BlockSpec((8, columns), lambda i: (0, 0))
        out_shape = jax.ShapeDtypeStruct((8, columns), F32)
    else:
        out_spec = pl.BlockSpec((rows, columns), lambda i: (i, 0))
        out_shape = jax.ShapeDtypeStruct((steps * rows, columns), out_dtype)
    return pl.pallas_call(
        kernel,
        grid=(steps,),
        in_specs=ins,
        out_specs=out_spec,
        out_shape=out_shape,
        compiler_params=params(),
        cost_estimate=cost(ops * steps * rows * columns, 8 * steps * rows * columns),
        name=name,
    )(*big, *tiles, *smalls)


def backward_kernel(layer_one, first, *refs):
    refs = refs[1:]
    xs, ws = refs[:4], refs[4:8]
    total = None
    for b in range(4):
        term = dot_t(xs[b][...], ws[b][...])
        total = term if total is None else total + term
    if layer_one:
        refs[-1][...] = total
        return
    lin_ref, val_ref, g_ref, gamma_ref, beta_ref = refs[8:13]
    out_ref, st_ref = refs[-2:]
    _, mean, inv_std, gamma, beta = coefficients(g_ref, gamma_ref, beta_ref)
    normed, slope = slope_of(lin_ref[...], mean, inv_std, gamma, beta)
    grad = total * flat(val_ref, lin_ref.shape[1]) * slope
    out_ref[...] = grad

    @pl.when(pl.program_id(0) == 0)
    def _():
        st_ref[...] = jnp.zeros_like(st_ref) if first else refs[13][...]

    st_ref[0:1, :] += jnp.sum(grad, axis=0, keepdims=True)
    st_ref[1:2, :] += jnp.sum(grad * normed, axis=0, keepdims=True)


def backward_chunk(ids, plan, k, blocks, pieces, norm, carried):
    step, starts, sizes = plan
    base, steps = starts[k], sizes[k]
    rows = step * SLOT
    nodes = sum(sizes) * rows
    depth = blocks[0].shape[1]
    columns = depth
    layer_one = norm is None
    first = carried is None
    ins = [pl.BlockSpec((rows, depth), lambda i, ids: (i, 0)) for _ in blocks]
    where = (lambda i, ids: (ids[0], 0), lambda i, ids: (0, 0), lambda i, ids: (ids[4], 0), lambda i, ids: (0, 0))
    ins += [pl.BlockSpec((depth, columns), w) for w in where]
    args = [*blocks, *pieces]
    out_specs = [pl.BlockSpec((rows, columns), lambda i, ids: (i + base, 0))]
    out_shape = [jax.ShapeDtypeStruct((nodes, columns), F32)]
    small = pl.BlockSpec((8, columns), lambda i, ids: (0, 0))
    if not layer_one:
        lin, val, g, gamma, beta = norm
        ins += [
            pl.BlockSpec((rows, columns), lambda i, ids: (i + base, 0)),
            pl.BlockSpec((step, SLOT, SLOT), lambda i, ids: (i + base, 0, 0)),
            pl.BlockSpec(g.shape, lambda i, ids: (0, 0, 0)),
            pl.BlockSpec(gamma.shape, lambda i, ids: (0, 0)),
            pl.BlockSpec(beta.shape, lambda i, ids: (0, 0)),
        ]
        args += [lin, val, g, gamma, beta]
        out_specs.append(small)
        out_shape.append(jax.ShapeDtypeStruct((8, columns), F32))
    aliases = {}
    if not first:
        if not layer_one:
            ins.append(small)
            args.append(carried[1])
        ins.append(ANY)
        args.append(carried[0])
        aliases = {len(args): 0}
    return pl.pallas_call(
        functools.partial(backward_kernel, layer_one, first),
        grid_spec=pltpu.PrefetchScalarGridSpec(
            num_scalar_prefetch=1, grid=(steps,), in_specs=ins, out_specs=out_specs
        ),
        out_shape=out_shape,
        input_output_aliases=aliases,
        compiler_params=params(),
        cost_estimate=cost(2 * steps * rows * 4 * depth * columns, steps * rows * (8 * depth + 4 * columns) + 8 * depth * columns),
        name=f"backward_{1 if layer_one else 2}_{k}",
    )(ids, *args)


def weight_kernel(spans, ids_ref, x_ref, *refs):
    hs, out_ref = refs[:-1], refs[-1]
    total = None
    for (low, high), h_ref in zip(spans, hs):
        term = lax.dot_general(
            x_ref[0, low:high, :], h_ref[...], (((0,), (0,)), ((), ())), preferred_element_type=F32
        )
        total = term if total is None else total + term
    out_ref[...] = total.astype(out_ref.dtype)


def weight_terms(ids, everything, hs):
    _, nodes, depth = everything.shape
    columns = hs[0].shape[1]
    spans, low = [], 0
    for h in hs:
        spans.append((low, low + h.shape[0]))
        low += h.shape[0]
    return pl.pallas_call(
        functools.partial(weight_kernel, tuple(spans)),
        grid_spec=pltpu.PrefetchScalarGridSpec(
            num_scalar_prefetch=1,
            grid=(4,),
            in_specs=[pl.BlockSpec((1, nodes, depth), lambda i, ids: (i, 0, 0))]
            + [pl.BlockSpec(h.shape, lambda i, ids: (0, 0)) for h in hs],
            out_specs=pl.BlockSpec((depth, columns), lambda i, ids: (ids[i], 0)),
        ),
        out_shape=jax.ShapeDtypeStruct((4 * depth, columns), BF),
        compiler_params=params(),
        cost_estimate=cost(8 * nodes * depth * columns, 10 * nodes * depth + 8 * depth * columns),
        name="weight_terms",
    )(ids, everything, *hs)


def across(value, axis, distance):
    size = lax.axis_size(axis)
    return lax.ppermute(value, axis, [(i, i ^ distance) for i in range(size)])


def gather_chunks(chunks):
    far = [across(c, "col", 2) for c in chunks]
    near = [across(c, "col", 1) for c in chunks]
    beyond = [across(c, "col", 1) for c in far]
    return [list(blocks) for blocks in zip(chunks, near, far, beyond)]


def weight_rows(weight, q):
    depth = weight.shape[0] // 4
    low, high = q % 2, q // 2
    sent = lax.dynamic_slice_in_dim(weight, (1 - high) * 2 * depth, 2 * depth, 0)
    got = across(sent, "col", 2)
    near = across(lax.dynamic_slice_in_dim(weight, (q ^ 1) * depth, depth, 0), "col", 1)
    beyond = across(lax.dynamic_slice_in_dim(got, (1 - low) * depth, depth, 0), "col", 1)
    return [weight, near, got, beyond]


def reduce_rows(value, axis):
    size = lax.axis_size(axis)
    bits = size.bit_length() - 1
    place = lax.axis_index(axis)
    orders = [list(range(bits)), list(range(1, bits)) + [0]]
    held = list(jnp.split(value, 2, axis=0))
    for s in range(bits):
        for n, order in enumerate(orders):
            bit = (place >> order[s]) & 1
            half = held[n].shape[0] // 2
            keep = lax.dynamic_slice_in_dim(held[n], bit * half, half, 0)
            send = lax.dynamic_slice_in_dim(held[n], (1 - bit) * half, half, 0)
            got = across(send, axis, 1 << order[s])
            held[n] = (keep.astype(F32) + got.astype(F32)).astype(value.dtype)
    for s in reversed(range(bits)):
        for n, order in enumerate(orders):
            bit = (place >> order[s]) & 1
            got = across(held[n], axis, 1 << order[s])
            held[n] = jnp.concatenate(
                [jnp.where(bit == 0, held[n], got), jnp.where(bit == 0, got, held[n])], axis=0
            )
    return jnp.concatenate(held, axis=0).astype(F32)


def chunk_plan(slots):
    step = 2 if slots % 2 == 0 else 1
    total = slots // step
    sizes = []
    while total > 0:
        sizes.append(min(2, total))
        total -= sizes[-1]
    starts = [sum(sizes[:k]) for k in range(len(sizes))]
    return step, starts, sizes


def local(
    features,
    neighbours,
    node_valid,
    weight_one,
    gamma_one,
    beta_one,
    weight_two,
    gamma_two,
    beta_two,
    cotangent,
):
    nodes, columns = features.shape
    plan = chunk_plan(nodes // SLOT)
    step, starts, sizes = plan
    count = len(sizes)
    q = lax.axis_index("col")
    ids = jnp.stack([q, q ^ 1, q ^ 2, q ^ 3, q % 2]).astype(jnp.int32)
    g1, b1, g2, b2 = (v.reshape(1, columns) for v in (gamma_one, beta_one, gamma_two, beta_two))

    rows = [(starts[k] * step * SLOT, (starts[k] + sizes[k]) * step * SLOT) for k in range(count)]
    far = [across(features[a:b], "col", 2) for a, b in rows]
    near = across(features, "col", 1)
    beyond = [across(c, "col", 1) for c in far]
    tiles = build_tiles(neighbours, node_valid)
    _, ht, inv, val = tiles

    carried = None
    for k in range(count):
        carried = forward_chunk(ids, plan, k, [features, near, far[k], beyond[k]], weight_one, tiles, carried)
    lin_one, all_one, stats = carried
    norm_one = small_gather(stats, "row")
    rows_two = weight_rows(weight_two, q)

    hidden = [
        rows_call(hidden_kernel, plan, k, [lin_one], [val], [norm_one, g1, b1], BF, False, f"hidden_{k}", 12)
        for k in range(count)
    ]
    gathered = gather_chunks(hidden)
    carried = None
    for k in range(count):
        carried = forward_chunk(ids, plan, k, gathered[k], weight_two, tiles, carried)
    lin_two, all_two, stats = carried
    norm_two = small_gather(stats, "row")
    rows_one = weight_rows(weight_one, q)

    sums = rows_call(
        sums_kernel, plan, None, [lin_two, cotangent], [val], [norm_two, g2, b2], None, False, "sums_two", 20
    )
    grads_two = small_gather(sums, "row")
    turned = [
        rows_call(
            functools.partial(turn_kernel, step, True),
            plan, k, [lin_two, cotangent], [val, inv, ht], [norm_two, grads_two, g2, b2], BF, False, f"turn_two_{k}", 500,
        )
        for k in range(count)
    ]
    gathered = gather_chunks(turned)
    output = rows_call(hidden_kernel, plan, None, [lin_two], [val], [norm_two, g2, b2], F32, False, "output", 12)
    terms_two = weight_terms(ids, all_two, turned)
    grad_weight_two = lax.psum(terms_two, "row").astype(F32)

    carried = None
    for k in range(count):
        carried = backward_chunk(ids, plan, k, gathered[k], rows_two, (lin_one, val, norm_one, g1, b1), carried)
    grad_one, sums = carried
    grads_one = small_gather(sums, "row")
    turned = [
        rows_call(
            functools.partial(turn_kernel, step, False),
            plan, k, [lin_one, grad_one], [val, inv, ht], [norm_one, grads_one, g1, b1], BF, False, f"turn_one_{k}", 500,
        )
        for k in range(count)
    ]
    gathered = gather_chunks(turned)
    terms_one = weight_terms(ids, all_one, turned)
    grad_weight_one = reduce_rows(terms_one, "row")
    carried = None
    for k in range(count):
        carried = backward_chunk(ids, plan, k, gathered[k], rows_one, None, carried)
    (grad_features,) = carried

    sums_one, sums_two = jnp.sum(grads_one, axis=0), jnp.sum(grads_two, axis=0)
    return (
        output,
        grad_features,
        grad_weight_one,
        sums_one[1],
        sums_one[0],
        grad_weight_two,
        sums_two[1],
        sums_two[0],
    )


def solution(mesh):
    placed = (
        P("row", "col"),
        P("row", None),
        P("row"),
        P(None, "col"),
        P("col"),
        P("col"),
        P(None, "col"),
        P("col"),
        P("col"),
        P("row", "col"),
    )
    return jax.shard_map(
        local,
        mesh=mesh,
        in_specs=placed,
        out_specs=(
            P("row", "col"),
            P("row", "col"),
            P(None, "col"),
            P("col"),
            P("col"),
            P(None, "col"),
            P("col"),
            P("col"),
        ),
        check_vma=False,
    )
```

time: 857 us -> 473 us (0.55)
  waiting for transfers between devices: 568 us -> 205 us
  Pallas kernels: 0 us -> 134 us
  blocking collectives: 118 us -> 23.3 us
  matrix products: 78.2 us -> 0 us
  starting transfers between devices: 0.87 us -> 50.9 us
  other arithmetic: 57.2 us -> 10.6 us
  local copies, waits for them, and re-layouts: 18.1 us -> 33.1 us
    psum x1, waiting for transfers between devices: 267 us -> 46.7 us  [local(): grad_weight_two = lax.psum(terms_two, 'row').astype(F32)]
    reduce_scatter x2 -> x0, waiting for transfers between devices: 197 us -> none  [backward_layer(): lax.psum_scatter(partial_terms, 'col', scatter_dimension=1, tiled=True)]
    ppermute x0 -> x63, waiting for transfers between devices: none -> 155 us  [across(): return lax.ppermute(value, axis, [(i, i ^ distance) for i in range(size)])]
    pallas_call x0 -> x33, Pallas kernels: none -> 134 us  [the longest x8 42.4 us: forward_chunk(): pl.pallas_call(functools.partial(forward_kernel, step, first), grid_spec=...]
    psum x6 -> x0, blocking collectives: 118 us -> none  [the longest x2 43.4 us: moments(): lax.psum((jnp.sum(valid), jnp.sum(valid * linear, axis=0)), 'row')]
    all_gather x2 -> x0, waiting for transfers between devices: 105 us -> none  [forward_layer(): gathered = lax.all_gather(mixed, 'col', axis=1, tiled=True)]
    dot_general x10 -> x0, matrix products: 78.2 us -> none  [the longest x2 20.4 us: backward_layer(): lax.dot_general(gathered, grad_low, (((0,), (0,)), ((), ())), preferred_e...]
    ppermute x0 -> x63, starting transfers between devices: none -> 43.7 us  [across(): return lax.ppermute(value, axis, [(i, i ^ distance) for i in range(size)])]
  transfers between devices with their start and end apart: 5 -> 66, of which waited for: 5 -> 22; matrix products, arithmetic and copies ran while one was open for 3% -> 6% of each run, Pallas kernels for 0% -> 27%
where the time goes in v1:
time: 473 us; the launch traced here: 472 us
  waiting for transfers between devices  205 us (43%)
  Pallas kernels  134 us (28%)
  starting transfers between devices  50.9 us (11%)
  local copies, waits for them, and re-layouts  33.1 us (7%)
  blocking collectives  23.3 us (5%)
  between operations  14.8 us (3%)
  other arithmetic  10.6 us (2%)
    ppermute x63, waiting for transfers between devices, across(): return lax.ppermute(value, axis, [(i, i ^ distance) for i in range(size)])  155 us
    psum x1, waiting for transfers between devices, local(): grad_weight_two = lax.psum(terms_two, 'row').astype(F32)  46.7 us
    ppermute x63, starting transfers between devices, across(): return lax.ppermute(value, axis, [(i, i ^ distance) for i in range(size)])  43.7 us
    pallas_call x8, Pallas kernels, forward_chunk(): pl.pallas_call(functools.partial(forward_kernel, step, first), grid_spec=...  42.4 us
    pallas_call x8, Pallas kernels, backward_chunk(): pl.pallas_call(functools.partial(backward_kernel, layer_one, first), grid...  36.1 us
    pallas_call x14, Pallas kernels, rows_call(): pl.pallas_call(kernel, grid=(steps,), in_specs=ins, out_specs=out_spec, o...  35.8 us
    all_to_all x2, blocking collectives, small_gather(): return lax.all_to_all(copies, axis, split_axis=0, concat_axis=0, tiled=True)  23.3 us
    unnamed x94, local copies, waits for them, and re-layouts  14.8 us
  transfers between devices with their start and end apart: 66, of which 22 were waited for; matrix products, arithmetic and copies ran while one was open for 6% of the time, Pallas kernels for 27%

profile of v1, /device:TPU:0, one launch (start us, length us, event | category | flops | bytes accessed | tf_op | source)
XLA Modules:
  0.0 471.5 jit_solution(15867720152130494472)
XLA Ops:
  14.0 10.8 %collective-permute-done.7.refs_3_ = bf16[512,512]{1,0:T(8,128)(2,1)} collective-permute-done((bf16[512,512]{1,0:T(8,128)(2,1)S(1)}, bf16[512,512]{1,0:T(8,128)(2,1)}, u32[]{:S(2)}, u32[]{:S(2)}) %collective-permute-start.7) | collective-permute-done | bytes 524320 | tf_op jit(solution)/shard_map/ppermute | solution.py:382
  24.8 11.2 %collective-permute-done.5.refs_3_ = bf16[512,512]{1,0:T(8,128)(2,1)} collective-permute-done((bf16[512,512]{1,0:T(8,128)(2,1)S(1)}, bf16[512,512]{1,0:T(8,128)(2,1)}, u32[]{:S(2)}, u32[]{:S(2)}) %collective-permute-start.5) | collective-permute-done | bytes 524320 | tf_op jit(solution)/shard_map/ppermute | solution.py:382
  36.0 10.8 %collective-permute-done.3.refs_3_ = bf16[512,512]{1,0:T(8,128)(2,1)S(1)} collective-permute-done((bf16[512,512]{1,0:T(8,128)(2,1)S(1)}, bf16[512,512]{1,0:T(8,128)(2,1)S(1)}, u32[]{:S(2)}, u32[]{:S(2)}) %collective-permute-start.3) | collective-permute-done | bytes 524320 | tf_op jit(solution)/shard_map/ppermute | solution.py:382
  50.4 5.1 %tiles.1 = (bf16[14,128,128]{2,1,0:T(8,128)(2,1)S(1)}, bf16[14,128,128]{2,1,0:T(8,128)(2,1)S(1)}, f32[14,128,128]{2,1,0:T(8,128)S(1)}, f32[14,128,128]{2,1,0:T(8,128)S(1)}) custom-call(s32[14,32,128]{2,1,0:T(8,128)S(1)} %bitcast_bitcast_fusion.nbr_ref, s32[14,1,128]{2,1,0:T(1,128)S(1)} %reshape.39.valid_ref), custom_call_target="tpu_custom_call" | custom-call | flops 22020096 | bytes 2752512 | tf_op jit(solution)/shard_map/tiles/pallas_call | solution.py:66
  57.6 5.7 %forward_0.2 = (f32[1792,512]{1,0:T(8,128)}, bf16[4,1792,512]{2,1,0:T(8,128)(2,1)}, f32[8,512]{1,0:T(8,128)S(1)}) custom-call(s32[5]{0:T(128)S(1)} %stack.23.refs_0_.ids_ref, bf16[1792,512]{1,0:T(8,128)(2,1)S(1)} %copy-done.11, bf16[1792,512]{1,0:T(8,128)(2,1)} %collective-permute-done.refs_2_, bf16[512,512]{1,0:T(8,128)(2,1)} %collective-permute-done.7.refs_3_, ...), custom_call_target="tpu_custom_call" | custom-call | flops 1073741824 | bytes 5242880 | tf_op jit(solution)/shard_map/forward_0/pallas_call | solution.py:173
  63.3 5.7 %forward_1.2 = (f32[1792,512]{1,0:T(8,128)}, bf16[4,1792,512]{2,1,0:T(8,128)(2,1)}, f32[8,512]{1,0:T(8,128)S(1)}) custom-call(s32[5]{0:T(128)S(1)} %stack.23.refs_0_.ids_ref, bf16[1792,512]{1,0:T(8,128)(2,1)S(1)} %copy-done.11, bf16[1792,512]{1,0:T(8,128)(2,1)} %collective-permute-done.refs_2_, ...), custom_call_target="tpu_custom_call", output_to_operand_aliasing={{0}: (13, {}), {1}: (14, {})} | custom-call | flops 1073741824 | bytes 5242880 | tf_op jit(solution)/shard_map/forward_1/pallas_call | solution.py:173
  69.0 5.5 %forward_2.2 = (f32[1792,512]{1,0:T(8,128)}, bf16[4,1792,512]{2,1,0:T(8,128)(2,1)}, f32[8,512]{1,0:T(8,128)S(1)}) custom-call(s32[5]{0:T(128)S(1)} %stack.23.refs_0_.ids_ref, bf16[1792,512]{1,0:T(8,128)(2,1)S(1)} %copy-done.11, bf16[1792,512]{1,0:T(8,128)(2,1)} %collective-permute-done.refs_2_, ...), custom_call_target="tpu_custom_call", output_to_operand_aliasing={{0}: (13, {}), {1}: (14, {})} | custom-call | flops 1073741824 | bytes 5242880 | tf_op jit(solution)/shard_map/forward_2/pallas_call | solution.py:173
  74.6 4.4 forward_3.2
  79.0 13.5 %all_to_all.20.g_ref.refs_11_ = f32[8,8,512]{2,1,0:T(8,128)S(1)} all-to-all(f32[8,8,512]{2,1,0:T(8,128)S(1)} %broadcast_in_dim.8), channel_id=1, replica_groups=mesh['row'=8,'col'=4] {'row'}, dimensions={0} | all-to-all | bytes 262144 | tf_op jit(solution)/shard_map/all_to_all | solution.py:96
  108.0 7.5 %collective-permute-done.19.refs_3_ = bf16[512,512]{1,0:T(8,128)(2,1)} collective-permute-done((bf16[512,512]{1,0:T(8,128)(2,1)}, bf16[512,512]{1,0:T(8,128)(2,1)}, u32[]{:S(2)}, u32[]{:S(2)}) %collective-permute-start.19) | collective-permute-done | bytes 524320 | tf_op jit(solution)/shard_map/ppermute | solution.py:382
  117.0 9.7 %collective-permute-done.16.refs_3_ = bf16[512,512]{1,0:T(8,128)(2,1)} collective-permute-done((bf16[512,512]{1,0:T(8,128)(2,1)}, bf16[512,512]{1,0:T(8,128)(2,1)}, u32[]{:S(2)}, u32[]{:S(2)}) %collective-permute-start.16) | collective-permute-done | bytes 524320 | tf_op jit(solution)/shard_map/ppermute | solution.py:382
  127.2 10.7 %collective-permute-done.13.refs_3_ = bf16[512,512]{1,0:T(8,128)(2,1)} collective-permute-done((bf16[512,512]{1,0:T(8,128)(2,1)}, bf16[512,512]{1,0:T(8,128)(2,1)}, u32[]{:S(2)}, u32[]{:S(2)}) %collective-permute-start.13) | collective-permute-done | bytes 524320 | tf_op jit(solution)/shard_map/ppermute | solution.py:382
  143.2 5.8 %forward_0.3 = (f32[1792,512]{1,0:T(8,128)}, bf16[4,1792,512]{2,1,0:T(8,128)(2,1)}, f32[8,512]{1,0:T(8,128)S(1)}) custom-call(s32[5]{0:T(128)S(1)} %stack.23.refs_0_.ids_ref, bf16[512,512]{1,0:T(8,128)(2,1)} %hidden_0.1.refs_1_, bf16[512,512]{1,0:T(8,128)(2,1)} %collective-permute-done.18.refs_2_, bf16[512,512]{1,0:T(8,128)(2,1)} %collective-permute-done.19.refs_3_, ...), custom_call_target="tpu_custom_call" | custom-call | flops 1073741824 | bytes 5242880 | tf_op jit(solution)/shard_map/forward_0/pallas_call | solution.py:173
  149.0 5.8 %forward_1.3 = (f32[1792,512]{1,0:T(8,128)}, bf16[4,1792,512]{2,1,0:T(8,128)(2,1)}, f32[8,512]{1,0:T(8,128)S(1)}) custom-call(s32[5]{0:T(128)S(1)} %stack.23.refs_0_.ids_ref, bf16[512,512]{1,0:T(8,128)(2,1)} %hidden_1.1.refs_1_, bf16[512,512]{1,0:T(8,128)(2,1)} %collective-permute-done.15.refs_2_, ...), custom_call_target="tpu_custom_call", output_to_operand_aliasing={{0}: (13, {}), {1}: (14, {})} | custom-call | flops 1073741824 | bytes 5242880 | tf_op jit(solution)/shard_map/forward_1/pallas_call | solution.py:173
  154.8 5.8 %forward_2.3 = (f32[1792,512]{1,0:T(8,128)}, bf16[4,1792,512]{2,1,0:T(8,128)(2,1)}, f32[8,512]{1,0:T(8,128)S(1)}) custom-call(s32[5]{0:T(128)S(1)} %stack.23.refs_0_.ids_ref, bf16[512,512]{1,0:T(8,128)(2,1)} %hidden_2.1.refs_1_, bf16[512,512]{1,0:T(8,128)(2,1)} %collective-permute-done.12.refs_2_, ...), custom_call_target="tpu_custom_call", output_to_operand_aliasing={{0}: (13, {}), {1}: (14, {})} | custom-call | flops 1073741824 | bytes 5242880 | tf_op jit(solution)/shard_map/forward_2/pallas_call | solution.py:173
  160.6 3.7 forward_3.3
  165.0 3.5 all-to-all-start.1
  172.8 3.2 all-to-all-done.1.g_ref
  177.5 6.6 %sums_two.1 = f32[8,512]{1,0:T(8,128)S(1)} custom-call(f32[1792,512]{1,0:T(8,128)} %get-tuple-element.67.lin_ref, bf16[1792,512]{1,0:T(8,128)(2,1)S(1)} %copy-done.12, f32[14,128,128]{2,1,0:T(8,128)S(1)} %get-tuple-element.46.refs_11_.val_ref.refs_10_, f32[8,8,512]{2,1,0:T(8,128)S(1)} %all-to-all-done.1.g_ref, f32[1,512]{1,0:T(1,128)S(1)} %bitcast.44, ...), custom_call_target="tpu_custom_call" | custom-call | flops 18350080 | bytes 7340032 | tf_op jit(solution)/shard_map/sums_two/pallas_call | solution.py:260
  184.2 9.8 %all_to_all.21.sg_ref = f32[8,8,512]{2,1,0:T(8,128)S(1)} all-to-all(f32[8,8,512]{2,1,0:T(8,128)S(1)} %broadcast_in_dim.10), channel_id=1, replica_groups=mesh['row'=8,'col'=4] {'row'}, dimensions={0} | all-to-all | bytes 262144 | tf_op jit(solution)/shard_map/all_to_all | solution.py:96
  198.2 3.3 turn_two_1.1.refs_1_
  203.1 3.3 turn_two_2.1.refs_1_.refs_2_
  210.4 27.8 %collective-permute-done.22.refs_3_ = bf16[256,512]{1,0:T(8,128)(2,1)S(1)} collective-permute-done((bf16[256,512]{1,0:T(8,128)(2,1)S(1)}, bf16[256,512]{1,0:T(8,128)(2,1)S(1)}, u32[]{:S(2)}, u32[]{:S(2)}) %collective-permute-start.22) | collective-permute-done | bytes 262176 | tf_op jit(solution)/shard_map/ppermute | solution.py:382
  245.6 4.2 output.1
  250.4 5.2 %backward_2_0.1 = (f32[1792,512]{1,0:T(8,128)}, f32[8,512]{1,0:T(8,128)S(1)}) custom-call(s32[5]{0:T(128)S(1)} %stack.23.refs_0_.ids_ref, bf16[512,512]{1,0:T(8,128)(2,1)S(1)} %copy-done.23, bf16[512,512]{1,0:T(8,128)(2,1)S(1)} %copy-done.32, bf16[512,512]{1,0:T(8,128)(2,1)} %collective-permute-done.34.refs_3_, ...), custom_call_target="tpu_custom_call" | custom-call | flops 1073741824 | bytes 5242880 | tf_op jit(solution)/shard_map/backward_2_0/pallas_call | solution.py:333
  255.9 5.4 %backward_2_1.1 = (f32[1792,512]{1,0:T(8,128)}, f32[8,512]{1,0:T(8,128)S(1)}) custom-call(s32[5]{0:T(128)S(1)} %stack.23.refs_0_.ids_ref, bf16[512,512]{1,0:T(8,128)(2,1)} %turn_two_1.1.refs_1_, bf16[512,512]{1,0:T(8,128)(2,1)} %collective-permute-done.30.refs_2_, ...), custom_call_target="tpu_custom_call", output_to_operand_aliasing={{0}: (15, {})} | custom-call | flops 1073741824 | bytes 5242880 | tf_op jit(solution)/shard_map/backward_2_1/pallas_call | solution.py:333
  261.6 5.4 %backward_2_2.1 = (f32[1792,512]{1,0:T(8,128)}, f32[8,512]{1,0:T(8,128)S(1)}) custom-call(s32[5]{0:T(128)S(1)} %stack.23.refs_0_.ids_ref, bf16[512,512]{1,0:T(8,128)(2,1)} %turn_two_2.1.refs_1_.refs_2_, bf16[512,512]{1,0:T(8,128)(2,1)} %collective-permute-done.27.refs_2_, ...), custom_call_target="tpu_custom_call", output_to_operand_aliasing={{0}: (15, {})} | custom-call | flops 1073741824 | bytes 5242880 | tf_op jit(solution)/shard_map/backward_2_2/pallas_call | solution.py:333
  267.0 4.0 backward_2_3.1
  271.6 3.4 all-to-all-start.3
  276.3 7.3 %weight_terms.3 = bf16[2048,512]{1,0:T(8,128)(2,1)S(1)} custom-call(s32[5]{0:T(128)S(1)} %stack.23.refs_0_.ids_ref, bf16[4,1792,512]{2,1,0:T(8,128)(2,1)} %get-tuple-element.79.x_ref, bf16[512,512]{1,0:T(8,128)(2,1)S(1)} %copy-done.24, bf16[512,512]{1,0:T(8,128)(2,1)} %turn_two_1.1.refs_1_, bf16[512,512]{1,0:T(8,128)(2,1)} %turn_two_2.1.refs_1_.refs_2_, ...), custom_call_target="tpu_custom_call" | custom-call | flops 3758096384 | bytes 11272192 | tf_op jit(solution)/shard_map/weight_terms/pallas_call | solution.py:364
  285.1 3.1 turn_one_0.1.refs_1_.refs_0_
  295.1 7.2 %weight_terms.2 = bf16[2048,512]{1,0:T(8,128)(2,1)S(1)} custom-call(s32[5]{0:T(128)S(1)} %stack.23.refs_0_.ids_ref, bf16[4,1792,512]{2,1,0:T(8,128)(2,1)} %get-tuple-element.78.x_ref, bf16[512,512]{1,0:T(8,128)(2,1)} %turn_one_0.1.refs_1_.refs_0_, bf16[512,512]{1,0:T(8,128)(2,1)S(1)} %turn_one_1.1.refs_1_, bf16[512,512]{1,0:T(8,128)(2,1)S(1)} %turn_one_2.1.refs_1_.refs_2_, ...), custom_call_target="tpu_custom_call" | custom-call | flops 3758096384 | bytes 11272192 | tf_op jit(solution)/shard_map/weight_terms/pallas_call | solution.py:364
  309.1 8.8 %collective-permute-done.51 = bf16[512,512]{1,0:T(8,128)(2,1)} collective-permute-done((bf16[512,512]{1,0:T(8,128)(2,1)}, bf16[512,512]{1,0:T(8,128)(2,1)}, u32[]{:S(2)}, u32[]{:S(2)}) %collective-permute-start.51) | collective-permute-done | bytes 524320 | tf_op jit(solution)/shard_map/ppermute | solution.py:382
  320.0 6.8 %collective-permute-done.57 = bf16[512,512]{1,0:T(8,128)(2,1)} collective-permute-done((bf16[512,512]{1,0:T(8,128)(2,1)}, bf16[512,512]{1,0:T(8,128)(2,1)}, u32[]{:S(2)}, u32[]{:S(2)}) %collective-permute-start.57) | collective-permute-done | bytes 524320 | tf_op jit(solution)/shard_map/ppermute | solution.py:382
  328.4 10.7 %collective-permute-done.52 = bf16[256,512]{1,0:T(8,128)(2,1)S(1)} collective-permute-done((bf16[256,512]{1,0:T(8,128)(2,1)S(1)}, bf16[256,512]{1,0:T(8,128)(2,1)S(1)}, u32[]{:S(2)}, u32[]{:S(2)}) %collective-permute-start.52) | collective-permute-done | bytes 262176 | tf_op jit(solution)/shard_map/ppermute | solution.py:382
  339.1 2.8 collective-permute-start.58
  342.0 10.9 %collective-permute-done.58 = bf16[256,512]{1,0:T(8,128)(2,1)S(1)} collective-permute-done((bf16[256,512]{1,0:T(8,128)(2,1)S(1)}, bf16[256,512]{1,0:T(8,128)(2,1)S(1)}, u32[]{:S(2)}, u32[]{:S(2)}) %collective-permute-start.58) | collective-permute-done | bytes 262176 | tf_op jit(solution)/shard_map/ppermute | solution.py:382
  353.7 46.7 %all-reduce.2.cloned.1.call-done = bf16[2048,512]{1,0:T(8,128)(2,1)} async-done(((bf16[2048,512]{1,0:T(8,128)(2,1)}), bf16[2048,512]{1,0:T(8,128)(2,1)}) %all-reduce.2.cloned.1.call-update) | async-done | bytes 2097168 | tf_op jit(solution)/shard_map/psum | solution.py:497
  400.4 4.2 convert_element_type.79
  406.1 3.5 collective-permute-done.59
  413.8 3.6 collective-permute-done.54
  422.5 4.4 collective-permute-done.46.refs_3_
  430.6 7.1 %collective-permute-done.43.refs_3_ = bf16[512,512]{1,0:T(8,128)(2,1)S(1)} collective-permute-done((bf16[512,512]{1,0:T(8,128)(2,1)S(1)}, bf16[512,512]{1,0:T(8,128)(2,1)S(1)}, u32[]{:S(2)}, u32[]{:S(2)}) %collective-permute-start.43) | collective-permute-done | bytes 524320 | tf_op jit(solution)/shard_map/ppermute | solution.py:382
  437.7 4.3 collective-permute-done.61
  445.5 4.3 backward_1_0.1.refs_9_
  449.8 4.2 backward_1_1.1.refs_9_
  454.0 4.3 backward_1_2.1.refs_9_
  458.3 3.3 backward_1_3.1
  (258 shorter events, 102.4 us)
Async XLA Ops:
  7.2 50.3 %collective-permute-start = (bf16[1792,512]{1,0:T(8,128)(2,1)}, bf16[1792,512]{1,0:T(8,128)(2,1)}, u32[]{:S(2)}, u32[]{:S(2)}) collective-permute-start(bf16[1792,512]{1,0:T(8,128)(2,1)} %refs_1_.7), channel_id=1, source_target_pairs={{0,1},{1,0},{2,3},{3,2},{4,5},{5,4},{6,7},{7,6},{8,9},{9,8},{10,11... | collective-permute-start | bytes 5505032 | tf_op jit(solution)/shard_map/ppermute | solution.py:382
  9.3 15.5 %collective-permute-start.7 = (bf16[512,512]{1,0:T(8,128)(2,1)S(1)}, bf16[512,512]{1,0:T(8,128)(2,1)}, u32[]{:S(2)}, u32[]{:S(2)}) collective-permute-start(bf16[512,512]{1,0:T(8,128)(2,1)S(1)} %get-tuple-element.82), channel_id=1, source_target_pairs={{0,2},{1,3},{2,0},{3,1},{4,6},{5,7},{6,4},{7,5},{8,10},{9,11},{10,... | collective-permute-start | bytes 1572872 | tf_op jit(solution)/shard_map/ppermute | solution.py:382
  11.9 24.1 %collective-permute-start.5 = (bf16[512,512]{1,0:T(8,128)(2,1)S(1)}, bf16[512,512]{1,0:T(8,128)(2,1)}, u32[]{:S(2)}, u32[]{:S(2)}) collective-permute-start(bf16[512,512]{1,0:T(8,128)(2,1)S(1)} %get-tuple-element.83), channel_id=1, source_target_pairs={{0,2},{1,3},{2,0},{3,1},{4,6},{5,7},{6,4},{7,5},{8,10},{9,11},{10,... | collective-permute-start | bytes 1572872 | tf_op jit(solution)/shard_map/ppermute | solution.py:382
  12.0 34.8 %collective-permute-start.3 = (bf16[512,512]{1,0:T(8,128)(2,1)S(1)}, bf16[512,512]{1,0:T(8,128)(2,1)S(1)}, u32[]{:S(2)}, u32[]{:S(2)}) collective-permute-start(bf16[512,512]{1,0:T(8,128)(2,1)S(1)} %get-tuple-element.84), channel_id=1, source_target_pairs={{0,2},{1,3},{2,0},{3,1},{4,6},{5,7},{6,4},{7,5},{8,10},{9,11},{10,... | collective-permute-start | bytes 1572872 | tf_op jit(solution)/shard_map/ppermute | solution.py:382
  24.8 32.7 %collective-permute-start.8 = (bf16[512,512]{1,0:T(8,128)(2,1)}, bf16[512,512]{1,0:T(8,128)(2,1)}, u32[]{:S(2)}, u32[]{:S(2)}) collective-permute-start(bf16[512,512]{1,0:T(8,128)(2,1)} %collective-permute-done.7.refs_3_), channel_id=1, source_target_pairs={{0,1},{1,0},{2,3},{3,2},{4,5},{5,4},{6,7},{7,6},{8,9},{9,8},{10,11... | collective-permute-start | bytes 1572872 | tf_op jit(solution)/shard_map/ppermute | solution.py:382
  36.0 27.3 %collective-permute-start.6 = (bf16[512,512]{1,0:T(8,128)(2,1)}, bf16[512,512]{1,0:T(8,128)(2,1)}, u32[]{:S(2)}, u32[]{:S(2)}) collective-permute-start(bf16[512,512]{1,0:T(8,128)(2,1)} %collective-permute-done.5.refs_3_), channel_id=1, source_target_pairs={{0,1},{1,0},{2,3},{3,2},{4,5},{5,4},{6,7},{7,6},{8,9},{9,8},{10,11... | collective-permute-start | bytes 1572872 | tf_op jit(solution)/shard_map/ppermute | solution.py:382
  46.8 22.2 %collective-permute-start.4 = (bf16[512,512]{1,0:T(8,128)(2,1)S(1)}, bf16[512,512]{1,0:T(8,128)(2,1)}, u32[]{:S(2)}, u32[]{:S(2)}) collective-permute-start(bf16[512,512]{1,0:T(8,128)(2,1)S(1)} %collective-permute-done.3.refs_3_), channel_id=1, source_target_pairs={{0,1},{1,0},{2,3},{3,2},{4,5},{5,4},{6,7},{7,6},{8,9},{9,8},{10,11... | collective-permute-start | bytes 1572872 | tf_op jit(solution)/shard_map/ppermute | solution.py:382
  57.5 17.0 %collective-permute-start.2 = (bf16[256,512]{1,0:T(8,128)(2,1)}, bf16[256,512]{1,0:T(8,128)(2,1)S(1)}, u32[]{:S(2)}, u32[]{:S(2)}) collective-permute-start(bf16[256,512]{1,0:T(8,128)(2,1)} %collective-permute-done.1.refs_3_), channel_id=1, source_target_pairs={{0,1},{1,0},{2,3},{3,2},{4,5},{5,4},{6,7},{7,6},{8,9},{9,8},{10,11... | collective-permute-start | bytes 786440 | tf_op jit(solution)/shard_map/ppermute | solution.py:382
  97.6 17.8 %collective-permute-start.19 = (bf16[512,512]{1,0:T(8,128)(2,1)}, bf16[512,512]{1,0:T(8,128)(2,1)}, u32[]{:S(2)}, u32[]{:S(2)}) collective-permute-start(bf16[512,512]{1,0:T(8,128)(2,1)} %hidden_0.1.refs_1_), channel_id=1, source_target_pairs={{0,2},{1,3},{2,0},{3,1},{4,6},{5,7},{6,4},{7,5},{8,10},{9,11},{10,... | collective-permute-start | bytes 1572872 | tf_op jit(solution)/shard_map/ppermute | solution.py:382
  98.2 18.8 %collective-permute-start.18 = (bf16[512,512]{1,0:T(8,128)(2,1)}, bf16[512,512]{1,0:T(8,128)(2,1)}, u32[]{:S(2)}, u32[]{:S(2)}) collective-permute-start(bf16[512,512]{1,0:T(8,128)(2,1)} %hidden_0.1.refs_1_), channel_id=1, source_target_pairs={{0,1},{1,0},{2,3},{3,2},{4,5},{5,4},{6,7},{7,6},{8,9},{9,8},{10,11... | collective-permute-start | bytes 1572872 | tf_op jit(solution)/shard_map/ppermute | solution.py:382
  99.4 27.3 %collective-permute-start.16 = (bf16[512,512]{1,0:T(8,128)(2,1)}, bf16[512,512]{1,0:T(8,128)(2,1)}, u32[]{:S(2)}, u32[]{:S(2)}) collective-permute-start(bf16[512,512]{1,0:T(8,128)(2,1)} %hidden_1.1.refs_1_), channel_id=1, source_target_pairs={{0,2},{1,3},{2,0},{3,1},{4,6},{5,7},{6,4},{7,5},{8,10},{9,11},{10,... | collective-permute-start | bytes 1572872 | tf_op jit(solution)/shard_map/ppermute | solution.py:382
  100.9 25.7 %collective-permute-start.15 = (bf16[512,512]{1,0:T(8,128)(2,1)}, bf16[512,512]{1,0:T(8,128)(2,1)}, u32[]{:S(2)}, u32[]{:S(2)}) collective-permute-start(bf16[512,512]{1,0:T(8,128)(2,1)} %hidden_1.1.refs_1_), channel_id=1, source_target_pairs={{0,1},{1,0},{2,3},{3,2},{4,5},{5,4},{6,7},{7,6},{8,9},{9,8},{10,11... | collective-permute-start | bytes 1572872 | tf_op jit(solution)/shard_map/ppermute | solution.py:382
  104.2 33.7 %collective-permute-start.13 = (bf16[512,512]{1,0:T(8,128)(2,1)}, bf16[512,512]{1,0:T(8,128)(2,1)}, u32[]{:S(2)}, u32[]{:S(2)}) collective-permute-start(bf16[512,512]{1,0:T(8,128)(2,1)} %hidden_2.1.refs_1_), channel_id=1, source_target_pairs={{0,2},{1,3},{2,0},{3,1},{4,6},{5,7},{6,4},{7,5},{8,10},{9,11},{10,... | collective-permute-start | bytes 1572872 | tf_op jit(solution)/shard_map/ppermute | solution.py:382
  115.5 55.2 %collective-permute-start.25 = (bf16[1024,512]{1,0:T(8,128)(2,1)}, bf16[1024,512]{1,0:T(8,128)(2,1)}, u32[]{:S(2)}, u32[]{:S(2)}) collective-permute-start(bf16[1024,512]{1,0:T(8,128)(2,1)} %constant_dynamic-slice_fusion.10), channel_id=1, source_target_pairs={{0,2},{1,3},{2,0},{3,1},{4,6},{5,7},{6,4},{7,5},{8,10},{9,11},{10,... | collective-permute-start | bytes 3145736 | tf_op jit(solution)/shard_map/ppermute | solution.py:382
  117.0 22.0 %collective-permute-start.12 = (bf16[512,512]{1,0:T(8,128)(2,1)}, bf16[512,512]{1,0:T(8,128)(2,1)}, u32[]{:S(2)}, u32[]{:S(2)}) collective-permute-start(bf16[512,512]{1,0:T(8,128)(2,1)} %hidden_2.1.refs_1_), channel_id=1, source_target_pairs={{0,1},{1,0},{2,3},{3,2},{4,5},{5,4},{6,7},{7,6},{8,9},{9,8},{10,11... | collective-permute-start | bytes 1572872 | tf_op jit(solution)/shard_map/ppermute | solution.py:382
  137.9 16.9 %collective-permute-start.14 = (bf16[512,512]{1,0:T(8,128)(2,1)}, bf16[512,512]{1,0:T(8,128)(2,1)}, u32[]{:S(2)}, u32[]{:S(2)}) collective-permute-start(bf16[512,512]{1,0:T(8,128)(2,1)} %collective-permute-done.13.refs_3_), channel_id=1, source_target_pairs={{0,1},{1,0},{2,3},{3,2},{4,5},{5,4},{6,7},{7,6},{8,9},{9,8},{10,11... | collective-permute-start | bytes 1572872 | tf_op jit(solution)/shard_map/ppermute | solution.py:382
  139.0 67.4 %collective-permute-start.40 = (bf16[1024,512]{1,0:T(8,128)(2,1)}, bf16[1024,512]{1,0:T(8,128)(2,1)}, u32[]{:S(2)}, u32[]{:S(2)}) collective-permute-start(bf16[1024,512]{1,0:T(8,128)(2,1)} %constant_dynamic-slice_fusion.7), channel_id=1, source_target_pairs={{0,2},{1,3},{2,0},{3,1},{4,6},{5,7},{6,4},{7,5},{8,10},{9,11},{10,... | collective-permute-start | bytes 3145736 | tf_op jit(solution)/shard_map/ppermute | solution.py:382
  140.5 20.1 %collective-permute-start.9 = (bf16[256,512]{1,0:T(8,128)(2,1)S(1)}, bf16[256,512]{1,0:T(8,128)(2,1)S(1)}, u32[]{:S(2)}, u32[]{:S(2)}) collective-permute-start(bf16[256,512]{1,0:T(8,128)(2,1)S(1)} %hidden_3.1.refs_1_), channel_id=1, source_target_pairs={{0,1},{1,0},{2,3},{3,2},{4,5},{5,4},{6,7},{7,6},{8,9},{9,8},{10,11... | collective-permute-start | bytes 786440 | tf_op jit(solution)/shard_map/ppermute | solution.py:382
  140.7 19.9 %collective-permute-start.11 = (bf16[256,512]{1,0:T(8,128)(2,1)}, bf16[256,512]{1,0:T(8,128)(2,1)S(1)}, u32[]{:S(2)}, u32[]{:S(2)}) collective-permute-start(bf16[256,512]{1,0:T(8,128)(2,1)} %collective-permute-done.10.refs_3_), channel_id=1, source_target_pairs={{0,1},{1,0},{2,3},{3,2},{4,5},{5,4},{6,7},{7,6},{8,9},{9,8},{10,11... | collective-permute-start | bytes 786440 | tf_op jit(solution)/shard_map/ppermute | solution.py:382
  170.4 36.0 %collective-permute-start.24 = (bf16[512,512]{1,0:T(8,128)(2,1)}, bf16[512,512]{1,0:T(8,128)(2,1)}, u32[]{:S(2)}, u32[]{:S(2)}) collective-permute-start(bf16[512,512]{1,0:T(8,128)(2,1)} %constant_dynamic-slice_fusion.11), channel_id=1, source_target_pairs={{0,1},{1,0},{2,3},{3,2},{4,5},{5,4},{6,7},{7,6},{8,9},{9,8},{10,11... | collective-permute-start | bytes 1572872 | tf_op jit(solution)/shard_map/ppermute | solution.py:382
  172.5 36.3 %collective-permute-start.26 = (bf16[512,512]{1,0:T(8,128)(2,1)}, bf16[512,512]{1,0:T(8,128)(2,1)}, u32[]{:S(2)}, u32[]{:S(2)}) collective-permute-start(bf16[512,512]{1,0:T(8,128)(2,1)} %constant_dynamic-slice_fusion.9), channel_id=1, source_target_pairs={{0,1},{1,0},{2,3},{3,2},{4,5},{5,4},{6,7},{7,6},{8,9},{9,8},{10,11... | collective-permute-start | bytes 1572872 | tf_op jit(solution)/shard_map/ppermute | solution.py:382
  197.7 40.5 %collective-permute-start.34 = (bf16[512,512]{1,0:T(8,128)(2,1)S(1)}, bf16[512,512]{1,0:T(8,128)(2,1)}, u32[]{:S(2)}, u32[]{:S(2)}) collective-permute-start(bf16[512,512]{1,0:T(8,128)(2,1)S(1)} %turn_two_0.1.refs_1_.refs_0_), channel_id=1, source_target_pairs={{0,2},{1,3},{2,0},{3,1},{4,6},{5,7},{6,4},{7,5},{8,10},{9,11},{10,... | collective-permute-start | bytes 1572872 | tf_op jit(solution)/shard_map/ppermute | solution.py:382
  201.5 37.1 %collective-permute-start.31 = (bf16[512,512]{1,0:T(8,128)(2,1)}, bf16[512,512]{1,0:T(8,128)(2,1)}, u32[]{:S(2)}, u32[]{:S(2)}) collective-permute-start(bf16[512,512]{1,0:T(8,128)(2,1)} %turn_two_1.1.refs_1_), channel_id=1, source_target_pairs={{0,2},{1,3},{2,0},{3,1},{4,6},{5,7},{6,4},{7,5},{8,10},{9,11},{10,... | collective-permute-start | bytes 1572872 | tf_op jit(solution)/shard_map/ppermute | solution.py:382
  206.4 32.4 %collective-permute-start.33 = (bf16[512,512]{1,0:T(8,128)(2,1)S(1)}, bf16[512,512]{1,0:T(8,128)(2,1)S(1)}, u32[]{:S(2)}, u32[]{:S(2)}) collective-permute-start(bf16[512,512]{1,0:T(8,128)(2,1)S(1)} %turn_two_0.1.refs_1_.refs_0_), channel_id=1, source_target_pairs={{0,1},{1,0},{2,3},{3,2},{4,5},{5,4},{6,7},{7,6},{8,9},{9,8},{10,11... | collective-permute-start | bytes 1572872 | tf_op jit(solution)/shard_map/ppermute | solution.py:382
  206.4 33.6 %collective-permute-start.28 = (bf16[512,512]{1,0:T(8,128)(2,1)}, bf16[512,512]{1,0:T(8,128)(2,1)}, u32[]{:S(2)}, u32[]{:S(2)}) collective-permute-start(bf16[512,512]{1,0:T(8,128)(2,1)} %turn_two_2.1.refs_1_.refs_2_), channel_id=1, source_target_pairs={{0,2},{1,3},{2,0},{3,1},{4,6},{5,7},{6,4},{7,5},{8,10},{9,11},{10,... | collective-permute-start | bytes 1572872 | tf_op jit(solution)/shard_map/ppermute | solution.py:382
  208.8 29.4 %collective-permute-start.22 = (bf16[256,512]{1,0:T(8,128)(2,1)S(1)}, bf16[256,512]{1,0:T(8,128)(2,1)S(1)}, u32[]{:S(2)}, u32[]{:S(2)}) collective-permute-start(bf16[256,512]{1,0:T(8,128)(2,1)S(1)} %turn_two_3.1.refs_1_.refs_3_), channel_id=1, source_target_pairs={{0,2},{1,3},{2,0},{3,1},{4,6},{5,7},{6,4},{7,5},{8,10},{9,11},{10,... | collective-permute-start | bytes 786440 | tf_op jit(solution)/shard_map/ppermute | solution.py:382
  238.7 16.9 %collective-permute-start.32 = (bf16[512,512]{1,0:T(8,128)(2,1)}, bf16[512,512]{1,0:T(8,128)(2,1)}, u32[]{:S(2)}, u32[]{:S(2)}) collective-permute-start(bf16[512,512]{1,0:T(8,128)(2,1)} %collective-permute-done.31.refs_3_), channel_id=1, source_target_pairs={{0,1},{1,0},{2,3},{3,2},{4,5},{5,4},{6,7},{7,6},{8,9},{9,8},{10,11... | collective-permute-start | bytes 1572872 | tf_op jit(solution)/shard_map/ppermute | solution.py:382
  239.7 21.7 %collective-permute-start.27 = (bf16[512,512]{1,0:T(8,128)(2,1)}, bf16[512,512]{1,0:T(8,128)(2,1)}, u32[]{:S(2)}, u32[]{:S(2)}) collective-permute-start(bf16[512,512]{1,0:T(8,128)(2,1)} %turn_two_2.1.refs_1_.refs_2_), channel_id=1, source_target_pairs={{0,1},{1,0},{2,3},{3,2},{4,5},{5,4},{6,7},{7,6},{8,9},{9,8},{10,11... | collective-permute-start | bytes 1572872 | tf_op jit(solution)/shard_map/ppermute | solution.py:382
  240.0 21.6 %collective-permute-start.29 = (bf16[512,512]{1,0:T(8,128)(2,1)}, bf16[512,512]{1,0:T(8,128)(2,1)}, u32[]{:S(2)}, u32[]{:S(2)}) collective-permute-start(bf16[512,512]{1,0:T(8,128)(2,1)} %collective-permute-done.28.refs_3_), channel_id=1, source_target_pairs={{0,1},{1,0},{2,3},{3,2},{4,5},{5,4},{6,7},{7,6},{8,9},{9,8},{10,11... | collective-permute-start | bytes 1572872 | tf_op jit(solution)/shard_map/ppermute | solution.py:382
  249.8 17.2 %collective-permute-start.21 = (bf16[256,512]{1,0:T(8,128)(2,1)S(1)}, bf16[256,512]{1,0:T(8,128)(2,1)S(1)}, u32[]{:S(2)}, u32[]{:S(2)}) collective-permute-start(bf16[256,512]{1,0:T(8,128)(2,1)S(1)} %turn_two_3.1.refs_1_.refs_3_), channel_id=1, source_target_pairs={{0,1},{1,0},{2,3},{3,2},{4,5},{5,4},{6,7},{7,6},{8,9},{9,8},{10,11... | collective-permute-start | bytes 786440 | tf_op jit(solution)/shard_map/ppermute | solution.py:382
  250.2 16.8 %collective-permute-start.23 = (bf16[256,512]{1,0:T(8,128)(2,1)S(1)}, bf16[256,512]{1,0:T(8,128)(2,1)S(1)}, u32[]{:S(2)}, u32[]{:S(2)}) collective-permute-start(bf16[256,512]{1,0:T(8,128)(2,1)S(1)} %copy-done.36), channel_id=1, source_target_pairs={{0,1},{1,0},{2,3},{3,2},{4,5},{5,4},{6,7},{7,6},{8,9},{9,8},{10,11... | collective-permute-start | bytes 786440 | tf_op jit(solution)/shard_map/ppermute | solution.py:382
  255.5 156.5 %collective-permute-start.39 = (bf16[512,512]{1,0:T(8,128)(2,1)}, bf16[512,512]{1,0:T(8,128)(2,1)S(1)}, u32[]{:S(2)}, u32[]{:S(2)}) collective-permute-start(bf16[512,512]{1,0:T(8,128)(2,1)} %constant_dynamic-slice_fusion.8), channel_id=1, source_target_pairs={{0,1},{1,0},{2,3},{3,2},{4,5},{5,4},{6,7},{7,6},{8,9},{9,8},{10,11... | collective-permute-start | bytes 1572872 | tf_op jit(solution)/shard_map/ppermute | solution.py:382
  261.3 150.8 %collective-permute-start.41 = (bf16[512,512]{1,0:T(8,128)(2,1)}, bf16[512,512]{1,0:T(8,128)(2,1)}, u32[]{:S(2)}, u32[]{:S(2)}) collective-permute-start(bf16[512,512]{1,0:T(8,128)(2,1)} %constant_dynamic-slice_fusion.6), channel_id=1, source_target_pairs={{0,1},{1,0},{2,3},{3,2},{4,5},{5,4},{6,7},{7,6},{8,9},{9,8},{10,11... | collective-permute-start | bytes 1572872 | tf_op jit(solution)/shard_map/ppermute | solution.py:382
  275.0 125.4 %all-reduce.2.cloned.1.call-start = ((), (), s32[]{:S(2)}) async-start(), calls=%async_computation.4 | async-start | bytes 4194304 | tf_op jit(solution)/shard_map/psum | solution.py:497
  303.4 14.5 %collective-permute-start.51 = (bf16[512,512]{1,0:T(8,128)(2,1)}, bf16[512,512]{1,0:T(8,128)(2,1)}, u32[]{:S(2)}, u32[]{:S(2)}) collective-permute-start(bf16[512,512]{1,0:T(8,128)(2,1)} %constant_dynamic-slice_fusion.5), channel_id=1, source_target_pairs={{0,4},{4,0},{8,12},{12,8},{16,20},{20,16},{24,28},{28,24},{1,5},{5... | collective-permute-start | bytes 1572872 | tf_op jit(solution)/shard_map/ppermute | solution.py:382
  305.6 113.3 %collective-permute-start.49 = (bf16[512,512]{1,0:T(8,128)(2,1)}, bf16[512,512]{1,0:T(8,128)(2,1)S(1)}, u32[]{:S(2)}, u32[]{:S(2)}) collective-permute-start(bf16[512,512]{1,0:T(8,128)(2,1)} %turn_one_0.1.refs_1_.refs_0_), channel_id=1, source_target_pairs={{0,2},{1,3},{2,0},{3,1},{4,6},{5,7},{6,4},{7,5},{8,10},{9,11},{10,... | collective-permute-start | bytes 1572872 | tf_op jit(solution)/shard_map/ppermute | solution.py:382
  307.1 19.7 %collective-permute-start.57 = (bf16[512,512]{1,0:T(8,128)(2,1)}, bf16[512,512]{1,0:T(8,128)(2,1)}, u32[]{:S(2)}, u32[]{:S(2)}) collective-permute-start(bf16[512,512]{1,0:T(8,128)(2,1)} %constant_dynamic-slice_fusion.2), channel_id=1, source_target_pairs={{0,8},{4,12},{8,0},{12,4},{16,24},{20,28},{24,16},{28,20},{1,9},{5... | collective-permute-start | bytes 1572872 | tf_op jit(solution)/shard_map/ppermute | solution.py:382
  317.9 95.8 %collective-permute-start.37 = (bf16[256,512]{1,0:T(8,128)(2,1)S(1)}, bf16[256,512]{1,0:T(8,128)(2,1)S(1)}, u32[]{:S(2)}, u32[]{:S(2)}) collective-permute-start(bf16[256,512]{1,0:T(8,128)(2,1)S(1)} %turn_one_3.1.refs_1_.refs_3_), channel_id=1, source_target_pairs={{0,2},{1,3},{2,0},{3,1},{4,6},{5,7},{6,4},{7,5},{8,10},{9,11},{10,... | collective-permute-start | bytes 786440 | tf_op jit(solution)/shard_map/ppermute | solution.py:382
  352.9 51.7 %collective-permute-start.53 = (bf16[128,512]{1,0:T(8,128)(2,1)S(1)}, bf16[128,512]{1,0:T(8,128)(2,1)S(1)}, u32[]{:S(2)}, u32[]{:S(2)}) collective-permute-start(bf16[128,512]{1,0:T(8,128)(2,1)S(1)} %constant_dynamic-slice_fusion.3), channel_id=1, source_target_pairs={{0,16},{4,20},{8,24},{12,28},{16,0},{20,4},{24,8},{28,12},{1,17},{... | collective-permute-start | bytes 393224 | tf_op jit(solution)/shard_map/ppermute | solution.py:382
  412.1 14.8 %collective-permute-start.46 = (bf16[512,512]{1,0:T(8,128)(2,1)S(1)}, bf16[512,512]{1,0:T(8,128)(2,1)S(1)}, u32[]{:S(2)}, u32[]{:S(2)}) collective-permute-start(bf16[512,512]{1,0:T(8,128)(2,1)S(1)} %copy-done.28), channel_id=1, source_target_pairs={{0,2},{1,3},{2,0},{3,1},{4,6},{5,7},{6,4},{7,5},{8,10},{9,11},{10,... | collective-permute-start | bytes 1572872 | tf_op jit(solution)/shard_map/ppermute | solution.py:382
  419.0 18.7 %collective-permute-start.43 = (bf16[512,512]{1,0:T(8,128)(2,1)S(1)}, bf16[512,512]{1,0:T(8,128)(2,1)S(1)}, u32[]{:S(2)}, u32[]{:S(2)}) collective-permute-start(bf16[512,512]{1,0:T(8,128)(2,1)S(1)} %copy-done.26), channel_id=1, source_target_pairs={{0,2},{1,3},{2,0},{3,1},{4,6},{5,7},{6,4},{7,5},{8,10},{9,11},{10,... | collective-permute-start | bytes 1572872 | tf_op jit(solution)/shard_map/ppermute | solution.py:382
  422.5 21.4 %collective-permute-start.42 = (bf16[512,512]{1,0:T(8,128)(2,1)S(1)}, bf16[512,512]{1,0:T(8,128)(2,1)S(1)}, u32[]{:S(2)}, u32[]{:S(2)}) collective-permute-start(bf16[512,512]{1,0:T(8,128)(2,1)S(1)} %copy-done.26), channel_id=1, source_target_pairs={{0,1},{1,0},{2,3},{3,2},{4,5},{5,4},{6,7},{7,6},{8,9},{9,8},{10,11... | collective-permute-start | bytes 1572872 | tf_op jit(solution)/shard_map/ppermute | solution.py:382
  426.9 17.0 %collective-permute-start.50 = (bf16[512,512]{1,0:T(8,128)(2,1)S(1)}, bf16[512,512]{1,0:T(8,128)(2,1)S(1)}, u32[]{:S(2)}, u32[]{:S(2)}) collective-permute-start(bf16[512,512]{1,0:T(8,128)(2,1)S(1)} %collective-permute-done.49.refs_3_), channel_id=1, source_target_pairs={{0,1},{1,0},{2,3},{3,2},{4,5},{5,4},{6,7},{7,6},{8,9},{9,8},{10,11... | collective-permute-start | bytes 1572872 | tf_op jit(solution)/shard_map/ppermute | solution.py:382
  426.9 17.5 %collective-permute-start.47 = (bf16[512,512]{1,0:T(8,128)(2,1)S(1)}, bf16[512,512]{1,0:T(8,128)(2,1)S(1)}, u32[]{:S(2)}, u32[]{:S(2)}) collective-permute-start(bf16[512,512]{1,0:T(8,128)(2,1)S(1)} %collective-permute-done.46.refs_3_), channel_id=1, source_target_pairs={{0,1},{1,0},{2,3},{3,2},{4,5},{5,4},{6,7},{7,6},{8,9},{9,8},{10,11... | collective-permute-start | bytes 1572872 | tf_op jit(solution)/shard_map/ppermute | solution.py:382
  437.7 16.3 %collective-permute-start.44 = (bf16[512,512]{1,0:T(8,128)(2,1)S(1)}, bf16[512,512]{1,0:T(8,128)(2,1)S(1)}, u32[]{:S(2)}, u32[]{:S(2)}) collective-permute-start(bf16[512,512]{1,0:T(8,128)(2,1)S(1)} %collective-permute-done.43.refs_3_), channel_id=1, source_target_pairs={{0,1},{1,0},{2,3},{3,2},{4,5},{5,4},{6,7},{7,6},{8,9},{9,8},{10,11... | collective-permute-start | bytes 1572872 | tf_op jit(solution)/shard_map/ppermute | solution.py:382
  442.1 19.6 %collective-permute-start.56 = (bf16[512,512]{1,0:T(8,128)(2,1)S(1)}, bf16[512,512]{1,0:T(8,128)(2,1)S(1)}, u32[]{:S(2)}, u32[]{:S(2)}) collective-permute-start(bf16[512,512]{1,0:T(8,128)(2,1)S(1)} %pad_maximum_fusion), channel_id=1, source_target_pairs={{0,4},{4,0},{8,12},{12,8},{16,20},{20,16},{24,28},{28,24},{1,5},{5... | collective-permute-start | bytes 1572872 | tf_op jit(solution)/shard_map/ppermute | solution.py:382
  443.9 14.4 %collective-permute-start.36 = (bf16[256,512]{1,0:T(8,128)(2,1)S(1)}, bf16[256,512]{1,0:T(8,128)(2,1)S(1)}, u32[]{:S(2)}, u32[]{:S(2)}) collective-permute-start(bf16[256,512]{1,0:T(8,128)(2,1)S(1)} %turn_one_3.1.refs_1_.refs_3_), channel_id=1, source_target_pairs={{0,1},{1,0},{2,3},{3,2},{4,5},{5,4},{6,7},{7,6},{8,9},{9,8},{10,11... | collective-permute-start | bytes 786440 | tf_op jit(solution)/shard_map/ppermute | solution.py:382
  444.5 17.4 %collective-permute-start.62 = (bf16[512,512]{1,0:T(8,128)(2,1)S(1)}, bf16[512,512]{1,0:T(8,128)(2,1)S(1)}, u32[]{:S(2)}, u32[]{:S(2)}) collective-permute-start(bf16[512,512]{1,0:T(8,128)(2,1)S(1)} %pad_maximum_fusion.1), channel_id=1, source_target_pairs={{0,8},{4,12},{8,0},{12,4},{16,24},{20,28},{24,16},{28,20},{1,9},{5... | collective-permute-start | bytes 1572872 | tf_op jit(solution)/shard_map/ppermute | solution.py:382
  (65 other events, 826.7 us)
Sparse Core Ops, SparseCore 0:
  285.1 115.1 all-reduce.1

commit v2 on v1

v2 whole, which is shorter than its diff:
```python
import functools

import jax
import jax.numpy as jnp
from jax import lax
from jax.experimental import pallas as pl
from jax.experimental.pallas import tpu as pltpu
from jax.sharding import PartitionSpec as P

SLOT = 128
NBR = 32
LANES = 128
EPSILON = 1e-05
ANY = pl.BlockSpec(memory_space=pl.ANY)
BF = jnp.bfloat16
F32 = jnp.float32


def params(limit=48 << 20):
    return pltpu.CompilerParams(dimension_semantics=("arbitrary",), vmem_limit_bytes=limit)


def cost(flops, moved):
    return pl.CostEstimate(flops=int(flops) // 1000, bytes_accessed=int(moved) // 1000, transcendentals=0)


def dot(a, b):
    return jnp.dot(a, b, preferred_element_type=F32)


def dot_t(a, b):
    return lax.dot_general(a, b, (((1,), (1,)), ((), ())), preferred_element_type=F32)


def wide(v, columns):
    return jnp.concatenate([v] * (columns // LANES), axis=1)


def tiles_kernel(nbr_ref, valid_ref, h_ref, ht_ref, inv_ref, val_ref):
    entries = nbr_ref[0]
    rows = lax.broadcasted_iota(jnp.int32, (SLOT, SLOT), 0)
    cols = lax.broadcasted_iota(jnp.int32, (SLOT, SLOT), 1)
    hits = jnp.zeros((SLOT, SLOT), F32)
    degree = jnp.zeros((1, SLOT), F32)
    for k in range(entries.shape[0]):
        one = entries[k : k + 1, :]
        hits += (one == rows).astype(F32)
        degree += (one >= 0).astype(F32)
    eye = (rows == cols).astype(F32)
    joined = hits + eye
    counts = joined + joined * eye
    ht_ref[0] = wide(counts.astype(BF), 2 * SLOT)
    h_ref[0] = wide(counts.T.astype(BF), 2 * SLOT)
    inv_ref[0] = jnp.broadcast_to(1.0 / (degree + 1.0), (SLOT, SLOT)).T
    val_ref[0] = jnp.broadcast_to(valid_ref[0].astype(F32), (SLOT, SLOT)).T


def build_tiles(neighbours, node_valid):
    slots = neighbours.shape[0] // SLOT
    turned = neighbours.reshape(slots, SLOT, NBR).transpose(0, 2, 1)
    square = pl.BlockSpec((1, SLOT, SLOT), lambda i: (i, 0, 0))
    double = pl.BlockSpec((1, SLOT, 2 * SLOT), lambda i: (i, 0, 0))
    return pl.pallas_call(
        tiles_kernel,
        grid=(slots,),
        in_specs=[
            pl.BlockSpec((1, NBR, SLOT), lambda i: (i, 0, 0)),
            pl.BlockSpec((1, 1, SLOT), lambda i: (i, 0, 0)),
        ],
        out_specs=[double, double, square, square],
        out_shape=[jax.ShapeDtypeStruct((slots, SLOT, 2 * SLOT), BF)] * 2
        + [jax.ShapeDtypeStruct((slots, SLOT, SLOT), F32)] * 2,
        compiler_params=params(),
        cost_estimate=cost(slots * SLOT * SLOT * NBR * 3, slots * SLOT * SLOT * 12),
        name="tiles",
    )(turned, node_valid.reshape(slots, 1, SLOT))


def combine(g_ref):
    mref, first, second, count = (g_ref[:, k, :] for k in range(4))
    shift = first / count
    mean_each = mref + shift
    spread_each = second - first * shift
    total = jnp.sum(count, axis=0, keepdims=True)
    mean = jnp.sum(count * mean_each, axis=0, keepdims=True) / total
    away = mean_each - mean
    variance = jnp.sum(spread_each + count * away * away, axis=0, keepdims=True) / total
    return total, mean, lax.rsqrt(variance + EPSILON)


def small_gather(block, axis):
    parts = lax.axis_size(axis)
    copies = jnp.broadcast_to(block[None], (parts,) + block.shape)
    return lax.all_to_all(copies, axis, split_axis=0, concat_axis=0, tiled=True)


def split(value):
    high = value.astype(BF)
    return high, (value - high.astype(F32)).astype(BF)


def fold(value):
    return jnp.sum(value.reshape(value.shape[0] // 8, 8, value.shape[1]), axis=0)


def at(ref, k):
    return ref[k : k + 1, :]


def put(ref, k, value):
    ref[k : k + 1, :] = value


def forward_kernel(step, first, *refs):
    refs = refs[1:]
    xs, ws, (h_ref, inv_ref, val_ref) = refs[:4], refs[4:8], refs[8:11]
    lin_ref, all_ref, st_ref, acc_ref = refs[-4:]
    i = pl.program_id(0)
    columns = lin_ref.shape[1]
    total = None
    for b in range(4):
        x = xs[b][...]
        all_ref[b] = x
        term = dot(x, ws[b][...])
        total = term if total is None else total + term
    high, low = split(total)
    for s in range(step):
        rows = slice(s * SLOT, (s + 1) * SLOT)
        both = jnp.concatenate([high[rows], low[rows]], axis=0)
        lin_ref[rows, :] = dot(h_ref[s], both) * wide(inv_ref[s], columns)

    @pl.when(i == 0)
    def _():
        acc_ref[...] = jnp.zeros_like(acc_ref)
        if first:
            v = jnp.concatenate([val_ref[s] for s in range(step)], axis=0)
            count = jnp.sum(v, axis=0, keepdims=True)
            st_ref[...] = jnp.zeros_like(st_ref)
            put(st_ref, 0, jnp.sum(lin_ref[...] * wide(v, columns), axis=0, keepdims=True) / wide(count, columns))
        else:
            st_ref[...] = refs[11][...]

    mref = at(st_ref, 0)
    for s, inner, rows in parts_of(step):
        v = val_ref[s, inner, :]
        away = (lin_ref[rows, :] - mref) * wide(v, columns)
        acc_ref[0] += fold(away)
        acc_ref[1] += fold(away * away)
        acc_ref[2, :, :LANES] += fold(v)

    @pl.when(i == pl.num_programs(0) - 1)
    def _():
        st_ref[1:2, :] += jnp.sum(acc_ref[0], axis=0, keepdims=True)
        st_ref[2:3, :] += jnp.sum(acc_ref[1], axis=0, keepdims=True)
        st_ref[3:4, :] += wide(jnp.sum(acc_ref[2, :, :LANES], axis=0, keepdims=True), columns)


def forward_chunk(ids, plan, k, blocks, weight, tiles, carried, name):
    step, starts, sizes = plan
    base, steps = starts[k], sizes[k]
    rows = step * SLOT
    h, _, inv, val = tiles
    nodes, columns = h.shape[0] * SLOT, weight.shape[1]
    depth = weight.shape[0] // 4
    first = carried is None

    def rows_of(x):
        off = base if x.shape[0] == nodes else 0
        return pl.BlockSpec((rows, depth), lambda i, ids: (i + off, 0))

    tile = pl.BlockSpec((step, SLOT, SLOT), lambda i, ids: (i + base, 0, 0))
    double = pl.BlockSpec((step, SLOT, 2 * SLOT), lambda i, ids: (i + base, 0, 0))
    small = pl.BlockSpec((8, columns), lambda i, ids: (0, 0))
    ins = [rows_of(x) for x in blocks]
    ins += [pl.BlockSpec((depth, columns), lambda i, ids, b=b: (ids[b], 0)) for b in range(4)]
    ins += [double, tile, tile]
    args = [*blocks, *[weight] * 4, h, inv, val]
    aliases = {}
    if not first:
        lin, everything, stats = carried
        ins += [small, ANY, ANY]
        args += [stats, lin, everything]
        aliases = {13: 0, 14: 1}
    return pl.pallas_call(
        functools.partial(forward_kernel, step, first),
        grid_spec=pltpu.PrefetchScalarGridSpec(
            num_scalar_prefetch=1,
            grid=(steps,),
            in_specs=ins,
            out_specs=[
                pl.BlockSpec((rows, columns), lambda i, ids: (i + base, 0)),
                pl.BlockSpec((4, rows, depth), lambda i, ids: (0, i + base, 0)),
                small,
            ],
            scratch_shapes=[pltpu.VMEM((3, 8, columns), F32)],
        ),
        out_shape=[
            jax.ShapeDtypeStruct((nodes, columns), F32),
            jax.ShapeDtypeStruct((4, nodes, depth), BF),
            jax.ShapeDtypeStruct((8, columns), F32),
        ],
        input_output_aliases=aliases,
        compiler_params=params(),
        cost_estimate=cost(32 * steps * rows * depth * columns, steps * rows * 40 * depth),
        name=name,
    )(ids, *args)


def columns_of(g_ref, gamma_ref, beta_ref, co_ref):
    total, mean, inv_std = combine(g_ref)
    put(co_ref, 0, mean)
    put(co_ref, 1, 0.5 * gamma_ref[...] * inv_std)
    put(co_ref, 2, 0.5 * beta_ref[...])
    put(co_ref, 3, inv_std)
    put(co_ref, 4, total)


def silu_of(away, co_ref):
    u = away * at(co_ref, 1) + at(co_ref, 2)
    return u + u * jnp.tanh(u)


def double_slope(away, co_ref):
    u = away * at(co_ref, 1) + at(co_ref, 2)
    t = jnp.tanh(u)
    return (1.0 + t) * (1.0 + u * (1.0 - t))


def parts_of(step, part=32):
    for s in range(step):
        for r in range(SLOT // part):
            yield s, slice(r * part, (r + 1) * part), slice(s * SLOT + r * part, s * SLOT + (r + 1) * part)


def result_kernel(step, lin_ref, val_ref, g_ref, gamma_ref, beta_ref, out_ref, co_ref):
    @pl.when(pl.program_id(0) == 0)
    def _():
        columns_of(g_ref, gamma_ref, beta_ref, co_ref)

    columns = lin_ref.shape[1]
    for s, inner, rows in parts_of(step):
        value = silu_of(lin_ref[rows, :] - at(co_ref, 0), co_ref)
        out_ref[rows, :] = (wide(val_ref[s, inner, :], columns) * value).astype(out_ref.dtype)


def sums_kernel(step, lin_ref, cot_ref, val_ref, g_ref, gamma_ref, beta_ref, st_ref, co_ref, acc_ref):
    i = pl.program_id(0)

    @pl.when(i == 0)
    def _():
        columns_of(g_ref, gamma_ref, beta_ref, co_ref)
        acc_ref[...] = jnp.zeros_like(acc_ref)

    columns = lin_ref.shape[1]
    for s, inner, rows in parts_of(step):
        away = lin_ref[rows, :] - at(co_ref, 0)
        grad = cot_ref[rows, :].astype(F32) * wide(val_ref[s, inner, :], columns) * double_slope(away, co_ref)
        acc_ref[0] += fold(grad)
        acc_ref[1] += fold(grad * away)

    finish_sums(st_ref, co_ref, acc_ref)


def finish_sums(st_ref, co_ref, acc_ref, before_ref=None):
    @pl.when(pl.program_id(0) == pl.num_programs(0) - 1)
    def _():
        st_ref[...] = jnp.zeros_like(st_ref) if before_ref is None else before_ref[...]
        st_ref[0:1, :] += 0.5 * jnp.sum(acc_ref[0], axis=0, keepdims=True)
        st_ref[1:2, :] += 0.5 * at(co_ref, 3) * jnp.sum(acc_ref[1], axis=0, keepdims=True)


def turn_kernel(step, from_cot, lin_ref, grad_ref, val_ref, inv_ref, ht_ref, g_ref, sg_ref, gamma_ref, beta_ref, out_ref, co_ref, lg_ref):
    @pl.when(pl.program_id(0) == 0)
    def _():
        columns_of(g_ref, gamma_ref, beta_ref, co_ref)
        sg = sg_ref[...]
        twice = 2.0 / at(co_ref, 4)
        put(co_ref, 5, twice * jnp.sum(sg[:, 0, :], axis=0, keepdims=True))
        put(co_ref, 6, twice * at(co_ref, 3) * jnp.sum(sg[:, 1, :], axis=0, keepdims=True))

    columns = lin_ref.shape[1]
    for s, inner, rows in parts_of(step):
        away = lin_ref[rows, :] - at(co_ref, 0)
        if from_cot:
            grad = grad_ref[rows, :].astype(F32) * double_slope(away, co_ref)
        else:
            grad = grad_ref[rows, :]
        weight = wide(val_ref[s, inner, :] * inv_ref[s, inner, :], columns)
        high, low = split(weight * (grad - (at(co_ref, 5) + away * at(co_ref, 6))))
        lg_ref[s, inner, :] = high
        lg_ref[s, slice(inner.start + SLOT, inner.stop + SLOT), :] = low
    for s in range(step):
        out_ref[s * SLOT : (s + 1) * SLOT, :] = (dot(ht_ref[s], lg_ref[s]) * at(co_ref, 1)).astype(BF)


def rows_call(kernel, plan, k, big, tiles, smalls, out_dtype, scratch, name, ops):
    step, starts, sizes = plan
    base, steps = (0, sum(sizes)) if k is None else (starts[k], sizes[k])
    rows = step * SLOT
    columns = big[0].shape[1]
    ins = [pl.BlockSpec((rows, columns), lambda i: (i + base, 0)) for _ in big]
    ins += [pl.BlockSpec((step,) + t.shape[1:], lambda i: (i + base, 0, 0)) for t in tiles]
    ins += [pl.BlockSpec(s.shape, lambda i, n=s.ndim: (0,) * n) for s in smalls]
    if out_dtype is None:
        out_spec = pl.BlockSpec((8, columns), lambda i: (0, 0))
        out_shape = jax.ShapeDtypeStruct((8, columns), F32)
    else:
        out_spec = pl.BlockSpec((rows, columns), lambda i: (i, 0))
        out_shape = jax.ShapeDtypeStruct((steps * rows, columns), out_dtype)
    return pl.pallas_call(
        functools.partial(kernel, step),
        grid=(steps,),
        in_specs=ins,
        out_specs=out_spec,
        out_shape=out_shape,
        scratch_shapes=[pltpu.VMEM((8, columns), F32)] + scratch,
        compiler_params=params(),
        cost_estimate=cost(ops * steps * rows * columns, 8 * steps * rows * columns),
        name=name,
    )(*big, *tiles, *smalls)


def result_call(plan, k, lin, val, norm, dtype, name):
    return rows_call(result_kernel, plan, k, [lin], [val], norm, dtype, [], name, 12)


def turn_call(from_cot, plan, k, lin, grad, tiles, norm, sums, name):
    _, ht, inv, val = tiles
    columns = lin.shape[1]

    def kernel(step, *refs):
        return turn_kernel(step, from_cot, *refs)

    return rows_call(
        kernel, plan, k, [lin, grad], [val, inv, ht], [norm[0], sums, *norm[1:]], BF,
        [pltpu.VMEM((plan[0], 2 * SLOT, columns), BF)], name, 500,
    )


def backward_kernel(step, last, first, *refs):
    xs, ws, refs = refs[:4], refs[4:8], refs[8:]
    total = dot_t(xs[0][...], ws[0][...])
    for b in range(1, 4):
        total += dot_t(xs[b][...], ws[b][...])
    if last:
        refs[-1][...] = total
        return
    lin_ref, g_ref, gamma_ref, beta_ref = refs[:4]
    out_ref, st_ref, co_ref, acc_ref = refs[-4:]

    @pl.when(pl.program_id(0) == 0)
    def _():
        columns_of(g_ref, gamma_ref, beta_ref, co_ref)
        acc_ref[...] = jnp.zeros_like(acc_ref)

    for _, _, rows in parts_of(step):
        away = lin_ref[rows, :] - at(co_ref, 0)
        grad = total[rows] * double_slope(away, co_ref)
        out_ref[rows, :] = grad
        acc_ref[0] += fold(grad)
        acc_ref[1] += fold(grad * away)

    finish_sums(st_ref, co_ref, acc_ref, None if first else refs[4])


def backward_chunk(plan, k, blocks, pieces, lin, norm, carried, name):
    step, starts, sizes = plan
    base, steps = starts[k], sizes[k]
    rows = step * SLOT
    nodes = sum(sizes) * rows
    depth, columns = blocks[0].shape[1], pieces[0].shape[0]
    last, first = norm is None, carried is None
    flat = pl.BlockSpec((rows, columns), lambda i: (i + base, 0))
    fixed = lambda s: pl.BlockSpec(s.shape, lambda i, n=s.ndim: (0,) * n)
    ins = [pl.BlockSpec((rows, depth), lambda i: (i, 0)) for _ in blocks]
    ins += map(fixed, pieces)
    args = [*blocks, *pieces]
    out_specs = [flat]
    out_shape = [jax.ShapeDtypeStruct((nodes, columns), F32)]
    scratch = []
    small = pl.BlockSpec((8, columns), lambda i: (0, 0))
    if not last:
        ins += [flat, *map(fixed, norm)]
        args += [lin, *norm]
        out_specs.append(small)
        out_shape.append(jax.ShapeDtypeStruct((8, columns), F32))
        scratch = [pltpu.VMEM((8, columns), F32), pltpu.VMEM((2, 8, columns), F32)]
    aliases = {}
    if not first:
        if not last:
            ins.append(small)
            args.append(carried[1])
        aliases = {len(args): 0}
        ins.append(ANY)
        args.append(carried[0])
    return pl.pallas_call(
        functools.partial(backward_kernel, step, last, first),
        grid=(steps,),
        in_specs=ins,
        out_specs=out_specs,
        out_shape=out_shape,
        scratch_shapes=scratch,
        input_output_aliases=aliases,
        compiler_params=params(),
        cost_estimate=cost(32 * steps * rows * depth * columns, steps * rows * 40 * depth),
        name=name,
    )(*args)


def weight_kernel(spans, x_ref, *refs):
    hs, out_ref = refs[:-1], refs[-1]
    total = None
    for (low, high), h_ref in zip(spans, hs):
        x = x_ref[0, low:high, :]
        term = lax.dot_general(x, h_ref[...], (((0,), (0,)), ((), ())), preferred_element_type=F32)
        total = term if total is None else total + term
    out_ref[...] = total.astype(out_ref.dtype)


def weight_terms(everything, base, hs, name):
    _, nodes, depth = everything.shape
    columns = hs[0].shape[1]
    spans, low = [], 0
    for h in hs:
        spans.append((low, low + h.shape[0]))
        low += h.shape[0]
    return pl.pallas_call(
        functools.partial(weight_kernel, tuple(spans)),
        grid=(2,),
        in_specs=[pl.BlockSpec((1, nodes, depth), lambda i: (i + base, 0, 0))]
        + [pl.BlockSpec(h.shape, lambda i: (0, 0)) for h in hs],
        out_specs=pl.BlockSpec((depth, columns), lambda i: (i, 0)),
        out_shape=jax.ShapeDtypeStruct((2 * depth, columns), BF),
        compiler_params=params(),
        cost_estimate=cost(16 * nodes * depth * columns, 6 * nodes * depth),
        name=name,
    )(everything, *hs)


def place_kernel(where_ref, *refs):
    out_ref = refs[-1]
    for k in range(4):

        @pl.when(pl.program_id(0) == k)
        def _():
            out_ref[...] = refs[k][...].astype(F32)


def place_blocks(where, blocks, name):
    depth, columns = blocks[0].shape
    return pl.pallas_call(
        place_kernel,
        grid_spec=pltpu.PrefetchScalarGridSpec(
            num_scalar_prefetch=1,
            grid=(4,),
            in_specs=[pl.BlockSpec((depth, columns), lambda i, where: (0, 0))] * 4,
            out_specs=pl.BlockSpec((depth, columns), lambda i, where: (where[i], 0)),
        ),
        out_shape=jax.ShapeDtypeStruct((4 * depth, columns), F32),
        compiler_params=params(),
        cost_estimate=cost(4 * depth * columns, 24 * depth * columns),
        name=name,
    )(where, *blocks)


def after(value, *deps):
    return lax.optimization_barrier((value, deps))[0]


def across(value, axis, distance):
    size = lax.axis_size(axis)
    return lax.ppermute(value, axis, [(i, i ^ distance) for i in range(size)])


def weight_slices(weight, q):
    depth = weight.shape[0] // 4
    return [lax.dynamic_slice_in_dim(weight, (q ^ d) * depth, depth, 0) for d in range(4)]


def weight_rows(slices):
    far = across(slices[2], "col", 2)
    other = across(slices[3], "col", 2)
    return [slices[0], across(slices[1], "col", 1), far, across(other, "col", 1)]


def reduce_stages(halves, axis):
    size = lax.axis_size(axis)
    bits = size.bit_length() - 1
    place = lax.axis_index(axis)
    orders = [list(range(bits)), list(range(1, bits)) + [0]]
    held = list(halves)
    dtype = held[0].dtype
    for s in range(bits):
        for n, order in enumerate(orders):
            bit = (place >> order[s]) & 1
            part = held[n].shape[0] // 2
            keep = lax.dynamic_slice_in_dim(held[n], bit * part, part, 0)
            send = lax.dynamic_slice_in_dim(held[n], (1 - bit) * part, part, 0)
            got = across(send, axis, 1 << order[s])
            held[n] = (keep.astype(F32) + got.astype(F32)).astype(dtype)
        tie = yield tuple(held)
        if tie is not None:
            held = list(tie)
    for s in reversed(range(1, bits)):
        for n, order in enumerate(orders):
            bit = (place >> order[s]) & 1
            got = across(held[n], axis, 1 << order[s])
            held[n] = jnp.concatenate(
                [jnp.where(bit == 0, held[n], got), jnp.where(bit == 0, got, held[n])], axis=0
            )
        tie = yield tuple(held)
        if tie is not None:
            held = list(tie)
    out = []
    for n, order in enumerate(orders):
        out.append((held[n], across(held[n], axis, 1 << order[0]), (place >> order[0]) & 1))
    yield out


def placed_sum(stages, q, name):
    (held_a, got_a, bit_a), (held_b, got_b, bit_b) = stages
    where = jnp.stack([q ^ bit_a, q ^ 1 ^ bit_a, q ^ 2 ^ bit_b, q ^ 3 ^ bit_b]).astype(jnp.int32)
    return place_blocks(where, [held_a, got_a, held_b, got_b], name)


def chunk_plan(slots):
    step = 2 if slots % 2 == 0 else 1
    total = slots // step
    last = max(1, (2 * total) // 7)
    sizes = [size for size in (total - last, last) if size > 0]
    starts = [sum(sizes[:k]) for k in range(len(sizes))]
    return step, starts, sizes


def gathered_chunks(chunks, near, work, ready=()):
    far = [across(c, "col", 2) for c in chunks]
    carried = None
    for k in range(len(chunks)):
        ties = carried if k else ready
        source = after(far[k], ties) if ties else far[k]
        carried = work(k, [near[k], source, across(source, "col", 1)], carried)
    return carried


def local(
    features,
    neighbours,
    node_valid,
    weight_one,
    gamma_one,
    beta_one,
    weight_two,
    gamma_two,
    beta_two,
    cotangent,
):
    nodes, columns = features.shape
    plan = chunk_plan(nodes // SLOT)
    step, starts, sizes = plan
    chunks = range(len(sizes))
    q = lax.axis_index("col")
    ids = jnp.stack([q, q ^ 1, q ^ 2, q ^ 3]).astype(jnp.int32)
    g1, b1, g2, b2 = (v.reshape(1, columns) for v in (gamma_one, beta_one, gamma_two, beta_two))

    rows = [(starts[k] * step * SLOT, (starts[k] + sizes[k]) * step * SLOT) for k in chunks]
    near = across(features, "col", 1)
    tiles = build_tiles(neighbours, node_valid)
    val = tiles[3]
    slices_one, slices_two = weight_slices(weight_one, q), weight_slices(weight_two, q)

    def work(k, blocks, carried):
        return forward_chunk(ids, plan, k, [features, *blocks], weight_one, tiles, carried, f"forward_one_{k}")

    lin_one, all_one, stats = gathered_chunks(
        [features[a:b] for a, b in rows], [near] * len(sizes), work, (tiles, slices_one, slices_two)
    )
    norm_one = (small_gather(stats, "row"), g1, b1)

    hidden = []
    for k in chunks:
        source = after(lin_one, hidden[-1]) if hidden else lin_one
        hidden.append(result_call(plan, k, source, val, norm_one, BF, f"hidden_{k}"))

    def work(k, blocks, carried):
        return forward_chunk(ids, plan, k, [hidden[k], *blocks], weight_two, tiles, carried, f"forward_two_{k}")

    lin_two, all_two, stats = gathered_chunks(hidden, [across(c, "col", 1) for c in hidden], work)
    norm_two = (small_gather(stats, "row"), g2, b2)
    rows_two = weight_rows(after(slices_two, stats))

    sums = rows_call(
        sums_kernel, plan, None, [lin_two, cotangent], [val], norm_two, None,
        [pltpu.VMEM((2, 8, columns), F32)], "sums_two", 20,
    )
    grads_two = small_gather(sums, "row")
    grads_two = after(grads_two, rows_two[2])
    turned = []
    for k in chunks:
        source = after(lin_two, turned[-1]) if turned else lin_two
        turned.append(turn_call(True, plan, k, source, cotangent, tiles, norm_two, grads_two, f"turn_two_{k}"))
    terms_two = [weight_terms(all_two, b, turned, f"terms_two_{b}") for b in (0, 2)]
    output = result_call(plan, None, lin_two, val, norm_two, F32, "output")
    reduce_two = reduce_stages(terms_two, "row")
    stages = 2 * (lax.axis_size("row").bit_length() - 1)
    state = {"n": 1, "held": next(reduce_two)}

    def beside(value):
        if state["n"] >= stages - 1:
            return value
        value, held = lax.optimization_barrier((value, state["held"]))
        state["held"] = reduce_two.send(held)
        state["n"] += 1
        return value

    def work(k, blocks, carried):
        blocks[0] = beside(blocks[0])
        return backward_chunk(plan, k, [turned[k], *blocks], rows_two, lin_one, norm_one, carried, f"backward_two_{k}")

    grad_one, sums = gathered_chunks(turned, [across(c, "col", 1) for c in turned], work, tuple(terms_two))
    grads_one = small_gather(beside(sums), "row")

    lin_one = beside(lin_one)
    turned = []
    for k in chunks:
        source = after(lin_one, turned[-1]) if turned else lin_one
        turned.append(turn_call(False, plan, k, source, grad_one, tiles, norm_one, grads_one, f"turn_one_{k}"))
    while state["n"] < stages - 1:
        turned[0] = beside(turned[0])
    terms_one = [weight_terms(all_one, b, turned, f"terms_one_{b}") for b in (0, 2)]
    reduce_one = reduce_stages(terms_one, "row")
    held_one, held = lax.optimization_barrier((next(reduce_one), state["held"]))
    stage_last = reduce_two.send(held)
    grad_weight_two = placed_sum(stage_last, q, "place_two")
    held_one = reduce_one.send(held_one)
    for _ in range(stages - 4):
        held_one = next(reduce_one)
    next(reduce_one)
    grad_weight_one = placed_sum(next(reduce_one), q, "place_one")

    rows_one = weight_rows(after(slices_one, turned[-1]))

    def work(k, blocks, carried):
        if k == 1:
            blocks[0] = after(blocks[0], output)
        return backward_chunk(plan, k, [turned[k], *blocks], rows_one, None, None, carried, f"backward_one_{k}")

    (grad_features,) = gathered_chunks(turned, [across(c, "col", 1) for c in turned], work, held_one)

    sums_one, sums_two = jnp.sum(grads_one, axis=0), jnp.sum(grads_two, axis=0)
    return (
        output,
        grad_features,
        grad_weight_one,
        sums_one[1],
        sums_one[0],
        grad_weight_two,
        sums_two[1],
        sums_two[0],
    )


def solution(mesh):
    placed = (
        P("row", "col"),
        P("row", None),
        P("row"),
        P(None, "col"),
        P("col"),
        P("col"),
        P(None, "col"),
        P("col"),
        P("col"),
        P("row", "col"),
    )
    return jax.shard_map(
        local,
        mesh=mesh,
        in_specs=placed,
        out_specs=(
            P("row", "col"),
            P("row", "col"),
            P(None, "col"),
            P("col"),
            P("col"),
            P(None, "col"),
            P("col"),
            P("col"),
        ),
        check_vma=False,
    )
```

time: 473 us -> 386 us (0.82)
  waiting for transfers between devices: 205 us -> 150 us
  Pallas kernels: 134 us -> 109 us
  between operations: 14.8 us -> 1.25 us
  blocking collectives: 23.3 us -> 33.7 us
  starting transfers between devices: 50.9 us -> 40.7 us
  other arithmetic: 10.6 us -> 18 us
    psum x1 -> x0, waiting for transfers between devices: 46.7 us -> none  [local(): grad_weight_two = lax.psum(terms_two, 'row').astype(F32)]
    pallas_call x24 -> x18, Pallas kernels: 86.5 us -> 73.7 us  [the longest x8 25.1 us: rows_call(): pl.pallas_call(functools.partial(kernel, step), grid=(steps,), in_specs=i...]
    pallas_call x8 -> x4, Pallas kernels: 42.4 us -> 30.2 us  [forward_chunk(): pl.pallas_call(functools.partial(forward_kernel, step, first), grid_spec=...]
    all_to_all x2 -> x3, blocking collectives: 23.3 us -> 33.7 us  [small_gather(): return lax.all_to_all(copies, axis, split_axis=0, concat_axis=0, tiled=True)]
    ppermute x63 -> x55, starting transfers between devices: 43.7 us -> 36.5 us  [across(): return lax.ppermute(value, axis, [(i, i ^ distance) for i in range(size)])]
    concatenate x4 -> x8, other arithmetic: 0.11 us -> 6.34 us  [reduce_stages(): jnp.concatenate([jnp.where(bit == 0, held[n], got), jnp.where(bit == 0, g...]
    ppermute x63 -> x55, waiting for transfers between devices: 155 us -> 150 us  [across(): return lax.ppermute(value, axis, [(i, i ^ distance) for i in range(size)])]
    dynamic_slice x12 -> x13, local copies, waits for them, and re-layouts: 12.2 us -> 8.13 us  [the longest x12 4.18 us: reduce_stages(): send = lax.dynamic_slice_in_dim(held[n], (1 - bit) * part, part, 0)]
  transfers between devices with their start and end apart: 66 -> 56, of which waited for: 22 -> 27; matrix products, arithmetic and copies ran while one was open for 6% -> 8% of each run, Pallas kernels for 27% -> 22%
where the time goes in v2:
time: 386 us; the launch traced here: 384 us
  waiting for transfers between devices  150 us (39%)
  Pallas kernels  109 us (28%)
  starting transfers between devices  40.7 us (11%)
  blocking collectives  33.7 us (9%)
  local copies, waits for them, and re-layouts  31 us (8%)
  other arithmetic  18 us (5%)
    ppermute x55, waiting for transfers between devices, across(): return lax.ppermute(value, axis, [(i, i ^ distance) for i in range(size)])  150 us
    ppermute x55, starting transfers between devices, across(): return lax.ppermute(value, axis, [(i, i ^ distance) for i in range(size)])  36.5 us
    all_to_all x3, blocking collectives, small_gather(): return lax.all_to_all(copies, axis, split_axis=0, concat_axis=0, tiled=True)  33.7 us
    pallas_call x4, Pallas kernels, forward_chunk(): pl.pallas_call(functools.partial(forward_kernel, step, first), grid_spec=...  30.2 us
    pallas_call x8, Pallas kernels, rows_call(): pl.pallas_call(functools.partial(kernel, step), grid=(steps,), in_specs=i...  25.1 us
    pallas_call x4, Pallas kernels, backward_chunk(): pl.pallas_call(functools.partial(backward_kernel, step, last, first), gri...  24.1 us
    unnamed x94, local copies, waits for them, and re-layouts  17.4 us
    pallas_call x4, Pallas kernels, weight_terms(): pl.pallas_call(functools.partial(weight_kernel, tuple(spans)), grid=(2,),...  15.6 us
  transfers between devices with their start and end apart: 56, of which 27 were waited for; matrix products, arithmetic and copies ran while one was open for 8% of the time, Pallas kernels for 22%

profile of v2, /device:TPU:0, one launch (start us, length us, event | category | flops | bytes accessed | tf_op | source)
XLA Modules:
  0.0 384.0 jit_solution(1016251665325032159)
XLA Ops:
  0.7 2.5 slice.19
  3.2 3.0 collective-permute-start.2
  6.2 5.0 %tiles.1 = (bf16[14,128,256]{2,1,0:T(8,128)(2,1)S(1)}, bf16[14,128,256]{2,1,0:T(8,128)(2,1)S(1)}, f32[14,128,128]{2,1,0:T(8,128)S(1)}, f32[14,128,128]{2,1,0:T(8,128)S(1)}) custom-call(s32[14,32,128]{2,1,0:T(8,128)S(1)} %bitcast_bitcast_fusion.nbr_ref, s32[14,1,128]{2,1,0:T(1,128)S(1)} %reshape.39.valid_ref), custom_call_target="tpu_custom_call" | custom-call | flops 22020 | bytes 2752 | tf_op jit(solution)/shard_map/tiles/pallas_call | solution.py:63
  12.2 4.0 %constant_dynamic-slice_fusion.12 = (bf16[512,512]{1,0:T(8,128)(2,1)}, bf16[512,512]{1,0:T(8,128)(2,1)S(1)}, bf16[512,512]{1,0:T(8,128)(2,1)}, bf16[512,512]{1,0...) fusion(bf16[2048,512]{1,0:T(8,128)(2,1)} %refs_8_.7, ...), kind=kLoop, calls=%fused_computation.49 | loop fusion | bytes 8388624 | tf_op jit(solution)/shard_map/dynamic_slice | solution.py:477
  16.1 19.1 %collective-permute-done.2.refs_3_ = bf16[1280,512]{1,0:T(8,128)(2,1)} collective-permute-done((bf16[1280,512]{1,0:T(8,128)(2,1)}, bf16[1280,512]{1,0:T(8,128)(2,1)}, u32[]{:S(2)}, u32[]{:S(2)}) %collective-permute-start.2) | collective-permute-done | bytes 1310752 | tf_op jit(solution)/shard_map/ppermute | solution.py:472
  38.5 10.0 %forward_one_0.1 = (f32[1792,512]{1,0:T(8,128)}, bf16[4,1792,512]{2,1,0:T(8,128)(2,1)}, f32[8,512]{1,0:T(8,128)S(1)}) custom-call(s32[4]{0:T(128)S(1)} %pad_add_fusion.refs_0_, bf16[1792,512]{1,0:T(8,128)(2,1)} %refs_1_.5, bf16[1792,512]{1,0:T(8,128)(2,1)} %collective-permute-done.refs_2_, bf16[1280,512]{1,0:T(8,128)(2,1)} %collective-permute-done.2.refs_3_, ...), custom_call_target="tpu_custom_call" | custom-call | flops 10737418 | bytes 26214 | tf_op jit(solution)/shard_map/forward_one_0/pallas_call | solution.py:184
  48.5 2.2 collective-permute-done.1.refs_3_
  52.6 5.5 %forward_one_1.1 = (f32[1792,512]{1,0:T(8,128)}, bf16[4,1792,512]{2,1,0:T(8,128)(2,1)}, f32[8,512]{1,0:T(8,128)S(1)}) custom-call(s32[4]{0:T(128)S(1)} %pad_add_fusion.refs_0_, bf16[1792,512]{1,0:T(8,128)(2,1)} %refs_1_.5, bf16[1792,512]{1,0:T(8,128)(2,1)} %collective-permute-done.refs_2_, ...), custom_call_target="tpu_custom_call", output_to_operand_aliasing={{0}: (13, {}), {1}: (14, {})} | custom-call | flops 4294967 | bytes 10485 | tf_op jit(solution)/shard_map/forward_one_1/pallas_call | solution.py:184
  58.1 13.2 %all_to_all.20.g_ref.refs_9_.refs_5_ = f32[8,8,512]{2,1,0:T(8,128)S(1)} all-to-all(f32[8,8,512]{2,1,0:T(8,128)S(1)} %broadcast_in_dim.8), channel_id=1, replica_groups=mesh['row'=8,'col'=4] {'row'}, dimensions={0} | all-to-all | bytes 262144 | tf_op jit(solution)/shard_map/all_to_all | solution.py:94
  71.3 2.0 copy-done.2
  75.8 27.9 %collective-permute-done.8.refs_3_ = bf16[1280,512]{1,0:T(8,128)(2,1)S(1)} collective-permute-done((bf16[1280,512]{1,0:T(8,128)(2,1)S(1)}, bf16[1280,512]{1,0:T(8,128)(2,1)S(1)}, u32[]{:S(2)}, u32[]{:S(2)}) %collective-permute-start.8) | collective-permute-done | bytes 1310752 | tf_op jit(solution)/shard_map/ppermute | solution.py:472
  107.7 9.4 %forward_two_0.1 = (f32[1792,512]{1,0:T(8,128)}, bf16[4,1792,512]{2,1,0:T(8,128)(2,1)}, f32[8,512]{1,0:T(8,128)S(1)}) custom-call(s32[4]{0:T(128)S(1)} %pad_add_fusion.refs_0_, bf16[1280,512]{1,0:T(8,128)(2,1)S(1)} %hidden_0.1.refs_1_, bf16[1280,512]{1,0:T(8,128)(2,1)S(1)} %collective-permute-done.7.refs_2_, bf16[1280,512]{1,0:T(8,128)(2,1)} %copy-done.38, ...), custom_call_target="tpu_custom_call" | custom-call | flops 10737418 | bytes 26214 | tf_op jit(solution)/shard_map/forward_two_0/pallas_call | solution.py:184
  120.3 5.3 %forward_two_1.1 = (f32[1792,512]{1,0:T(8,128)}, bf16[4,1792,512]{2,1,0:T(8,128)(2,1)}, f32[8,512]{1,0:T(8,128)S(1)}) custom-call(s32[4]{0:T(128)S(1)} %pad_add_fusion.refs_0_, bf16[512,512]{1,0:T(8,128)(2,1)S(1)} %hidden_1.1.refs_1_, bf16[512,512]{1,0:T(8,128)(2,1)S(1)} %collective-permute-done.5.refs_2_, ...), custom_call_target="tpu_custom_call", output_to_operand_aliasing={{0}: (13, {}), {1}: (14, {})} | custom-call | flops 4294967 | bytes 10485 | tf_op jit(solution)/shard_map/forward_two_1/pallas_call | solution.py:184
  127.2 10.7 %all_to_all.21.g_ref.refs_5_ = f32[8,8,512]{2,1,0:T(8,128)S(1)} all-to-all(f32[8,8,512]{2,1,0:T(8,128)S(1)} %broadcast_in_dim.9), channel_id=1, replica_groups=mesh['row'=8,'col'=4] {'row'}, dimensions={0} | all-to-all | bytes 262144 | tf_op jit(solution)/shard_map/all_to_all | solution.py:94
  138.0 5.5 %sums_two.1 = f32[8,512]{1,0:T(8,128)S(1)} custom-call(f32[1792,512]{1,0:T(8,128)} %get-tuple-element.84.lin_ref.refs_0_, bf16[1792,512]{1,0:T(8,128)(2,1)S(1)} %copy-done.4, f32[14,128,128]{2,1,0:T(8,128)S(1)} %get-tuple-element.67.refs_11_.val_ref.refs_2_, f32[8,8,512]{2,1,0:T(8,128)S(1)} %all_to_all.21.g_ref.refs_5_, f32[1,512]{1,0:T(1,128)S(1)} %bitcast.35, ...), custom_call_target="tpu_custom_call" | custom-call | flops 18350 | bytes 7340 | tf_op jit(solution)/shard_map/sums_two/pallas_call | solution.py:310
  143.5 9.7 %all_to_all.22.refs_6_ = f32[8,8,512]{2,1,0:T(8,128)S(1)} all-to-all(f32[8,8,512]{2,1,0:T(8,128)S(1)} %broadcast_in_dim.10), channel_id=1, replica_groups=mesh['row'=8,'col'=4] {'row'}, dimensions={0} | all-to-all | bytes 262144 | tf_op jit(solution)/shard_map/all_to_all | solution.py:94
  154.0 4.9 %turn_two_0.1.refs_0_ = bf16[1280,512]{1,0:T(8,128)(2,1)S(1)} custom-call(f32[1792,512]{1,0:T(8,128)} %get-tuple-element.84.lin_ref.refs_0_, bf16[1792,512]{1,0:T(8,128)(2,1)S(1)} %copy-done.4, f32[14,128,128]{2,1,0:T(8,128)S(1)} %get-tuple-element.67.refs_11_.val_ref.refs_2_, f32[14,128,128]{2,1,0:T(8,128)S(1)} %get-tuple-element.66.refs_10_.refs_3_, ...), custom_call_target="tpu_custom_call" | custom-call | flops 327680 | bytes 5242 | tf_op jit(solution)/shard_map/turn_two_0/pallas_call | solution.py:310
  162.2 2.9 turn_two_1.1.refs_1_.refs_0_
  165.1 3.9 %terms_two_2.1 = bf16[1024,512]{1,0:T(8,128)(2,1)S(1)} custom-call(bf16[4,1792,512]{2,1,0:T(8,128)(2,1)} %get-tuple-element.85.x_ref, bf16[1280,512]{1,0:T(8,128)(2,1)S(1)} %turn_two_0.1.refs_0_, bf16[512,512]{1,0:T(8,128)(2,1)} %turn_two_1.1.refs_1_.refs_0_), custom_call_target="tpu_custom_call" | custom-call | flops 7516192 | bytes 5505 | tf_op jit(solution)/shard_map/terms_two_2/pallas_call | solution.py:427
  170.9 3.9 %terms_two_0.1 = bf16[1024,512]{1,0:T(8,128)(2,1)S(1)} custom-call(bf16[4,1792,512]{2,1,0:T(8,128)(2,1)} %get-tuple-element.85.x_ref, bf16[1280,512]{1,0:T(8,128)(2,1)S(1)} %turn_two_0.1.refs_0_, bf16[512,512]{1,0:T(8,128)(2,1)} %turn_two_1.1.refs_1_.refs_0_), custom_call_target="tpu_custom_call" | custom-call | flops 7516192 | bytes 5505 | tf_op jit(solution)/shard_map/terms_two_0/pallas_call | solution.py:427
  179.4 6.1 %collective-permute-done.15 = bf16[512,512]{1,0:T(8,128)(2,1)} collective-permute-done((bf16[512,512]{1,0:T(8,128)(2,1)}, bf16[512,512]{1,0:T(8,128)(2,1)}, u32[]{:S(2)}, u32[]{:S(2)}) %collective-permute-start.15) | collective-permute-done | bytes 524320 | tf_op jit(solution)/shard_map/ppermute | solution.py:472
  186.9 3.9 %collective-permute-done.19.refs_2_ = bf16[1280,512]{1,0:T(8,128)(2,1)} collective-permute-done((bf16[1280,512]{1,0:T(8,128)(2,1)S(1)}, bf16[1280,512]{1,0:T(8,128)(2,1)}, u32[]{:S(2)}, u32[]{:S(2)}) %collective-permute-start.19) | collective-permute-done | bytes 1310752 | tf_op jit(solution)/shard_map/ppermute | solution.py:472
  196.4 2.1 collective-permute-done.22
  198.5 10.1 %collective-permute-done.17 = bf16[256,512]{1,0:T(8,128)(2,1)} collective-permute-done((bf16[256,512]{1,0:T(8,128)(2,1)}, bf16[256,512]{1,0:T(8,128)(2,1)}, u32[]{:S(2)}, u32[]{:S(2)}) %collective-permute-start.17) | collective-permute-done | bytes 262176 | tf_op jit(solution)/shard_map/ppermute | solution.py:472
  216.3 8.7 %backward_two_0.1 = (f32[1792,512]{1,0:T(8,128)}, f32[8,512]{1,0:T(8,128)S(1)}) custom-call(bf16[1280,512]{1,0:T(8,128)(2,1)S(1)} %turn_two_0.1.refs_0_, bf16[1280,512]{1,0:T(8,128)(2,1)} %collective-permute-done.13.refs_1_, bf16[1280,512]{1,0:T(8,128)(2,1)} %collective-permute-done.19.refs_2_, bf16[1280,512]{1,0:T(8,128)(2,1)} %collective-permute-done.20.refs_3_, ...), custom_call_target="tpu_custom_call" | custom-call | flops 10737418 | bytes 26214 | tf_op jit(solution)/shard_map/backward_two_0/pallas_call | solution.py:396
  226.3 6.8 %collective-permute-done.25 = bf16[128,512]{1,0:T(8,128)(2,1)S(1)} collective-permute-done((bf16[128,512]{1,0:T(8,128)(2,1)S(1)}, bf16[128,512]{1,0:T(8,128)(2,1)S(1)}, u32[]{:S(2)}, u32[]{:S(2)}) %collective-permute-start.25) | collective-permute-done | bytes 131104 | tf_op jit(solution)/shard_map/ppermute | solution.py:472
  233.2 4.6 %backward_two_1.1 = (f32[1792,512]{1,0:T(8,128)}, f32[8,512]{1,0:T(8,128)S(1)}) custom-call(bf16[512,512]{1,0:T(8,128)(2,1)} %turn_two_1.1.refs_1_.refs_0_, bf16[512,512]{1,0:T(8,128)(2,1)} %collective-permute-done.12.refs_1_, bf16[512,512]{1,0:T(8,128)(2,1)} %collective-permute-done.18.refs_2_, ...), custom_call_target="tpu_custom_call", output_to_operand_aliasing={{0}: (13, {})} | custom-call | flops 4294967 | bytes 10485 | tf_op jit(solution)/shard_map/backward_two_1/pallas_call | solution.py:396
  240.2 4.3 %all-to-all-start.3 = ((f32[8,8,512]{2,1,0:T(8,128)}), f32[8,8,512]{2,1,0:T(8,128)S(1)}, u32[]{:S(2)}, u32[]{:S(2)}) async-start(f32[8,8,512]{2,1,0:T(8,128)} %broadcast_in_dim.11), calls=%async_computation.3 | async-start | bytes 262144 | tf_op jit(solution)/shard_map/all_to_all | solution.py:94
  244.5 3.8 collective-permute-done.27
  249.8 3.0 collective-permute-start.35
  255.5 4.8 %turn_one_0.1.refs_0_ = bf16[1280,512]{1,0:T(8,128)(2,1)S(1)} custom-call(f32[1792,512]{1,0:T(8,128)} %get-tuple-element.105.lin_ref.refs_8_.refs_0_, f32[1792,512]{1,0:T(8,128)} %get-tuple-element.103.refs_1_, f32[14,128,128]{2,1,0:T(8,128)S(1)} %get-tuple-element.67.refs_11_.val_ref.refs_2_, f32[14,128,128]{2,1,0:T(8,128)S(1)} %get-tuple-element.66.refs_10_.refs_3_, ...), custom_call_target="tpu_custom_call" | custom-call | flops 327680 | bytes 5242 | tf_op jit(solution)/shard_map/turn_one_0/pallas_call | solution.py:310
  262.4 4.0 %terms_one_2.1 = bf16[1024,512]{1,0:T(8,128)(2,1)S(1)} custom-call(bf16[4,1792,512]{2,1,0:T(8,128)(2,1)} %get-tuple-element.107.x_ref, bf16[1280,512]{1,0:T(8,128)(2,1)S(1)} %turn_one_0.1.refs_0_, bf16[512,512]{1,0:T(8,128)(2,1)S(1)} %turn_one_1.1.refs_1_.refs_0_), custom_call_target="tpu_custom_call" | custom-call | flops 7516192 | bytes 5505 | tf_op jit(solution)/shard_map/terms_one_2/pallas_call | solution.py:427
  266.5 3.8 terms_one_0.1
  274.7 4.8 %collective-permute-done.34 = bf16[512,512]{1,0:T(8,128)(2,1)S(1)} collective-permute-done((bf16[512,512]{1,0:T(8,128)(2,1)S(1)}, bf16[512,512]{1,0:T(8,128)(2,1)S(1)}, u32[]{:S(2)}, u32[]{:S(2)}) %collective-permute-start.34) | collective-permute-done | bytes 524320 | tf_op jit(solution)/shard_map/ppermute | solution.py:472
  279.7 3.8 collective-permute-done.33
  287.8 8.9 %collective-permute-done.40 = bf16[256,512]{1,0:T(8,128)(2,1)S(1)} collective-permute-done((bf16[256,512]{1,0:T(8,128)(2,1)S(1)}, bf16[256,512]{1,0:T(8,128)(2,1)S(1)}, u32[]{:S(2)}, u32[]{:S(2)}) %collective-permute-start.40) | collective-permute-done | bytes 262176 | tf_op jit(solution)/shard_map/ppermute | solution.py:472
  296.8 7.2 %collective-permute-done.37 = bf16[256,512]{1,0:T(8,128)(2,1)S(1)} collective-permute-done((bf16[256,512]{1,0:T(8,128)(2,1)S(1)}, bf16[256,512]{1,0:T(8,128)(2,1)S(1)}, u32[]{:S(2)}, u32[]{:S(2)}) %collective-permute-start.37) | collective-permute-done | bytes 262176 | tf_op jit(solution)/shard_map/ppermute | solution.py:472
  304.1 4.9 %collective-permute-done.41 = bf16[128,512]{1,0:T(8,128)(2,1)S(1)} collective-permute-done((bf16[128,512]{1,0:T(8,128)(2,1)S(1)}, bf16[128,512]{1,0:T(8,128)(2,1)S(1)}, u32[]{:S(2)}, u32[]{:S(2)}) %collective-permute-start.41) | collective-permute-done | bytes 131104 | tf_op jit(solution)/shard_map/ppermute | solution.py:472
  309.5 6.5 %collective-permute-done.38 = bf16[128,512]{1,0:T(8,128)(2,1)S(1)} collective-permute-done((bf16[128,512]{1,0:T(8,128)(2,1)S(1)}, bf16[128,512]{1,0:T(8,128)(2,1)S(1)}, u32[]{:S(2)}, u32[]{:S(2)}) %collective-permute-start.38) | collective-permute-done | bytes 131104 | tf_op jit(solution)/shard_map/ppermute | solution.py:472
  316.0 4.9 %collective-permute-done.42 = bf16[128,512]{1,0:T(8,128)(2,1)S(1)} collective-permute-done((bf16[128,512]{1,0:T(8,128)(2,1)S(1)}, bf16[128,512]{1,0:T(8,128)(2,1)S(1)}, u32[]{:S(2)}, u32[]{:S(2)}) %collective-permute-start.42) | collective-permute-done | bytes 131104 | tf_op jit(solution)/shard_map/ppermute | solution.py:472
  321.0 6.0 %collective-permute-done.39 = bf16[128,512]{1,0:T(8,128)(2,1)S(1)} collective-permute-done((bf16[128,512]{1,0:T(8,128)(2,1)S(1)}, bf16[128,512]{1,0:T(8,128)(2,1)S(1)}, u32[]{:S(2)}, u32[]{:S(2)}) %collective-permute-start.39) | collective-permute-done | bytes 131104 | tf_op jit(solution)/shard_map/ppermute | solution.py:472
  333.7 9.4 %collective-permute-done.45.refs_6_ = bf16[512,512]{1,0:T(8,128)(2,1)} collective-permute-done((bf16[512,512]{1,0:T(8,128)(2,1)}, bf16[512,512]{1,0:T(8,128)(2,1)}, u32[]{:S(2)}, u32[]{:S(2)}) %collective-permute-start.45) | collective-permute-done | bytes 524320 | tf_op jit(solution)/shard_map/ppermute | solution.py:472
  352.5 7.2 %backward_one_0.1.refs_8_ = f32[1792,512]{1,0:T(8,128)} custom-call(bf16[1280,512]{1,0:T(8,128)(2,1)S(1)} %turn_one_0.1.refs_0_, bf16[1280,512]{1,0:T(8,128)(2,1)} %collective-permute-done.31.refs_1_, bf16[1280,512]{1,0:T(8,128)(2,1)} %collective-permute-done.32.refs_2_, bf16[1280,512]{1,0:T(8,128)(2,1)} %collective-permute-done.43.refs_3_, ...), custom_call_target="tpu_custom_call" | custom-call | flops 10737418 | bytes 26214 | tf_op jit(solution)/shard_map/backward_one_0/pallas_call | solution.py:396
  362.2 3.8 output.1
  367.2 4.5 %place_two.1 = f32[2048,512]{1,0:T(8,128)} custom-call(s32[4]{0:T(128)S(1)} %pad_add_fusion.1.where_ref, bf16[512,512]{1,0:T(8,128)(2,1)} %pad_maximum_fusion.refs_0_, bf16[512,512]{1,0:T(8,128)(2,1)} %collective-permute-done.53.refs_1_, bf16[512,512]{1,0:T(8,128)(2,1)} %pad_maximum_fusion.1.refs_2_, bf16[512,512]{1,0:T(8,128)(2,1)} %collective-permute-done.54.refs_3_), custom_call_target="tpu_custom_call" | custom-call | flops 1048 | bytes 6291 | tf_op jit(solution)/shard_map/place_two/pallas_call | solution.py:451
  371.7 4.3 %collective-permute-done.52.refs_3_ = bf16[512,512]{1,0:T(8,128)(2,1)} collective-permute-done((bf16[512,512]{1,0:T(8,128)(2,1)}, bf16[512,512]{1,0:T(8,128)(2,1)}, u32[]{:S(2)}, u32[]{:S(2)}) %collective-permute-start.52) | collective-permute-done | bytes 524320 | tf_op jit(solution)/shard_map/ppermute | solution.py:472
  376.1 4.4 %place_one.1 = f32[2048,512]{1,0:T(8,128)} custom-call(s32[4]{0:T(128)S(1)} %pad_add_fusion.1.where_ref, bf16[512,512]{1,0:T(8,128)(2,1)} %pad_maximum_fusion.2.refs_0_, bf16[512,512]{1,0:T(8,128)(2,1)S(1)} %collective-permute-done.50.refs_1_, bf16[512,512]{1,0:T(8,128)(2,1)} %pad_maximum_fusion.3.refs_2_, bf16[512,512]{1,0:T(8,128)(2,1)} %collective-permute-done.52.refs_3_), custom_call_target="tpu_custom_call" | custom-call | flops 1048 | bytes 6291 | tf_op jit(solution)/shard_map/place_one/pallas_call | solution.py:451
  380.5 3.5 backward_one_1.1
  (239 shorter events, 81.9 us)
Async XLA Ops:
  3.2 32.1 %collective-permute-start.2 = (bf16[1280,512]{1,0:T(8,128)(2,1)}, bf16[1280,512]{1,0:T(8,128)(2,1)}, u32[]{:S(2)}, u32[]{:S(2)}) collective-permute-start(bf16[1280,512]{1,0:T(8,128)(2,1)} %slice.19), channel_id=1, source_target_pairs={{0,2},{1,3},{2,0},{3,1},{4,6},{5,7},{6,4},{7,5},{8,10},{9,11},{10,... | collective-permute-start | bytes 3932168 | tf_op jit(solution)/shard_map/ppermute | solution.py:472
  6.1 32.1 %collective-permute-start = (bf16[1792,512]{1,0:T(8,128)(2,1)}, bf16[1792,512]{1,0:T(8,128)(2,1)}, u32[]{:S(2)}, u32[]{:S(2)}) collective-permute-start(bf16[1792,512]{1,0:T(8,128)(2,1)} %refs_1_.5), channel_id=1, source_target_pairs={{0,1},{1,0},{2,3},{3,2},{4,5},{5,4},{6,7},{7,6},{8,9},{9,8},{10,11... | collective-permute-start | bytes 5505032 | tf_op jit(solution)/shard_map/ppermute | solution.py:472
  36.3 14.4 %collective-permute-start.1 = (bf16[512,512]{1,0:T(8,128)(2,1)S(1)}, bf16[512,512]{1,0:T(8,128)(2,1)S(1)}, u32[]{:S(2)}, u32[]{:S(2)}) collective-permute-start(bf16[512,512]{1,0:T(8,128)(2,1)S(1)} %slice.18), channel_id=1, source_target_pairs={{0,2},{1,3},{2,0},{3,1},{4,6},{5,7},{6,4},{7,5},{8,10},{9,11},{10,... | collective-permute-start | bytes 1572872 | tf_op jit(solution)/shard_map/ppermute | solution.py:472
  74.2 29.5 %collective-permute-start.8 = (bf16[1280,512]{1,0:T(8,128)(2,1)S(1)}, bf16[1280,512]{1,0:T(8,128)(2,1)S(1)}, u32[]{:S(2)}, u32[]{:S(2)}) collective-permute-start(bf16[1280,512]{1,0:T(8,128)(2,1)S(1)} %hidden_0.1.refs_1_), channel_id=1, source_target_pairs={{0,2},{1,3},{2,0},{3,1},{4,6},{5,7},{6,4},{7,5},{8,10},{9,11},{10,... | collective-permute-start | bytes 3932168 | tf_op jit(solution)/shard_map/ppermute | solution.py:472
  75.7 30.5 %collective-permute-start.7 = (bf16[1280,512]{1,0:T(8,128)(2,1)S(1)}, bf16[1280,512]{1,0:T(8,128)(2,1)S(1)}, u32[]{:S(2)}, u32[]{:S(2)}) collective-permute-start(bf16[1280,512]{1,0:T(8,128)(2,1)S(1)} %hidden_0.1.refs_1_), channel_id=1, source_target_pairs={{0,1},{1,0},{2,3},{3,2},{4,5},{5,4},{6,7},{7,6},{8,9},{9,8},{10,11... | collective-permute-start | bytes 3932168 | tf_op jit(solution)/shard_map/ppermute | solution.py:472
  104.7 13.7 %collective-permute-start.6 = (bf16[512,512]{1,0:T(8,128)(2,1)S(1)}, bf16[512,512]{1,0:T(8,128)(2,1)S(1)}, u32[]{:S(2)}, u32[]{:S(2)}) collective-permute-start(bf16[512,512]{1,0:T(8,128)(2,1)S(1)} %hidden_1.1.refs_1_), channel_id=1, source_target_pairs={{0,2},{1,3},{2,0},{3,1},{4,6},{5,7},{6,4},{7,5},{8,10},{9,11},{10,... | collective-permute-start | bytes 1572872 | tf_op jit(solution)/shard_map/ppermute | solution.py:472
  106.2 12.2 %collective-permute-start.5 = (bf16[512,512]{1,0:T(8,128)(2,1)S(1)}, bf16[512,512]{1,0:T(8,128)(2,1)S(1)}, u32[]{:S(2)}, u32[]{:S(2)}) collective-permute-start(bf16[512,512]{1,0:T(8,128)(2,1)S(1)} %hidden_1.1.refs_1_), channel_id=1, source_target_pairs={{0,1},{1,0},{2,3},{3,2},{4,5},{5,4},{6,7},{7,6},{8,9},{9,8},{10,11... | collective-permute-start | bytes 1572872 | tf_op jit(solution)/shard_map/ppermute | solution.py:472
  125.7 27.5 %collective-permute-start.11 = (bf16[512,512]{1,0:T(8,128)(2,1)S(1)}, bf16[512,512]{1,0:T(8,128)(2,1)S(1)}, u32[]{:S(2)}, u32[]{:S(2)}) collective-permute-start(bf16[512,512]{1,0:T(8,128)(2,1)S(1)} %get-tuple-element.82), channel_id=1, source_target_pairs={{0,2},{1,3},{2,0},{3,1},{4,6},{5,7},{6,4},{7,5},{8,10},{9,11},{10,... | collective-permute-start | bytes 1572872 | tf_op jit(solution)/shard_map/ppermute | solution.py:472
  158.9 31.9 %collective-permute-start.19 = (bf16[1280,512]{1,0:T(8,128)(2,1)S(1)}, bf16[1280,512]{1,0:T(8,128)(2,1)}, u32[]{:S(2)}, u32[]{:S(2)}) collective-permute-start(bf16[1280,512]{1,0:T(8,128)(2,1)S(1)} %turn_two_0.1.refs_0_), channel_id=1, source_target_pairs={{0,2},{1,3},{2,0},{3,1},{4,6},{5,7},{6,4},{7,5},{8,10},{9,11},{10,... | collective-permute-start | bytes 3932168 | tf_op jit(solution)/shard_map/ppermute | solution.py:472
  159.5 33.1 %collective-permute-start.13 = (bf16[1280,512]{1,0:T(8,128)(2,1)S(1)}, bf16[1280,512]{1,0:T(8,128)(2,1)}, u32[]{:S(2)}, u32[]{:S(2)}) collective-permute-start(bf16[1280,512]{1,0:T(8,128)(2,1)S(1)} %turn_two_0.1.refs_0_), channel_id=1, source_target_pairs={{0,1},{1,0},{2,3},{3,2},{4,5},{5,4},{6,7},{7,6},{8,9},{9,8},{10,11... | collective-permute-start | bytes 3932168 | tf_op jit(solution)/shard_map/ppermute | solution.py:472
  170.9 14.7 %collective-permute-start.15 = (bf16[512,512]{1,0:T(8,128)(2,1)}, bf16[512,512]{1,0:T(8,128)(2,1)}, u32[]{:S(2)}, u32[]{:S(2)}) collective-permute-start(bf16[512,512]{1,0:T(8,128)(2,1)} %constant_dynamic-slice_fusion.10), channel_id=1, source_target_pairs={{0,8},{4,12},{8,0},{12,4},{16,24},{20,28},{24,16},{28,20},{1,9},{5... | collective-permute-start | bytes 1572872 | tf_op jit(solution)/shard_map/ppermute | solution.py:472
  176.6 14.7 %collective-permute-start.14 = (bf16[512,512]{1,0:T(8,128)(2,1)}, bf16[512,512]{1,0:T(8,128)(2,1)}, u32[]{:S(2)}, u32[]{:S(2)}) collective-permute-start(bf16[512,512]{1,0:T(8,128)(2,1)} %constant_dynamic-slice_fusion.11), channel_id=1, source_target_pairs={{0,4},{4,0},{8,12},{12,8},{16,20},{20,16},{24,28},{28,24},{1,5},{5... | collective-permute-start | bytes 1572872 | tf_op jit(solution)/shard_map/ppermute | solution.py:472
  177.9 20.6 %collective-permute-start.22 = (bf16[512,512]{1,0:T(8,128)(2,1)}, bf16[512,512]{1,0:T(8,128)(2,1)}, u32[]{:S(2)}, u32[]{:S(2)}) collective-permute-start(bf16[512,512]{1,0:T(8,128)(2,1)} %get-tuple-element.93), channel_id=1, source_target_pairs={{0,2},{1,3},{2,0},{3,1},{4,6},{5,7},{6,4},{7,5},{8,10},{9,11},{10,... | collective-permute-start | bytes 1572872 | tf_op jit(solution)/shard_map/ppermute | solution.py:472
  190.8 23.4 %collective-permute-start.20 = (bf16[1280,512]{1,0:T(8,128)(2,1)}, bf16[1280,512]{1,0:T(8,128)(2,1)}, u32[]{:S(2)}, u32[]{:S(2)}) collective-permute-start(bf16[1280,512]{1,0:T(8,128)(2,1)} %collective-permute-done.19.refs_2_), channel_id=1, source_target_pairs={{0,1},{1,0},{2,3},{3,2},{4,5},{5,4},{6,7},{7,6},{8,9},{9,8},{10,11... | collective-permute-start | bytes 3932168 | tf_op jit(solution)/shard_map/ppermute | solution.py:472
  193.5 15.1 %collective-permute-start.17 = (bf16[256,512]{1,0:T(8,128)(2,1)}, bf16[256,512]{1,0:T(8,128)(2,1)}, u32[]{:S(2)}, u32[]{:S(2)}) collective-permute-start(bf16[256,512]{1,0:T(8,128)(2,1)} %constant_dynamic-slice_fusion.8), channel_id=1, source_target_pairs={{0,16},{4,20},{8,24},{12,28},{16,0},{20,4},{24,8},{28,12},{1,17},{... | collective-permute-start | bytes 786440 | tf_op jit(solution)/shard_map/ppermute | solution.py:472
  195.1 14.7 %collective-permute-start.16 = (bf16[256,512]{1,0:T(8,128)(2,1)}, bf16[256,512]{1,0:T(8,128)(2,1)}, u32[]{:S(2)}, u32[]{:S(2)}) collective-permute-start(bf16[256,512]{1,0:T(8,128)(2,1)} %constant_dynamic-slice_fusion.9), channel_id=1, source_target_pairs={{0,8},{4,12},{8,0},{12,4},{16,24},{20,28},{24,16},{28,20},{1,9},{5... | collective-permute-start | bytes 786440 | tf_op jit(solution)/shard_map/ppermute | solution.py:472
  196.4 16.4 %collective-permute-start.12 = (bf16[512,512]{1,0:T(8,128)(2,1)}, bf16[512,512]{1,0:T(8,128)(2,1)}, u32[]{:S(2)}, u32[]{:S(2)}) collective-permute-start(bf16[512,512]{1,0:T(8,128)(2,1)} %turn_two_1.1.refs_1_.refs_0_), channel_id=1, source_target_pairs={{0,1},{1,0},{2,3},{3,2},{4,5},{5,4},{6,7},{7,6},{8,9},{9,8},{10,11... | collective-permute-start | bytes 1572872 | tf_op jit(solution)/shard_map/ppermute | solution.py:472
  198.5 15.7 %collective-permute-start.21 = (bf16[512,512]{1,0:T(8,128)(2,1)}, bf16[512,512]{1,0:T(8,128)(2,1)}, u32[]{:S(2)}, u32[]{:S(2)}) collective-permute-start(bf16[512,512]{1,0:T(8,128)(2,1)} %get-tuple-element.92), channel_id=1, source_target_pairs={{0,1},{1,0},{2,3},{3,2},{4,5},{5,4},{6,7},{7,6},{8,9},{9,8},{10,11... | collective-permute-start | bytes 1572872 | tf_op jit(solution)/shard_map/ppermute | solution.py:472
  208.6 16.4 %collective-permute-start.18 = (bf16[512,512]{1,0:T(8,128)(2,1)}, bf16[512,512]{1,0:T(8,128)(2,1)}, u32[]{:S(2)}, u32[]{:S(2)}) collective-permute-start(bf16[512,512]{1,0:T(8,128)(2,1)} %turn_two_1.1.refs_1_.refs_0_), channel_id=1, source_target_pairs={{0,2},{1,3},{2,0},{3,1},{4,6},{5,7},{6,4},{7,5},{8,10},{9,11},{10,... | collective-permute-start | bytes 1572872 | tf_op jit(solution)/shard_map/ppermute | solution.py:472
  213.5 11.9 %collective-permute-start.26 = (bf16[128,512]{1,0:T(8,128)(2,1)}, bf16[128,512]{1,0:T(8,128)(2,1)}, u32[]{:S(2)}, u32[]{:S(2)}) collective-permute-start(bf16[128,512]{1,0:T(8,128)(2,1)} %constant_dynamic-slice_fusion.6), channel_id=1, source_target_pairs={{0,4},{4,0},{8,12},{12,8},{16,20},{20,16},{24,28},{28,24},{1,5},{5... | collective-permute-start | bytes 393224 | tf_op jit(solution)/shard_map/ppermute | solution.py:472
  225.0 8.2 %collective-permute-start.24 = (bf16[512,512]{1,0:T(8,128)(2,1)}, bf16[512,512]{1,0:T(8,128)(2,1)S(1)}, u32[]{:S(2)}, u32[]{:S(2)}) collective-permute-start(bf16[512,512]{1,0:T(8,128)(2,1)} %collective-permute-done.18.refs_2_), channel_id=1, source_target_pairs={{0,1},{1,0},{2,3},{3,2},{4,5},{5,4},{6,7},{7,6},{8,9},{9,8},{10,11... | collective-permute-start | bytes 1572872 | tf_op jit(solution)/shard_map/ppermute | solution.py:472
  225.3 7.8 %collective-permute-start.25 = (bf16[128,512]{1,0:T(8,128)(2,1)S(1)}, bf16[128,512]{1,0:T(8,128)(2,1)S(1)}, u32[]{:S(2)}, u32[]{:S(2)}) collective-permute-start(bf16[128,512]{1,0:T(8,128)(2,1)S(1)} %constant_dynamic-slice_fusion.7), channel_id=1, source_target_pairs={{0,16},{4,20},{8,24},{12,28},{16,0},{20,4},{24,8},{28,12},{1,17},{... | collective-permute-start | bytes 393224 | tf_op jit(solution)/shard_map/ppermute | solution.py:472
  237.8 6.6 %collective-permute-start.28 = (bf16[128,512]{1,0:T(8,128)(2,1)S(1)}, bf16[128,512]{1,0:T(8,128)(2,1)S(1)}, u32[]{:S(2)}, u32[]{:S(2)}) collective-permute-start(bf16[128,512]{1,0:T(8,128)(2,1)S(1)} %add_convert_fusion.10), channel_id=1, source_target_pairs={{0,4},{4,0},{8,12},{12,8},{16,20},{20,16},{24,28},{28,24},{1,5},{5... | collective-permute-start | bytes 393224 | tf_op jit(solution)/shard_map/ppermute | solution.py:472
  239.5 8.8 %collective-permute-start.27 = (bf16[128,512]{1,0:T(8,128)(2,1)S(1)}, bf16[128,512]{1,0:T(8,128)(2,1)S(1)}, u32[]{:S(2)}, u32[]{:S(2)}) collective-permute-start(bf16[128,512]{1,0:T(8,128)(2,1)S(1)} %add_convert_fusion.11), channel_id=1, source_target_pairs={{0,16},{4,20},{8,24},{12,28},{16,0},{20,4},{24,8},{28,12},{1,17},{... | collective-permute-start | bytes 393224 | tf_op jit(solution)/shard_map/ppermute | solution.py:472
  240.2 12.6 %all-to-all-start.3 = ((f32[8,8,512]{2,1,0:T(8,128)}), f32[8,8,512]{2,1,0:T(8,128)S(1)}, u32[]{:S(2)}, u32[]{:S(2)}) async-start(f32[8,8,512]{2,1,0:T(8,128)} %broadcast_in_dim.11), calls=%async_computation.3 | async-start | bytes 262144 | tf_op jit(solution)/shard_map/all_to_all | solution.py:94
  249.8 21.1 %collective-permute-start.36 = (bf16[256,512]{1,0:T(8,128)(2,1)}, bf16[256,512]{1,0:T(8,128)(2,1)}, u32[]{:S(2)}, u32[]{:S(2)}) collective-permute-start(bf16[256,512]{1,0:T(8,128)(2,1)} %pad_maximum_fusion.5), channel_id=1, source_target_pairs={{0,16},{4,20},{8,24},{12,28},{16,0},{20,4},{24,8},{28,12},{1,17},{... | collective-permute-start | bytes 786440 | tf_op jit(solution)/shard_map/ppermute | solution.py:472
  249.8 22.2 %collective-permute-start.35 = (bf16[256,512]{1,0:T(8,128)(2,1)}, bf16[256,512]{1,0:T(8,128)(2,1)}, u32[]{:S(2)}, u32[]{:S(2)}) collective-permute-start(bf16[256,512]{1,0:T(8,128)(2,1)} %pad_maximum_fusion.4), channel_id=1, source_target_pairs={{0,8},{4,12},{8,0},{12,4},{16,24},{20,28},{24,16},{28,20},{1,9},{5... | collective-permute-start | bytes 786440 | tf_op jit(solution)/shard_map/ppermute | solution.py:472
  266.5 13.1 %collective-permute-start.34 = (bf16[512,512]{1,0:T(8,128)(2,1)S(1)}, bf16[512,512]{1,0:T(8,128)(2,1)S(1)}, u32[]{:S(2)}, u32[]{:S(2)}) collective-permute-start(bf16[512,512]{1,0:T(8,128)(2,1)S(1)} %constant_dynamic-slice_fusion.4), channel_id=1, source_target_pairs={{0,8},{4,12},{8,0},{12,4},{16,24},{20,28},{24,16},{28,20},{1,9},{5... | collective-permute-start | bytes 1572872 | tf_op jit(solution)/shard_map/ppermute | solution.py:472
  270.4 13.1 %collective-permute-start.33 = (bf16[512,512]{1,0:T(8,128)(2,1)S(1)}, bf16[512,512]{1,0:T(8,128)(2,1)S(1)}, u32[]{:S(2)}, u32[]{:S(2)}) collective-permute-start(bf16[512,512]{1,0:T(8,128)(2,1)S(1)} %constant_dynamic-slice_fusion.5), channel_id=1, source_target_pairs={{0,4},{4,0},{8,12},{12,8},{16,20},{20,16},{24,28},{28,24},{1,5},{5... | collective-permute-start | bytes 1572872 | tf_op jit(solution)/shard_map/ppermute | solution.py:472
  283.7 13.1 %collective-permute-start.40 = (bf16[256,512]{1,0:T(8,128)(2,1)S(1)}, bf16[256,512]{1,0:T(8,128)(2,1)S(1)}, u32[]{:S(2)}, u32[]{:S(2)}) collective-permute-start(bf16[256,512]{1,0:T(8,128)(2,1)S(1)} %constant_dynamic-slice_fusion.1), channel_id=1, source_target_pairs={{0,16},{4,20},{8,24},{12,28},{16,0},{20,4},{24,8},{28,12},{1,17},{... | collective-permute-start | bytes 786440 | tf_op jit(solution)/shard_map/ppermute | solution.py:472
  285.6 42.9 %collective-permute-start.32 = (bf16[1280,512]{1,0:T(8,128)(2,1)S(1)}, bf16[1280,512]{1,0:T(8,128)(2,1)}, u32[]{:S(2)}, u32[]{:S(2)}) collective-permute-start(bf16[1280,512]{1,0:T(8,128)(2,1)S(1)} %turn_one_0.1.refs_0_), channel_id=1, source_target_pairs={{0,2},{1,3},{2,0},{3,1},{4,6},{5,7},{6,4},{7,5},{8,10},{9,11},{10,... | collective-permute-start | bytes 3932168 | tf_op jit(solution)/shard_map/ppermute | solution.py:472
  286.7 63.7 %collective-permute-start.31 = (bf16[1280,512]{1,0:T(8,128)(2,1)S(1)}, bf16[1280,512]{1,0:T(8,128)(2,1)}, u32[]{:S(2)}, u32[]{:S(2)}) collective-permute-start(bf16[1280,512]{1,0:T(8,128)(2,1)S(1)} %turn_one_0.1.refs_0_), channel_id=1, source_target_pairs={{0,1},{1,0},{2,3},{3,2},{4,5},{5,4},{6,7},{7,6},{8,9},{9,8},{10,11... | collective-permute-start | bytes 3932168 | tf_op jit(solution)/shard_map/ppermute | solution.py:472
  286.7 43.4 %collective-permute-start.46 = (bf16[512,512]{1,0:T(8,128)(2,1)S(1)}, bf16[512,512]{1,0:T(8,128)(2,1)S(1)}, u32[]{:S(2)}, u32[]{:S(2)}) collective-permute-start(bf16[512,512]{1,0:T(8,128)(2,1)S(1)} %copy-done.44), channel_id=1, source_target_pairs={{0,2},{1,3},{2,0},{3,1},{4,6},{5,7},{6,4},{7,5},{8,10},{9,11},{10,... | collective-permute-start | bytes 1572872 | tf_op jit(solution)/shard_map/ppermute | solution.py:472
  287.6 42.5 %collective-permute-start.44 = (bf16[512,512]{1,0:T(8,128)(2,1)S(1)}, bf16[512,512]{1,0:T(8,128)(2,1)S(1)}, u32[]{:S(2)}, u32[]{:S(2)}) collective-permute-start(bf16[512,512]{1,0:T(8,128)(2,1)S(1)} %copy-done.43), channel_id=1, source_target_pairs={{0,1},{1,0},{2,3},{3,2},{4,5},{5,4},{6,7},{7,6},{8,9},{9,8},{10,11... | collective-permute-start | bytes 1572872 | tf_op jit(solution)/shard_map/ppermute | solution.py:472
  296.7 7.3 %collective-permute-start.37 = (bf16[256,512]{1,0:T(8,128)(2,1)S(1)}, bf16[256,512]{1,0:T(8,128)(2,1)S(1)}, u32[]{:S(2)}, u32[]{:S(2)}) collective-permute-start(bf16[256,512]{1,0:T(8,128)(2,1)S(1)} %constant_dynamic-slice_fusion.3), channel_id=1, source_target_pairs={{0,8},{4,12},{8,0},{12,4},{16,24},{20,28},{24,16},{28,20},{1,9},{5... | collective-permute-start | bytes 786440 | tf_op jit(solution)/shard_map/ppermute | solution.py:472
  309.0 7.0 %collective-permute-start.38 = (bf16[128,512]{1,0:T(8,128)(2,1)S(1)}, bf16[128,512]{1,0:T(8,128)(2,1)S(1)}, u32[]{:S(2)}, u32[]{:S(2)}) collective-permute-start(bf16[128,512]{1,0:T(8,128)(2,1)S(1)} %constant_dynamic-slice_fusion.2), channel_id=1, source_target_pairs={{0,16},{4,20},{8,24},{12,28},{16,0},{20,4},{24,8},{28,12},{1,17},{... | collective-permute-start | bytes 393224 | tf_op jit(solution)/shard_map/ppermute | solution.py:472
  320.9 6.0 %collective-permute-start.39 = (bf16[128,512]{1,0:T(8,128)(2,1)S(1)}, bf16[128,512]{1,0:T(8,128)(2,1)S(1)}, u32[]{:S(2)}, u32[]{:S(2)}) collective-permute-start(bf16[128,512]{1,0:T(8,128)(2,1)S(1)} %add_convert_fusion.9), channel_id=1, source_target_pairs={{0,16},{4,20},{8,24},{12,28},{16,0},{20,4},{24,8},{28,12},{1,17},{... | collective-permute-start | bytes 393224 | tf_op jit(solution)/shard_map/ppermute | solution.py:472
  328.5 22.0 %collective-permute-start.43 = (bf16[1280,512]{1,0:T(8,128)(2,1)}, bf16[1280,512]{1,0:T(8,128)(2,1)}, u32[]{:S(2)}, u32[]{:S(2)}) collective-permute-start(bf16[1280,512]{1,0:T(8,128)(2,1)} %collective-permute-done.32.refs_2_), channel_id=1, source_target_pairs={{0,1},{1,0},{2,3},{3,2},{4,5},{5,4},{6,7},{7,6},{8,9},{9,8},{10,11... | collective-permute-start | bytes 3932168 | tf_op jit(solution)/shard_map/ppermute | solution.py:472
  328.5 14.7 %collective-permute-start.45 = (bf16[512,512]{1,0:T(8,128)(2,1)}, bf16[512,512]{1,0:T(8,128)(2,1)}, u32[]{:S(2)}, u32[]{:S(2)}) collective-permute-start(bf16[512,512]{1,0:T(8,128)(2,1)} %get-tuple-element.115), channel_id=1, source_target_pairs={{0,2},{1,3},{2,0},{3,1},{4,6},{5,7},{6,4},{7,5},{8,10},{9,11},{10,... | collective-permute-start | bytes 1572872 | tf_op jit(solution)/shard_map/ppermute | solution.py:472
  330.1 14.9 %collective-permute-start.51 = (bf16[256,512]{1,0:T(8,128)(2,1)}, bf16[256,512]{1,0:T(8,128)(2,1)}, u32[]{:S(2)}, u32[]{:S(2)}) collective-permute-start(bf16[256,512]{1,0:T(8,128)(2,1)} %pad_maximum_fusion.7), channel_id=1, source_target_pairs={{0,16},{4,20},{8,24},{12,28},{16,0},{20,4},{24,8},{28,12},{1,17},{... | collective-permute-start | bytes 786440 | tf_op jit(solution)/shard_map/ppermute | solution.py:472
  331.7 14.3 %collective-permute-start.49 = (bf16[256,512]{1,0:T(8,128)(2,1)}, bf16[256,512]{1,0:T(8,128)(2,1)}, u32[]{:S(2)}, u32[]{:S(2)}) collective-permute-start(bf16[256,512]{1,0:T(8,128)(2,1)} %pad_maximum_fusion.6), channel_id=1, source_target_pairs={{0,8},{4,12},{8,0},{12,4},{16,24},{20,28},{24,16},{28,20},{1,9},{5... | collective-permute-start | bytes 786440 | tf_op jit(solution)/shard_map/ppermute | solution.py:472
  343.1 16.6 %collective-permute-start.30 = (bf16[512,512]{1,0:T(8,128)(2,1)S(1)}, bf16[512,512]{1,0:T(8,128)(2,1)}, u32[]{:S(2)}, u32[]{:S(2)}) collective-permute-start(bf16[512,512]{1,0:T(8,128)(2,1)S(1)} %copy-done.11), channel_id=1, source_target_pairs={{0,2},{1,3},{2,0},{3,1},{4,6},{5,7},{6,4},{7,5},{8,10},{9,11},{10,... | collective-permute-start | bytes 1572872 | tf_op jit(solution)/shard_map/ppermute | solution.py:472
  345.1 16.2 %collective-permute-start.29 = (bf16[512,512]{1,0:T(8,128)(2,1)S(1)}, bf16[512,512]{1,0:T(8,128)(2,1)S(1)}, u32[]{:S(2)}, u32[]{:S(2)}) collective-permute-start(bf16[512,512]{1,0:T(8,128)(2,1)S(1)} %copy-done.11), channel_id=1, source_target_pairs={{0,1},{1,0},{2,3},{3,2},{4,5},{5,4},{6,7},{7,6},{8,9},{9,8},{10,11... | collective-permute-start | bytes 1572872 | tf_op jit(solution)/shard_map/ppermute | solution.py:472
  349.9 17.3 %collective-permute-start.53 = (bf16[512,512]{1,0:T(8,128)(2,1)}, bf16[512,512]{1,0:T(8,128)(2,1)}, u32[]{:S(2)}, u32[]{:S(2)}) collective-permute-start(bf16[512,512]{1,0:T(8,128)(2,1)} %pad_maximum_fusion.refs_0_), channel_id=1, source_target_pairs={{0,4},{4,0},{8,12},{12,8},{16,20},{20,16},{24,28},{28,24},{1,5},{5... | collective-permute-start | bytes 1572872 | tf_op jit(solution)/shard_map/ppermute | solution.py:472
  350.4 16.7 %collective-permute-start.54 = (bf16[512,512]{1,0:T(8,128)(2,1)}, bf16[512,512]{1,0:T(8,128)(2,1)}, u32[]{:S(2)}, u32[]{:S(2)}) collective-permute-start(bf16[512,512]{1,0:T(8,128)(2,1)} %pad_maximum_fusion.1.refs_2_), channel_id=1, source_target_pairs={{0,8},{4,12},{8,0},{12,4},{16,24},{20,28},{24,16},{28,20},{1,9},{5... | collective-permute-start | bytes 1572872 | tf_op jit(solution)/shard_map/ppermute | solution.py:472
  350.5 25.6 %collective-permute-start.52 = (bf16[512,512]{1,0:T(8,128)(2,1)}, bf16[512,512]{1,0:T(8,128)(2,1)}, u32[]{:S(2)}, u32[]{:S(2)}) collective-permute-start(bf16[512,512]{1,0:T(8,128)(2,1)} %pad_maximum_fusion.3.refs_2_), channel_id=1, source_target_pairs={{0,8},{4,12},{8,0},{12,4},{16,24},{20,28},{24,16},{28,20},{1,9},{5... | collective-permute-start | bytes 1572872 | tf_op jit(solution)/shard_map/ppermute | solution.py:472
  359.7 16.3 %collective-permute-start.50 = (bf16[512,512]{1,0:T(8,128)(2,1)}, bf16[512,512]{1,0:T(8,128)(2,1)S(1)}, u32[]{:S(2)}, u32[]{:S(2)}) collective-permute-start(bf16[512,512]{1,0:T(8,128)(2,1)} %pad_maximum_fusion.2.refs_0_), channel_id=1, source_target_pairs={{0,4},{4,0},{8,12},{12,8},{16,20},{20,16},{24,28},{28,24},{1,5},{5... | collective-permute-start | bytes 1572872 | tf_op jit(solution)/shard_map/ppermute | solution.py:472
  362.1 18.3 %collective-permute-start.48 = (bf16[512,512]{1,0:T(8,128)(2,1)}, bf16[512,512]{1,0:T(8,128)(2,1)S(1)}, u32[]{:S(2)}, u32[]{:S(2)}) collective-permute-start(bf16[512,512]{1,0:T(8,128)(2,1)} %collective-permute-done.30.refs_2_), channel_id=1, source_target_pairs={{0,1},{1,0},{2,3},{3,2},{4,5},{5,4},{6,7},{7,6},{8,9},{9,8},{10,11... | collective-permute-start | bytes 1572872 | tf_op jit(solution)/shard_map/ppermute | solution.py:472
  (55 other events, 414.5 us)

commit v3 on v0

v3 whole, which is shorter than its diff:
```python
import functools

import jax
import jax.numpy as jnp
from jax import lax
from jax.experimental import pallas as pl
from jax.experimental.pallas import tpu as pltpu
from jax.sharding import PartitionSpec as P

SLOT = 128
NBR = 32
LANES = 128
EPSILON = 1e-05
ANY = pl.BlockSpec(memory_space=pl.ANY)
BF = jnp.bfloat16
F32 = jnp.float32


def params(limit):
    return pltpu.CompilerParams(dimension_semantics=("arbitrary",), vmem_limit_bytes=limit << 20)


SMALL = pl.CostEstimate(flops=1000000, bytes_accessed=1000, transcendentals=0)


TOKEN = jax.ShapeDtypeStruct((8, LANES), F32)


def token_spec():
    return pl.BlockSpec((8, LANES), lambda i, *_: (0, 0))


def mark(token_ref):
    token_ref[...] = jnp.zeros_like(token_ref)


def launch(kernel, grid, ins, outs, shapes, args, name, prefetch=(), scratch=(), tokens=(), limit=24):
    count = len(prefetch) + len(args)

    def body(*refs):
        kernel(*refs[:count], *refs[count + len(tokens) :])

    return pl.pallas_call(
        body,
        grid_spec=pltpu.PrefetchScalarGridSpec(
            num_scalar_prefetch=len(prefetch),
            grid=grid,
            in_specs=[*ins, *[pl.BlockSpec(memory_space=pl.ANY)] * len(tokens)],
            out_specs=outs,
            scratch_shapes=list(scratch),
        ),
        out_shape=shapes,
        compiler_params=params(limit),
        cost_estimate=SMALL,
        name=name,
    )(*prefetch, *args, *tokens)


def dot(a, b):
    return jnp.dot(a, b, preferred_element_type=F32)


def dot_t(a, b):
    return lax.dot_general(a, b, (((1,), (1,)), ((), ())), preferred_element_type=F32)


def wide(v, columns):
    return jnp.concatenate([v] * (columns // LANES), axis=1)


def tiles_kernel(nbr_ref, valid_ref, h_ref, ht_ref, inv_ref, val_ref, token_ref):
    mark(token_ref)
    entries = nbr_ref[0]
    rows = lax.broadcasted_iota(jnp.int32, (SLOT, SLOT), 0)
    cols = lax.broadcasted_iota(jnp.int32, (SLOT, SLOT), 1)
    hits = jnp.zeros((SLOT, SLOT), F32)
    degree = jnp.zeros((1, SLOT), F32)
    for k in range(entries.shape[0]):
        one = entries[k : k + 1, :]
        hits += (one == rows).astype(F32)
        degree += (one >= 0).astype(F32)
    eye = (rows == cols).astype(F32)
    joined = hits + eye
    counts = joined + joined * eye
    ht_ref[0] = wide(counts.astype(BF), 2 * SLOT)
    h_ref[0] = wide(counts.T.astype(BF), 2 * SLOT)
    inv_ref[0] = jnp.broadcast_to(1.0 / (degree + 1.0), (SLOT, SLOT)).T
    val_ref[0] = jnp.broadcast_to(valid_ref[0].astype(F32), (SLOT, SLOT)).T


def build_tiles(neighbours, node_valid):
    slots = neighbours.shape[0] // SLOT
    turned = neighbours.reshape(slots, SLOT, NBR).transpose(0, 2, 1)
    square = pl.BlockSpec((1, SLOT, SLOT), lambda i: (i, 0, 0))
    double = pl.BlockSpec((1, SLOT, 2 * SLOT), lambda i: (i, 0, 0))
    return launch(
        tiles_kernel, (slots,),
        [pl.BlockSpec((1, NBR, SLOT), lambda i: (i, 0, 0)), pl.BlockSpec((1, 1, SLOT), lambda i: (i, 0, 0))],
        [double, double, square, square, token_spec()],
        [jax.ShapeDtypeStruct((slots, SLOT, 2 * SLOT), BF)] * 2 + [jax.ShapeDtypeStruct((slots, SLOT, SLOT), F32)] * 2 + [TOKEN],
        [turned, node_valid.reshape(slots, 1, SLOT)], "tiles",
    )


def combine(g_ref):
    mref, first, second, count = (g_ref[:, k, :] for k in range(4))
    shift = first / count
    mean_each = mref + shift
    spread_each = second - first * shift
    total = jnp.sum(count, axis=0, keepdims=True)
    mean = jnp.sum(count * mean_each, axis=0, keepdims=True) / total
    away = mean_each - mean
    variance = jnp.sum(spread_each + count * away * away, axis=0, keepdims=True) / total
    return total, mean, lax.rsqrt(variance + EPSILON)


def small_gather(copies, axis):
    return lax.all_to_all(copies, axis, split_axis=0, concat_axis=0, tiled=True)


def copies_shape(columns):
    return (lax.axis_size("row"), 8, columns)


def spread_rows(out_ref, rows):
    block = jnp.concatenate([*rows, jnp.zeros((8 - len(rows), out_ref.shape[2]), F32)], axis=0)

    def one(n, carry):
        out_ref[n] = block
        return carry

    lax.fori_loop(0, out_ref.shape[0], one, 0)


def split(value):
    high = value.astype(BF)
    return high, (value - high.astype(F32)).astype(BF)


def fold(value):
    return jnp.sum(value.reshape(value.shape[0] // 8, 8, value.shape[1]), axis=0)


def at(ref, k):
    return ref[k : k + 1, :]


def put(ref, k, value):
    ref[k : k + 1, :] = value


def half_kernel(turned, x_ref, y_ref, w_own, w_near, out_ref, token_ref):
    mark(token_ref)
    product = dot_t if turned else dot
    out_ref[...] = product(x_ref[...], w_own[...]) + product(y_ref[...], w_near[...])


def half(ids, big, own, near, weights, turned, name, tokens=()):
    nodes, depth = own.shape
    columns = weights[0][0].shape[1]
    rows = big * SLOT
    flat = pl.BlockSpec((rows, depth), lambda i, ids: (i, 0))

    def kernel(ids_ref, *refs):
        half_kernel(turned, *refs)

    return launch(
        kernel, (nodes // rows,), [flat, flat, *[spec for _, spec in weights]],
        [pl.BlockSpec((rows, columns), lambda i, ids: (i, 0)), token_spec()],
        [jax.ShapeDtypeStruct((nodes, columns), F32), TOKEN],
        [own, near, *[w for w, _ in weights]], name, prefetch=[ids], tokens=tokens,
    )


def weight_block(weight, b):
    depth = weight.shape[0] // 4
    return weight, pl.BlockSpec((depth, weight.shape[1]), lambda i, ids: (ids[b], 0))


def whole_block(piece):
    return piece, pl.BlockSpec(piece.shape, lambda i, ids: (0, 0))


def each_part(big, body, part=32, inner=4):
    def slot(s, carry):
        for r in range(SLOT // part):
            start = pl.multiple_of(s * SLOT + r * part, part)
            body(s, slice(r * part, (r + 1) * part), pl.ds(start, part))
        return carry

    lax.fori_loop(0, big, slot, 0)


def forward_kernel(big, ids_ref, early_ref, x_ref, y_ref, w_far, w_beyond, h_ref, inv_ref, val_ref, lin_ref, st_ref, tot_ref, acc_ref, ref_ref):
    i = pl.program_id(0)
    columns = lin_ref.shape[1]
    tot_ref[...] = early_ref[...] + dot(x_ref[...], w_far[...]) + dot(y_ref[...], w_beyond[...])

    def mix(s, carry):
        rows = pl.ds(pl.multiple_of(s * SLOT, SLOT), SLOT)
        high, low = split(tot_ref[rows, :])
        both = jnp.concatenate([high, low], axis=0)
        lin_ref[rows, :] = dot(h_ref[s], both) * wide(inv_ref[s], columns)
        return carry

    lax.fori_loop(0, big, mix, 0)

    @pl.when(i == 0)
    def _():
        acc_ref[...] = jnp.zeros_like(acc_ref)
        v = val_ref[0]
        count = jnp.sum(v, axis=0, keepdims=True)
        put(ref_ref, 0, jnp.sum(lin_ref[:SLOT, :] * wide(v, columns), axis=0, keepdims=True) / wide(count, columns))

    mref = at(ref_ref, 0)

    def part(s, inner, rows):
        v = val_ref[s, inner, :]
        away = (lin_ref[rows, :] - mref) * wide(v, columns)
        acc_ref[0] += fold(away)
        acc_ref[1] += fold(away * away)
        acc_ref[2, :, :LANES] += fold(v)

    each_part(big, part)

    @pl.when(i == pl.num_programs(0) - 1)
    def _():
        first, second = (jnp.sum(acc_ref[k], axis=0, keepdims=True) for k in range(2))
        count = wide(jnp.sum(acc_ref[2, :, :LANES], axis=0, keepdims=True), columns)
        spread_rows(st_ref, (at(ref_ref, 0), first, second, count))


def forward(ids, big, early, far, beyond, weight, tiles, name, tokens=()):
    h, _, inv, val = tiles
    nodes, columns = early.shape
    rows = big * SLOT
    flat = pl.BlockSpec((rows, columns), lambda i, ids: (i, 0))
    tile = pl.BlockSpec((big, SLOT, SLOT), lambda i, ids: (i, 0, 0))
    double = pl.BlockSpec((big, SLOT, 2 * SLOT), lambda i, ids: (i, 0, 0))
    blocks = [weight_block(weight, 2), weight_block(weight, 3)]
    return launch(
        functools.partial(forward_kernel, big), (nodes // rows,),
        [flat, flat, flat, *[spec for _, spec in blocks], double, tile, tile],
        [flat, pl.BlockSpec(copies_shape(columns), lambda i, ids: (0, 0, 0))],
        [jax.ShapeDtypeStruct((nodes, columns), F32), jax.ShapeDtypeStruct(copies_shape(columns), F32)],
        [early, far, beyond, weight, weight, h, inv, val], name, prefetch=[ids],
        scratch=[pltpu.VMEM((rows, columns), F32), pltpu.VMEM((3, 8, columns), F32), pltpu.VMEM((8, columns), F32)],
        tokens=tokens,
    )


def columns_of(g_ref, gamma_ref, beta_ref, co_ref):
    total, mean, inv_std = combine(g_ref)
    put(co_ref, 0, mean)
    put(co_ref, 1, 0.5 * gamma_ref[...] * inv_std)
    put(co_ref, 2, 0.5 * beta_ref[...])
    put(co_ref, 3, inv_std)
    put(co_ref, 4, total)


def silu_of(away, co_ref):
    u = away * at(co_ref, 1) + at(co_ref, 2)
    return u + u * jnp.tanh(u)


def double_slope(away, co_ref):
    u = away * at(co_ref, 1) + at(co_ref, 2)
    t = jnp.tanh(u)
    return (1.0 + t) * (1.0 + u * (1.0 - t))


def result_kernel(big, lin_ref, val_ref, g_ref, gamma_ref, beta_ref, out_ref, token_ref, co_ref):
    mark(token_ref)

    @pl.when(pl.program_id(0) == 0)
    def _():
        columns_of(g_ref, gamma_ref, beta_ref, co_ref)

    def part(s, inner, rows):
        value = silu_of(lin_ref[rows, :] - at(co_ref, 0), co_ref)
        out_ref[rows, :] = (wide(val_ref[s, inner, :], lin_ref.shape[1]) * value).astype(out_ref.dtype)

    each_part(big, part)


def sums_kernel(big, lin_ref, cot_ref, val_ref, g_ref, gamma_ref, beta_ref, st_ref, co_ref, acc_ref):
    @pl.when(pl.program_id(0) == 0)
    def _():
        columns_of(g_ref, gamma_ref, beta_ref, co_ref)
        acc_ref[...] = jnp.zeros_like(acc_ref)

    def part(s, inner, rows):
        away = lin_ref[rows, :] - at(co_ref, 0)
        valid = wide(val_ref[s, inner, :], lin_ref.shape[1])
        grad = cot_ref[rows, :].astype(F32) * valid * double_slope(away, co_ref)
        acc_ref[0] += fold(grad)
        acc_ref[1] += fold(grad * away)

    each_part(big, part)
    finish_sums(st_ref, co_ref, acc_ref)


def finish_sums(st_ref, co_ref, acc_ref):
    @pl.when(pl.program_id(0) == pl.num_programs(0) - 1)
    def _():
        grad_beta = 0.5 * jnp.sum(acc_ref[0], axis=0, keepdims=True)
        grad_gamma = 0.5 * at(co_ref, 3) * jnp.sum(acc_ref[1], axis=0, keepdims=True)
        spread_rows(st_ref, (grad_beta, grad_gamma))


def turn_kernel(from_cot, big, lin_ref, grad_ref, val_ref, inv_ref, ht_ref, g_ref, sg_ref, gamma_ref, beta_ref, out_ref, token_ref, co_ref, lg_ref):
    mark(token_ref)

    @pl.when(pl.program_id(0) == 0)
    def _():
        columns_of(g_ref, gamma_ref, beta_ref, co_ref)
        sg = sg_ref[...]
        twice = 2.0 / at(co_ref, 4)
        put(co_ref, 5, twice * jnp.sum(sg[:, 0, :], axis=0, keepdims=True))
        put(co_ref, 6, twice * at(co_ref, 3) * jnp.sum(sg[:, 1, :], axis=0, keepdims=True))

    columns = lin_ref.shape[1]

    def part(s, inner, rows):
        away = lin_ref[rows, :] - at(co_ref, 0)
        if from_cot:
            grad = grad_ref[rows, :].astype(F32) * double_slope(away, co_ref)
        else:
            grad = grad_ref[rows, :]
        weight = wide(val_ref[s, inner, :] * inv_ref[s, inner, :], columns)
        high, low = split(weight * (grad - (at(co_ref, 5) + away * at(co_ref, 6))))
        lg_ref[s, inner, :] = high
        lg_ref[s, slice(inner.start + SLOT, inner.stop + SLOT), :] = low

    each_part(big, part)

    def mix(s, carry):
        rows = pl.ds(pl.multiple_of(s * SLOT, SLOT), SLOT)
        out_ref[rows, :] = (dot(ht_ref[s], lg_ref[s]) * at(co_ref, 1)).astype(BF)
        return carry

    lax.fori_loop(0, big, mix, 0)


def rows_call(kernel, big, arrays, tiles, smalls, out_dtype, scratch, name, tokens=(), limit=24):
    rows = big * SLOT
    nodes, columns = arrays[0].shape
    flat = pl.BlockSpec((rows, columns), lambda i: (i, 0))
    ins = [flat for _ in arrays]
    ins += [pl.BlockSpec((big,) + t.shape[1:], lambda i: (i, 0, 0)) for t in tiles]
    ins += [pl.BlockSpec(s.shape, lambda i, n=s.ndim: (0,) * n) for s in smalls]
    if out_dtype is None:
        out_spec = pl.BlockSpec(copies_shape(columns), lambda i: (0, 0, 0))
        out_shape = jax.ShapeDtypeStruct(copies_shape(columns), F32)
    else:
        out_spec = [flat, token_spec()]
        out_shape = [jax.ShapeDtypeStruct((nodes, columns), out_dtype), TOKEN]
    return launch(
        functools.partial(kernel, big), (nodes // rows,), ins, out_spec, out_shape, [*arrays, *tiles, *smalls], name,
        scratch=[pltpu.VMEM((8, columns), F32)] + scratch, tokens=tokens, limit=limit,
    )


def turn_call(from_cot, big, lin, grad, tiles, norm, sums, name, tokens=()):
    _, ht, inv, val = tiles
    return rows_call(
        functools.partial(turn_kernel, from_cot), big, [lin, grad], [val, inv, ht], [norm[0], sums, *norm[1:]], BF,
        [pltpu.VMEM((big, 2 * SLOT, lin.shape[1]), BF)], name, tokens, 60,
    )


def backward_kernel(big, last, early_ref, x_ref, y_ref, w_far, w_beyond, *refs):
    total = early_ref[...] + dot_t(x_ref[...], w_far[...]) + dot_t(y_ref[...], w_beyond[...])
    if last:
        refs[-2][...] = total
        mark(refs[-1])
        return
    lin_ref, g_ref, gamma_ref, beta_ref, out_ref, st_ref, co_ref, acc_ref = refs
    out_ref[...] = total

    @pl.when(pl.program_id(0) == 0)
    def _():
        columns_of(g_ref, gamma_ref, beta_ref, co_ref)
        acc_ref[...] = jnp.zeros_like(acc_ref)

    def part(s, inner, rows):
        away = lin_ref[rows, :] - at(co_ref, 0)
        grad = out_ref[rows, :] * double_slope(away, co_ref)
        out_ref[rows, :] = grad
        acc_ref[0] += fold(grad)
        acc_ref[1] += fold(grad * away)

    each_part(big, part)
    finish_sums(st_ref, co_ref, acc_ref)


def backward(big, early, far, beyond, pieces, lin, norm, name, tokens=()):
    nodes, columns = early.shape
    depth = far.shape[1]
    rows = big * SLOT
    last = norm is None
    flat = pl.BlockSpec((rows, columns), lambda i: (i, 0))
    fixed = lambda s: pl.BlockSpec(s.shape, lambda i, n=s.ndim: (0,) * n)
    ins = [flat, flat, flat, *map(fixed, pieces)]
    args = [early, far, beyond, *pieces]
    out_specs = [flat]
    out_shape = [jax.ShapeDtypeStruct((nodes, columns), F32)]
    scratch = []
    if last:
        out_specs.append(token_spec())
        out_shape.append(TOKEN)
    else:
        ins += [flat, *map(fixed, norm)]
        args += [lin, *norm]
        out_specs.append(pl.BlockSpec(copies_shape(columns), lambda i: (0, 0, 0)))
        out_shape.append(jax.ShapeDtypeStruct(copies_shape(columns), F32))
        scratch = [pltpu.VMEM((8, columns), F32), pltpu.VMEM((2, 8, columns), F32)]
    return launch(
        functools.partial(backward_kernel, big, last), (nodes // rows,), ins, out_specs, out_shape, args, name,
        scratch=scratch, tokens=tokens,
    )


def weight_kernel(spans, other, meta_ref, *refs):
    sources, h_hbm, outs, (token_ref, buf_ref, h_ref, sem) = refs[:4], refs[4], refs[5:7], refs[7:]
    mark(token_ref)
    for m in range(2):
        for n, span in enumerate(spans):
            rows = pl.ds(*span)
            if m == 0:
                pltpu.make_async_copy(h_hbm.at[rows, :], h_ref.at[rows, :], sem.at[2, n]).start()
            for k in range(2):

                @pl.when((meta_ref[4 + m] ^ other) == k)
                def _():
                    pltpu.make_async_copy(
                        sources[2 * m + k].at[rows, :], buf_ref.at[m, rows, :], sem.at[m, n]
                    ).start()

    for m in range(2):
        total = None
        for n, (start, size) in enumerate(spans):
            rows = pl.ds(start, size)
            if m == 0:
                pltpu.make_async_copy(h_hbm.at[rows, :], h_ref.at[rows, :], sem.at[2, n]).wait()
            pltpu.make_async_copy(sources[2 * m].at[rows, :], buf_ref.at[m, rows, :], sem.at[m, n]).wait()
            x, h = buf_ref[m, start : start + size, :], h_ref[start : start + size, :]
            term = lax.dot_general(x, h, (((0,), (0,)), ((), ())), preferred_element_type=F32)
            total = term if total is None else total + term
        outs[m][...] = total.astype(outs[m].dtype)


def weight_terms(meta, other, pairs, h, name, tokens=()):
    nodes, depth = pairs[0][0].shape
    columns = h.shape[1]
    pieces = 2 if nodes % 32 == 0 else 1
    spans = tuple((n * (nodes // pieces), nodes // pieces) for n in range(pieces))
    whole = pl.BlockSpec((depth, columns), lambda i, meta: (0, 0))
    return launch(
        functools.partial(weight_kernel, spans, other), (1,), [pl.BlockSpec(memory_space=pl.ANY)] * 5,
        [whole, whole, token_spec()],
        [jax.ShapeDtypeStruct((depth, columns), BF)] * 2 + [TOKEN], [*pairs[0], *pairs[1], h], name, prefetch=[meta],
        scratch=[
            pltpu.VMEM((2, nodes, depth), BF), pltpu.VMEM((nodes, columns), BF), pltpu.SemaphoreType.DMA((3, pieces))
        ],
        tokens=tokens, limit=60,
    )


def place_kernel(orders, meta_ref, *refs):
    out_ref, token_ref = refs[-2:]
    mark(token_ref)
    pieces = 1 << (len(orders[0]) - 1)
    size = out_ref.shape[0] // pieces
    for k in range(4):

        @pl.when(pl.program_id(0) == k)
        def _():
            mask = 0
            for b in orders[k // 2][1:]:
                mask = 2 * mask + meta_ref[4 + b]
            for n in range(pieces):
                start = pl.multiple_of((mask ^ n) * size, size)
                out_ref[pl.ds(start, size), :] = refs[k][n * size : (n + 1) * size, :].astype(F32)


def place_blocks(meta, blocks, orders, name, limit, tokens):
    depth, columns = blocks[0].shape
    return launch(
        functools.partial(place_kernel, orders), (4,), [pl.BlockSpec((depth, columns), lambda i, meta: (0, 0))] * 4,
        [
            pl.BlockSpec((depth, columns), lambda i, meta: (meta[0] ^ (i // 2 * 2) ^ (i % 2) ^ meta[4 + i // 2], 0)),
            token_spec(),
        ],
        [jax.ShapeDtypeStruct((4 * depth, columns), F32), TOKEN], blocks, name, prefetch=[meta], limit=limit,
        tokens=tokens,
    )


def after(value, *tokens):
    value, tokens = lax.optimization_barrier((value, tokens))
    return value, tokens


def across(value, axis, distance):
    size = lax.axis_size(axis)
    return lax.ppermute(value, axis, [(i, i ^ distance) for i in range(size)])


def slices_kernel(ids_ref, one_ref, two_ref, *refs):
    outs, (token_ref, sem) = refs[:6], refs[6:]
    mark(token_ref)
    depth = outs[0].shape[0]
    copies = []
    for n, out_ref in enumerate(outs):
        start = pl.multiple_of(ids_ref[1 + n % 3] * depth, depth)
        source = (one_ref, two_ref)[n // 3].at[pl.ds(start, depth), :]
        copies.append(pltpu.make_async_copy(source, out_ref, sem.at[n]))
    for copy in copies:
        copy.start()
    for copy in copies:
        copy.wait()


def weight_slices(ids, one, two):
    depth, columns = one.shape[0] // 4, one.shape[1]
    hbm = pl.BlockSpec(memory_space=pltpu.HBM)
    outs = launch(
        slices_kernel, (1,), [hbm, hbm], [hbm] * 6 + [token_spec()],
        [jax.ShapeDtypeStruct((depth, columns), one.dtype)] * 6 + [TOKEN], [one, two], "weight_slices",
        prefetch=[ids], scratch=[pltpu.SemaphoreType.DMA((6,))],
    )
    return outs[:3], outs[3:6], outs[6]


def weight_rows(slices):
    far = across(slices[1], "col", 2)
    other = across(slices[2], "col", 2)
    return [across(slices[0], "col", 1), far, across(other, "col", 1)], (far, other)


def fold_kernel(last, place, meta_ref, keep_ref, got_ref, *refs):
    mark(refs[-1])
    if last:
        refs[0][...] = (keep_ref[...].astype(F32) + got_ref[...].astype(F32)).astype(BF)
        return
    part = refs[0].shape[0]
    bit = meta_ref[4 + place]
    for out_ref, which in zip(refs[:2], (1 - bit, bit)):
        rows = pl.ds(pl.multiple_of(which * part, part), part)
        out_ref[...] = (keep_ref[rows, :].astype(F32) + got_ref[rows, :].astype(F32)).astype(BF)


def join_kernel(meta_ref, keep_ref, got_ref, out_ref, token_ref):
    mark(token_ref)
    part = keep_ref.shape[0]
    out_ref[:part, :] = keep_ref[...]
    out_ref[part:, :] = got_ref[...]


def small_call(kernel, meta, keep, got, rows, name, tokens):
    columns = keep.shape[1]
    whole = lambda r: pl.BlockSpec((r, columns), lambda i, bit: (0, 0))
    return launch(
        kernel, (1,), [whole(keep.shape[0])] * 2, [whole(r) for r in rows] + [token_spec()],
        [jax.ShapeDtypeStruct((r, columns), BF) for r in rows] + [TOKEN], [keep, got], name, prefetch=[meta], tokens=tokens,
    )


class RowSum:
    def __init__(self, axis, meta, terms, name):
        self.axis, self.meta, self.name = axis, meta, name
        self.bits = lax.axis_size(axis).bit_length() - 1
        self.stages = 2 * self.bits
        self.orders = [list(range(self.bits)), list(range(1, self.bits)) + [0]]
        *self.send, self.sent = terms(1, ())
        *self.keep, self.kept = terms(0, (self.sent,))
        self.stage = 0
        self.step(())

    def step(self, tokens):
        s, bits = self.stage, self.bits
        self.stage += 1
        started = []
        for n in range(2):
            rows = self.keep[n].shape[0]
            call = lambda kernel, sizes: small_call(
                kernel, self.meta, self.keep[n], self.got[n], sizes, f"{self.name}_{n}_{s}", tokens
            )
            if 0 < s < bits:
                fold = functools.partial(fold_kernel, False, self.orders[n][s])
                self.send[n], self.keep[n], token = call(fold, [rows // 2] * 2)
            elif s == bits:
                self.keep[n], token = call(functools.partial(fold_kernel, True, 0), [rows])
            elif s > bits:
                self.keep[n], token = call(join_kernel, [2 * rows])
            if s > 0:
                started.append(token)
        level = s if s < bits else 2 * bits - 1 - s
        moved = self.send if s < bits else self.keep
        self.got = [across(moved[n], self.axis, 1 << self.orders[n][level]) for n in range(2)]
        return tuple(started)

    def next(self, *tokens):
        return self.step(tokens) if self.stage < self.stages else tokens

    def placed(self, limit, tokens=()):
        while self.stage < self.stages:
            self.step(())
        blocks = [v for n in range(2) for v in (self.keep[n], self.got[n])]
        return place_blocks(self.meta, blocks, self.orders, f"place_{self.name}", limit, tokens)


def local(
    features,
    neighbours,
    node_valid,
    weight_one,
    gamma_one,
    beta_one,
    weight_two,
    gamma_two,
    beta_two,
    cotangent,
):
    nodes, columns = features.shape
    slots = nodes // SLOT
    big = slots // 2 if slots % 2 == 0 else slots
    q = lax.axis_index("col")
    place = lax.axis_index("row")
    bits = [(place >> b) & 1 for b in range(lax.axis_size("row").bit_length() - 1)]
    ids = jnp.stack([q, q ^ 1, q ^ 2, q ^ 3, *bits]).astype(jnp.int32)
    g1, b1, g2, b2 = (v.reshape(1, columns) for v in (gamma_one, beta_one, gamma_two, beta_two))

    far_one = across(features, "col", 2)
    near_one = across(features, "col", 1)
    *tiles, tiles_token = build_tiles(neighbours, node_valid)
    val = tiles[3]
    slices_one, slices_two, slices_token = weight_slices(ids, weight_one, weight_two)
    early, token = half(ids, big, features, near_one, [weight_block(weight_one, b) for b in (0, 1)], False, "half_one")
    far_one, tokens = after(far_one, token, tiles_token, slices_token)
    beyond_one = across(far_one, "col", 1)
    lin_one, stats = forward(ids, big, early, far_one, beyond_one, weight_one, tiles, "forward_one", tokens)
    norm_one = (small_gather(stats, "row"), g1, b1)

    hidden, _ = rows_call(result_kernel, big, [lin_one], [val], norm_one, BF, [], "hidden")
    far_two, near_two = across(hidden, "col", 2), across(hidden, "col", 1)
    early, token = half(ids, big, hidden, near_two, [weight_block(weight_two, b) for b in (0, 1)], False, "half_two")
    far_two, tokens = after(far_two, token)
    beyond_two = across(far_two, "col", 1)
    slices_two, (far_two,) = after(slices_two, far_two)
    rows_two, crossing = weight_rows(slices_two)
    lin_two, stats = forward(ids, big, early, far_two, beyond_two, weight_two, tiles, "forward_two", tokens)
    norm_two = (small_gather(stats, "row"), g2, b2)

    sums = rows_call(
        sums_kernel, big, [lin_two, cotangent], [val], norm_two, None, [pltpu.VMEM((2, 8, columns), F32)], "sums_two"
    )
    grads_two = small_gather(sums, "row")
    turned, _ = turn_call(True, big, lin_two, cotangent, tiles, norm_two, grads_two, "turn_two", crossing)
    far, near = across(turned, "col", 2), across(turned, "col", 1)

    def terms_two(other, tokens, h=turned):
        return weight_terms(ids, other, ((hidden, near_two), (far_two, beyond_two)), h, "terms_two", tokens)

    sum_two = RowSum("row", ids, terms_two, "two")
    weights = [weight_block(weight_two, 0), whole_block(rows_two[0])]
    early, token = half(ids, big, turned, near, weights, True, "half_back_two", (sum_two.kept,))
    far, tokens = after(far, *sum_two.next(*sum_two.next(token)))
    beyond = across(far, "col", 1)
    slices_one, (far,) = after(slices_one, far)
    rows_one, crossing = weight_rows(slices_one)
    grad_one, sums = backward(big, early, far, beyond, rows_two[1:], lin_one, norm_one, "backward_two", tokens)
    sums, tokens = after(sums, *sum_two.next(sums))
    grads_one = small_gather(sums, "row")

    tokens = (*tokens, *crossing, *sum_two.next())
    turned, _ = turn_call(False, big, lin_one, grad_one, tiles, norm_one, grads_one, "turn_one", tokens)
    far, near = across(turned, "col", 2), across(turned, "col", 1)

    def terms_one(other, tokens, h=turned):
        return weight_terms(ids, other, ((features, near_one), (far_one, beyond_one)), h, "terms_one", tokens)

    sum_one = RowSum("row", ids, terms_one, "one")
    weights = [weight_block(weight_one, 0), whole_block(rows_one[0])]
    early, token = half(ids, big, turned, near, weights, True, "half_back_one", (sum_one.kept,))
    sum_two.next(sum_one.kept)
    output, token = rows_call(result_kernel, big, [lin_two], [val], norm_two, F32, [], "output", sum_one.next(token))
    grad_weight_two, token = sum_two.placed(60, (token,))
    sum_one.next(token)
    far, tokens = after(far, *sum_one.next())
    beyond = across(far, "col", 1)
    grad_features, token = backward(big, early, far, beyond, rows_one[1:], None, None, "backward_one", tokens)
    while sum_one.stage < sum_one.stages - 1:
        sum_one.next()
    sum_one.next(token)
    grad_weight_one, _ = sum_one.placed(24)

    sums_one, sums_two = jnp.sum(grads_one, axis=0), jnp.sum(grads_two, axis=0)
    return (
        output,
        grad_features,
        grad_weight_one,
        sums_one[1],
        sums_one[0],
        grad_weight_two,
        sums_two[1],
        sums_two[0],
    )


def solution(mesh):
    placed = (
        P("row", "col"),
        P("row", None),
        P("row"),
        P(None, "col"),
        P("col"),
        P("col"),
        P(None, "col"),
        P("col"),
        P("col"),
        P("row", "col"),
    )
    return jax.shard_map(
        local,
        mesh=mesh,
        in_specs=placed,
        out_specs=(
            P("row", "col"),
            P("row", "col"),
            P(None, "col"),
            P("col"),
            P("col"),
            P(None, "col"),
            P("col"),
            P("col"),
        ),
        check_vma=False,
    )
```

time: 857 us -> 355 us (0.41)
  waiting for transfers between devices: 568 us -> 135 us
  Pallas kernels: 0 us -> 124 us
  blocking collectives: 118 us -> 23.1 us
  matrix products: 78.2 us -> 0 us
  other arithmetic: 57.2 us -> 0.03 us
  starting transfers between devices: 0.87 us -> 42.9 us
  between operations: 14 us -> 1.36 us
  local copies, waits for them, and re-layouts: 18.1 us -> 27.3 us
    psum x1 -> x0, waiting for transfers between devices: 267 us -> none  [backward_layer(): grad_weight = lax.psum(weight_terms, 'row')]
    reduce_scatter x2 -> x0, waiting for transfers between devices: 197 us -> none  [backward_layer(): lax.psum_scatter(partial_terms, 'col', scatter_dimension=1, tiled=True)]
    ppermute x0 -> x44, waiting for transfers between devices: none -> 128 us  [across(): return lax.ppermute(value, axis, [(i, i ^ distance) for i in range(size)])]
    pallas_call x0 -> x41, Pallas kernels: none -> 124 us  [launch(): pl.pallas_call(body, grid_spec=pltpu.PrefetchScalarGridSpec(num_scalar_pr...]
    psum x6 -> x0, blocking collectives: 118 us -> none  [the longest x2 43.4 us: moments(): lax.psum((jnp.sum(valid), jnp.sum(valid * linear, axis=0)), 'row')]
    all_gather x2 -> x0, waiting for transfers between devices: 105 us -> none  [forward_layer(): gathered = lax.all_gather(mixed, 'col', axis=1, tiled=True)]
    dot_general x10 -> x0, matrix products: 78.2 us -> none  [the longest x2 20.4 us: backward_layer(): lax.dot_general(gathered, grad_low, (((0,), (0,)), ((), ())), preferred_e...]
    reduce_sum x33 -> x2, other arithmetic: 41.4 us -> 0.03 us  [the longest x1 0.01 us: local(): jnp.sum(grads_two, axis=0)]
  transfers between devices with their start and end apart: 5 -> 46, of which waited for: 5 -> 19; matrix products, arithmetic and copies ran while one was open for 3% -> 1% of each run, Pallas kernels for 0% -> 27%
where the time goes in v3:
time: 355 us; the launch traced here: 354 us
  waiting for transfers between devices  135 us (38%)
  Pallas kernels  124 us (35%)
  starting transfers between devices  42.9 us (12%)
  local copies, waits for them, and re-layouts  27.3 us (8%)
  blocking collectives  23.1 us (7%)
    ppermute x44, waiting for transfers between devices, across(): return lax.ppermute(value, axis, [(i, i ^ distance) for i in range(size)])  128 us
    pallas_call x41, Pallas kernels, launch(): pl.pallas_call(body, grid_spec=pltpu.PrefetchScalarGridSpec(num_scalar_pr...  124 us
    ppermute x44, starting transfers between devices, across(): return lax.ppermute(value, axis, [(i, i ^ distance) for i in range(size)])  35.4 us
    unnamed x142, local copies, waits for them, and re-layouts  25.3 us
    all_to_all x2, blocking collectives, small_gather(): return lax.all_to_all(copies, axis, split_axis=0, concat_axis=0, tiled=True)  23.1 us
    all_to_all x2, starting transfers between devices, small_gather(): return lax.all_to_all(copies, axis, split_axis=0, concat_axis=0, tiled=True)  7.54 us
  transfers between devices with their start and end apart: 46, of which 19 were waited for; matrix products, arithmetic and copies ran while one was open for 1% of the time, Pallas kernels for 27%

profile of v3, /device:TPU:0, one launch (start us, length us, event | category | flops | bytes accessed | tf_op | source)
XLA Modules:
  0.0 354.1 jit_solution(3701968571063869901)
XLA Ops:
  1.2 2.6 collective-permute-start.1
  4.6 5.0 %tiles.1 = (bf16[14,128,256]{2,1,0:T(8,128)(2,1)S(1)}, bf16[14,128,256]{2,1,0:T(8,128)(2,1)S(1)}, f32[14,128,128]{2,1,0:T(8,128)S(1)}, f32[14,128,128]{2,1,0:T(8,128)S(1)}, f32[8,128]{1,0:T(8,128)S(1)}) custom-call(s32[14,32,128]{2,1,0:T(8,128)S(1)} %bitcast_bitcast_fusion.refs_0_, s32[14,1,128]{2,1,0:T(1,128)S(1)} %reshape.35.refs_1_), custom_call_target="tpu_custom_call" | custom-call | flops 1000000 | bytes 1000 | tf_op jit(solution)/shard_map/tiles/pallas_call | solution.py:43
  13.8 2.3 weight_slices.1
  17.7 2.8 half_one.1
  20.5 24.2 %collective-permute-done.1.refs_2_.refs_3_ = bf16[1792,512]{1,0:T(8,128)(2,1)} collective-permute-done((bf16[1792,512]{1,0:T(8,128)(2,1)}, bf16[1792,512]{1,0:T(8,128)(2,1)}, u32[]{:S(2)}, u32[]{:S(2)}) %collective-permute-start.1) | collective-permute-done | bytes 1835040 | tf_op jit(solution)/shard_map/ppermute | solution.py:507
  44.7 4.0 %collective-permute-done.2.refs_3_.refs_4_ = bf16[1792,512]{1,0:T(8,128)(2,1)S(1)} collective-permute-done((bf16[1792,512]{1,0:T(8,128)(2,1)}, bf16[1792,512]{1,0:T(8,128)(2,1)S(1)}, u32[]{:S(2)}, u32[]{:S(2)}) %collective-permute-start.2) | collective-permute-done | bytes 1835040 | tf_op jit(solution)/shard_map/ppermute | solution.py:507
  48.7 7.6 %forward_one.1 = (f32[1792,512]{1,0:T(8,128)S(1)}, f32[8,8,512]{2,1,0:T(8,128)S(1)}) custom-call(s32[7]{0:T(128)S(1)} %stack.31.refs_0_, f32[1792,512]{1,0:T(8,128)S(1)} %get-tuple-element.119.refs_1_, bf16[1792,512]{1,0:T(8,128)(2,1)} %collective-permute-done.1.refs_2_.refs_3_, bf16[1792,512]{1,0:T(8,128)(2,1)S(1)} %collective-permute-done.2.refs_3_.refs_4_, ...), custom_call_target="tpu_custom_call" | custom-call | flops 1000000 | bytes 1000 | tf_op jit(solution)/shard_map/forward_one/pallas_call | solution.py:43
  56.3 13.2 %all_to_all.20.refs_2_.refs_6_.refs_5_ = f32[8,8,512]{2,1,0:T(8,128)S(1)} all-to-all(f32[8,8,512]{2,1,0:T(8,128)S(1)} %get-tuple-element.131), channel_id=1, replica_groups=mesh['row'=8,'col'=4] {'row'}, dimensions={0} | all-to-all | bytes 262144 | tf_op jit(solution)/shard_map/all_to_all | solution.py:118
  72.9 2.2 collective-permute-done.3.refs_2_
  75.1 2.8 half_two.1
  77.9 35.8 %collective-permute-done.4.refs_2_.refs_3_ = bf16[1792,512]{1,0:T(8,128)(2,1)S(1)} collective-permute-done((bf16[1792,512]{1,0:T(8,128)(2,1)S(1)}, bf16[1792,512]{1,0:T(8,128)(2,1)S(1)}, u32[]{:S(2)}, u32[]{:S(2)}) %collective-permute-start.4) | collective-permute-done | bytes 1835040 | tf_op jit(solution)/shard_map/ppermute | solution.py:507
  117.5 6.4 %forward_two.1 = (f32[1792,512]{1,0:T(8,128)S(1)}, f32[8,8,512]{2,1,0:T(8,128)S(1)}) custom-call(s32[7]{0:T(128)S(1)} %stack.31.refs_0_, f32[1792,512]{1,0:T(8,128)S(1)} %get-tuple-element.133.refs_1_, bf16[1792,512]{1,0:T(8,128)(2,1)S(1)} %collective-permute-done.4.refs_2_.refs_3_, bf16[1792,512]{1,0:T(8,128)(2,1)S(1)} %collective-permute-done.5.refs_3_.refs_4_, ...), custom_call_target="tpu_custom_call" | custom-call | flops 1000000 | bytes 1000 | tf_op jit(solution)/shard_map/forward_two/pallas_call | solution.py:43
  123.9 10.0 %all_to_all.21.refs_3_.refs_5_.refs_2_ = f32[8,8,512]{2,1,0:T(8,128)S(1)} all-to-all(f32[8,8,512]{2,1,0:T(8,128)S(1)} %get-tuple-element.142), channel_id=1, replica_groups=mesh['row'=8,'col'=4] {'row'}, dimensions={0} | all-to-all | bytes 262144 | tf_op jit(solution)/shard_map/all_to_all | solution.py:118
  133.9 2.8 sums_two.1
  138.5 3.5 %all-to-all-start.2 = ((f32[8,8,512]{2,1,0:T(8,128)}), f32[8,8,512]{2,1,0:T(8,128)S(1)}, u32[]{:S(2)}, u32[]{:S(2)}) async-start(f32[8,8,512]{2,1,0:T(8,128)} %sums_two.1), calls=%async_computation.2 | async-start | bytes 262144 | tf_op jit(solution)/shard_map/all_to_all | solution.py:118
  142.1 7.1 %all-to-all-done.2.refs_6_ = f32[8,8,512]{2,1,0:T(8,128)S(1)} async-done(((f32[8,8,512]{2,1,0:T(8,128)}), f32[8,8,512]{2,1,0:T(8,128)S(1)}, u32[]{:S(2)}, u32[]{:S(2)}) %all-to-all-start.2) | async-done | bytes 131104 | tf_op jit(solution)/shard_map/all_to_all | solution.py:118
  149.8 8.7 %turn_two.1 = (bf16[1792,512]{1,0:T(8,128)(2,1)}, f32[8,128]{1,0:T(8,128)}) custom-call(f32[1792,512]{1,0:T(8,128)} %copy-done.9, bf16[1792,512]{1,0:T(8,128)(2,1)} %refs_1_.9, f32[14,128,128]{2,1,0:T(8,128)} %copy-done.7, f32[14,128,128]{2,1,0:T(8,128)} %copy-done.22, bf16[14,128,256]{2,1,0:T(8,128)(2,1)} %copy-done.24, f32[8,8,512]{2,1,0:T(8,128)} %copy-done.28, ...), custom_call_target="tpu_custom_call" | custom-call | flops 1000000 | bytes 1000 | tf_op jit(solution)/shard_map/turn_two/pallas_call | solution.py:43
  160.3 6.2 %terms_two.2 = (bf16[512,512]{1,0:T(8,128)(2,1)}, bf16[512,512]{1,0:T(8,128)(2,1)}, f32[8,128]{1,0:T(8,128)}) custom-call(s32[7]{0:T(128)} %copy-done.33, bf16[1792,512]{1,0:T(8,128)(2,1)} %copy-done.20, bf16[1792,512]{1,0:T(8,128)(2,1)} %copy-done.21, bf16[1792,512]{1,0:T(8,128)(2,1)} %copy-done.13, bf16[1792,512]{1,0:T(8,128)(2,1)} %copy-done.14, ...), custom_call_target="tpu_custom_call" | custom-call | flops 1000000 | bytes 1000 | tf_op jit(solution)/shard_map/terms_two/pallas_call | solution.py:43
  167.9 6.4 %terms_two.3 = (bf16[512,512]{1,0:T(8,128)(2,1)}, bf16[512,512]{1,0:T(8,128)(2,1)}, f32[8,128]{1,0:T(8,128)}) custom-call(s32[7]{0:T(128)} %copy-done.33, bf16[1792,512]{1,0:T(8,128)(2,1)} %copy-done.20, bf16[1792,512]{1,0:T(8,128)(2,1)} %copy-done.21, bf16[1792,512]{1,0:T(8,128)(2,1)} %copy-done.13, bf16[1792,512]{1,0:T(8,128)(2,1)} %copy-done.14, ...), custom_call_target="tpu_custom_call" | custom-call | flops 1000000 | bytes 1000 | tf_op jit(solution)/shard_map/terms_two/pallas_call | solution.py:43
  176.5 4.3 %half_back_two.1 = (f32[1792,512]{1,0:T(8,128)S(1)}, f32[8,128]{1,0:T(8,128)S(1)}) custom-call(s32[7]{0:T(128)S(1)} %copy-done.34, bf16[1792,512]{1,0:T(8,128)(2,1)S(1)} %copy-done.16, bf16[1792,512]{1,0:T(8,128)(2,1)} %collective-permute-done.8.refs_2_, bf16[2048,512]{1,0:T(8,128)(2,1)S(1)} %copy-done.3, ...), custom_call_target="tpu_custom_call" | custom-call | flops 1000000 | bytes 1000 | tf_op jit(solution)/shard_map/half_back_two/pallas_call | solution.py:43
  184.7 12.4 %collective-permute-done.14.refs_2_ = bf16[256,512]{1,0:T(8,128)(2,1)S(1)} collective-permute-done((bf16[256,512]{1,0:T(8,128)(2,1)S(1)}, bf16[256,512]{1,0:T(8,128)(2,1)S(1)}, u32[]{:S(2)}, u32[]{:S(2)}) %collective-permute-start.14) | collective-permute-done | bytes 262176 | tf_op jit(solution)/shard_map/ppermute | solution.py:507
  198.4 3.0 collective-permute-done.10.refs_1_
  204.1 2.0 collective-permute-done.16.refs_4_
  206.5 6.2 %backward_two.1 = (f32[1792,512]{1,0:T(8,128)S(1)}, f32[8,8,512]{2,1,0:T(8,128)}) custom-call(f32[1792,512]{1,0:T(8,128)S(1)} %get-tuple-element.150.refs_0_, bf16[1792,512]{1,0:T(8,128)(2,1)} %collective-permute-done.10.refs_1_, bf16[1792,512]{1,0:T(8,128)(2,1)S(1)} %collective-permute-done.15.refs_2_, ...), custom_call_target="tpu_custom_call" | custom-call | flops 1000000 | bytes 1000 | tf_op jit(solution)/shard_map/backward_two/pallas_call | solution.py:43
  215.7 4.0 %all-to-all-start.3 = ((f32[8,8,512]{2,1,0:T(8,128)}), f32[8,8,512]{2,1,0:T(8,128)S(1)}, u32[]{:S(2)}, u32[]{:S(2)}) async-start(f32[8,8,512]{2,1,0:T(8,128)} %get-tuple-element.179.refs_3_), calls=%async_computation.3 | async-start | bytes 262144 | tf_op jit(solution)/shard_map/all_to_all | solution.py:118
  219.7 2.0 collective-permute-start.22
  221.7 2.4 collective-permute-start.21
  226.6 5.2 %collective-permute-done.21.refs_2_ = bf16[128,512]{1,0:T(8,128)(2,1)S(1)} collective-permute-done((bf16[128,512]{1,0:T(8,128)(2,1)S(1)}, bf16[128,512]{1,0:T(8,128)(2,1)S(1)}, u32[]{:S(2)}, u32[]{:S(2)}) %collective-permute-start.21) | collective-permute-done | bytes 131104 | tf_op jit(solution)/shard_map/ppermute | solution.py:507
  233.8 8.0 %turn_one.1 = (bf16[1792,512]{1,0:T(8,128)(2,1)}, f32[8,128]{1,0:T(8,128)}) custom-call(f32[1792,512]{1,0:T(8,128)} %copy-done.11, f32[1792,512]{1,0:T(8,128)} %copy-done.27, f32[14,128,128]{2,1,0:T(8,128)} %copy-done.7, f32[14,128,128]{2,1,0:T(8,128)} %copy-done.22, bf16[14,128,256]{2,1,0:T(8,128)(2,1)} %copy-done.24, f32[8,8,512]{2,1,0:T(8,128)} %copy-done.30, ...), custom_call_target="tpu_custom_call" | custom-call | flops 1000000 | bytes 1000 | tf_op jit(solution)/shard_map/turn_one/pallas_call | solution.py:43
  246.2 6.2 %terms_one.2 = (bf16[512,512]{1,0:T(8,128)(2,1)}, bf16[512,512]{1,0:T(8,128)(2,1)}, f32[8,128]{1,0:T(8,128)}) custom-call(s32[7]{0:T(128)} %copy-done.33, bf16[1792,512]{1,0:T(8,128)(2,1)} %refs_1_.11, bf16[1792,512]{1,0:T(8,128)(2,1)} %copy-done.18, bf16[1792,512]{1,0:T(8,128)(2,1)} %collective-permute-done.1.refs_2_.refs_3_, bf16[1792,512]{1,0:T(8,128)(2,1)} %copy-done.19, ...), custom_call_target="tpu_custom_call" | custom-call | flops 1000000 | bytes 1000 | tf_op jit(solution)/shard_map/terms_one/pallas_call | solution.py:43
  252.4 5.1 %collective-permute-done.31.refs_2_ = bf16[256,512]{1,0:T(8,128)(2,1)S(1)} collective-permute-done((bf16[256,512]{1,0:T(8,128)(2,1)S(1)}, bf16[256,512]{1,0:T(8,128)(2,1)S(1)}, u32[]{:S(2)}, u32[]{:S(2)}) %collective-permute-start.31) | collective-permute-done | bytes 262176 | tf_op jit(solution)/shard_map/ppermute | solution.py:507
  260.1 6.7 %terms_one.3 = (bf16[512,512]{1,0:T(8,128)(2,1)}, bf16[512,512]{1,0:T(8,128)(2,1)}, f32[8,128]{1,0:T(8,128)}) custom-call(s32[7]{0:T(128)} %copy-done.33, bf16[1792,512]{1,0:T(8,128)(2,1)} %refs_1_.11, bf16[1792,512]{1,0:T(8,128)(2,1)} %copy-done.18, bf16[1792,512]{1,0:T(8,128)(2,1)} %collective-permute-done.1.refs_2_.refs_3_, bf16[1792,512]{1,0:T(8,128)(2,1)} %copy-done.19, ...), custom_call_target="tpu_custom_call" | custom-call | flops 1000000 | bytes 1000 | tf_op jit(solution)/shard_map/terms_one/pallas_call | solution.py:43
  273.7 2.0 collective-permute-start.32
  276.5 4.5 %half_back_one.1 = (f32[1792,512]{1,0:T(8,128)S(1)}, f32[8,128]{1,0:T(8,128)S(1)}) custom-call(s32[7]{0:T(128)S(1)} %copy-done.35, bf16[1792,512]{1,0:T(8,128)(2,1)S(1)} %copy-done.15, bf16[1792,512]{1,0:T(8,128)(2,1)} %collective-permute-done.24.refs_2_, bf16[2048,512]{1,0:T(8,128)(2,1)S(1)} %copy-done.6, bf16[512,512]{1,0:T(8,128)(2,1)} %collective-permute-done.25.refs_4_, ...), custom_call_target="tpu_custom_call" | custom-call | flops 1000000 | bytes 1000 | tf_op jit(solution)/shard_map/half_back_one/pallas_call | solution.py:43
  281.1 2.7 one_1_1.1
  286.7 2.0 collective-permute-start.28
  288.7 2.6 output.1
  293.5 4.8 %place_two.1 = (f32[2048,512]{1,0:T(8,128)}, f32[8,128]{1,0:T(8,128)}) custom-call(s32[7]{0:T(128)} %copy-done.33, bf16[512,512]{1,0:T(8,128)(2,1)} %copy-done.38, bf16[512,512]{1,0:T(8,128)(2,1)} %copy-done.70, bf16[512,512]{1,0:T(8,128)(2,1)} %copy-done.37, bf16[512,512]{1,0:T(8,128)(2,1)} %copy-done.69, f32[8,128]{1,0:T(8,128)} %copy-done.63), custom_call_target="tpu_custom_call" | custom-call | flops 1000000 | bytes 1000 | tf_op jit(solution)/shard_map/place_two/pallas_call | solution.py:43
  302.5 2.7 collective-permute-done.35.refs_2_
  305.7 3.6 %collective-permute-done.33.refs_2_ = bf16[128,512]{1,0:T(8,128)(2,1)S(1)} collective-permute-done((bf16[128,512]{1,0:T(8,128)(2,1)S(1)}, bf16[128,512]{1,0:T(8,128)(2,1)S(1)}, u32[]{:S(2)}, u32[]{:S(2)}) %collective-permute-start.33) | collective-permute-done | bytes 131104 | tf_op jit(solution)/shard_map/ppermute | solution.py:507
  311.4 4.5 %collective-permute-done.41.refs_2_ = bf16[128,512]{1,0:T(8,128)(2,1)S(1)} collective-permute-done((bf16[128,512]{1,0:T(8,128)(2,1)S(1)}, bf16[128,512]{1,0:T(8,128)(2,1)S(1)}, u32[]{:S(2)}, u32[]{:S(2)}) %collective-permute-start.41) | collective-permute-done | bytes 131104 | tf_op jit(solution)/shard_map/ppermute | solution.py:507
  317.1 7.8 %collective-permute-done.38.refs_2_ = bf16[128,512]{1,0:T(8,128)(2,1)S(1)} collective-permute-done((bf16[128,512]{1,0:T(8,128)(2,1)S(1)}, bf16[128,512]{1,0:T(8,128)(2,1)S(1)}, u32[]{:S(2)}, u32[]{:S(2)}) %collective-permute-start.38) | collective-permute-done | bytes 131104 | tf_op jit(solution)/shard_map/ppermute | solution.py:507
  326.1 2.0 copy-done.26
  328.1 4.8 %backward_one.1 = (f32[1792,512]{1,0:T(8,128)}, f32[8,128]{1,0:T(8,128)S(1)}) custom-call(f32[1792,512]{1,0:T(8,128)S(1)} %copy-done.26, bf16[1792,512]{1,0:T(8,128)(2,1)} %collective-permute-done.27.refs_1_, bf16[1792,512]{1,0:T(8,128)(2,1)S(1)} %collective-permute-done.36.refs_2_, bf16[512,512]{1,0:T(8,128)(2,1)S(1)} %copy-done.32, ...), custom_call_target="tpu_custom_call" | custom-call | flops 1000000 | bytes 1000 | tf_op jit(solution)/shard_map/backward_one/pallas_call | solution.py:43
  334.1 2.0 collective-permute-start.43
  339.5 8.3 %collective-permute-done.43.refs_4_ = bf16[512,512]{1,0:T(8,128)(2,1)S(1)} collective-permute-done((bf16[512,512]{1,0:T(8,128)(2,1)S(1)}, bf16[512,512]{1,0:T(8,128)(2,1)S(1)}, u32[]{:S(2)}, u32[]{:S(2)}) %collective-permute-start.43) | collective-permute-done | bytes 524320 | tf_op jit(solution)/shard_map/ppermute | solution.py:507
  347.8 3.2 collective-permute-done.40.refs_2_
  351.0 3.1 place_one.1
  (236 shorter events, 71.3 us)
Async XLA Ops:
  0.6 15.4 %collective-permute-start = (bf16[1792,512]{1,0:T(8,128)(2,1)}, bf16[1792,512]{1,0:T(8,128)(2,1)S(1)}, u32[]{:S(2)}, u32[]{:S(2)}) collective-permute-start(bf16[1792,512]{1,0:T(8,128)(2,1)} %refs_1_.11), channel_id=1, source_target_pairs={{0,1},{1,0},{2,3},{3,2},{4,5},{5,4},{6,7},{7,6},{8,9},{9,8},{10,11... | collective-permute-start | bytes 5505032 | tf_op jit(solution)/shard_map/ppermute | solution.py:507
  1.2 43.5 %collective-permute-start.1 = (bf16[1792,512]{1,0:T(8,128)(2,1)}, bf16[1792,512]{1,0:T(8,128)(2,1)}, u32[]{:S(2)}, u32[]{:S(2)}) collective-permute-start(bf16[1792,512]{1,0:T(8,128)(2,1)} %refs_1_.11), channel_id=1, source_target_pairs={{0,2},{1,3},{2,0},{3,1},{4,6},{5,7},{6,4},{7,5},{8,10},{9,11},{10,... | collective-permute-start | bytes 5505032 | tf_op jit(solution)/shard_map/ppermute | solution.py:507
  13.8 120.1 %copy-start.7 = (f32[14,128,128]{2,1,0:T(8,128)}, f32[14,128,128]{2,1,0:T(8,128)S(1)}, u32[]{:S(2)}) copy-start(f32[14,128,128]{2,1,0:T(8,128)S(1)} %get-tuple-element.126.refs_8_.refs_1_.refs_2_) | copy-start | bytes 2752516
  44.7 4.0 %collective-permute-start.2 = (bf16[1792,512]{1,0:T(8,128)(2,1)}, bf16[1792,512]{1,0:T(8,128)(2,1)S(1)}, u32[]{:S(2)}, u32[]{:S(2)}) collective-permute-start(bf16[1792,512]{1,0:T(8,128)(2,1)} %collective-permute-done.1.refs_2_.refs_3_), channel_id=1, source_target_pairs={{0,1},{1,0},{2,3},{3,2},{4,5},{5,4},{6,7},{7,6},{8,9},{9,8},{10,11... | collective-permute-start | bytes 5505032 | tf_op jit(solution)/shard_map/ppermute | solution.py:507
  69.5 137.0 %copy-start.30 = (f32[8,8,512]{2,1,0:T(8,128)}, f32[8,8,512]{2,1,0:T(8,128)S(1)}, u32[]{:S(2)}) copy-start(f32[8,8,512]{2,1,0:T(8,128)S(1)} %all_to_all.20.refs_2_.refs_6_.refs_5_) | copy-start | bytes 393220
  71.3 3.8 %collective-permute-start.3 = (bf16[1792,512]{1,0:T(8,128)(2,1)S(1)}, bf16[1792,512]{1,0:T(8,128)(2,1)S(1)}, u32[]{:S(2)}, u32[]{:S(2)}) collective-permute-start(bf16[1792,512]{1,0:T(8,128)(2,1)S(1)} %get-tuple-element.132.refs_1_), channel_id=1, source_target_pairs={{0,1},{1,0},{2,3},{3,2},{4,5},{5,4},{6,7},{7,6},{8,9},{9,8},{10,11... | collective-permute-start | bytes 5505032 | tf_op jit(solution)/shard_map/ppermute | solution.py:507
  71.3 42.4 %collective-permute-start.4 = (bf16[1792,512]{1,0:T(8,128)(2,1)S(1)}, bf16[1792,512]{1,0:T(8,128)(2,1)S(1)}, u32[]{:S(2)}, u32[]{:S(2)}) collective-permute-start(bf16[1792,512]{1,0:T(8,128)(2,1)S(1)} %get-tuple-element.132.refs_1_), channel_id=1, source_target_pairs={{0,2},{1,3},{2,0},{3,1},{4,6},{5,7},{6,4},{7,5},{8,10},{9,11},{10,... | collective-permute-start | bytes 5505032 | tf_op jit(solution)/shard_map/ppermute | solution.py:507
  113.7 3.8 %collective-permute-start.5 = (bf16[1792,512]{1,0:T(8,128)(2,1)S(1)}, bf16[1792,512]{1,0:T(8,128)(2,1)S(1)}, u32[]{:S(2)}, u32[]{:S(2)}) collective-permute-start(bf16[1792,512]{1,0:T(8,128)(2,1)S(1)} %collective-permute-done.4.refs_2_.refs_3_), channel_id=1, source_target_pairs={{0,1},{1,0},{2,3},{3,2},{4,5},{5,4},{6,7},{7,6},{8,9},{9,8},{10,11... | collective-permute-start | bytes 5505032 | tf_op jit(solution)/shard_map/ppermute | solution.py:507
  113.7 28.4 %collective-permute-start.6 = (bf16[512,512]{1,0:T(8,128)(2,1)}, bf16[512,512]{1,0:T(8,128)(2,1)}, u32[]{:S(2)}, u32[]{:S(2)}) collective-permute-start(bf16[512,512]{1,0:T(8,128)(2,1)} %get-tuple-element.144), channel_id=1, source_target_pairs={{0,2},{1,3},{2,0},{3,1},{4,6},{5,7},{6,4},{7,5},{8,10},{9,11},{10,... | collective-permute-start | bytes 1572872 | tf_op jit(solution)/shard_map/ppermute | solution.py:507
  115.2 26.9 %collective-permute-start.7 = (bf16[512,512]{1,0:T(8,128)(2,1)}, bf16[512,512]{1,0:T(8,128)(2,1)}, u32[]{:S(2)}, u32[]{:S(2)}) collective-permute-start(bf16[512,512]{1,0:T(8,128)(2,1)} %get-tuple-element.145), channel_id=1, source_target_pairs={{0,2},{1,3},{2,0},{3,1},{4,6},{5,7},{6,4},{7,5},{8,10},{9,11},{10,... | collective-permute-start | bytes 1572872 | tf_op jit(solution)/shard_map/ppermute | solution.py:507
  138.5 10.7 %all-to-all-start.2 = ((f32[8,8,512]{2,1,0:T(8,128)}), f32[8,8,512]{2,1,0:T(8,128)S(1)}, u32[]{:S(2)}, u32[]{:S(2)}) async-start(f32[8,8,512]{2,1,0:T(8,128)} %sums_two.1), calls=%async_computation.2 | async-start | bytes 262144 | tf_op jit(solution)/shard_map/all_to_all | solution.py:118
  158.5 15.7 %collective-permute-start.8 = (bf16[1792,512]{1,0:T(8,128)(2,1)}, bf16[1792,512]{1,0:T(8,128)(2,1)}, u32[]{:S(2)}, u32[]{:S(2)}) collective-permute-start(bf16[1792,512]{1,0:T(8,128)(2,1)} %get-tuple-element.146.refs_5_.refs_1_), channel_id=1, source_target_pairs={{0,1},{1,0},{2,3},{3,2},{4,5},{5,4},{6,7},{7,6},{8,9},{9,8},{10,11... | collective-permute-start | bytes 5505032 | tf_op jit(solution)/shard_map/ppermute | solution.py:507
  158.6 42.7 %collective-permute-start.10 = (bf16[1792,512]{1,0:T(8,128)(2,1)}, bf16[1792,512]{1,0:T(8,128)(2,1)}, u32[]{:S(2)}, u32[]{:S(2)}) collective-permute-start(bf16[1792,512]{1,0:T(8,128)(2,1)} %get-tuple-element.146.refs_5_.refs_1_), channel_id=1, source_target_pairs={{0,2},{1,3},{2,0},{3,1},{4,6},{5,7},{6,4},{7,5},{8,10},{9,11},{10,... | collective-permute-start | bytes 5505032 | tf_op jit(solution)/shard_map/ppermute | solution.py:507
  160.2 14.1 %collective-permute-start.9 = (bf16[512,512]{1,0:T(8,128)(2,1)}, bf16[512,512]{1,0:T(8,128)(2,1)S(1)}, u32[]{:S(2)}, u32[]{:S(2)}) collective-permute-start(bf16[512,512]{1,0:T(8,128)(2,1)} %get-tuple-element.147), channel_id=1, source_target_pairs={{0,1},{1,0},{2,3},{3,2},{4,5},{5,4},{6,7},{7,6},{8,9},{9,8},{10,11... | collective-permute-start | bytes 1572872 | tf_op jit(solution)/shard_map/ppermute | solution.py:507
  166.5 14.6 %collective-permute-start.13 = (bf16[512,512]{1,0:T(8,128)(2,1)}, bf16[512,512]{1,0:T(8,128)(2,1)}, u32[]{:S(2)}, u32[]{:S(2)}) collective-permute-start(bf16[512,512]{1,0:T(8,128)(2,1)} %get-tuple-element.161), channel_id=1, source_target_pairs={{0,8},{4,12},{8,0},{12,4},{16,24},{20,28},{24,16},{28,20},{1,9},{5... | collective-permute-start | bytes 1572872 | tf_op jit(solution)/shard_map/ppermute | solution.py:507
  166.6 16.9 %collective-permute-start.11 = (bf16[512,512]{1,0:T(8,128)(2,1)}, bf16[512,512]{1,0:T(8,128)(2,1)S(1)}, u32[]{:S(2)}, u32[]{:S(2)}) collective-permute-start(bf16[512,512]{1,0:T(8,128)(2,1)} %get-tuple-element.155), channel_id=1, source_target_pairs={{0,4},{4,0},{8,12},{12,8},{16,20},{20,16},{24,28},{28,24},{1,5},{5... | collective-permute-start | bytes 1572872 | tf_op jit(solution)/shard_map/ppermute | solution.py:507
  182.8 14.3 %collective-permute-start.14 = (bf16[256,512]{1,0:T(8,128)(2,1)S(1)}, bf16[256,512]{1,0:T(8,128)(2,1)S(1)}, u32[]{:S(2)}, u32[]{:S(2)}) collective-permute-start(bf16[256,512]{1,0:T(8,128)(2,1)S(1)} %get-tuple-element.165), channel_id=1, source_target_pairs={{0,16},{4,20},{8,24},{12,28},{16,0},{20,4},{24,8},{28,12},{1,17},{... | collective-permute-start | bytes 786440 | tf_op jit(solution)/shard_map/ppermute | solution.py:507
  184.2 13.6 %collective-permute-start.12 = (bf16[256,512]{1,0:T(8,128)(2,1)S(1)}, bf16[256,512]{1,0:T(8,128)(2,1)S(1)}, u32[]{:S(2)}, u32[]{:S(2)}) collective-permute-start(bf16[256,512]{1,0:T(8,128)(2,1)S(1)} %get-tuple-element.158), channel_id=1, source_target_pairs={{0,8},{4,12},{8,0},{12,4},{16,24},{20,28},{24,16},{28,20},{1,9},{5... | collective-permute-start | bytes 786440 | tf_op jit(solution)/shard_map/ppermute | solution.py:507
  201.3 5.1 %collective-permute-start.15 = (bf16[1792,512]{1,0:T(8,128)(2,1)}, bf16[1792,512]{1,0:T(8,128)(2,1)S(1)}, u32[]{:S(2)}, u32[]{:S(2)}) collective-permute-start(bf16[1792,512]{1,0:T(8,128)(2,1)} %collective-permute-done.10.refs_1_), channel_id=1, source_target_pairs={{0,1},{1,0},{2,3},{3,2},{4,5},{5,4},{6,7},{7,6},{8,9},{9,8},{10,11... | collective-permute-start | bytes 5505032 | tf_op jit(solution)/shard_map/ppermute | solution.py:507
  201.3 4.7 %collective-permute-start.16 = (bf16[512,512]{1,0:T(8,128)(2,1)}, bf16[512,512]{1,0:T(8,128)(2,1)S(1)}, u32[]{:S(2)}, u32[]{:S(2)}) collective-permute-start(bf16[512,512]{1,0:T(8,128)(2,1)} %collective-permute-done.7.refs_10_), channel_id=1, source_target_pairs={{0,1},{1,0},{2,3},{3,2},{4,5},{5,4},{6,7},{7,6},{8,9},{9,8},{10,11... | collective-permute-start | bytes 1572872 | tf_op jit(solution)/shard_map/ppermute | solution.py:507
  201.8 31.1 %collective-permute-start.19 = (bf16[512,512]{1,0:T(8,128)(2,1)}, bf16[512,512]{1,0:T(8,128)(2,1)S(1)}, u32[]{:S(2)}, u32[]{:S(2)}) collective-permute-start(bf16[512,512]{1,0:T(8,128)(2,1)} %get-tuple-element.182), channel_id=1, source_target_pairs={{0,2},{1,3},{2,0},{3,1},{4,6},{5,7},{6,4},{7,5},{8,10},{9,11},{10,... | collective-permute-start | bytes 1572872 | tf_op jit(solution)/shard_map/ppermute | solution.py:507
  203.4 29.6 %collective-permute-start.20 = (bf16[512,512]{1,0:T(8,128)(2,1)}, bf16[512,512]{1,0:T(8,128)(2,1)}, u32[]{:S(2)}, u32[]{:S(2)}) collective-permute-start(bf16[512,512]{1,0:T(8,128)(2,1)} %get-tuple-element.183), channel_id=1, source_target_pairs={{0,2},{1,3},{2,0},{3,1},{4,6},{5,7},{6,4},{7,5},{8,10},{9,11},{10,... | collective-permute-start | bytes 1572872 | tf_op jit(solution)/shard_map/ppermute | solution.py:507
  203.9 10.6 %collective-permute-start.18 = (bf16[128,512]{1,0:T(8,128)(2,1)S(1)}, bf16[128,512]{1,0:T(8,128)(2,1)S(1)}, u32[]{:S(2)}, u32[]{:S(2)}) collective-permute-start(bf16[128,512]{1,0:T(8,128)(2,1)S(1)} %get-tuple-element.177), channel_id=1, source_target_pairs={{0,4},{4,0},{8,12},{12,8},{16,20},{20,16},{24,28},{28,24},{1,5},{5... | collective-permute-start | bytes 393224 | tf_op jit(solution)/shard_map/ppermute | solution.py:507
  206.1 9.0 %collective-permute-start.17 = (bf16[128,512]{1,0:T(8,128)(2,1)S(1)}, bf16[128,512]{1,0:T(8,128)(2,1)S(1)}, u32[]{:S(2)}, u32[]{:S(2)}) collective-permute-start(bf16[128,512]{1,0:T(8,128)(2,1)S(1)} %get-tuple-element.174), channel_id=1, source_target_pairs={{0,16},{4,20},{8,24},{12,28},{16,0},{20,4},{24,8},{28,12},{1,17},{... | collective-permute-start | bytes 393224 | tf_op jit(solution)/shard_map/ppermute | solution.py:507
  215.7 17.2 %all-to-all-start.3 = ((f32[8,8,512]{2,1,0:T(8,128)}), f32[8,8,512]{2,1,0:T(8,128)S(1)}, u32[]{:S(2)}, u32[]{:S(2)}) async-start(f32[8,8,512]{2,1,0:T(8,128)} %get-tuple-element.179.refs_3_), calls=%async_computation.3 | async-start | bytes 262144 | tf_op jit(solution)/shard_map/all_to_all | solution.py:118
  219.7 6.3 %collective-permute-start.22 = (bf16[128,512]{1,0:T(8,128)(2,1)S(1)}, bf16[128,512]{1,0:T(8,128)(2,1)S(1)}, u32[]{:S(2)}, u32[]{:S(2)}) collective-permute-start(bf16[128,512]{1,0:T(8,128)(2,1)S(1)} %get-tuple-element.186.refs_1_), channel_id=1, source_target_pairs={{0,4},{4,0},{8,12},{12,8},{16,20},{20,16},{24,28},{28,24},{1,5},{5... | collective-permute-start | bytes 393224 | tf_op jit(solution)/shard_map/ppermute | solution.py:507
  221.7 10.1 %collective-permute-start.21 = (bf16[128,512]{1,0:T(8,128)(2,1)S(1)}, bf16[128,512]{1,0:T(8,128)(2,1)S(1)}, u32[]{:S(2)}, u32[]{:S(2)}) collective-permute-start(bf16[128,512]{1,0:T(8,128)(2,1)S(1)} %get-tuple-element.184.refs_1_), channel_id=1, source_target_pairs={{0,16},{4,20},{8,24},{12,28},{16,0},{20,4},{24,8},{28,12},{1,17},{... | collective-permute-start | bytes 393224 | tf_op jit(solution)/shard_map/ppermute | solution.py:507
  241.8 33.9 %collective-permute-start.24 = (bf16[1792,512]{1,0:T(8,128)(2,1)}, bf16[1792,512]{1,0:T(8,128)(2,1)}, u32[]{:S(2)}, u32[]{:S(2)}) collective-permute-start(bf16[1792,512]{1,0:T(8,128)(2,1)} %get-tuple-element.188.refs_5_.refs_1_), channel_id=1, source_target_pairs={{0,1},{1,0},{2,3},{3,2},{4,5},{5,4},{6,7},{7,6},{8,9},{9,8},{10,11... | collective-permute-start | bytes 5505032 | tf_op jit(solution)/shard_map/ppermute | solution.py:507
  241.8 68.1 %collective-permute-start.27 = (bf16[1792,512]{1,0:T(8,128)(2,1)}, bf16[1792,512]{1,0:T(8,128)(2,1)}, u32[]{:S(2)}, u32[]{:S(2)}) collective-permute-start(bf16[1792,512]{1,0:T(8,128)(2,1)} %get-tuple-element.188.refs_5_.refs_1_), channel_id=1, source_target_pairs={{0,2},{1,3},{2,0},{3,1},{4,6},{5,7},{6,4},{7,5},{8,10},{9,11},{10,... | collective-permute-start | bytes 5505032 | tf_op jit(solution)/shard_map/ppermute | solution.py:507
  243.4 30.3 %collective-permute-start.25 = (bf16[512,512]{1,0:T(8,128)(2,1)}, bf16[512,512]{1,0:T(8,128)(2,1)}, u32[]{:S(2)}, u32[]{:S(2)}) collective-permute-start(bf16[512,512]{1,0:T(8,128)(2,1)} %get-tuple-element.192), channel_id=1, source_target_pairs={{0,1},{1,0},{2,3},{3,2},{4,5},{5,4},{6,7},{7,6},{8,9},{9,8},{10,11... | collective-permute-start | bytes 1572872 | tf_op jit(solution)/shard_map/ppermute | solution.py:507
  243.6 13.9 %collective-permute-start.31 = (bf16[256,512]{1,0:T(8,128)(2,1)S(1)}, bf16[256,512]{1,0:T(8,128)(2,1)S(1)}, u32[]{:S(2)}, u32[]{:S(2)}) collective-permute-start(bf16[256,512]{1,0:T(8,128)(2,1)S(1)} %get-tuple-element.205.refs_1_), channel_id=1, source_target_pairs={{0,16},{4,20},{8,24},{12,28},{16,0},{20,4},{24,8},{28,12},{1,17},{... | collective-permute-start | bytes 786440 | tf_op jit(solution)/shard_map/ppermute | solution.py:507
  243.6 14.6 %collective-permute-start.29 = (bf16[256,512]{1,0:T(8,128)(2,1)S(1)}, bf16[256,512]{1,0:T(8,128)(2,1)S(1)}, u32[]{:S(2)}, u32[]{:S(2)}) collective-permute-start(bf16[256,512]{1,0:T(8,128)(2,1)S(1)} %get-tuple-element.203.refs_1_), channel_id=1, source_target_pairs={{0,8},{4,12},{8,0},{12,4},{16,24},{20,28},{24,16},{28,20},{1,9},{5... | collective-permute-start | bytes 786440 | tf_op jit(solution)/shard_map/ppermute | solution.py:507
  258.2 22.9 %collective-permute-start.26 = (bf16[512,512]{1,0:T(8,128)(2,1)}, bf16[512,512]{1,0:T(8,128)(2,1)}, u32[]{:S(2)}, u32[]{:S(2)}) collective-permute-start(bf16[512,512]{1,0:T(8,128)(2,1)} %get-tuple-element.197), channel_id=1, source_target_pairs={{0,8},{4,12},{8,0},{12,4},{16,24},{20,28},{24,16},{28,20},{1,9},{5... | collective-permute-start | bytes 1572872 | tf_op jit(solution)/shard_map/ppermute | solution.py:507
  258.9 26.1 %collective-permute-start.23 = (bf16[512,512]{1,0:T(8,128)(2,1)}, bf16[512,512]{1,0:T(8,128)(2,1)}, u32[]{:S(2)}, u32[]{:S(2)}) collective-permute-start(bf16[512,512]{1,0:T(8,128)(2,1)} %get-tuple-element.191), channel_id=1, source_target_pairs={{0,4},{4,0},{8,12},{12,8},{16,20},{20,16},{24,28},{28,24},{1,5},{5... | collective-permute-start | bytes 1572872 | tf_op jit(solution)/shard_map/ppermute | solution.py:507
  273.7 18.2 %collective-permute-start.32 = (bf16[512,512]{1,0:T(8,128)(2,1)S(1)}, bf16[512,512]{1,0:T(8,128)(2,1)S(1)}, u32[]{:S(2)}, u32[]{:S(2)}) collective-permute-start(bf16[512,512]{1,0:T(8,128)(2,1)S(1)} %get-tuple-element.206.refs_3_), channel_id=1, source_target_pairs={{0,8},{4,12},{8,0},{12,4},{16,24},{20,28},{24,16},{28,20},{1,9},{5... | collective-permute-start | bytes 1572872 | tf_op jit(solution)/shard_map/ppermute | solution.py:507
  275.7 16.2 %collective-permute-start.30 = (bf16[512,512]{1,0:T(8,128)(2,1)S(1)}, bf16[512,512]{1,0:T(8,128)(2,1)S(1)}, u32[]{:S(2)}, u32[]{:S(2)}) collective-permute-start(bf16[512,512]{1,0:T(8,128)(2,1)S(1)} %get-tuple-element.204.refs_1_), channel_id=1, source_target_pairs={{0,4},{4,0},{8,12},{12,8},{16,20},{20,16},{24,28},{28,24},{1,5},{5... | collective-permute-start | bytes 1572872 | tf_op jit(solution)/shard_map/ppermute | solution.py:507
  283.8 14.6 %collective-permute-start.34 = (bf16[256,512]{1,0:T(8,128)(2,1)S(1)}, bf16[256,512]{1,0:T(8,128)(2,1)S(1)}, u32[]{:S(2)}, u32[]{:S(2)}) collective-permute-start(bf16[256,512]{1,0:T(8,128)(2,1)S(1)} %get-tuple-element.213), channel_id=1, source_target_pairs={{0,16},{4,20},{8,24},{12,28},{16,0},{20,4},{24,8},{28,12},{1,17},{... | collective-permute-start | bytes 786440 | tf_op jit(solution)/shard_map/ppermute | solution.py:507
  286.7 14.6 %collective-permute-start.28 = (bf16[256,512]{1,0:T(8,128)(2,1)S(1)}, bf16[256,512]{1,0:T(8,128)(2,1)S(1)}, u32[]{:S(2)}, u32[]{:S(2)}) collective-permute-start(bf16[256,512]{1,0:T(8,128)(2,1)S(1)} %get-tuple-element.202), channel_id=1, source_target_pairs={{0,8},{4,12},{8,0},{12,4},{16,24},{20,28},{24,16},{28,20},{1,9},{5... | collective-permute-start | bytes 786440 | tf_op jit(solution)/shard_map/ppermute | solution.py:507
  300.2 5.0 %collective-permute-start.35 = (bf16[128,512]{1,0:T(8,128)(2,1)S(1)}, bf16[128,512]{1,0:T(8,128)(2,1)S(1)}, u32[]{:S(2)}, u32[]{:S(2)}) collective-permute-start(bf16[128,512]{1,0:T(8,128)(2,1)S(1)} %get-tuple-element.215), channel_id=1, source_target_pairs={{0,4},{4,0},{8,12},{12,8},{16,20},{20,16},{24,28},{28,24},{1,5},{5... | collective-permute-start | bytes 393224 | tf_op jit(solution)/shard_map/ppermute | solution.py:507
  302.4 7.0 %collective-permute-start.33 = (bf16[128,512]{1,0:T(8,128)(2,1)S(1)}, bf16[128,512]{1,0:T(8,128)(2,1)S(1)}, u32[]{:S(2)}, u32[]{:S(2)}) collective-permute-start(bf16[128,512]{1,0:T(8,128)(2,1)S(1)} %get-tuple-element.210), channel_id=1, source_target_pairs={{0,16},{4,20},{8,24},{12,28},{16,0},{20,4},{24,8},{28,12},{1,17},{... | collective-permute-start | bytes 393224 | tf_op jit(solution)/shard_map/ppermute | solution.py:507
  309.9 16.1 %collective-permute-start.36 = (bf16[1792,512]{1,0:T(8,128)(2,1)}, bf16[1792,512]{1,0:T(8,128)(2,1)S(1)}, u32[]{:S(2)}, u32[]{:S(2)}) collective-permute-start(bf16[1792,512]{1,0:T(8,128)(2,1)} %collective-permute-done.27.refs_1_), channel_id=1, source_target_pairs={{0,1},{1,0},{2,3},{3,2},{4,5},{5,4},{6,7},{7,6},{8,9},{9,8},{10,11... | collective-permute-start | bytes 5505032 | tf_op jit(solution)/shard_map/ppermute | solution.py:507
  310.0 16.0 %collective-permute-start.37 = (bf16[512,512]{1,0:T(8,128)(2,1)}, bf16[512,512]{1,0:T(8,128)(2,1)S(1)}, u32[]{:S(2)}, u32[]{:S(2)}) collective-permute-start(bf16[512,512]{1,0:T(8,128)(2,1)} %collective-permute-done.20.refs_12_), channel_id=1, source_target_pairs={{0,1},{1,0},{2,3},{3,2},{4,5},{5,4},{6,7},{7,6},{8,9},{9,8},{10,11... | collective-permute-start | bytes 1572872 | tf_op jit(solution)/shard_map/ppermute | solution.py:507
  310.5 5.5 %collective-permute-start.41 = (bf16[128,512]{1,0:T(8,128)(2,1)S(1)}, bf16[128,512]{1,0:T(8,128)(2,1)S(1)}, u32[]{:S(2)}, u32[]{:S(2)}) collective-permute-start(bf16[128,512]{1,0:T(8,128)(2,1)S(1)} %get-tuple-element.225.refs_1_), channel_id=1, source_target_pairs={{0,4},{4,0},{8,12},{12,8},{16,20},{20,16},{24,28},{28,24},{1,5},{5... | collective-permute-start | bytes 393224 | tf_op jit(solution)/shard_map/ppermute | solution.py:507
  311.4 13.4 %collective-permute-start.38 = (bf16[128,512]{1,0:T(8,128)(2,1)S(1)}, bf16[128,512]{1,0:T(8,128)(2,1)S(1)}, u32[]{:S(2)}, u32[]{:S(2)}) collective-permute-start(bf16[128,512]{1,0:T(8,128)(2,1)S(1)} %get-tuple-element.221.refs_1_), channel_id=1, source_target_pairs={{0,16},{4,20},{8,24},{12,28},{16,0},{20,4},{24,8},{28,12},{1,17},{... | collective-permute-start | bytes 393224 | tf_op jit(solution)/shard_map/ppermute | solution.py:507
  317.1 15.8 %collective-permute-start.42 = (bf16[256,512]{1,0:T(8,128)(2,1)S(1)}, bf16[256,512]{1,0:T(8,128)(2,1)S(1)}, u32[]{:S(2)}, u32[]{:S(2)}) collective-permute-start(bf16[256,512]{1,0:T(8,128)(2,1)S(1)} %get-tuple-element.226.refs_1_), channel_id=1, source_target_pairs={{0,16},{4,20},{8,24},{12,28},{16,0},{20,4},{24,8},{28,12},{1,17},{... | collective-permute-start | bytes 786440 | tf_op jit(solution)/shard_map/ppermute | solution.py:507
  326.0 10.0 %collective-permute-start.39 = (bf16[256,512]{1,0:T(8,128)(2,1)S(1)}, bf16[256,512]{1,0:T(8,128)(2,1)S(1)}, u32[]{:S(2)}, u32[]{:S(2)}) collective-permute-start(bf16[256,512]{1,0:T(8,128)(2,1)S(1)} %get-tuple-element.222.refs_1_), channel_id=1, source_target_pairs={{0,8},{4,12},{8,0},{12,4},{16,24},{20,28},{24,16},{28,20},{1,9},{5... | collective-permute-start | bytes 786440 | tf_op jit(solution)/shard_map/ppermute | solution.py:507
  334.1 13.8 %collective-permute-start.43 = (bf16[512,512]{1,0:T(8,128)(2,1)S(1)}, bf16[512,512]{1,0:T(8,128)(2,1)S(1)}, u32[]{:S(2)}, u32[]{:S(2)}) collective-permute-start(bf16[512,512]{1,0:T(8,128)(2,1)S(1)} %get-tuple-element.227.refs_3_), channel_id=1, source_target_pairs={{0,8},{4,12},{8,0},{12,4},{16,24},{20,28},{24,16},{28,20},{1,9},{5... | collective-permute-start | bytes 1572872 | tf_op jit(solution)/shard_map/ppermute | solution.py:507
  337.2 13.8 %collective-permute-start.40 = (bf16[512,512]{1,0:T(8,128)(2,1)S(1)}, bf16[512,512]{1,0:T(8,128)(2,1)S(1)}, u32[]{:S(2)}, u32[]{:S(2)}) collective-permute-start(bf16[512,512]{1,0:T(8,128)(2,1)S(1)} %get-tuple-element.224.refs_1_), channel_id=1, source_target_pairs={{0,4},{4,0},{8,12},{12,8},{16,20},{20,16},{24,28},{28,24},{1,5},{5... | collective-permute-start | bytes 1572872 | tf_op jit(solution)/shard_map/ppermute | solution.py:507
  (69 other events, 718.3 us)

commit v4 on v3

--- a/solution.py
+++ b/solution.py
@@ -84,8 +84,9 @@
     counts = joined + joined * eye
     ht_ref[0] = wide(counts.astype(BF), 2 * SLOT)
     h_ref[0] = wide(counts.T.astype(BF), 2 * SLOT)
-    inv_ref[0] = jnp.broadcast_to(1.0 / (degree + 1.0), (SLOT, SLOT)).T
-    val_ref[0] = jnp.broadcast_to(valid_ref[0].astype(F32), (SLOT, SLOT)).T
+    valid = valid_ref[0].astype(F32)
+    inv_ref[0] = jnp.broadcast_to(valid / (degree + 1.0), (SLOT, SLOT)).T
+    val_ref[0] = jnp.broadcast_to(valid, (SLOT, SLOT)).T
 
 
 def build_tiles(neighbours, node_valid):
@@ -308,7 +309,7 @@
         spread_rows(st_ref, (grad_beta, grad_gamma))
 
 
-def turn_kernel(from_cot, big, lin_ref, grad_ref, val_ref, inv_ref, ht_ref, g_ref, sg_ref, gamma_ref, beta_ref, out_ref, token_ref, co_ref, lg_ref):
+def turn_kernel(from_cot, big, lin_ref, grad_ref, inv_ref, ht_ref, g_ref, sg_ref, gamma_ref, beta_ref, out_ref, token_ref, co_ref, lg_ref):
     mark(token_ref)
 
     @pl.when(pl.program_id(0) == 0)
@@ -327,7 +328,7 @@
             grad = grad_ref[rows, :].astype(F32) * double_slope(away, co_ref)
         else:
             grad = grad_ref[rows, :]
-        weight = wide(val_ref[s, inner, :] * inv_ref[s, inner, :], columns)
+        weight = wide(inv_ref[s, inner, :], columns)
         high, low = split(weight * (grad - (at(co_ref, 5) + away * at(co_ref, 6))))
         lg_ref[s, inner, :] = high
         lg_ref[s, slice(inner.start + SLOT, inner.stop + SLOT), :] = low
@@ -362,9 +363,9 @@
 
 
 def turn_call(from_cot, big, lin, grad, tiles, norm, sums, name, tokens=()):
-    _, ht, inv, val = tiles
+    _, ht, inv, _ = tiles
     return rows_call(
-        functools.partial(turn_kernel, from_cot), big, [lin, grad], [val, inv, ht], [norm[0], sums, *norm[1:]], BF,
+        functools.partial(turn_kernel, from_cot), big, [lin, grad], [inv, ht], [norm[0], sums, *norm[1:]], BF,
         [pltpu.VMEM((big, 2 * SLOT, lin.shape[1]), BF)], name, tokens, 60,
     )
 
@@ -470,14 +471,14 @@
 def place_kernel(orders, meta_ref, *refs):
     out_ref, token_ref = refs[-2:]
     mark(token_ref)
-    pieces = 1 << (len(orders[0]) - 1)
+    pieces = 1 << (len(orders[0]) - 2)
     size = out_ref.shape[0] // pieces
     for k in range(4):
 
         @pl.when(pl.program_id(0) == k)
         def _():
             mask = 0
-            for b in orders[k // 2][1:]:
+            for b in orders[k // 2][1:-1]:
                 mask = 2 * mask + meta_ref[4 + b]
             for n in range(pieces):
                 start = pl.multiple_of((mask ^ n) * size, size)
@@ -568,18 +569,18 @@
 
 
 class RowSum:
-    def __init__(self, axis, meta, terms, name):
+    def __init__(self, axis, meta, terms, name, between=tuple):
         self.axis, self.meta, self.name = axis, meta, name
         self.bits = lax.axis_size(axis).bit_length() - 1
-        self.stages = 2 * self.bits
+        self.stages = 2 * self.bits - 1
         self.orders = [list(range(self.bits)), list(range(1, self.bits)) + [0]]
         *self.send, self.sent = terms(1, ())
-        *self.keep, self.kept = terms(0, (self.sent,))
+        *self.keep, self.kept = terms(0, (self.sent, *between()))
         self.stage = 0
         self.step(())
 
     def step(self, tokens):
-        s, bits = self.stage, self.bits
+        s, last = self.stage, self.bits - 1
         self.stage += 1
         started = []
         for n in range(2):
@@ -587,17 +588,17 @@
             call = lambda kernel, sizes: small_call(
                 kernel, self.meta, self.keep[n], self.got[n], sizes, f"{self.name}_{n}_{s}", tokens
             )
-            if 0 < s < bits:
+            if 0 < s < last:
                 fold = functools.partial(fold_kernel, False, self.orders[n][s])
                 self.send[n], self.keep[n], token = call(fold, [rows // 2] * 2)
-            elif s == bits:
+            elif s == last or s == last + 1:
                 self.keep[n], token = call(functools.partial(fold_kernel, True, 0), [rows])
-            elif s > bits:
+            elif s > last + 1:
                 self.keep[n], token = call(join_kernel, [2 * rows])
             if s > 0:
                 started.append(token)
-        level = s if s < bits else 2 * bits - 1 - s
-        moved = self.send if s < bits else self.keep
+        level = s if s <= last else 2 * last - s
+        moved = self.send if s < last else self.keep
         self.got = [across(moved[n], self.axis, 1 << self.orders[n][level]) for n in range(2)]
         return tuple(started)
 
@@ -671,10 +672,9 @@
     slices_one, (far,) = after(slices_one, far)
     rows_one, crossing = weight_rows(slices_one)
     grad_one, sums = backward(big, early, far, beyond, rows_two[1:], lin_one, norm_one, "backward_two", tokens)
-    sums, tokens = after(sums, *sum_two.next(sums))
+    tokens = (*crossing, *sum_two.next(*sum_two.next(sums)))
     grads_one = small_gather(sums, "row")
 
-    tokens = (*tokens, *crossing, *sum_two.next())
     turned, _ = turn_call(False, big, lin_one, grad_one, tiles, norm_one, grads_one, "turn_one", tokens)
     far, near = across(turned, "col", 2), across(turned, "col", 1)
 
@@ -684,7 +684,6 @@
     sum_one = RowSum("row", ids, terms_one, "one")
     weights = [weight_block(weight_one, 0), whole_block(rows_one[0])]
     early, token = half(ids, big, turned, near, weights, True, "half_back_one", (sum_one.kept,))
-    sum_two.next(sum_one.kept)
     output, token = rows_call(result_kernel, big, [lin_two], [val], norm_two, F32, [], "output", sum_one.next(token))
     grad_weight_two, token = sum_two.placed(60, (token,))
     sum_one.next(token)

time: 355 us -> 339 us (0.955)
  Pallas kernels: 124 us -> 118 us
  starting transfers between devices: 42.9 us -> 38.9 us
    pallas_call x41 -> x37, Pallas kernels: 124 us -> 118 us  [launch(): pl.pallas_call(body, grid_spec=pltpu.PrefetchScalarGridSpec(num_scalar_pr...]
    ppermute x44 -> x40, starting transfers between devices: 35.4 us -> 30.8 us  [across(): return lax.ppermute(value, axis, [(i, i ^ distance) for i in range(size)])]
    ppermute x44 -> x40, waiting for transfers between devices: 128 us -> 125 us  [across(): return lax.ppermute(value, axis, [(i, i ^ distance) for i in range(size)])]
    unnamed x142 -> x124, local copies, waits for them, and re-layouts: 25.3 us -> 23.1 us
  transfers between devices with their start and end apart: 46 -> 42, of which waited for: 19 -> 20; matrix products, arithmetic and copies ran while one was open for 1% -> 1% of each run, Pallas kernels for 27% -> 26%
where the time goes in v4:
time: 339 us; the launch traced here: 338 us
  waiting for transfers between devices  132 us (39%)
  Pallas kernels  118 us (35%)
  starting transfers between devices  38.9 us (11%)
  local copies, waits for them, and re-layouts  25.1 us (7%)
  blocking collectives  23.1 us (7%)
    ppermute x40, waiting for transfers between devices, across(): return lax.ppermute(value, axis, [(i, i ^ distance) for i in range(size)])  125 us
    pallas_call x37, Pallas kernels, launch(): pl.pallas_call(body, grid_spec=pltpu.PrefetchScalarGridSpec(num_scalar_pr...  118 us
    ppermute x40, starting transfers between devices, across(): return lax.ppermute(value, axis, [(i, i ^ distance) for i in range(size)])  30.8 us
    unnamed x124, local copies, waits for them, and re-layouts  23.1 us
    all_to_all x2, blocking collectives, small_gather(): return lax.all_to_all(copies, axis, split_axis=0, concat_axis=0, tiled=True)  23.1 us
    all_to_all x2, starting transfers between devices, small_gather(): return lax.all_to_all(copies, axis, split_axis=0, concat_axis=0, tiled=True)  8.1 us
    all_to_all x2, waiting for transfers between devices, small_gather(): return lax.all_to_all(copies, axis, split_axis=0, concat_axis=0, tiled=True)  7.23 us
  transfers between devices with their start and end apart: 42, of which 20 were waited for; matrix products, arithmetic and copies ran while one was open for 1% of the time, Pallas kernels for 26%

profile of v4, /device:TPU:0, one launch (start us, length us, event | category | flops | bytes accessed | tf_op | source)
XLA Modules:
  0.0 338.4 jit_solution(10779582672695607969)
XLA Ops:
  1.2 2.6 collective-permute-start.1
  4.6 5.0 %tiles.1 = (bf16[14,128,256]{2,1,0:T(8,128)(2,1)S(1)}, bf16[14,128,256]{2,1,0:T(8,128)(2,1)S(1)}, f32[14,128,128]{2,1,0:T(8,128)S(1)}, f32[14,128,128]{2,1,0:T(8,128)S(1)}, f32[8,128]{1,0:T(8,128)S(1)}) custom-call(s32[14,32,128]{2,1,0:T(8,128)S(1)} %bitcast_bitcast_fusion.refs_0_, s32[14,1,128]{2,1,0:T(1,128)S(1)} %reshape.35.refs_1_), custom_call_target="tpu_custom_call" | custom-call | flops 1000000 | bytes 1000 | tf_op jit(solution)/shard_map/tiles/pallas_call | solution.py:43
  12.8 1.9 weight_slices.1
  16.5 2.8 half_one.1
  19.3 25.3 %collective-permute-done.1.refs_2_.refs_3_ = bf16[1792,512]{1,0:T(8,128)(2,1)} collective-permute-done((bf16[1792,512]{1,0:T(8,128)(2,1)}, bf16[1792,512]{1,0:T(8,128)(2,1)}, u32[]{:S(2)}, u32[]{:S(2)}) %collective-permute-start.1) | collective-permute-done | bytes 1835040 | tf_op jit(solution)/shard_map/ppermute | solution.py:508
  44.7 4.0 %collective-permute-done.2.refs_3_.refs_4_ = bf16[1792,512]{1,0:T(8,128)(2,1)S(1)} collective-permute-done((bf16[1792,512]{1,0:T(8,128)(2,1)}, bf16[1792,512]{1,0:T(8,128)(2,1)S(1)}, u32[]{:S(2)}, u32[]{:S(2)}) %collective-permute-start.2) | collective-permute-done | bytes 1835040 | tf_op jit(solution)/shard_map/ppermute | solution.py:508
  48.7 7.6 %forward_one.1 = (f32[1792,512]{1,0:T(8,128)S(1)}, f32[8,8,512]{2,1,0:T(8,128)S(1)}) custom-call(s32[7]{0:T(128)S(1)} %stack.31.refs_0_, f32[1792,512]{1,0:T(8,128)S(1)} %get-tuple-element.108.refs_1_, bf16[1792,512]{1,0:T(8,128)(2,1)} %collective-permute-done.1.refs_2_.refs_3_, bf16[1792,512]{1,0:T(8,128)(2,1)S(1)} %collective-permute-done.2.refs_3_.refs_4_, ...), custom_call_target="tpu_custom_call" | custom-call | flops 1000000 | bytes 1000 | tf_op jit(solution)/shard_map/forward_one/pallas_call | solution.py:43
  56.3 13.2 %all_to_all.20.refs_2_.refs_6_.refs_4_ = f32[8,8,512]{2,1,0:T(8,128)S(1)} all-to-all(f32[8,8,512]{2,1,0:T(8,128)S(1)} %get-tuple-element.120), channel_id=1, replica_groups=mesh['row'=8,'col'=4] {'row'}, dimensions={0} | all-to-all | bytes 262144 | tf_op jit(solution)/shard_map/all_to_all | solution.py:119
  69.5 1.7 hidden.1
  72.9 2.2 collective-permute-done.3.refs_2_
  75.1 2.8 half_two.1
  77.9 35.8 %collective-permute-done.4.refs_2_.refs_3_ = bf16[1792,512]{1,0:T(8,128)(2,1)S(1)} collective-permute-done((bf16[1792,512]{1,0:T(8,128)(2,1)S(1)}, bf16[1792,512]{1,0:T(8,128)(2,1)S(1)}, u32[]{:S(2)}, u32[]{:S(2)}) %collective-permute-start.4) | collective-permute-done | bytes 1835040 | tf_op jit(solution)/shard_map/ppermute | solution.py:508
  115.7 1.8 collective-permute-done.5.refs_3_.refs_4_
  117.5 6.3 %forward_two.1 = (f32[1792,512]{1,0:T(8,128)S(1)}, f32[8,8,512]{2,1,0:T(8,128)S(1)}) custom-call(s32[7]{0:T(128)S(1)} %stack.31.refs_0_, f32[1792,512]{1,0:T(8,128)S(1)} %get-tuple-element.122.refs_1_, bf16[1792,512]{1,0:T(8,128)(2,1)S(1)} %collective-permute-done.4.refs_2_.refs_3_, bf16[1792,512]{1,0:T(8,128)(2,1)S(1)} %collective-permute-done.5.refs_3_.refs_4_, ...), custom_call_target="tpu_custom_call" | custom-call | flops 1000000 | bytes 1000 | tf_op jit(solution)/shard_map/forward_two/pallas_call | solution.py:43
  123.9 10.0 %all_to_all.21.refs_3_.refs_4_.refs_2_ = f32[8,8,512]{2,1,0:T(8,128)S(1)} all-to-all(f32[8,8,512]{2,1,0:T(8,128)S(1)} %get-tuple-element.131), channel_id=1, replica_groups=mesh['row'=8,'col'=4] {'row'}, dimensions={0} | all-to-all | bytes 262144 | tf_op jit(solution)/shard_map/all_to_all | solution.py:119
  133.9 2.7 sums_two.1
  136.6 1.8 copy-done.7
  138.4 3.5 %all-to-all-start.2 = ((f32[8,8,512]{2,1,0:T(8,128)}), f32[8,8,512]{2,1,0:T(8,128)S(1)}, u32[]{:S(2)}, u32[]{:S(2)}) async-start(f32[8,8,512]{2,1,0:T(8,128)} %sums_two.1), calls=%async_computation.2 | async-start | bytes 262144 | tf_op jit(solution)/shard_map/all_to_all | solution.py:119
  142.0 7.1 %all-to-all-done.2.refs_5_ = f32[8,8,512]{2,1,0:T(8,128)S(1)} async-done(((f32[8,8,512]{2,1,0:T(8,128)}), f32[8,8,512]{2,1,0:T(8,128)S(1)}, u32[]{:S(2)}, u32[]{:S(2)}) %all-to-all-start.2) | async-done | bytes 131104 | tf_op jit(solution)/shard_map/all_to_all | solution.py:119
  149.7 8.4 %turn_two.1 = (bf16[1792,512]{1,0:T(8,128)(2,1)}, f32[8,128]{1,0:T(8,128)}) custom-call(f32[1792,512]{1,0:T(8,128)} %copy-done.7, bf16[1792,512]{1,0:T(8,128)(2,1)} %refs_1_.9, f32[14,128,128]{2,1,0:T(8,128)} %copy-done.20, bf16[14,128,256]{2,1,0:T(8,128)(2,1)} %copy-done.25, f32[8,8,512]{2,1,0:T(8,128)} %copy-done.27, f32[8,8,512]{2,1,0:T(8,128)} %copy-done.58, ...), custom_call_target="tpu_custom_call" | custom-call | flops 1000000 | bytes 1000 | tf_op jit(solution)/shard_map/turn_two/pallas_call | solution.py:43
  160.0 6.2 %terms_two.2 = (bf16[512,512]{1,0:T(8,128)(2,1)}, bf16[512,512]{1,0:T(8,128)(2,1)}, f32[8,128]{1,0:T(8,128)}) custom-call(s32[7]{0:T(128)} %copy-done.40, bf16[1792,512]{1,0:T(8,128)(2,1)} %copy-done.18, bf16[1792,512]{1,0:T(8,128)(2,1)} %copy-done.19, bf16[1792,512]{1,0:T(8,128)(2,1)} %copy-done.11, bf16[1792,512]{1,0:T(8,128)(2,1)} %copy-done.12, ...), custom_call_target="tpu_custom_call" | custom-call | flops 1000000 | bytes 1000 | tf_op jit(solution)/shard_map/terms_two/pallas_call | solution.py:43
  167.5 6.3 %terms_two.3 = (bf16[512,512]{1,0:T(8,128)(2,1)}, bf16[512,512]{1,0:T(8,128)(2,1)}, f32[8,128]{1,0:T(8,128)}) custom-call(s32[7]{0:T(128)} %copy-done.40, bf16[1792,512]{1,0:T(8,128)(2,1)} %copy-done.18, bf16[1792,512]{1,0:T(8,128)(2,1)} %copy-done.19, bf16[1792,512]{1,0:T(8,128)(2,1)} %copy-done.11, bf16[1792,512]{1,0:T(8,128)(2,1)} %copy-done.12, ...), custom_call_target="tpu_custom_call" | custom-call | flops 1000000 | bytes 1000 | tf_op jit(solution)/shard_map/terms_two/pallas_call | solution.py:43
  176.1 4.3 %half_back_two.1 = (f32[1792,512]{1,0:T(8,128)S(1)}, f32[8,128]{1,0:T(8,128)S(1)}) custom-call(s32[7]{0:T(128)S(1)} %copy-done.41, bf16[1792,512]{1,0:T(8,128)(2,1)S(1)} %copy-done.14, bf16[1792,512]{1,0:T(8,128)(2,1)} %collective-permute-done.8.refs_2_, bf16[2048,512]{1,0:T(8,128)(2,1)S(1)} %copy-done.3, ...), custom_call_target="tpu_custom_call" | custom-call | flops 1000000 | bytes 1000 | tf_op jit(solution)/shard_map/half_back_two/pallas_call | solution.py:43
  185.4 11.5 %collective-permute-done.14.refs_2_ = bf16[256,512]{1,0:T(8,128)(2,1)S(1)} collective-permute-done((bf16[256,512]{1,0:T(8,128)(2,1)S(1)}, bf16[256,512]{1,0:T(8,128)(2,1)S(1)}, u32[]{:S(2)}, u32[]{:S(2)}) %collective-permute-start.14) | collective-permute-done | bytes 262176 | tf_op jit(solution)/shard_map/ppermute | solution.py:508
  198.3 2.6 collective-permute-done.10.refs_1_
  203.6 2.1 collective-permute-done.16.refs_4_
  207.2 6.2 %backward_two.1 = (f32[1792,512]{1,0:T(8,128)S(1)}, f32[8,8,512]{2,1,0:T(8,128)}) custom-call(f32[1792,512]{1,0:T(8,128)S(1)} %get-tuple-element.139.refs_0_, bf16[1792,512]{1,0:T(8,128)(2,1)} %collective-permute-done.10.refs_1_, bf16[1792,512]{1,0:T(8,128)(2,1)S(1)} %collective-permute-done.15.refs_2_, ...), custom_call_target="tpu_custom_call" | custom-call | flops 1000000 | bytes 1000 | tf_op jit(solution)/shard_map/backward_two/pallas_call | solution.py:43
  213.4 1.8 copy-done.24
  217.7 4.6 %all-to-all-start.3 = ((f32[8,8,512]{2,1,0:T(8,128)}), f32[8,8,512]{2,1,0:T(8,128)S(1)}, u32[]{:S(2)}, u32[]{:S(2)}) async-start(f32[8,8,512]{2,1,0:T(8,128)} %get-tuple-element.161.refs_3_), calls=%async_computation.3 | async-start | bytes 262144 | tf_op jit(solution)/shard_map/all_to_all | solution.py:119
  222.2 8.2 %collective-permute-done.22.refs_2_ = bf16[256,512]{1,0:T(8,128)(2,1)S(1)} collective-permute-done((bf16[256,512]{1,0:T(8,128)(2,1)S(1)}, bf16[256,512]{1,0:T(8,128)(2,1)S(1)}, u32[]{:S(2)}, u32[]{:S(2)}) %collective-permute-start.22) | collective-permute-done | bytes 262176 | tf_op jit(solution)/shard_map/ppermute | solution.py:508
  233.3 7.7 %turn_one.1 = (bf16[1792,512]{1,0:T(8,128)(2,1)}, f32[8,128]{1,0:T(8,128)}) custom-call(f32[1792,512]{1,0:T(8,128)} %copy-done.9, f32[1792,512]{1,0:T(8,128)} %copy-done.24, f32[14,128,128]{2,1,0:T(8,128)} %copy-done.20, bf16[14,128,256]{2,1,0:T(8,128)(2,1)} %copy-done.25, f32[8,8,512]{2,1,0:T(8,128)} %copy-done.26, f32[8,8,512]{2,1,0:T(8,128)} %copy-done.60, ...), custom_call_target="tpu_custom_call" | custom-call | flops 1000000 | bytes 1000 | tf_op jit(solution)/shard_map/turn_one/pallas_call | solution.py:43
  241.1 2.4 collective-permute-start.27
  243.7 6.2 %terms_one.2 = (bf16[512,512]{1,0:T(8,128)(2,1)}, bf16[512,512]{1,0:T(8,128)(2,1)}, f32[8,128]{1,0:T(8,128)}) custom-call(s32[7]{0:T(128)} %copy-done.40, bf16[1792,512]{1,0:T(8,128)(2,1)} %refs_1_.11, bf16[1792,512]{1,0:T(8,128)(2,1)} %copy-done.16, bf16[1792,512]{1,0:T(8,128)(2,1)} %collective-permute-done.1.refs_2_.refs_3_, bf16[1792,512]{1,0:T(8,128)(2,1)} %copy-done.17, ...), custom_call_target="tpu_custom_call" | custom-call | flops 1000000 | bytes 1000 | tf_op jit(solution)/shard_map/terms_one/pallas_call | solution.py:43
  251.0 1.9 collective-permute-start.30
  255.3 6.3 %terms_one.3 = (bf16[512,512]{1,0:T(8,128)(2,1)}, bf16[512,512]{1,0:T(8,128)(2,1)}, f32[8,128]{1,0:T(8,128)}) custom-call(s32[7]{0:T(128)} %copy-done.40, bf16[1792,512]{1,0:T(8,128)(2,1)} %refs_1_.11, bf16[1792,512]{1,0:T(8,128)(2,1)} %copy-done.16, bf16[1792,512]{1,0:T(8,128)(2,1)} %collective-permute-done.1.refs_2_.refs_3_, bf16[1792,512]{1,0:T(8,128)(2,1)} %copy-done.17, ...), custom_call_target="tpu_custom_call" | custom-call | flops 1000000 | bytes 1000 | tf_op jit(solution)/shard_map/terms_one/pallas_call | solution.py:43
  265.3 4.2 %half_back_one.1 = (f32[1792,512]{1,0:T(8,128)S(1)}, f32[8,128]{1,0:T(8,128)S(1)}) custom-call(s32[7]{0:T(128)S(1)} %copy-done.42, bf16[1792,512]{1,0:T(8,128)(2,1)S(1)} %copy-done.13, bf16[1792,512]{1,0:T(8,128)(2,1)S(1)} %copy-done.32, bf16[2048,512]{1,0:T(8,128)(2,1)S(1)} %copy-done.6, bf16[512,512]{1,0:T(8,128)(2,1)} %collective-permute-done.25.refs_4_, ...), custom_call_target="tpu_custom_call" | custom-call | flops 1000000 | bytes 1000 | tf_op jit(solution)/shard_map/half_back_one/pallas_call | solution.py:43
  269.5 1.8 copy-done.22
  276.5 2.5 output.1
  279.7 4.8 %place_two.1 = (f32[2048,512]{1,0:T(8,128)}, f32[8,128]{1,0:T(8,128)}) custom-call(s32[7]{0:T(128)} %copy-done.40, bf16[512,512]{1,0:T(8,128)(2,1)} %copy-done.34, bf16[512,512]{1,0:T(8,128)(2,1)} %collective-permute-done.29.refs_2_, bf16[512,512]{1,0:T(8,128)(2,1)} %copy-done.33, bf16[512,512]{1,0:T(8,128)(2,1)} %collective-permute-done.30.refs_4_, ...), custom_call_target="tpu_custom_call" | custom-call | flops 1000000 | bytes 1000 | tf_op jit(solution)/shard_map/place_two/pallas_call | solution.py:43
  284.5 2.5 collective-permute-done.32.refs_2_
  291.0 6.0 %collective-permute-done.33.refs_2_ = bf16[256,512]{1,0:T(8,128)(2,1)S(1)} collective-permute-done((bf16[256,512]{1,0:T(8,128)(2,1)S(1)}, bf16[256,512]{1,0:T(8,128)(2,1)S(1)}, u32[]{:S(2)}, u32[]{:S(2)}) %collective-permute-start.33) | collective-permute-done | bytes 262176 | tf_op jit(solution)/shard_map/ppermute | solution.py:508
  297.6 5.4 %collective-permute-done.31.refs_2_ = bf16[256,512]{1,0:T(8,128)(2,1)S(1)} collective-permute-done((bf16[256,512]{1,0:T(8,128)(2,1)S(1)}, bf16[256,512]{1,0:T(8,128)(2,1)S(1)}, u32[]{:S(2)}, u32[]{:S(2)}) %collective-permute-start.31) | collective-permute-done | bytes 262176 | tf_op jit(solution)/shard_map/ppermute | solution.py:508
  304.2 3.2 collective-permute-start.36
  308.5 2.0 copy-done.23
  310.5 4.8 %backward_one.1 = (f32[1792,512]{1,0:T(8,128)}, f32[8,128]{1,0:T(8,128)S(1)}) custom-call(f32[1792,512]{1,0:T(8,128)S(1)} %copy-done.23, bf16[1792,512]{1,0:T(8,128)(2,1)} %collective-permute-done.27.refs_1_, bf16[1792,512]{1,0:T(8,128)(2,1)S(1)} %collective-permute-done.34.refs_2_, bf16[512,512]{1,0:T(8,128)(2,1)S(1)} %copy-done.30, ...), custom_call_target="tpu_custom_call" | custom-call | flops 1000000 | bytes 1000 | tf_op jit(solution)/shard_map/backward_one/pallas_call | solution.py:43
  315.3 3.9 %collective-permute-done.38.refs_2_ = bf16[256,512]{1,0:T(8,128)(2,1)S(1)} collective-permute-done((bf16[256,512]{1,0:T(8,128)(2,1)S(1)}, bf16[256,512]{1,0:T(8,128)(2,1)S(1)}, u32[]{:S(2)}, u32[]{:S(2)}) %collective-permute-start.38) | collective-permute-done | bytes 262176 | tf_op jit(solution)/shard_map/ppermute | solution.py:508
  323.8 10.3 %collective-permute-done.39.refs_4_ = bf16[512,512]{1,0:T(8,128)(2,1)S(1)} collective-permute-done((bf16[512,512]{1,0:T(8,128)(2,1)S(1)}, bf16[512,512]{1,0:T(8,128)(2,1)S(1)}, u32[]{:S(2)}, u32[]{:S(2)}) %collective-permute-start.39) | collective-permute-done | bytes 524320 | tf_op jit(solution)/shard_map/ppermute | solution.py:508
  335.3 3.1 place_one.1
  (206 shorter events, 57.5 us)
Async XLA Ops:
  0.6 15.7 %collective-permute-start = (bf16[1792,512]{1,0:T(8,128)(2,1)}, bf16[1792,512]{1,0:T(8,128)(2,1)S(1)}, u32[]{:S(2)}, u32[]{:S(2)}) collective-permute-start(bf16[1792,512]{1,0:T(8,128)(2,1)} %refs_1_.11), channel_id=1, source_target_pairs={{0,1},{1,0},{2,3},{3,2},{4,5},{5,4},{6,7},{7,6},{8,9},{9,8},{10,11... | collective-permute-start | bytes 5505032 | tf_op jit(solution)/shard_map/ppermute | solution.py:508
  1.2 43.5 %collective-permute-start.1 = (bf16[1792,512]{1,0:T(8,128)(2,1)}, bf16[1792,512]{1,0:T(8,128)(2,1)}, u32[]{:S(2)}, u32[]{:S(2)}) collective-permute-start(bf16[1792,512]{1,0:T(8,128)(2,1)} %refs_1_.11), channel_id=1, source_target_pairs={{0,2},{1,3},{2,0},{3,1},{4,6},{5,7},{6,4},{7,5},{8,10},{9,11},{10,... | collective-permute-start | bytes 5505032 | tf_op jit(solution)/shard_map/ppermute | solution.py:508
  4.6 112.9 %copy-start.40 = (s32[7]{0:T(128)}, s32[7]{0:T(128)S(1)}, u32[]{:S(2)}) copy-start(s32[7]{0:T(128)S(1)} %stack.31.refs_0_) | copy-start | bytes 88
  12.8 104.7 %copy-start.20 = (f32[14,128,128]{2,1,0:T(8,128)}, f32[14,128,128]{2,1,0:T(8,128)S(1)}, u32[]{:S(2)}) copy-start(f32[14,128,128]{2,1,0:T(8,128)S(1)} %get-tuple-element.114.refs_7_.refs_2_) | copy-start | bytes 2752516
  44.7 4.0 %collective-permute-start.2 = (bf16[1792,512]{1,0:T(8,128)(2,1)}, bf16[1792,512]{1,0:T(8,128)(2,1)S(1)}, u32[]{:S(2)}, u32[]{:S(2)}) collective-permute-start(bf16[1792,512]{1,0:T(8,128)(2,1)} %collective-permute-done.1.refs_2_.refs_3_), channel_id=1, source_target_pairs={{0,1},{1,0},{2,3},{3,2},{4,5},{5,4},{6,7},{7,6},{8,9},{9,8},{10,11... | collective-permute-start | bytes 5505032 | tf_op jit(solution)/shard_map/ppermute | solution.py:508
  69.5 137.7 %copy-start.26 = (f32[8,8,512]{2,1,0:T(8,128)}, f32[8,8,512]{2,1,0:T(8,128)S(1)}, u32[]{:S(2)}) copy-start(f32[8,8,512]{2,1,0:T(8,128)S(1)} %all_to_all.20.refs_2_.refs_6_.refs_4_) | copy-start | bytes 393220
  71.3 3.8 %collective-permute-start.3 = (bf16[1792,512]{1,0:T(8,128)(2,1)S(1)}, bf16[1792,512]{1,0:T(8,128)(2,1)S(1)}, u32[]{:S(2)}, u32[]{:S(2)}) collective-permute-start(bf16[1792,512]{1,0:T(8,128)(2,1)S(1)} %get-tuple-element.121.refs_1_), channel_id=1, source_target_pairs={{0,1},{1,0},{2,3},{3,2},{4,5},{5,4},{6,7},{7,6},{8,9},{9,8},{10,11... | collective-permute-start | bytes 5505032 | tf_op jit(solution)/shard_map/ppermute | solution.py:508
  71.3 42.4 %collective-permute-start.4 = (bf16[1792,512]{1,0:T(8,128)(2,1)S(1)}, bf16[1792,512]{1,0:T(8,128)(2,1)S(1)}, u32[]{:S(2)}, u32[]{:S(2)}) collective-permute-start(bf16[1792,512]{1,0:T(8,128)(2,1)S(1)} %get-tuple-element.121.refs_1_), channel_id=1, source_target_pairs={{0,2},{1,3},{2,0},{3,1},{4,6},{5,7},{6,4},{7,5},{8,10},{9,11},{10,... | collective-permute-start | bytes 5505032 | tf_op jit(solution)/shard_map/ppermute | solution.py:508
  113.7 3.8 %collective-permute-start.5 = (bf16[1792,512]{1,0:T(8,128)(2,1)S(1)}, bf16[1792,512]{1,0:T(8,128)(2,1)S(1)}, u32[]{:S(2)}, u32[]{:S(2)}) collective-permute-start(bf16[1792,512]{1,0:T(8,128)(2,1)S(1)} %collective-permute-done.4.refs_2_.refs_3_), channel_id=1, source_target_pairs={{0,1},{1,0},{2,3},{3,2},{4,5},{5,4},{6,7},{7,6},{8,9},{9,8},{10,11... | collective-permute-start | bytes 5505032 | tf_op jit(solution)/shard_map/ppermute | solution.py:508
  113.7 28.3 %collective-permute-start.6 = (bf16[512,512]{1,0:T(8,128)(2,1)}, bf16[512,512]{1,0:T(8,128)(2,1)}, u32[]{:S(2)}, u32[]{:S(2)}) collective-permute-start(bf16[512,512]{1,0:T(8,128)(2,1)} %get-tuple-element.133), channel_id=1, source_target_pairs={{0,2},{1,3},{2,0},{3,1},{4,6},{5,7},{6,4},{7,5},{8,10},{9,11},{10,... | collective-permute-start | bytes 1572872 | tf_op jit(solution)/shard_map/ppermute | solution.py:508
  115.2 26.8 %collective-permute-start.7 = (bf16[512,512]{1,0:T(8,128)(2,1)}, bf16[512,512]{1,0:T(8,128)(2,1)}, u32[]{:S(2)}, u32[]{:S(2)}) collective-permute-start(bf16[512,512]{1,0:T(8,128)(2,1)} %get-tuple-element.134), channel_id=1, source_target_pairs={{0,2},{1,3},{2,0},{3,1},{4,6},{5,7},{6,4},{7,5},{8,10},{9,11},{10,... | collective-permute-start | bytes 1572872 | tf_op jit(solution)/shard_map/ppermute | solution.py:508
  138.4 10.7 %all-to-all-start.2 = ((f32[8,8,512]{2,1,0:T(8,128)}), f32[8,8,512]{2,1,0:T(8,128)S(1)}, u32[]{:S(2)}, u32[]{:S(2)}) async-start(f32[8,8,512]{2,1,0:T(8,128)} %sums_two.1), calls=%async_computation.2 | async-start | bytes 262144 | tf_op jit(solution)/shard_map/all_to_all | solution.py:119
  158.2 15.7 %collective-permute-start.8 = (bf16[1792,512]{1,0:T(8,128)(2,1)}, bf16[1792,512]{1,0:T(8,128)(2,1)}, u32[]{:S(2)}, u32[]{:S(2)}) collective-permute-start(bf16[1792,512]{1,0:T(8,128)(2,1)} %get-tuple-element.135.refs_5_.refs_1_), channel_id=1, source_target_pairs={{0,1},{1,0},{2,3},{3,2},{4,5},{5,4},{6,7},{7,6},{8,9},{9,8},{10,11... | collective-permute-start | bytes 5505032 | tf_op jit(solution)/shard_map/ppermute | solution.py:508
  158.2 42.7 %collective-permute-start.10 = (bf16[1792,512]{1,0:T(8,128)(2,1)}, bf16[1792,512]{1,0:T(8,128)(2,1)}, u32[]{:S(2)}, u32[]{:S(2)}) collective-permute-start(bf16[1792,512]{1,0:T(8,128)(2,1)} %get-tuple-element.135.refs_5_.refs_1_), channel_id=1, source_target_pairs={{0,2},{1,3},{2,0},{3,1},{4,6},{5,7},{6,4},{7,5},{8,10},{9,11},{10,... | collective-permute-start | bytes 5505032 | tf_op jit(solution)/shard_map/ppermute | solution.py:508
  159.8 14.1 %collective-permute-start.9 = (bf16[512,512]{1,0:T(8,128)(2,1)}, bf16[512,512]{1,0:T(8,128)(2,1)S(1)}, u32[]{:S(2)}, u32[]{:S(2)}) collective-permute-start(bf16[512,512]{1,0:T(8,128)(2,1)} %copy-done.57), channel_id=1, source_target_pairs={{0,1},{1,0},{2,3},{3,2},{4,5},{5,4},{6,7},{7,6},{8,9},{9,8},{10,11... | collective-permute-start | bytes 1572872 | tf_op jit(solution)/shard_map/ppermute | solution.py:508
  166.2 14.6 %collective-permute-start.13 = (bf16[512,512]{1,0:T(8,128)(2,1)}, bf16[512,512]{1,0:T(8,128)(2,1)}, u32[]{:S(2)}, u32[]{:S(2)}) collective-permute-start(bf16[512,512]{1,0:T(8,128)(2,1)} %get-tuple-element.150), channel_id=1, source_target_pairs={{0,8},{4,12},{8,0},{12,4},{16,24},{20,28},{24,16},{28,20},{1,9},{5... | collective-permute-start | bytes 1572872 | tf_op jit(solution)/shard_map/ppermute | solution.py:508
  166.2 16.8 %collective-permute-start.11 = (bf16[512,512]{1,0:T(8,128)(2,1)}, bf16[512,512]{1,0:T(8,128)(2,1)}, u32[]{:S(2)}, u32[]{:S(2)}) collective-permute-start(bf16[512,512]{1,0:T(8,128)(2,1)} %get-tuple-element.144), channel_id=1, source_target_pairs={{0,4},{4,0},{8,12},{12,8},{16,20},{20,16},{24,28},{28,24},{1,5},{5... | collective-permute-start | bytes 1572872 | tf_op jit(solution)/shard_map/ppermute | solution.py:508
  176.1 31.2 %copy-start.10 = (f32[1792,512]{1,0:T(8,128)S(1)}, f32[1792,512]{1,0:T(8,128)}, u32[]{:S(2)}) copy-start(f32[1792,512]{1,0:T(8,128)} %copy-done.9) | copy-start | bytes 11010052
  182.4 14.4 %collective-permute-start.14 = (bf16[256,512]{1,0:T(8,128)(2,1)S(1)}, bf16[256,512]{1,0:T(8,128)(2,1)S(1)}, u32[]{:S(2)}, u32[]{:S(2)}) collective-permute-start(bf16[256,512]{1,0:T(8,128)(2,1)S(1)} %get-tuple-element.154), channel_id=1, source_target_pairs={{0,16},{4,20},{8,24},{12,28},{16,0},{20,4},{24,8},{28,12},{1,17},{... | collective-permute-start | bytes 786440 | tf_op jit(solution)/shard_map/ppermute | solution.py:508
  184.8 12.9 %collective-permute-start.12 = (bf16[256,512]{1,0:T(8,128)(2,1)S(1)}, bf16[256,512]{1,0:T(8,128)(2,1)S(1)}, u32[]{:S(2)}, u32[]{:S(2)}) collective-permute-start(bf16[256,512]{1,0:T(8,128)(2,1)S(1)} %get-tuple-element.147), channel_id=1, source_target_pairs={{0,8},{4,12},{8,0},{12,4},{16,24},{20,28},{24,16},{28,20},{1,9},{5... | collective-permute-start | bytes 786440 | tf_op jit(solution)/shard_map/ppermute | solution.py:508
  200.9 6.3 %collective-permute-start.15 = (bf16[1792,512]{1,0:T(8,128)(2,1)}, bf16[1792,512]{1,0:T(8,128)(2,1)S(1)}, u32[]{:S(2)}, u32[]{:S(2)}) collective-permute-start(bf16[1792,512]{1,0:T(8,128)(2,1)} %collective-permute-done.10.refs_1_), channel_id=1, source_target_pairs={{0,1},{1,0},{2,3},{3,2},{4,5},{5,4},{6,7},{7,6},{8,9},{9,8},{10,11... | collective-permute-start | bytes 5505032 | tf_op jit(solution)/shard_map/ppermute | solution.py:508
  200.9 4.7 %collective-permute-start.16 = (bf16[512,512]{1,0:T(8,128)(2,1)}, bf16[512,512]{1,0:T(8,128)(2,1)S(1)}, u32[]{:S(2)}, u32[]{:S(2)}) collective-permute-start(bf16[512,512]{1,0:T(8,128)(2,1)} %collective-permute-done.7.refs_9_), channel_id=1, source_target_pairs={{0,1},{1,0},{2,3},{3,2},{4,5},{5,4},{6,7},{7,6},{8,9},{9,8},{10,11... | collective-permute-start | bytes 1572872 | tf_op jit(solution)/shard_map/ppermute | solution.py:508
  201.5 13.8 %collective-permute-start.21 = (bf16[256,512]{1,0:T(8,128)(2,1)S(1)}, bf16[256,512]{1,0:T(8,128)(2,1)S(1)}, u32[]{:S(2)}, u32[]{:S(2)}) collective-permute-start(bf16[256,512]{1,0:T(8,128)(2,1)S(1)} %get-tuple-element.167.refs_1_), channel_id=1, source_target_pairs={{0,4},{4,0},{8,12},{12,8},{16,20},{20,16},{24,28},{28,24},{1,5},{5... | collective-permute-start | bytes 786440 | tf_op jit(solution)/shard_map/ppermute | solution.py:508
  201.7 14.6 %collective-permute-start.19 = (bf16[256,512]{1,0:T(8,128)(2,1)S(1)}, bf16[256,512]{1,0:T(8,128)(2,1)S(1)}, u32[]{:S(2)}, u32[]{:S(2)}) collective-permute-start(bf16[256,512]{1,0:T(8,128)(2,1)S(1)} %get-tuple-element.164.refs_1_), channel_id=1, source_target_pairs={{0,16},{4,20},{8,24},{12,28},{16,0},{20,4},{24,8},{28,12},{1,17},{... | collective-permute-start | bytes 786440 | tf_op jit(solution)/shard_map/ppermute | solution.py:508
  202.1 30.4 %collective-permute-start.17 = (bf16[512,512]{1,0:T(8,128)(2,1)}, bf16[512,512]{1,0:T(8,128)(2,1)S(1)}, u32[]{:S(2)}, u32[]{:S(2)}) collective-permute-start(bf16[512,512]{1,0:T(8,128)(2,1)} %get-tuple-element.162), channel_id=1, source_target_pairs={{0,2},{1,3},{2,0},{3,1},{4,6},{5,7},{6,4},{7,5},{8,10},{9,11},{10,... | collective-permute-start | bytes 1572872 | tf_op jit(solution)/shard_map/ppermute | solution.py:508
  205.7 26.8 %collective-permute-start.18 = (bf16[512,512]{1,0:T(8,128)(2,1)}, bf16[512,512]{1,0:T(8,128)(2,1)}, u32[]{:S(2)}, u32[]{:S(2)}) collective-permute-start(bf16[512,512]{1,0:T(8,128)(2,1)} %get-tuple-element.163), channel_id=1, source_target_pairs={{0,2},{1,3},{2,0},{3,1},{4,6},{5,7},{6,4},{7,5},{8,10},{9,11},{10,... | collective-permute-start | bytes 1572872 | tf_op jit(solution)/shard_map/ppermute | solution.py:508
  215.8 14.6 %collective-permute-start.22 = (bf16[256,512]{1,0:T(8,128)(2,1)S(1)}, bf16[256,512]{1,0:T(8,128)(2,1)S(1)}, u32[]{:S(2)}, u32[]{:S(2)}) collective-permute-start(bf16[256,512]{1,0:T(8,128)(2,1)S(1)} %get-tuple-element.170.refs_1_), channel_id=1, source_target_pairs={{0,16},{4,20},{8,24},{12,28},{16,0},{20,4},{24,8},{28,12},{1,17},{... | collective-permute-start | bytes 786440 | tf_op jit(solution)/shard_map/ppermute | solution.py:508
  216.9 14.2 %collective-permute-start.20 = (bf16[256,512]{1,0:T(8,128)(2,1)S(1)}, bf16[256,512]{1,0:T(8,128)(2,1)S(1)}, u32[]{:S(2)}, u32[]{:S(2)}) collective-permute-start(bf16[256,512]{1,0:T(8,128)(2,1)S(1)} %get-tuple-element.165.refs_1_), channel_id=1, source_target_pairs={{0,8},{4,12},{8,0},{12,4},{16,24},{20,28},{24,16},{28,20},{1,9},{5... | collective-permute-start | bytes 786440 | tf_op jit(solution)/shard_map/ppermute | solution.py:508
  217.7 15.0 %all-to-all-start.3 = ((f32[8,8,512]{2,1,0:T(8,128)}), f32[8,8,512]{2,1,0:T(8,128)S(1)}, u32[]{:S(2)}, u32[]{:S(2)}) async-start(f32[8,8,512]{2,1,0:T(8,128)} %get-tuple-element.161.refs_3_), calls=%async_computation.3 | async-start | bytes 262144 | tf_op jit(solution)/shard_map/all_to_all | solution.py:119
  241.1 11.9 %collective-permute-start.24 = (bf16[1792,512]{1,0:T(8,128)(2,1)}, bf16[1792,512]{1,0:T(8,128)(2,1)S(1)}, u32[]{:S(2)}, u32[]{:S(2)}) collective-permute-start(bf16[1792,512]{1,0:T(8,128)(2,1)} %get-tuple-element.172.refs_5_.refs_1_), channel_id=1, source_target_pairs={{0,1},{1,0},{2,3},{3,2},{4,5},{5,4},{6,7},{7,6},{8,9},{9,8},{10,11... | collective-permute-start | bytes 5505032 | tf_op jit(solution)/shard_map/ppermute | solution.py:508
  241.1 62.5 %collective-permute-start.27 = (bf16[1792,512]{1,0:T(8,128)(2,1)}, bf16[1792,512]{1,0:T(8,128)(2,1)}, u32[]{:S(2)}, u32[]{:S(2)}) collective-permute-start(bf16[1792,512]{1,0:T(8,128)(2,1)} %get-tuple-element.172.refs_5_.refs_1_), channel_id=1, source_target_pairs={{0,2},{1,3},{2,0},{3,1},{4,6},{5,7},{6,4},{7,5},{8,10},{9,11},{10,... | collective-permute-start | bytes 5505032 | tf_op jit(solution)/shard_map/ppermute | solution.py:508
  243.6 7.5 %collective-permute-start.25 = (bf16[512,512]{1,0:T(8,128)(2,1)}, bf16[512,512]{1,0:T(8,128)(2,1)}, u32[]{:S(2)}, u32[]{:S(2)}) collective-permute-start(bf16[512,512]{1,0:T(8,128)(2,1)} %copy-done.56), channel_id=1, source_target_pairs={{0,1},{1,0},{2,3},{3,2},{4,5},{5,4},{6,7},{7,6},{8,9},{9,8},{10,11... | collective-permute-start | bytes 1572872 | tf_op jit(solution)/shard_map/ppermute | solution.py:508
  249.9 21.4 %collective-permute-start.26 = (bf16[512,512]{1,0:T(8,128)(2,1)}, bf16[512,512]{1,0:T(8,128)(2,1)}, u32[]{:S(2)}, u32[]{:S(2)}) collective-permute-start(bf16[512,512]{1,0:T(8,128)(2,1)} %get-tuple-element.181), channel_id=1, source_target_pairs={{0,8},{4,12},{8,0},{12,4},{16,24},{20,28},{24,16},{28,20},{1,9},{5... | collective-permute-start | bytes 1572872 | tf_op jit(solution)/shard_map/ppermute | solution.py:508
  250.0 23.2 %collective-permute-start.23 = (bf16[512,512]{1,0:T(8,128)(2,1)}, bf16[512,512]{1,0:T(8,128)(2,1)}, u32[]{:S(2)}, u32[]{:S(2)}) collective-permute-start(bf16[512,512]{1,0:T(8,128)(2,1)} %get-tuple-element.175), channel_id=1, source_target_pairs={{0,4},{4,0},{8,12},{12,8},{16,20},{20,16},{24,28},{28,24},{1,5},{5... | collective-permute-start | bytes 1572872 | tf_op jit(solution)/shard_map/ppermute | solution.py:508
  251.0 28.6 %collective-permute-start.30 = (bf16[512,512]{1,0:T(8,128)(2,1)S(1)}, bf16[512,512]{1,0:T(8,128)(2,1)}, u32[]{:S(2)}, u32[]{:S(2)}) collective-permute-start(bf16[512,512]{1,0:T(8,128)(2,1)S(1)} %get-tuple-element.188.refs_3_), channel_id=1, source_target_pairs={{0,8},{4,12},{8,0},{12,4},{16,24},{20,28},{24,16},{28,20},{1,9},{5... | collective-permute-start | bytes 1572872 | tf_op jit(solution)/shard_map/ppermute | solution.py:508
  254.2 25.4 %collective-permute-start.29 = (bf16[512,512]{1,0:T(8,128)(2,1)S(1)}, bf16[512,512]{1,0:T(8,128)(2,1)}, u32[]{:S(2)}, u32[]{:S(2)}) collective-permute-start(bf16[512,512]{1,0:T(8,128)(2,1)S(1)} %copy-done.35), channel_id=1, source_target_pairs={{0,4},{4,0},{8,12},{12,8},{16,20},{20,16},{24,28},{28,24},{1,5},{5... | collective-permute-start | bytes 1572872 | tf_op jit(solution)/shard_map/ppermute | solution.py:508
  273.1 13.9 %collective-permute-start.32 = (bf16[256,512]{1,0:T(8,128)(2,1)S(1)}, bf16[256,512]{1,0:T(8,128)(2,1)S(1)}, u32[]{:S(2)}, u32[]{:S(2)}) collective-permute-start(bf16[256,512]{1,0:T(8,128)(2,1)S(1)} %get-tuple-element.194), channel_id=1, source_target_pairs={{0,16},{4,20},{8,24},{12,28},{16,0},{20,4},{24,8},{28,12},{1,17},{... | collective-permute-start | bytes 786440 | tf_op jit(solution)/shard_map/ppermute | solution.py:508
  274.9 14.9 %collective-permute-start.28 = (bf16[256,512]{1,0:T(8,128)(2,1)S(1)}, bf16[256,512]{1,0:T(8,128)(2,1)S(1)}, u32[]{:S(2)}, u32[]{:S(2)}) collective-permute-start(bf16[256,512]{1,0:T(8,128)(2,1)S(1)} %get-tuple-element.186), channel_id=1, source_target_pairs={{0,8},{4,12},{8,0},{12,4},{16,24},{20,28},{24,16},{28,20},{1,9},{5... | collective-permute-start | bytes 786440 | tf_op jit(solution)/shard_map/ppermute | solution.py:508
  279.7 28.8 %copy-start.30 = (bf16[512,512]{1,0:T(8,128)(2,1)S(1)}, bf16[512,512]{1,0:T(8,128)(2,1)}, u32[]{:S(2)}) copy-start(bf16[512,512]{1,0:T(8,128)(2,1)} %copy-done.29) | copy-start | bytes 1572868
  288.8 8.2 %collective-permute-start.33 = (bf16[256,512]{1,0:T(8,128)(2,1)S(1)}, bf16[256,512]{1,0:T(8,128)(2,1)S(1)}, u32[]{:S(2)}, u32[]{:S(2)}) collective-permute-start(bf16[256,512]{1,0:T(8,128)(2,1)S(1)} %get-tuple-element.195.refs_1_), channel_id=1, source_target_pairs={{0,4},{4,0},{8,12},{12,8},{16,20},{20,16},{24,28},{28,24},{1,5},{5... | collective-permute-start | bytes 786440 | tf_op jit(solution)/shard_map/ppermute | solution.py:508
  291.0 12.1 %collective-permute-start.31 = (bf16[256,512]{1,0:T(8,128)(2,1)S(1)}, bf16[256,512]{1,0:T(8,128)(2,1)S(1)}, u32[]{:S(2)}, u32[]{:S(2)}) collective-permute-start(bf16[256,512]{1,0:T(8,128)(2,1)S(1)} %get-tuple-element.191.refs_1_), channel_id=1, source_target_pairs={{0,16},{4,20},{8,24},{12,28},{16,0},{20,4},{24,8},{28,12},{1,17},{... | collective-permute-start | bytes 786440 | tf_op jit(solution)/shard_map/ppermute | solution.py:508
  303.7 4.8 %collective-permute-start.34 = (bf16[1792,512]{1,0:T(8,128)(2,1)}, bf16[1792,512]{1,0:T(8,128)(2,1)S(1)}, u32[]{:S(2)}, u32[]{:S(2)}) collective-permute-start(bf16[1792,512]{1,0:T(8,128)(2,1)} %collective-permute-done.27.refs_1_), channel_id=1, source_target_pairs={{0,1},{1,0},{2,3},{3,2},{4,5},{5,4},{6,7},{7,6},{8,9},{9,8},{10,11... | collective-permute-start | bytes 5505032 | tf_op jit(solution)/shard_map/ppermute | solution.py:508
  303.7 4.7 %collective-permute-start.35 = (bf16[512,512]{1,0:T(8,128)(2,1)}, bf16[512,512]{1,0:T(8,128)(2,1)S(1)}, u32[]{:S(2)}, u32[]{:S(2)}) collective-permute-start(bf16[512,512]{1,0:T(8,128)(2,1)} %collective-permute-done.18.refs_9_), channel_id=1, source_target_pairs={{0,1},{1,0},{2,3},{3,2},{4,5},{5,4},{6,7},{7,6},{8,9},{9,8},{10,11... | collective-permute-start | bytes 1572872 | tf_op jit(solution)/shard_map/ppermute | solution.py:508
  304.2 14.9 %collective-permute-start.38 = (bf16[256,512]{1,0:T(8,128)(2,1)S(1)}, bf16[256,512]{1,0:T(8,128)(2,1)S(1)}, u32[]{:S(2)}, u32[]{:S(2)}) collective-permute-start(bf16[256,512]{1,0:T(8,128)(2,1)S(1)} %get-tuple-element.204.refs_1_), channel_id=1, source_target_pairs={{0,16},{4,20},{8,24},{12,28},{16,0},{20,4},{24,8},{28,12},{1,17},{... | collective-permute-start | bytes 786440 | tf_op jit(solution)/shard_map/ppermute | solution.py:508
  304.2 16.1 %collective-permute-start.36 = (bf16[256,512]{1,0:T(8,128)(2,1)S(1)}, bf16[256,512]{1,0:T(8,128)(2,1)S(1)}, u32[]{:S(2)}, u32[]{:S(2)}) collective-permute-start(bf16[256,512]{1,0:T(8,128)(2,1)S(1)} %get-tuple-element.201.refs_1_), channel_id=1, source_target_pairs={{0,8},{4,12},{8,0},{12,4},{16,24},{20,28},{24,16},{28,20},{1,9},{5... | collective-permute-start | bytes 786440 | tf_op jit(solution)/shard_map/ppermute | solution.py:508
  310.5 27.8 %copy-start.1 = (s32[1792,32]{0,1:T(8,128)S(1)}, s32[1792,32]{0,1:T(8,128)}, u32[]{:S(2)}) copy-start(s32[1792,32]{0,1:T(8,128)} %param.11) | copy-start | bytes 688132
  320.3 13.8 %collective-permute-start.39 = (bf16[512,512]{1,0:T(8,128)(2,1)S(1)}, bf16[512,512]{1,0:T(8,128)(2,1)S(1)}, u32[]{:S(2)}, u32[]{:S(2)}) collective-permute-start(bf16[512,512]{1,0:T(8,128)(2,1)S(1)} %get-tuple-element.205.refs_3_), channel_id=1, source_target_pairs={{0,8},{4,12},{8,0},{12,4},{16,24},{20,28},{24,16},{28,20},{1,9},{5... | collective-permute-start | bytes 1572872 | tf_op jit(solution)/shard_map/ppermute | solution.py:508
  321.5 13.8 %collective-permute-start.37 = (bf16[512,512]{1,0:T(8,128)(2,1)S(1)}, bf16[512,512]{1,0:T(8,128)(2,1)S(1)}, u32[]{:S(2)}, u32[]{:S(2)}) collective-permute-start(bf16[512,512]{1,0:T(8,128)(2,1)S(1)} %get-tuple-element.203.refs_1_), channel_id=1, source_target_pairs={{0,4},{4,0},{8,12},{12,8},{16,20},{20,16},{24,28},{28,24},{1,5},{5... | collective-permute-start | bytes 1572872 | tf_op jit(solution)/shard_map/ppermute | solution.py:508
  (56 other events, 325.9 us)

commit v5 on v4

--- a/solution.py
+++ b/solution.py
@@ -9,6 +9,7 @@
 
 SLOT = 128
 NBR = 32
+PART = 32
 LANES = 128
 EPSILON = 1e-05
 ANY = pl.BlockSpec(memory_space=pl.ANY)
@@ -150,26 +151,27 @@
     ref[k : k + 1, :] = value
 
 
-def half_kernel(turned, x_ref, y_ref, w_own, w_near, out_ref, token_ref):
-    mark(token_ref)
-    product = dot_t if turned else dot
-    out_ref[...] = product(x_ref[...], w_own[...]) + product(y_ref[...], w_near[...])
-
-
-def half(ids, big, own, near, weights, turned, name, tokens=()):
-    nodes, depth = own.shape
+def half(ids, big, sources, weights, turned, name, tokens=(), early=None):
+    nodes, depth = sources[0].shape
     columns = weights[0][0].shape[1]
     rows = big * SLOT
+    n = len(sources)
+    before = [] if early is None else [early]
+    product = dot_t if turned else dot
+
+    def kernel(ids_ref, *refs):
+        out_ref, token_ref = refs[-2:]
+        mark(token_ref)
+        terms = [product(x_ref[...], w_ref[...]) for x_ref, w_ref in zip(refs[:n], refs[n : 2 * n])]
+        terms += [e_ref[...] for e_ref in refs[2 * n : -2]]
+        out_ref[...] = sum(terms[1:], terms[0])
+
     flat = pl.BlockSpec((rows, depth), lambda i, ids: (i, 0))
-
-    def kernel(ids_ref, *refs):
-        half_kernel(turned, *refs)
-
+    wide_flat = pl.BlockSpec((rows, columns), lambda i, ids: (i, 0))
     return launch(
-        kernel, (nodes // rows,), [flat, flat, *[spec for _, spec in weights]],
-        [pl.BlockSpec((rows, columns), lambda i, ids: (i, 0)), token_spec()],
-        [jax.ShapeDtypeStruct((nodes, columns), F32), TOKEN],
-        [own, near, *[w for w, _ in weights]], name, prefetch=[ids], tokens=tokens,
+        kernel, (nodes // rows,), [flat] * n + [spec for _, spec in weights] + [wide_flat for _ in before],
+        [wide_flat, token_spec()], [jax.ShapeDtypeStruct((nodes, columns), F32), TOKEN],
+        [*sources, *[w for w, _ in weights], *before], name, prefetch=[ids], tokens=tokens,
     )
 
 
@@ -182,47 +184,37 @@
     return piece, pl.BlockSpec(piece.shape, lambda i, ids: (0, 0))
 
 
-def each_part(big, body, part=32, inner=4):
-    def slot(s, carry):
+def each_part(big, body, part=32):
+    for s in range(big):
         for r in range(SLOT // part):
-            start = pl.multiple_of(s * SLOT + r * part, part)
-            body(s, slice(r * part, (r + 1) * part), pl.ds(start, part))
-        return carry
-
-    lax.fori_loop(0, big, slot, 0)
-
-
-def forward_kernel(big, ids_ref, early_ref, x_ref, y_ref, w_far, w_beyond, h_ref, inv_ref, val_ref, lin_ref, st_ref, tot_ref, acc_ref, ref_ref):
+            body(s, slice(r * part, (r + 1) * part), slice(s * SLOT + r * part, s * SLOT + (r + 1) * part))
+
+
+def forward_kernel(big, ids_ref, early_ref, y_ref, w_beyond, h_ref, inv_ref, val_ref, lin_ref, st_ref, tot_ref, acc_ref, ref_ref):
     i = pl.program_id(0)
     columns = lin_ref.shape[1]
-    tot_ref[...] = early_ref[...] + dot(x_ref[...], w_far[...]) + dot(y_ref[...], w_beyond[...])
-
-    def mix(s, carry):
-        rows = pl.ds(pl.multiple_of(s * SLOT, SLOT), SLOT)
-        high, low = split(tot_ref[rows, :])
-        both = jnp.concatenate([high, low], axis=0)
-        lin_ref[rows, :] = dot(h_ref[s], both) * wide(inv_ref[s], columns)
-        return carry
-
-    lax.fori_loop(0, big, mix, 0)
+    tot_ref[...] = early_ref[...] + dot(y_ref[...], w_beyond[...])
+
+    def mixed(s):
+        high, low = split(tot_ref[s * SLOT : (s + 1) * SLOT, :])
+        return dot(h_ref[s], jnp.concatenate([high, low], axis=0)) * wide(inv_ref[s], columns)
 
     @pl.when(i == 0)
     def _():
         acc_ref[...] = jnp.zeros_like(acc_ref)
         v = val_ref[0]
         count = jnp.sum(v, axis=0, keepdims=True)
-        put(ref_ref, 0, jnp.sum(lin_ref[:SLOT, :] * wide(v, columns), axis=0, keepdims=True) / wide(count, columns))
+        put(ref_ref, 0, jnp.sum(mixed(0) * wide(v, columns), axis=0, keepdims=True) / wide(count, columns))
 
     mref = at(ref_ref, 0)
-
-    def part(s, inner, rows):
-        v = val_ref[s, inner, :]
-        away = (lin_ref[rows, :] - mref) * wide(v, columns)
-        acc_ref[0] += fold(away)
-        acc_ref[1] += fold(away * away)
-        acc_ref[2, :, :LANES] += fold(v)
-
-    each_part(big, part)
+    for s in range(big):
+        lin_ref[s * SLOT : (s + 1) * SLOT, :] = mixed(s)
+        for r in range(SLOT // 32):
+            v = val_ref[s, r * 32 : (r + 1) * 32, :]
+            away = (lin_ref[s * SLOT + r * 32 : s * SLOT + (r + 1) * 32, :] - mref) * wide(v, columns)
+            acc_ref[0] += fold(away)
+            acc_ref[1] += fold(away * away)
+            acc_ref[2, :, :LANES] += fold(v)
 
     @pl.when(i == pl.num_programs(0) - 1)
     def _():
@@ -231,20 +223,20 @@
         spread_rows(st_ref, (at(ref_ref, 0), first, second, count))
 
 
-def forward(ids, big, early, far, beyond, weight, tiles, name, tokens=()):
+def forward(ids, big, early, beyond, weight, tiles, name, tokens=()):
     h, _, inv, val = tiles
     nodes, columns = early.shape
     rows = big * SLOT
     flat = pl.BlockSpec((rows, columns), lambda i, ids: (i, 0))
     tile = pl.BlockSpec((big, SLOT, SLOT), lambda i, ids: (i, 0, 0))
     double = pl.BlockSpec((big, SLOT, 2 * SLOT), lambda i, ids: (i, 0, 0))
-    blocks = [weight_block(weight, 2), weight_block(weight, 3)]
+    _, block = weight_block(weight, 3)
     return launch(
         functools.partial(forward_kernel, big), (nodes // rows,),
-        [flat, flat, flat, *[spec for _, spec in blocks], double, tile, tile],
+        [flat, flat, block, double, tile, tile],
         [flat, pl.BlockSpec(copies_shape(columns), lambda i, ids: (0, 0, 0))],
         [jax.ShapeDtypeStruct((nodes, columns), F32), jax.ShapeDtypeStruct(copies_shape(columns), F32)],
-        [early, far, beyond, weight, weight, h, inv, val], name, prefetch=[ids],
+        [early, beyond, weight, h, inv, val], name, prefetch=[ids],
         scratch=[pltpu.VMEM((rows, columns), F32), pltpu.VMEM((3, 8, columns), F32), pltpu.VMEM((8, columns), F32)],
         tokens=tokens,
     )
@@ -322,25 +314,20 @@
 
     columns = lin_ref.shape[1]
 
-    def part(s, inner, rows):
-        away = lin_ref[rows, :] - at(co_ref, 0)
-        if from_cot:
-            grad = grad_ref[rows, :].astype(F32) * double_slope(away, co_ref)
-        else:
-            grad = grad_ref[rows, :]
-        weight = wide(inv_ref[s, inner, :], columns)
-        high, low = split(weight * (grad - (at(co_ref, 5) + away * at(co_ref, 6))))
-        lg_ref[s, inner, :] = high
-        lg_ref[s, slice(inner.start + SLOT, inner.stop + SLOT), :] = low
-
-    each_part(big, part)
-
-    def mix(s, carry):
-        rows = pl.ds(pl.multiple_of(s * SLOT, SLOT), SLOT)
-        out_ref[rows, :] = (dot(ht_ref[s], lg_ref[s]) * at(co_ref, 1)).astype(BF)
-        return carry
-
-    lax.fori_loop(0, big, mix, 0)
+    for s in range(big):
+        for r in range(SLOT // PART):
+            inner = slice(r * PART, (r + 1) * PART)
+            rows = slice(s * SLOT + r * PART, s * SLOT + (r + 1) * PART)
+            away = lin_ref[rows, :] - at(co_ref, 0)
+            if from_cot:
+                grad = grad_ref[rows, :].astype(F32) * double_slope(away, co_ref)
+            else:
+                grad = grad_ref[rows, :]
+            weight = wide(inv_ref[s, inner, :], columns)
+            high, low = split(weight * (grad - (at(co_ref, 5) + away * at(co_ref, 6))))
+            lg_ref[s, inner, :] = high
+            lg_ref[s, SLOT + r * PART : SLOT + (r + 1) * PART, :] = low
+        out_ref[s * SLOT : (s + 1) * SLOT, :] = (dot(ht_ref[s], lg_ref[s]) * at(co_ref, 1)).astype(BF)
 
 
 def rows_call(kernel, big, arrays, tiles, smalls, out_dtype, scratch, name, tokens=(), limit=24):
@@ -370,8 +357,8 @@
     )
 
 
-def backward_kernel(big, last, early_ref, x_ref, y_ref, w_far, w_beyond, *refs):
-    total = early_ref[...] + dot_t(x_ref[...], w_far[...]) + dot_t(y_ref[...], w_beyond[...])
+def backward_kernel(big, last, early_ref, y_ref, w_beyond, *refs):
+    total = early_ref[...] + dot_t(y_ref[...], w_beyond[...])
     if last:
         refs[-2][...] = total
         mark(refs[-1])
@@ -395,15 +382,14 @@
     finish_sums(st_ref, co_ref, acc_ref)
 
 
-def backward(big, early, far, beyond, pieces, lin, norm, name, tokens=()):
+def backward(big, early, beyond, piece, lin, norm, name, tokens=()):
     nodes, columns = early.shape
-    depth = far.shape[1]
     rows = big * SLOT
     last = norm is None
     flat = pl.BlockSpec((rows, columns), lambda i: (i, 0))
     fixed = lambda s: pl.BlockSpec(s.shape, lambda i, n=s.ndim: (0,) * n)
-    ins = [flat, flat, flat, *map(fixed, pieces)]
-    args = [early, far, beyond, *pieces]
+    ins = [flat, flat, fixed(piece)]
+    args = [early, beyond, piece]
     out_specs = [flat]
     out_shape = [jax.ShapeDtypeStruct((nodes, columns), F32)]
     scratch = []
@@ -638,20 +624,22 @@
     *tiles, tiles_token = build_tiles(neighbours, node_valid)
     val = tiles[3]
     slices_one, slices_two, slices_token = weight_slices(ids, weight_one, weight_two)
-    early, token = half(ids, big, features, near_one, [weight_block(weight_one, b) for b in (0, 1)], False, "half_one")
+    early, token = half(ids, big, [features, near_one], [weight_block(weight_one, b) for b in (0, 1)], False, "half_one")
     far_one, tokens = after(far_one, token, tiles_token, slices_token)
     beyond_one = across(far_one, "col", 1)
-    lin_one, stats = forward(ids, big, early, far_one, beyond_one, weight_one, tiles, "forward_one", tokens)
+    early, _ = half(ids, big, [far_one], [weight_block(weight_one, 2)], False, "far_half_one", tokens, early)
+    lin_one, stats = forward(ids, big, early, beyond_one, weight_one, tiles, "forward_one", tokens)
     norm_one = (small_gather(stats, "row"), g1, b1)
 
     hidden, _ = rows_call(result_kernel, big, [lin_one], [val], norm_one, BF, [], "hidden")
     far_two, near_two = across(hidden, "col", 2), across(hidden, "col", 1)
-    early, token = half(ids, big, hidden, near_two, [weight_block(weight_two, b) for b in (0, 1)], False, "half_two")
+    early, token = half(ids, big, [hidden, near_two], [weight_block(weight_two, b) for b in (0, 1)], False, "half_two")
     far_two, tokens = after(far_two, token)
     beyond_two = across(far_two, "col", 1)
     slices_two, (far_two,) = after(slices_two, far_two)
     rows_two, crossing = weight_rows(slices_two)
-    lin_two, stats = forward(ids, big, early, far_two, beyond_two, weight_two, tiles, "forward_two", tokens)
+    early, _ = half(ids, big, [far_two], [weight_block(weight_two, 2)], False, "far_half_two", tokens, early)
+    lin_two, stats = forward(ids, big, early, beyond_two, weight_two, tiles, "forward_two", tokens)
     norm_two = (small_gather(stats, "row"), g2, b2)
 
     sums = rows_call(
@@ -666,12 +654,13 @@
 
     sum_two = RowSum("row", ids, terms_two, "two")
     weights = [weight_block(weight_two, 0), whole_block(rows_two[0])]
-    early, token = half(ids, big, turned, near, weights, True, "half_back_two", (sum_two.kept,))
+    early, token = half(ids, big, [turned, near], weights, True, "half_back_two", (sum_two.kept,))
     far, tokens = after(far, *sum_two.next(*sum_two.next(token)))
     beyond = across(far, "col", 1)
     slices_one, (far,) = after(slices_one, far)
     rows_one, crossing = weight_rows(slices_one)
-    grad_one, sums = backward(big, early, far, beyond, rows_two[1:], lin_one, norm_one, "backward_two", tokens)
+    early, _ = half(ids, big, [far], [whole_block(rows_two[1])], True, "far_half_back_two", tokens, early)
+    grad_one, sums = backward(big, early, beyond, rows_two[2], lin_one, norm_one, "backward_two", tokens)
     tokens = (*crossing, *sum_two.next(*sum_two.next(sums)))
     grads_one = small_gather(sums, "row")
 
@@ -681,15 +670,17 @@
     def terms_one(other, tokens, h=turned):
         return weight_terms(ids, other, ((features, near_one), (far_one, beyond_one)), h, "terms_one", tokens)
 
-    sum_one = RowSum("row", ids, terms_one, "one")
+    sum_one = RowSum("row", ids, terms_one, "one", lambda: tuple(sum_two.got))
     weights = [weight_block(weight_one, 0), whole_block(rows_one[0])]
-    early, token = half(ids, big, turned, near, weights, True, "half_back_one", (sum_one.kept,))
-    output, token = rows_call(result_kernel, big, [lin_two], [val], norm_two, F32, [], "output", sum_one.next(token))
-    grad_weight_two, token = sum_two.placed(60, (token,))
-    sum_one.next(token)
-    far, tokens = after(far, *sum_one.next())
+    early, token = half(ids, big, [turned, near], weights, True, "half_back_one", sum_one.next())
+    output, token = rows_call(result_kernel, big, [lin_two], [val], norm_two, F32, [], "output", (token,))
+    started = sum_one.next(token)
+    far, tokens = after(far, *started)
     beyond = across(far, "col", 1)
-    grad_features, token = backward(big, early, far, beyond, rows_one[1:], None, None, "backward_one", tokens)
+    grad_weight_two, token = sum_two.placed(60, started)
+    tokens = (*tokens, *sum_one.next(token))
+    early, _ = half(ids, big, [far], [whole_block(rows_one[1])], True, "far_half_back_one", tokens, early)
+    grad_features, token = backward(big, early, beyond, rows_one[2], None, None, "backward_one", tokens)
     while sum_one.stage < sum_one.stages - 1:
         sum_one.next()
     sum_one.next(token)

time: 339 us -> 331 us (0.976)
  Pallas kernels: 118 us -> 113 us
    pallas_call x37 -> x41, Pallas kernels: 118 us -> 113 us  [launch(): pl.pallas_call(body, grid_spec=pltpu.PrefetchScalarGridSpec(num_scalar_pr...]
    unnamed x124 -> x128, local copies, waits for them, and re-layouts: 23.1 us -> 21.9 us
  transfers between devices with their start and end apart: 42 -> 42, of which waited for: 20 -> 19; matrix products, arithmetic and copies ran while one was open for 1% -> 1% of each run, Pallas kernels for 26% -> 28%
where the time goes in v5:
time: 331 us; the launch traced here: 329 us
  waiting for transfers between devices  129 us (39%)
  Pallas kernels  113 us (34%)
  starting transfers between devices  38.7 us (12%)
  local copies, waits for them, and re-layouts  23.9 us (7%)
  blocking collectives  23 us (7%)
    ppermute x40, waiting for transfers between devices, across(): return lax.ppermute(value, axis, [(i, i ^ distance) for i in range(size)])  122 us
    pallas_call x41, Pallas kernels, launch(): pl.pallas_call(body, grid_spec=pltpu.PrefetchScalarGridSpec(num_scalar_pr...  113 us
    ppermute x40, starting transfers between devices, across(): return lax.ppermute(value, axis, [(i, i ^ distance) for i in range(size)])  30.6 us
    all_to_all x2, blocking collectives, small_gather(): return lax.all_to_all(copies, axis, split_axis=0, concat_axis=0, tiled=True)  23 us
    unnamed x128, local copies, waits for them, and re-layouts  21.9 us
    all_to_all x2, starting transfers between devices, small_gather(): return lax.all_to_all(copies, axis, split_axis=0, concat_axis=0, tiled=True)  8.1 us
    all_to_all x2, waiting for transfers between devices, small_gather(): return lax.all_to_all(copies, axis, split_axis=0, concat_axis=0, tiled=True)  7.08 us
  transfers between devices with their start and end apart: 42, of which 19 were waited for; matrix products, arithmetic and copies ran while one was open for 1% of the time, Pallas kernels for 28%

profile of v5, /device:TPU:0, one launch (start us, length us, event | category | flops | bytes accessed | tf_op | source)
XLA Modules:
  0.0 329.5 jit_solution(6861738867348917643)
XLA Ops:
  1.2 2.6 collective-permute-start
  4.6 5.0 %tiles.1 = (bf16[14,128,256]{2,1,0:T(8,128)(2,1)S(1)}, bf16[14,128,256]{2,1,0:T(8,128)(2,1)S(1)}, f32[14,128,128]{2,1,0:T(8,128)S(1)}, f32[14,128,128]{2,1,0:T(8,128)S(1)}, f32[8,128]{1,0:T(8,128)S(1)}) custom-call(s32[14,32,128]{2,1,0:T(8,128)S(1)} %bitcast_bitcast_fusion.refs_0_, s32[14,1,128]{2,1,0:T(1,128)S(1)} %reshape.35.refs_1_), custom_call_target="tpu_custom_call" | custom-call | flops 1000000 | bytes 1000 | tf_op jit(solution)/shard_map/tiles/pallas_call | solution.py:44
  12.8 2.1 weight_slices.1
  16.7 4.0 %half_one.1 = (f32[1792,512]{1,0:T(8,128)S(1)}, f32[8,128]{1,0:T(8,128)S(1)}) custom-call(s32[7]{0:T(128)S(1)} %stack.31.refs_0_, bf16[1792,512]{1,0:T(8,128)(2,1)S(1)} %copy-done.13, bf16[1792,512]{1,0:T(8,128)(2,1)} %collective-permute-done.1.refs_2_, bf16[2048,512]{1,0:T(8,128)(2,1)S(1)} %copy-done.5, bf16[2048,512]{1,0:T(8,128)(2,1)S(1)} %copy-done.5), custom_call_target="tpu_custom_call" | custom-call | flops 1000000 | bytes 1000 | tf_op jit(solution)/shard_map/half_one/pallas_call | solution.py:44
  20.7 23.9 %collective-permute-done.refs_1_.refs_3_ = bf16[1792,512]{1,0:T(8,128)(2,1)S(1)} collective-permute-done((bf16[1792,512]{1,0:T(8,128)(2,1)}, bf16[1792,512]{1,0:T(8,128)(2,1)S(1)}, u32[]{:S(2)}, u32[]{:S(2)}) %collective-permute-start) | collective-permute-done | bytes 1835040 | tf_op jit(solution)/shard_map/ppermute | solution.py:494
  44.6 2.4 far_half_one.1
  48.4 3.5 %forward_one.1 = (f32[1792,512]{1,0:T(8,128)S(1)}, f32[8,8,512]{2,1,0:T(8,128)S(1)}) custom-call(s32[7]{0:T(128)S(1)} %stack.31.refs_0_, f32[1792,512]{1,0:T(8,128)S(1)} %get-tuple-element.124.refs_1_, bf16[1792,512]{1,0:T(8,128)(2,1)S(1)} %collective-permute-done.2.refs_2_.refs_4_, bf16[2048,512]{1,0:T(8,128)(2,1)S(1)} %copy-done.5, ...), custom_call_target="tpu_custom_call" | custom-call | flops 1000000 | bytes 1000 | tf_op jit(solution)/shard_map/forward_one/pallas_call | solution.py:44
  51.9 13.2 %all_to_all.20.refs_2_.refs_4_ = f32[8,8,512]{2,1,0:T(8,128)S(1)} all-to-all(f32[8,8,512]{2,1,0:T(8,128)S(1)} %get-tuple-element.129), channel_id=1, replica_groups=mesh['row'=8,'col'=4] {'row'}, dimensions={0} | all-to-all | bytes 262144 | tf_op jit(solution)/shard_map/all_to_all | solution.py:120
  67.9 2.2 collective-permute-done.4.refs_2_
  70.1 2.8 half_two.1
  72.9 35.8 %collective-permute-done.3.refs_1_.refs_3_ = bf16[1792,512]{1,0:T(8,128)(2,1)S(1)} collective-permute-done((bf16[1792,512]{1,0:T(8,128)(2,1)S(1)}, bf16[1792,512]{1,0:T(8,128)(2,1)S(1)}, u32[]{:S(2)}, u32[]{:S(2)}) %collective-permute-start.3) | collective-permute-done | bytes 1835040 | tf_op jit(solution)/shard_map/ppermute | solution.py:494
  110.7 2.4 far_half_two.1
  113.2 3.5 %forward_two.1 = (f32[1792,512]{1,0:T(8,128)S(1)}, f32[8,8,512]{2,1,0:T(8,128)S(1)}) custom-call(s32[7]{0:T(128)S(1)} %stack.31.refs_0_, f32[1792,512]{1,0:T(8,128)S(1)} %get-tuple-element.136.refs_1_, bf16[1792,512]{1,0:T(8,128)(2,1)S(1)} %collective-permute-done.5.refs_2_.refs_4_, bf16[2048,512]{1,0:T(8,128)(2,1)S(1)} %copy-done.3, ...), custom_call_target="tpu_custom_call" | custom-call | flops 1000000 | bytes 1000 | tf_op jit(solution)/shard_map/forward_two/pallas_call | solution.py:44
  116.7 9.8 %all_to_all.21.refs_3_.refs_4_.refs_2_ = f32[8,8,512]{2,1,0:T(8,128)S(1)} all-to-all(f32[8,8,512]{2,1,0:T(8,128)S(1)} %get-tuple-element.138), channel_id=1, replica_groups=mesh['row'=8,'col'=4] {'row'}, dimensions={0} | all-to-all | bytes 262144 | tf_op jit(solution)/shard_map/all_to_all | solution.py:120
  126.5 2.7 sums_two.1
  129.2 1.8 copy-done.7
  131.0 3.5 %all-to-all-start.2 = ((f32[8,8,512]{2,1,0:T(8,128)}), f32[8,8,512]{2,1,0:T(8,128)S(1)}, u32[]{:S(2)}, u32[]{:S(2)}) async-start(f32[8,8,512]{2,1,0:T(8,128)} %sums_two.1), calls=%async_computation.2 | async-start | bytes 262144 | tf_op jit(solution)/shard_map/all_to_all | solution.py:120
  134.6 7.1 %all-to-all-done.2.refs_5_ = f32[8,8,512]{2,1,0:T(8,128)S(1)} async-done(((f32[8,8,512]{2,1,0:T(8,128)}), f32[8,8,512]{2,1,0:T(8,128)S(1)}, u32[]{:S(2)}, u32[]{:S(2)}) %all-to-all-start.2) | async-done | bytes 131104 | tf_op jit(solution)/shard_map/all_to_all | solution.py:120
  142.4 6.4 %turn_two.1 = (bf16[1792,512]{1,0:T(8,128)(2,1)}, f32[8,128]{1,0:T(8,128)}) custom-call(f32[1792,512]{1,0:T(8,128)} %copy-done.7, bf16[1792,512]{1,0:T(8,128)(2,1)} %refs_1_.9, f32[14,128,128]{2,1,0:T(8,128)} %copy-done.20, bf16[14,128,256]{2,1,0:T(8,128)(2,1)} %copy-done.25, f32[8,8,512]{2,1,0:T(8,128)} %copy-done.26, f32[8,8,512]{2,1,0:T(8,128)} %copy-done.60, ...), custom_call_target="tpu_custom_call" | custom-call | flops 1000000 | bytes 1000 | tf_op jit(solution)/shard_map/turn_two/pallas_call | solution.py:44
  150.5 6.2 %terms_two.2 = (bf16[512,512]{1,0:T(8,128)(2,1)}, bf16[512,512]{1,0:T(8,128)(2,1)}, f32[8,128]{1,0:T(8,128)}) custom-call(s32[7]{0:T(128)} %copy-done.31, bf16[1792,512]{1,0:T(8,128)(2,1)} %copy-done.18, bf16[1792,512]{1,0:T(8,128)(2,1)} %copy-done.19, bf16[1792,512]{1,0:T(8,128)(2,1)} %copy-done.15, bf16[1792,512]{1,0:T(8,128)(2,1)} %copy-done.16, ...), custom_call_target="tpu_custom_call" | custom-call | flops 1000000 | bytes 1000 | tf_op jit(solution)/shard_map/terms_two/pallas_call | solution.py:44
  158.1 6.3 %terms_two.3 = (bf16[512,512]{1,0:T(8,128)(2,1)}, bf16[512,512]{1,0:T(8,128)(2,1)}, f32[8,128]{1,0:T(8,128)}) custom-call(s32[7]{0:T(128)} %copy-done.31, bf16[1792,512]{1,0:T(8,128)(2,1)} %copy-done.18, bf16[1792,512]{1,0:T(8,128)(2,1)} %copy-done.19, bf16[1792,512]{1,0:T(8,128)(2,1)} %copy-done.15, bf16[1792,512]{1,0:T(8,128)(2,1)} %copy-done.16, ...), custom_call_target="tpu_custom_call" | custom-call | flops 1000000 | bytes 1000 | tf_op jit(solution)/shard_map/terms_two/pallas_call | solution.py:44
  166.7 4.0 %half_back_two.1 = (f32[1792,512]{1,0:T(8,128)S(1)}, f32[8,128]{1,0:T(8,128)S(1)}) custom-call(s32[7]{0:T(128)S(1)} %copy-done.32, bf16[1792,512]{1,0:T(8,128)(2,1)S(1)} %copy-done.17, bf16[1792,512]{1,0:T(8,128)(2,1)} %collective-permute-done.10.refs_2_, bf16[2048,512]{1,0:T(8,128)(2,1)S(1)} %copy-done.3, ...), custom_call_target="tpu_custom_call" | custom-call | flops 1000000 | bytes 1000 | tf_op jit(solution)/shard_map/half_back_two/pallas_call | solution.py:44
  176.0 11.5 %collective-permute-done.14.refs_2_ = bf16[256,512]{1,0:T(8,128)(2,1)S(1)} collective-permute-done((bf16[256,512]{1,0:T(8,128)(2,1)S(1)}, bf16[256,512]{1,0:T(8,128)(2,1)S(1)}, u32[]{:S(2)}, u32[]{:S(2)}) %collective-permute-start.14) | collective-permute-done | bytes 262176 | tf_op jit(solution)/shard_map/ppermute | solution.py:494
  188.9 2.7 collective-permute-done.8.refs_1_
  194.2 2.1 collective-permute-done.16.refs_2_
  197.8 4.0 %far_half_back_two.1 = (f32[1792,512]{1,0:T(8,128)S(1)}, f32[8,128]{1,0:T(8,128)}) custom-call(s32[7]{0:T(128)S(1)} %copy-done.32, bf16[1792,512]{1,0:T(8,128)(2,1)} %collective-permute-done.8.refs_1_, bf16[512,512]{1,0:T(8,128)(2,1)} %collective-permute-done.6.refs_8_.refs_2_, f32[1792,512]{1,0:T(8,128)S(1)} %get-tuple-element.164.refs_3_, ...), custom_call_target="tpu_custom_call" | custom-call | flops 1000000 | bytes 1000 | tf_op jit(solution)/shard_map/far_half_back_two/pallas_call | solution.py:44
  201.8 3.8 %backward_two.1 = (f32[1792,512]{1,0:T(8,128)S(1)}, f32[8,8,512]{2,1,0:T(8,128)}) custom-call(f32[1792,512]{1,0:T(8,128)S(1)} %get-tuple-element.167.refs_0_, bf16[1792,512]{1,0:T(8,128)(2,1)S(1)} %collective-permute-done.15.refs_1_, bf16[512,512]{1,0:T(8,128)(2,1)S(1)} %collective-permute-done.16.refs_2_, f32[1792,512]{1,0:T(8,128)S(1)} %copy-done.10, ...), custom_call_target="tpu_custom_call" | custom-call | flops 1000000 | bytes 1000 | tf_op jit(solution)/shard_map/backward_two/pallas_call | solution.py:44
  210.0 4.5 %all-to-all-start.3 = ((f32[8,8,512]{2,1,0:T(8,128)}), f32[8,8,512]{2,1,0:T(8,128)S(1)}, u32[]{:S(2)}, u32[]{:S(2)}) async-start(f32[8,8,512]{2,1,0:T(8,128)} %get-tuple-element.169.refs_3_), calls=%async_computation.3 | async-start | bytes 262144 | tf_op jit(solution)/shard_map/all_to_all | solution.py:120
  214.5 8.2 %collective-permute-done.22.refs_2_ = bf16[256,512]{1,0:T(8,128)(2,1)S(1)} collective-permute-done((bf16[256,512]{1,0:T(8,128)(2,1)S(1)}, bf16[256,512]{1,0:T(8,128)(2,1)S(1)}, u32[]{:S(2)}, u32[]{:S(2)}) %collective-permute-start.22) | collective-permute-done | bytes 262176 | tf_op jit(solution)/shard_map/ppermute | solution.py:494
  227.1 5.6 %turn_one.1 = (bf16[1792,512]{1,0:T(8,128)(2,1)}, f32[8,128]{1,0:T(8,128)}) custom-call(f32[1792,512]{1,0:T(8,128)} %copy-done.9, f32[1792,512]{1,0:T(8,128)} %copy-done.24, f32[14,128,128]{2,1,0:T(8,128)} %copy-done.20, bf16[14,128,256]{2,1,0:T(8,128)(2,1)} %copy-done.25, f32[8,8,512]{2,1,0:T(8,128)} %copy-done.30, f32[8,8,512]{2,1,0:T(8,128)} %copy-done.62, ...), custom_call_target="tpu_custom_call" | custom-call | flops 1000000 | bytes 1000 | tf_op jit(solution)/shard_map/turn_one/pallas_call | solution.py:44
  234.7 6.2 %terms_one.2 = (bf16[512,512]{1,0:T(8,128)(2,1)}, bf16[512,512]{1,0:T(8,128)(2,1)}, f32[8,128]{1,0:T(8,128)}) custom-call(s32[7]{0:T(128)} %copy-done.31, bf16[1792,512]{1,0:T(8,128)(2,1)} %refs_1_.11, bf16[1792,512]{1,0:T(8,128)(2,1)} %collective-permute-done.1.refs_2_, bf16[1792,512]{1,0:T(8,128)(2,1)} %copy-done.11, bf16[1792,512]{1,0:T(8,128)(2,1)} %copy-done.14, ...), custom_call_target="tpu_custom_call" | custom-call | flops 1000000 | bytes 1000 | tf_op jit(solution)/shard_map/terms_one/pallas_call | solution.py:44
  240.9 2.1 collective-permute-start.28
  243.0 5.0 %collective-permute-done.26.refs_8_.refs_4_ = bf16[512,512]{1,0:T(8,128)(2,1)S(1)} collective-permute-done((bf16[512,512]{1,0:T(8,128)(2,1)S(1)}, bf16[512,512]{1,0:T(8,128)(2,1)S(1)}, u32[]{:S(2)}, u32[]{:S(2)}) %collective-permute-start.26) | collective-permute-done | bytes 524320 | tf_op jit(solution)/shard_map/ppermute | solution.py:494
  250.3 6.3 %terms_one.3 = (bf16[512,512]{1,0:T(8,128)(2,1)}, bf16[512,512]{1,0:T(8,128)(2,1)}, f32[8,128]{1,0:T(8,128)}) custom-call(s32[7]{0:T(128)} %copy-done.31, bf16[1792,512]{1,0:T(8,128)(2,1)} %refs_1_.11, bf16[1792,512]{1,0:T(8,128)(2,1)} %collective-permute-done.1.refs_2_, bf16[1792,512]{1,0:T(8,128)(2,1)} %copy-done.11, bf16[1792,512]{1,0:T(8,128)(2,1)} %copy-done.14, ...), custom_call_target="tpu_custom_call" | custom-call | flops 1000000 | bytes 1000 | tf_op jit(solution)/shard_map/terms_one/pallas_call | solution.py:44
  256.6 2.0 collective-permute-done.28.refs_2_
  265.6 4.3 %half_back_one.1 = (f32[1792,512]{1,0:T(8,128)S(1)}, f32[8,128]{1,0:T(8,128)S(1)}) custom-call(s32[7]{0:T(128)S(1)} %copy-done.33, bf16[1792,512]{1,0:T(8,128)(2,1)S(1)} %copy-done.12, bf16[1792,512]{1,0:T(8,128)(2,1)} %collective-permute-done.23.refs_2_, bf16[2048,512]{1,0:T(8,128)(2,1)S(1)} %copy-done.6, ...), custom_call_target="tpu_custom_call" | custom-call | flops 1000000 | bytes 1000 | tf_op jit(solution)/shard_map/half_back_one/pallas_call | solution.py:44
  270.0 2.6 output.1
  272.9 2.7 collective-permute-done.31.refs_2_
  279.9 4.7 %place_two.1 = (f32[2048,512]{1,0:T(8,128)}, f32[8,128]{1,0:T(8,128)}) custom-call(s32[7]{0:T(128)} %copy-done.31, bf16[512,512]{1,0:T(8,128)(2,1)} %copy-done.36, bf16[512,512]{1,0:T(8,128)(2,1)} %copy-done.59, bf16[512,512]{1,0:T(8,128)(2,1)} %copy-done.35, bf16[512,512]{1,0:T(8,128)(2,1)} %copy-done.58, f32[8,128]{1,0:T(8,128)} %copy-done.45, ...), custom_call_target="tpu_custom_call" | custom-call | flops 1000000 | bytes 1000 | tf_op jit(solution)/shard_map/place_two/pallas_call | solution.py:44
  284.6 1.8 collective-permute-done.33.refs_2_
  288.9 10.3 %collective-permute-done.32.refs_2_ = bf16[256,512]{1,0:T(8,128)(2,1)S(1)} collective-permute-done((bf16[256,512]{1,0:T(8,128)(2,1)S(1)}, bf16[256,512]{1,0:T(8,128)(2,1)S(1)}, u32[]{:S(2)}, u32[]{:S(2)}) %collective-permute-start.32) | collective-permute-done | bytes 262176 | tf_op jit(solution)/shard_map/ppermute | solution.py:494
  299.9 2.0 copy-done.23
  302.6 3.6 %far_half_back_one.1 = (f32[1792,512]{1,0:T(8,128)S(1)}, f32[8,128]{1,0:T(8,128)}) custom-call(s32[7]{0:T(128)S(1)} %copy-done.34, bf16[1792,512]{1,0:T(8,128)(2,1)} %collective-permute-done.29.refs_1_, bf16[512,512]{1,0:T(8,128)(2,1)S(1)} %copy-done.29, f32[1792,512]{1,0:T(8,128)S(1)} %copy-done.23, f32[8,128]{1,0:T(8,128)S(1)} %copy-done.46, ...), custom_call_target="tpu_custom_call" | custom-call | flops 1000000 | bytes 1000 | tf_op jit(solution)/shard_map/far_half_back_one/pallas_call | solution.py:44
  306.3 2.6 backward_one.1
  310.1 2.0 collective-permute-start.39
  315.0 8.8 %collective-permute-done.39.refs_4_ = bf16[512,512]{1,0:T(8,128)(2,1)S(1)} collective-permute-done((bf16[512,512]{1,0:T(8,128)(2,1)S(1)}, bf16[512,512]{1,0:T(8,128)(2,1)S(1)}, u32[]{:S(2)}, u32[]{:S(2)}) %collective-permute-start.39) | collective-permute-done | bytes 524320 | tf_op jit(solution)/shard_map/ppermute | solution.py:494
  323.8 2.6 collective-permute-done.37.refs_2_
  326.4 3.1 place_one.1
  (214 shorter events, 61.5 us)
Async XLA Ops:
  0.6 14.3 %collective-permute-start.1 = (bf16[1792,512]{1,0:T(8,128)(2,1)}, bf16[1792,512]{1,0:T(8,128)(2,1)}, u32[]{:S(2)}, u32[]{:S(2)}) collective-permute-start(bf16[1792,512]{1,0:T(8,128)(2,1)} %refs_1_.11), channel_id=1, source_target_pairs={{0,1},{1,0},{2,3},{3,2},{4,5},{5,4},{6,7},{7,6},{8,9},{9,8},{10,11... | collective-permute-start | bytes 5505032 | tf_op jit(solution)/shard_map/ppermute | solution.py:494
  1.2 43.4 %collective-permute-start = (bf16[1792,512]{1,0:T(8,128)(2,1)}, bf16[1792,512]{1,0:T(8,128)(2,1)S(1)}, u32[]{:S(2)}, u32[]{:S(2)}) collective-permute-start(bf16[1792,512]{1,0:T(8,128)(2,1)} %refs_1_.11), channel_id=1, source_target_pairs={{0,2},{1,3},{2,0},{3,1},{4,6},{5,7},{6,4},{7,5},{8,10},{9,11},{10,... | collective-permute-start | bytes 5505032 | tf_op jit(solution)/shard_map/ppermute | solution.py:494
  4.6 108.5 %copy-start.31 = (s32[7]{0:T(128)}, s32[7]{0:T(128)S(1)}, u32[]{:S(2)}) copy-start(s32[7]{0:T(128)S(1)} %stack.31.refs_0_) | copy-start | bytes 88
  12.8 100.3 %copy-start.20 = (f32[14,128,128]{2,1,0:T(8,128)}, f32[14,128,128]{2,1,0:T(8,128)S(1)}, u32[]{:S(2)}) copy-start(f32[14,128,128]{2,1,0:T(8,128)S(1)} %get-tuple-element.126.refs_5_.refs_2_) | copy-start | bytes 2752516
  14.9 29.7 %copy-start.57 = (bf16[512,512]{1,0:T(8,128)(2,1)}, bf16[512,512]{1,0:T(8,128)(2,1)S(1)}, u32[]{:S(2)}) copy-start(bf16[512,512]{1,0:T(8,128)(2,1)S(1)} %get-tuple-element.149) | copy-start | bytes 1572868
  44.6 3.8 %collective-permute-start.2 = (bf16[1792,512]{1,0:T(8,128)(2,1)S(1)}, bf16[1792,512]{1,0:T(8,128)(2,1)S(1)}, u32[]{:S(2)}, u32[]{:S(2)}) collective-permute-start(bf16[1792,512]{1,0:T(8,128)(2,1)S(1)} %collective-permute-done.refs_1_.refs_3_), channel_id=1, source_target_pairs={{0,1},{1,0},{2,3},{3,2},{4,5},{5,4},{6,7},{7,6},{8,9},{9,8},{10,11... | collective-permute-start | bytes 5505032 | tf_op jit(solution)/shard_map/ppermute | solution.py:494
  65.1 136.7 %copy-start.30 = (f32[8,8,512]{2,1,0:T(8,128)}, f32[8,8,512]{2,1,0:T(8,128)S(1)}, u32[]{:S(2)}) copy-start(f32[8,8,512]{2,1,0:T(8,128)S(1)} %all_to_all.20.refs_2_.refs_4_) | copy-start | bytes 393220
  66.3 3.8 %collective-permute-start.4 = (bf16[1792,512]{1,0:T(8,128)(2,1)S(1)}, bf16[1792,512]{1,0:T(8,128)(2,1)S(1)}, u32[]{:S(2)}, u32[]{:S(2)}) collective-permute-start(bf16[1792,512]{1,0:T(8,128)(2,1)S(1)} %get-tuple-element.130.refs_1_), channel_id=1, source_target_pairs={{0,1},{1,0},{2,3},{3,2},{4,5},{5,4},{6,7},{7,6},{8,9},{9,8},{10,11... | collective-permute-start | bytes 5505032 | tf_op jit(solution)/shard_map/ppermute | solution.py:494
  66.3 42.4 %collective-permute-start.3 = (bf16[1792,512]{1,0:T(8,128)(2,1)S(1)}, bf16[1792,512]{1,0:T(8,128)(2,1)S(1)}, u32[]{:S(2)}, u32[]{:S(2)}) collective-permute-start(bf16[1792,512]{1,0:T(8,128)(2,1)S(1)} %get-tuple-element.130.refs_1_), channel_id=1, source_target_pairs={{0,2},{1,3},{2,0},{3,1},{4,6},{5,7},{6,4},{7,5},{8,10},{9,11},{10,... | collective-permute-start | bytes 5505032 | tf_op jit(solution)/shard_map/ppermute | solution.py:494
  108.7 4.4 %collective-permute-start.5 = (bf16[1792,512]{1,0:T(8,128)(2,1)S(1)}, bf16[1792,512]{1,0:T(8,128)(2,1)S(1)}, u32[]{:S(2)}, u32[]{:S(2)}) collective-permute-start(bf16[1792,512]{1,0:T(8,128)(2,1)S(1)} %collective-permute-done.3.refs_1_.refs_3_), channel_id=1, source_target_pairs={{0,1},{1,0},{2,3},{3,2},{4,5},{5,4},{6,7},{7,6},{8,9},{9,8},{10,11... | collective-permute-start | bytes 5505032 | tf_op jit(solution)/shard_map/ppermute | solution.py:494
  108.7 25.9 %collective-permute-start.6 = (bf16[512,512]{1,0:T(8,128)(2,1)}, bf16[512,512]{1,0:T(8,128)(2,1)}, u32[]{:S(2)}, u32[]{:S(2)}) collective-permute-start(bf16[512,512]{1,0:T(8,128)(2,1)} %get-tuple-element.143), channel_id=1, source_target_pairs={{0,2},{1,3},{2,0},{3,1},{4,6},{5,7},{6,4},{7,5},{8,10},{9,11},{10,... | collective-permute-start | bytes 1572872 | tf_op jit(solution)/shard_map/ppermute | solution.py:494
  110.2 24.4 %collective-permute-start.7 = (bf16[512,512]{1,0:T(8,128)(2,1)}, bf16[512,512]{1,0:T(8,128)(2,1)}, u32[]{:S(2)}, u32[]{:S(2)}) collective-permute-start(bf16[512,512]{1,0:T(8,128)(2,1)} %get-tuple-element.144), channel_id=1, source_target_pairs={{0,2},{1,3},{2,0},{3,1},{4,6},{5,7},{6,4},{7,5},{8,10},{9,11},{10,... | collective-permute-start | bytes 1572872 | tf_op jit(solution)/shard_map/ppermute | solution.py:494
  131.0 10.7 %all-to-all-start.2 = ((f32[8,8,512]{2,1,0:T(8,128)}), f32[8,8,512]{2,1,0:T(8,128)S(1)}, u32[]{:S(2)}, u32[]{:S(2)}) async-start(f32[8,8,512]{2,1,0:T(8,128)} %sums_two.1), calls=%async_computation.2 | async-start | bytes 262144 | tf_op jit(solution)/shard_map/all_to_all | solution.py:120
  148.8 15.7 %collective-permute-start.10 = (bf16[1792,512]{1,0:T(8,128)(2,1)}, bf16[1792,512]{1,0:T(8,128)(2,1)}, u32[]{:S(2)}, u32[]{:S(2)}) collective-permute-start(bf16[1792,512]{1,0:T(8,128)(2,1)} %get-tuple-element.145.refs_5_.refs_1_), channel_id=1, source_target_pairs={{0,1},{1,0},{2,3},{3,2},{4,5},{5,4},{6,7},{7,6},{8,9},{9,8},{10,11... | collective-permute-start | bytes 5505032 | tf_op jit(solution)/shard_map/ppermute | solution.py:494
  148.8 42.7 %collective-permute-start.8 = (bf16[1792,512]{1,0:T(8,128)(2,1)}, bf16[1792,512]{1,0:T(8,128)(2,1)}, u32[]{:S(2)}, u32[]{:S(2)}) collective-permute-start(bf16[1792,512]{1,0:T(8,128)(2,1)} %get-tuple-element.145.refs_5_.refs_1_), channel_id=1, source_target_pairs={{0,2},{1,3},{2,0},{3,1},{4,6},{5,7},{6,4},{7,5},{8,10},{9,11},{10,... | collective-permute-start | bytes 5505032 | tf_op jit(solution)/shard_map/ppermute | solution.py:494
  150.4 14.1 %collective-permute-start.11 = (bf16[512,512]{1,0:T(8,128)(2,1)}, bf16[512,512]{1,0:T(8,128)(2,1)S(1)}, u32[]{:S(2)}, u32[]{:S(2)}) collective-permute-start(bf16[512,512]{1,0:T(8,128)(2,1)} %copy-done.57), channel_id=1, source_target_pairs={{0,1},{1,0},{2,3},{3,2},{4,5},{5,4},{6,7},{7,6},{8,9},{9,8},{10,11... | collective-permute-start | bytes 1572872 | tf_op jit(solution)/shard_map/ppermute | solution.py:494
  156.7 14.6 %collective-permute-start.13 = (bf16[512,512]{1,0:T(8,128)(2,1)}, bf16[512,512]{1,0:T(8,128)(2,1)}, u32[]{:S(2)}, u32[]{:S(2)}) collective-permute-start(bf16[512,512]{1,0:T(8,128)(2,1)} %get-tuple-element.156), channel_id=1, source_target_pairs={{0,8},{4,12},{8,0},{12,4},{16,24},{20,28},{24,16},{28,20},{1,9},{5... | collective-permute-start | bytes 1572872 | tf_op jit(solution)/shard_map/ppermute | solution.py:494
  156.8 16.6 %collective-permute-start.9 = (bf16[512,512]{1,0:T(8,128)(2,1)}, bf16[512,512]{1,0:T(8,128)(2,1)}, u32[]{:S(2)}, u32[]{:S(2)}) collective-permute-start(bf16[512,512]{1,0:T(8,128)(2,1)} %get-tuple-element.148), channel_id=1, source_target_pairs={{0,4},{4,0},{8,12},{12,8},{16,20},{20,16},{24,28},{28,24},{1,5},{5... | collective-permute-start | bytes 1572872 | tf_op jit(solution)/shard_map/ppermute | solution.py:494
  173.0 14.4 %collective-permute-start.14 = (bf16[256,512]{1,0:T(8,128)(2,1)S(1)}, bf16[256,512]{1,0:T(8,128)(2,1)S(1)}, u32[]{:S(2)}, u32[]{:S(2)}) collective-permute-start(bf16[256,512]{1,0:T(8,128)(2,1)S(1)} %get-tuple-element.160), channel_id=1, source_target_pairs={{0,16},{4,20},{8,24},{12,28},{16,0},{20,4},{24,8},{28,12},{1,17},{... | collective-permute-start | bytes 786440 | tf_op jit(solution)/shard_map/ppermute | solution.py:494
  175.2 13.1 %collective-permute-start.12 = (bf16[256,512]{1,0:T(8,128)(2,1)S(1)}, bf16[256,512]{1,0:T(8,128)(2,1)S(1)}, u32[]{:S(2)}, u32[]{:S(2)}) collective-permute-start(bf16[256,512]{1,0:T(8,128)(2,1)S(1)} %get-tuple-element.153), channel_id=1, source_target_pairs={{0,8},{4,12},{8,0},{12,4},{16,24},{20,28},{24,16},{28,20},{1,9},{5... | collective-permute-start | bytes 786440 | tf_op jit(solution)/shard_map/ppermute | solution.py:494
  191.5 10.3 %collective-permute-start.15 = (bf16[1792,512]{1,0:T(8,128)(2,1)}, bf16[1792,512]{1,0:T(8,128)(2,1)S(1)}, u32[]{:S(2)}, u32[]{:S(2)}) collective-permute-start(bf16[1792,512]{1,0:T(8,128)(2,1)} %collective-permute-done.8.refs_1_), channel_id=1, source_target_pairs={{0,1},{1,0},{2,3},{3,2},{4,5},{5,4},{6,7},{7,6},{8,9},{9,8},{10,11... | collective-permute-start | bytes 5505032 | tf_op jit(solution)/shard_map/ppermute | solution.py:494
  191.5 4.7 %collective-permute-start.16 = (bf16[512,512]{1,0:T(8,128)(2,1)}, bf16[512,512]{1,0:T(8,128)(2,1)S(1)}, u32[]{:S(2)}, u32[]{:S(2)}) collective-permute-start(bf16[512,512]{1,0:T(8,128)(2,1)} %collective-permute-done.7.refs_9_), channel_id=1, source_target_pairs={{0,1},{1,0},{2,3},{3,2},{4,5},{5,4},{6,7},{7,6},{8,9},{9,8},{10,11... | collective-permute-start | bytes 1572872 | tf_op jit(solution)/shard_map/ppermute | solution.py:494
  192.0 15.4 %collective-permute-start.21 = (bf16[256,512]{1,0:T(8,128)(2,1)S(1)}, bf16[256,512]{1,0:T(8,128)(2,1)S(1)}, u32[]{:S(2)}, u32[]{:S(2)}) collective-permute-start(bf16[256,512]{1,0:T(8,128)(2,1)S(1)} %get-tuple-element.175.refs_1_), channel_id=1, source_target_pairs={{0,4},{4,0},{8,12},{12,8},{16,20},{20,16},{24,28},{28,24},{1,5},{5... | collective-permute-start | bytes 786440 | tf_op jit(solution)/shard_map/ppermute | solution.py:494
  192.3 16.3 %collective-permute-start.19 = (bf16[256,512]{1,0:T(8,128)(2,1)S(1)}, bf16[256,512]{1,0:T(8,128)(2,1)S(1)}, u32[]{:S(2)}, u32[]{:S(2)}) collective-permute-start(bf16[256,512]{1,0:T(8,128)(2,1)S(1)} %get-tuple-element.172.refs_1_), channel_id=1, source_target_pairs={{0,16},{4,20},{8,24},{12,28},{16,0},{20,4},{24,8},{28,12},{1,17},{... | collective-permute-start | bytes 786440 | tf_op jit(solution)/shard_map/ppermute | solution.py:494
  192.6 33.5 %collective-permute-start.17 = (bf16[512,512]{1,0:T(8,128)(2,1)}, bf16[512,512]{1,0:T(8,128)(2,1)S(1)}, u32[]{:S(2)}, u32[]{:S(2)}) collective-permute-start(bf16[512,512]{1,0:T(8,128)(2,1)} %get-tuple-element.170), channel_id=1, source_target_pairs={{0,2},{1,3},{2,0},{3,1},{4,6},{5,7},{6,4},{7,5},{8,10},{9,11},{10,... | collective-permute-start | bytes 1572872 | tf_op jit(solution)/shard_map/ppermute | solution.py:494
  196.3 29.9 %collective-permute-start.18 = (bf16[512,512]{1,0:T(8,128)(2,1)}, bf16[512,512]{1,0:T(8,128)(2,1)}, u32[]{:S(2)}, u32[]{:S(2)}) collective-permute-start(bf16[512,512]{1,0:T(8,128)(2,1)} %get-tuple-element.171), channel_id=1, source_target_pairs={{0,2},{1,3},{2,0},{3,1},{4,6},{5,7},{6,4},{7,5},{8,10},{9,11},{10,... | collective-permute-start | bytes 1572872 | tf_op jit(solution)/shard_map/ppermute | solution.py:494
  208.1 14.6 %collective-permute-start.22 = (bf16[256,512]{1,0:T(8,128)(2,1)S(1)}, bf16[256,512]{1,0:T(8,128)(2,1)S(1)}, u32[]{:S(2)}, u32[]{:S(2)}) collective-permute-start(bf16[256,512]{1,0:T(8,128)(2,1)S(1)} %get-tuple-element.178.refs_1_), channel_id=1, source_target_pairs={{0,16},{4,20},{8,24},{12,28},{16,0},{20,4},{24,8},{28,12},{1,17},{... | collective-permute-start | bytes 786440 | tf_op jit(solution)/shard_map/ppermute | solution.py:494
  209.2 14.7 %collective-permute-start.20 = (bf16[256,512]{1,0:T(8,128)(2,1)S(1)}, bf16[256,512]{1,0:T(8,128)(2,1)S(1)}, u32[]{:S(2)}, u32[]{:S(2)}) collective-permute-start(bf16[256,512]{1,0:T(8,128)(2,1)S(1)} %get-tuple-element.173.refs_1_), channel_id=1, source_target_pairs={{0,8},{4,12},{8,0},{12,4},{16,24},{20,28},{24,16},{28,20},{1,9},{5... | collective-permute-start | bytes 786440 | tf_op jit(solution)/shard_map/ppermute | solution.py:494
  210.0 16.3 %all-to-all-start.3 = ((f32[8,8,512]{2,1,0:T(8,128)}), f32[8,8,512]{2,1,0:T(8,128)S(1)}, u32[]{:S(2)}, u32[]{:S(2)}) async-start(f32[8,8,512]{2,1,0:T(8,128)} %get-tuple-element.169.refs_3_), calls=%async_computation.3 | async-start | bytes 262144 | tf_op jit(solution)/shard_map/all_to_all | solution.py:120
  232.7 32.8 %collective-permute-start.23 = (bf16[1792,512]{1,0:T(8,128)(2,1)}, bf16[1792,512]{1,0:T(8,128)(2,1)}, u32[]{:S(2)}, u32[]{:S(2)}) collective-permute-start(bf16[1792,512]{1,0:T(8,128)(2,1)} %get-tuple-element.180.refs_5_.refs_1_), channel_id=1, source_target_pairs={{0,1},{1,0},{2,3},{3,2},{4,5},{5,4},{6,7},{7,6},{8,9},{9,8},{10,11... | collective-permute-start | bytes 5505032 | tf_op jit(solution)/shard_map/ppermute | solution.py:494
  232.7 44.8 %collective-permute-start.29 = (bf16[1792,512]{1,0:T(8,128)(2,1)}, bf16[1792,512]{1,0:T(8,128)(2,1)}, u32[]{:S(2)}, u32[]{:S(2)}) collective-permute-start(bf16[1792,512]{1,0:T(8,128)(2,1)} %get-tuple-element.180.refs_5_.refs_1_), channel_id=1, source_target_pairs={{0,2},{1,3},{2,0},{3,1},{4,6},{5,7},{6,4},{7,5},{8,10},{9,11},{10,... | collective-permute-start | bytes 5505032 | tf_op jit(solution)/shard_map/ppermute | solution.py:494
  233.3 14.8 %collective-permute-start.26 = (bf16[512,512]{1,0:T(8,128)(2,1)S(1)}, bf16[512,512]{1,0:T(8,128)(2,1)S(1)}, u32[]{:S(2)}, u32[]{:S(2)}) collective-permute-start(bf16[512,512]{1,0:T(8,128)(2,1)S(1)} %get-tuple-element.184.refs_3_), channel_id=1, source_target_pairs={{0,8},{4,12},{8,0},{12,4},{16,24},{20,28},{24,16},{28,20},{1,9},{5... | collective-permute-start | bytes 1572872 | tf_op jit(solution)/shard_map/ppermute | solution.py:494
  233.3 16.2 %collective-permute-start.25 = (bf16[512,512]{1,0:T(8,128)(2,1)S(1)}, bf16[512,512]{1,0:T(8,128)(2,1)S(1)}, u32[]{:S(2)}, u32[]{:S(2)}) collective-permute-start(bf16[512,512]{1,0:T(8,128)(2,1)S(1)} %get-tuple-element.183.refs_1_), channel_id=1, source_target_pairs={{0,4},{4,0},{8,12},{12,8},{16,20},{20,16},{24,28},{28,24},{1,5},{5... | collective-permute-start | bytes 1572872 | tf_op jit(solution)/shard_map/ppermute | solution.py:494
  240.9 17.7 %collective-permute-start.28 = (bf16[512,512]{1,0:T(8,128)(2,1)}, bf16[512,512]{1,0:T(8,128)(2,1)}, u32[]{:S(2)}, u32[]{:S(2)}) collective-permute-start(bf16[512,512]{1,0:T(8,128)(2,1)} %get-tuple-element.189), channel_id=1, source_target_pairs={{0,8},{4,12},{8,0},{12,4},{16,24},{20,28},{24,16},{28,20},{1,9},{5... | collective-permute-start | bytes 1572872 | tf_op jit(solution)/shard_map/ppermute | solution.py:494
  248.1 14.0 %collective-permute-start.27 = (bf16[512,512]{1,0:T(8,128)(2,1)}, bf16[512,512]{1,0:T(8,128)(2,1)S(1)}, u32[]{:S(2)}, u32[]{:S(2)}) collective-permute-start(bf16[512,512]{1,0:T(8,128)(2,1)} %get-tuple-element.186), channel_id=1, source_target_pairs={{0,4},{4,0},{8,12},{12,8},{16,20},{20,16},{24,28},{28,24},{1,5},{5... | collective-permute-start | bytes 1572872 | tf_op jit(solution)/shard_map/ppermute | solution.py:494
  249.5 16.1 %collective-permute-start.24 = (bf16[512,512]{1,0:T(8,128)(2,1)}, bf16[512,512]{1,0:T(8,128)(2,1)S(1)}, u32[]{:S(2)}, u32[]{:S(2)}) collective-permute-start(bf16[512,512]{1,0:T(8,128)(2,1)} %get-tuple-element.181), channel_id=1, source_target_pairs={{0,1},{1,0},{2,3},{3,2},{4,5},{5,4},{6,7},{7,6},{8,9},{9,8},{10,11... | collective-permute-start | bytes 1572872 | tf_op jit(solution)/shard_map/ppermute | solution.py:494
  261.4 14.2 %collective-permute-start.31 = (bf16[256,512]{1,0:T(8,128)(2,1)S(1)}, bf16[256,512]{1,0:T(8,128)(2,1)S(1)}, u32[]{:S(2)}, u32[]{:S(2)}) collective-permute-start(bf16[256,512]{1,0:T(8,128)(2,1)S(1)} %get-tuple-element.198), channel_id=1, source_target_pairs={{0,16},{4,20},{8,24},{12,28},{16,0},{20,4},{24,8},{28,12},{1,17},{... | collective-permute-start | bytes 786440 | tf_op jit(solution)/shard_map/ppermute | solution.py:494
  263.7 13.1 %collective-permute-start.30 = (bf16[256,512]{1,0:T(8,128)(2,1)S(1)}, bf16[256,512]{1,0:T(8,128)(2,1)S(1)}, u32[]{:S(2)}, u32[]{:S(2)}) collective-permute-start(bf16[256,512]{1,0:T(8,128)(2,1)S(1)} %get-tuple-element.194), channel_id=1, source_target_pairs={{0,8},{4,12},{8,0},{12,4},{16,24},{20,28},{24,16},{28,20},{1,9},{5... | collective-permute-start | bytes 786440 | tf_op jit(solution)/shard_map/ppermute | solution.py:494
  275.6 24.3 %copy-start.29 = (bf16[512,512]{1,0:T(8,128)(2,1)S(1)}, bf16[512,512]{1,0:T(8,128)(2,1)}, u32[]{:S(2)}) copy-start(bf16[512,512]{1,0:T(8,128)(2,1)} %copy-done.28) | copy-start | bytes 1572868
  277.5 28.7 %collective-permute-start.34 = (bf16[1792,512]{1,0:T(8,128)(2,1)}, bf16[1792,512]{1,0:T(8,128)(2,1)S(1)}, u32[]{:S(2)}, u32[]{:S(2)}) collective-permute-start(bf16[1792,512]{1,0:T(8,128)(2,1)} %collective-permute-done.29.refs_1_), channel_id=1, source_target_pairs={{0,1},{1,0},{2,3},{3,2},{4,5},{5,4},{6,7},{7,6},{8,9},{9,8},{10,11... | collective-permute-start | bytes 5505032 | tf_op jit(solution)/shard_map/ppermute | solution.py:494
  277.6 28.7 %collective-permute-start.35 = (bf16[512,512]{1,0:T(8,128)(2,1)}, bf16[512,512]{1,0:T(8,128)(2,1)S(1)}, u32[]{:S(2)}, u32[]{:S(2)}) collective-permute-start(bf16[512,512]{1,0:T(8,128)(2,1)} %collective-permute-done.18.refs_9_), channel_id=1, source_target_pairs={{0,1},{1,0},{2,3},{3,2},{4,5},{5,4},{6,7},{7,6},{8,9},{9,8},{10,11... | collective-permute-start | bytes 1572872 | tf_op jit(solution)/shard_map/ppermute | solution.py:494
  278.1 8.3 %collective-permute-start.33 = (bf16[256,512]{1,0:T(8,128)(2,1)S(1)}, bf16[256,512]{1,0:T(8,128)(2,1)S(1)}, u32[]{:S(2)}, u32[]{:S(2)}) collective-permute-start(bf16[256,512]{1,0:T(8,128)(2,1)S(1)} %get-tuple-element.207.refs_1_), channel_id=1, source_target_pairs={{0,4},{4,0},{8,12},{12,8},{16,20},{20,16},{24,28},{28,24},{1,5},{5... | collective-permute-start | bytes 786440 | tf_op jit(solution)/shard_map/ppermute | solution.py:494
  279.9 19.3 %collective-permute-start.32 = (bf16[256,512]{1,0:T(8,128)(2,1)S(1)}, bf16[256,512]{1,0:T(8,128)(2,1)S(1)}, u32[]{:S(2)}, u32[]{:S(2)}) collective-permute-start(bf16[256,512]{1,0:T(8,128)(2,1)S(1)} %get-tuple-element.204.refs_1_), channel_id=1, source_target_pairs={{0,16},{4,20},{8,24},{12,28},{16,0},{20,4},{24,8},{28,12},{1,17},{... | collective-permute-start | bytes 786440 | tf_op jit(solution)/shard_map/ppermute | solution.py:494
  287.7 21.2 %collective-permute-start.38 = (bf16[256,512]{1,0:T(8,128)(2,1)S(1)}, bf16[256,512]{1,0:T(8,128)(2,1)S(1)}, u32[]{:S(2)}, u32[]{:S(2)}) collective-permute-start(bf16[256,512]{1,0:T(8,128)(2,1)S(1)} %get-tuple-element.214.refs_1_), channel_id=1, source_target_pairs={{0,16},{4,20},{8,24},{12,28},{16,0},{20,4},{24,8},{28,12},{1,17},{... | collective-permute-start | bytes 786440 | tf_op jit(solution)/shard_map/ppermute | solution.py:494
  299.8 12.2 %collective-permute-start.36 = (bf16[256,512]{1,0:T(8,128)(2,1)S(1)}, bf16[256,512]{1,0:T(8,128)(2,1)S(1)}, u32[]{:S(2)}, u32[]{:S(2)}) collective-permute-start(bf16[256,512]{1,0:T(8,128)(2,1)S(1)} %get-tuple-element.211.refs_1_), channel_id=1, source_target_pairs={{0,8},{4,12},{8,0},{12,4},{16,24},{20,28},{24,16},{28,20},{1,9},{5... | collective-permute-start | bytes 786440 | tf_op jit(solution)/shard_map/ppermute | solution.py:494
  306.3 23.2 %copy-start.1 = (s32[1792,32]{0,1:T(8,128)S(1)}, s32[1792,32]{0,1:T(8,128)}, u32[]{:S(2)}) copy-start(s32[1792,32]{0,1:T(8,128)} %param.11) | copy-start | bytes 688132
  310.1 13.7 %collective-permute-start.39 = (bf16[512,512]{1,0:T(8,128)(2,1)S(1)}, bf16[512,512]{1,0:T(8,128)(2,1)S(1)}, u32[]{:S(2)}, u32[]{:S(2)}) collective-permute-start(bf16[512,512]{1,0:T(8,128)(2,1)S(1)} %get-tuple-element.215.refs_3_), channel_id=1, source_target_pairs={{0,8},{4,12},{8,0},{12,4},{16,24},{20,28},{24,16},{28,20},{1,9},{5... | collective-permute-start | bytes 1572872 | tf_op jit(solution)/shard_map/ppermute | solution.py:494
  313.2 13.2 %collective-permute-start.37 = (bf16[512,512]{1,0:T(8,128)(2,1)S(1)}, bf16[512,512]{1,0:T(8,128)(2,1)S(1)}, u32[]{:S(2)}, u32[]{:S(2)}) collective-permute-start(bf16[512,512]{1,0:T(8,128)(2,1)S(1)} %get-tuple-element.213.refs_1_), channel_id=1, source_target_pairs={{0,4},{4,0},{8,12},{12,8},{16,20},{20,16},{24,28},{28,24},{1,5},{5... | collective-permute-start | bytes 1572872 | tf_op jit(solution)/shard_map/ppermute | solution.py:494
  (58 other events, 308.3 us)

commit v6 on v5

--- a/solution.py
+++ b/solution.py
@@ -9,6 +9,7 @@
 
 SLOT = 128
 NBR = 32
+TAIL = 16
 PART = 32
 LANES = 128
 EPSILON = 1e-05
@@ -190,7 +191,101 @@
             body(s, slice(r * part, (r + 1) * part), slice(s * SLOT + r * part, s * SLOT + (r + 1) * part))
 
 
-def forward_kernel(big, ids_ref, early_ref, y_ref, w_beyond, h_ref, inv_ref, val_ref, lin_ref, st_ref, tot_ref, acc_ref, ref_ref):
+def split_three(value):
+    high, rest = split(value)
+    middle, low = split(value - high.astype(F32) - rest.astype(F32))
+    return high, rest, middle
+
+
+def coef_rows(ref, base):
+    rows = ref[base : base + TAIL, :].astype(F32)
+    return tuple(rows[k : k + 1] + rows[k + 1 : k + 2] + rows[k + 2 : k + 3] for k in (0, 3))
+
+
+def receive(big, lead, i, lead_ref, rest_ref, val_ref, to_ref):
+    columns = to_ref.shape[1]
+    scale, shift = coef_rows(rest_ref, rest_ref.shape[0] - TAIL)
+    for s in range(big):
+        rows = slice(s * SLOT, (s + 1) * SLOT)
+        if s < lead:
+
+            @pl.when(i == 0)
+            def _():
+                to_ref[rows, :] = lead_ref[rows, :]
+
+            @pl.when(i > 0)
+            def _():
+                to_ref[rows, :] = rest_ref[pl.ds(pl.multiple_of((i * big + s - lead) * SLOT, SLOT), SLOT), :]
+
+        else:
+            to_ref[rows, :] = rest_ref[pl.ds(pl.multiple_of((i * big + s - lead) * SLOT, SLOT), SLOT), :]
+
+    def part(s, inner, rows):
+        u = to_ref[rows, :].astype(F32) * scale + shift
+        to_ref[rows, :] = (wide(val_ref[s, inner, :], columns) * (u + u * jnp.tanh(u))).astype(BF)
+
+    each_part(big, part)
+
+
+def far_kernel(big, lead, ids_ref, lead_ref, rest_ref, val_ref, w_ref, early_ref, out_ref, to_ref):
+    receive(big, lead, pl.program_id(0), lead_ref, rest_ref, val_ref, to_ref)
+    out_ref[...] = early_ref[...] + dot(to_ref[...], w_ref[...])
+
+
+def far_half(ids, big, sent, weight, val, early, name, tokens=()):
+    nodes, columns = early.shape
+    block, spec = weight
+    depth = block.shape[1] if spec.block_shape is None else spec.block_shape[0]
+    rows = big * SLOT
+    flat = pl.BlockSpec((rows, columns), lambda i, ids: (i, 0))
+    to = pl.BlockSpec((rows, depth), lambda i, ids: (i, 0))
+    return launch(
+        functools.partial(far_kernel, big, sent[0].shape[0] // SLOT), (nodes // rows,),
+        [
+            *[pl.BlockSpec(x.shape, lambda i, ids: (0, 0)) for x in sent],
+            pl.BlockSpec((big, SLOT, SLOT), lambda i, ids: (i, 0, 0)), spec, flat,
+        ],
+        [flat, to], [jax.ShapeDtypeStruct((nodes, columns), F32), jax.ShapeDtypeStruct((nodes, depth), BF)],
+        [*sent, val, block, early], name, prefetch=[ids], tokens=tokens,
+    )
+
+
+def forward_kernel(big, lead, send, got, ids_ref, early_ref, *refs):
+    if got:
+        lead_ref, rest_ref, w_beyond, h_ref, inv_ref, val_ref, lin_ref, st_ref, y_ref, *refs = refs
+        receive(big, lead, pl.program_id(0), lead_ref, rest_ref, val_ref, y_ref)
+    else:
+        y_ref, w_beyond, h_ref, inv_ref, val_ref, lin_ref, st_ref, *refs = refs
+    token_ref, *refs = refs
+    mark(token_ref)
+    if send:
+        lead_ref, rest_ref, *refs = refs
+    tot_ref, acc_ref, ref_ref = refs
+    forward_body(
+        big, early_ref, y_ref, w_beyond, h_ref, inv_ref, val_ref, lin_ref, st_ref, tot_ref, acc_ref, ref_ref
+    )
+    if not send:
+        return
+    i = pl.program_id(0)
+    mref = at(ref_ref, 0)
+    for s in range(big):
+        value = (lin_ref[s * SLOT : (s + 1) * SLOT, :] - mref).astype(BF)
+        later = pl.ds(pl.multiple_of((i * big + s - lead) * SLOT, SLOT), SLOT)
+        if s < lead:
+
+            @pl.when(i == 0)
+            def _():
+                lead_ref[s * SLOT : (s + 1) * SLOT, :] = value
+
+            @pl.when(i > 0)
+            def _():
+                rest_ref[later, :] = value
+
+        else:
+            rest_ref[later, :] = value
+
+
+def forward_body(big, early_ref, y_ref, w_beyond, h_ref, inv_ref, val_ref, lin_ref, st_ref, tot_ref, acc_ref, ref_ref):
     i = pl.program_id(0)
     columns = lin_ref.shape[1]
     tot_ref[...] = early_ref[...] + dot(y_ref[...], w_beyond[...])
@@ -223,20 +318,33 @@
         spread_rows(st_ref, (at(ref_ref, 0), first, second, count))
 
 
-def forward(ids, big, early, beyond, weight, tiles, name, tokens=()):
+def forward(ids, big, lead, early, beyond, weight, tiles, name, tokens=(), send=False):
     h, _, inv, val = tiles
     nodes, columns = early.shape
+    depth = weight.shape[0] // 4
     rows = big * SLOT
+    got = len(beyond) == 2
     flat = pl.BlockSpec((rows, columns), lambda i, ids: (i, 0))
+    to = pl.BlockSpec((rows, depth), lambda i, ids: (i, 0))
+    whole = lambda shape: pl.BlockSpec(shape, lambda i, ids: (0, 0))
     tile = pl.BlockSpec((big, SLOT, SLOT), lambda i, ids: (i, 0, 0))
     double = pl.BlockSpec((big, SLOT, 2 * SLOT), lambda i, ids: (i, 0, 0))
     _, block = weight_block(weight, 3)
+    outs = [flat, pl.BlockSpec(copies_shape(columns), lambda i, ids: (0, 0, 0))]
+    shapes = [jax.ShapeDtypeStruct((nodes, columns), F32), jax.ShapeDtypeStruct(copies_shape(columns), F32)]
+    if got:
+        outs.append(to)
+        shapes.append(jax.ShapeDtypeStruct((nodes, depth), BF))
+    outs.append(token_spec())
+    shapes.append(TOKEN)
+    if send:
+        for r in (lead * SLOT, nodes - lead * SLOT + TAIL):
+            outs.append(whole((r, columns)))
+            shapes.append(jax.ShapeDtypeStruct((r, columns), BF))
     return launch(
-        functools.partial(forward_kernel, big), (nodes // rows,),
-        [flat, flat, block, double, tile, tile],
-        [flat, pl.BlockSpec(copies_shape(columns), lambda i, ids: (0, 0, 0))],
-        [jax.ShapeDtypeStruct((nodes, columns), F32), jax.ShapeDtypeStruct(copies_shape(columns), F32)],
-        [early, beyond, weight, h, inv, val], name, prefetch=[ids],
+        functools.partial(forward_kernel, big, lead, send, got), (nodes // rows,),
+        [flat, *([whole(x.shape) for x in beyond] if got else [to]), block, double, tile, tile],
+        outs, shapes, [early, *beyond, weight, h, inv, val], name, prefetch=[ids],
         scratch=[pltpu.VMEM((rows, columns), F32), pltpu.VMEM((3, 8, columns), F32), pltpu.VMEM((8, columns), F32)],
         tokens=tokens,
     )
@@ -260,6 +368,35 @@
     u = away * at(co_ref, 1) + at(co_ref, 2)
     t = jnp.tanh(u)
     return (1.0 + t) * (1.0 + u * (1.0 - t))
+
+
+def coefs_kernel(st_ref, g_ref, gamma_ref, beta_ref, rest_ref, out_ref, token_ref, co_ref):
+    mark(token_ref)
+    columns_of(g_ref, gamma_ref, beta_ref, co_ref)
+    scale = at(co_ref, 1)
+    shift = (st_ref[0, 0:1, :] - at(co_ref, 0)) * scale + at(co_ref, 2)
+    rows = [*split_three(scale), *split_three(shift)]
+    rows.append(jnp.zeros((TAIL - len(rows), scale.shape[1]), BF))
+    out_ref[...] = jnp.concatenate([r.astype(F32) for r in rows], axis=0).astype(BF)
+
+
+def with_coefs(rest, stats, norm, tokens):
+    nodes, columns = rest.shape
+    args = [stats, *norm, rest]
+    return pl.pallas_call(
+        lambda *refs: coefs_kernel(*refs[: len(args)], *refs[len(args) + len(tokens) :]),
+        grid=(1,),
+        in_specs=[pl.BlockSpec((1, 8, columns), lambda i: (0, 0, 0))]
+        + [pl.BlockSpec(v.shape, lambda i, n=v.ndim: (0,) * n) for v in norm]
+        + [pl.BlockSpec(memory_space=pl.ANY)] * (1 + len(tokens)),
+        out_specs=[pl.BlockSpec((TAIL, columns), lambda i: (nodes // TAIL - 1, 0)), token_spec()],
+        out_shape=[jax.ShapeDtypeStruct((nodes, columns), BF), TOKEN],
+        scratch_shapes=[pltpu.VMEM((8, columns), F32)],
+        input_output_aliases={len(args) - 1: 0},
+        compiler_params=params(24),
+        cost_estimate=SMALL,
+        name="coefs",
+    )(*args, *tokens)
 
 
 def result_kernel(big, lin_ref, val_ref, g_ref, gamma_ref, beta_ref, out_ref, token_ref, co_ref):
@@ -613,6 +750,7 @@
     nodes, columns = features.shape
     slots = nodes // SLOT
     big = slots // 2 if slots % 2 == 0 else slots
+    lead = max(1, min(big, 5 * slots // 14))
     q = lax.axis_index("col")
     place = lax.axis_index("row")
     bits = [(place >> b) & 1 for b in range(lax.axis_size("row").bit_length() - 1)]
@@ -628,22 +766,29 @@
     far_one, tokens = after(far_one, token, tiles_token, slices_token)
     beyond_one = across(far_one, "col", 1)
     early, _ = half(ids, big, [far_one], [weight_block(weight_one, 2)], False, "far_half_one", tokens, early)
-    lin_one, stats = forward(ids, big, early, beyond_one, weight_one, tiles, "forward_one", tokens)
+    lin_one, stats, _, sent, rest = forward(ids, big, lead, early, [beyond_one], weight_one, tiles, "forward_one", tokens, send=True)
+
+    far_lead = across(sent, "col", 2)
     norm_one = (small_gather(stats, "row"), g1, b1)
-
-    hidden, _ = rows_call(result_kernel, big, [lin_one], [val], norm_one, BF, [], "hidden")
-    far_two, near_two = across(hidden, "col", 2), across(hidden, "col", 1)
-    early, token = half(ids, big, [hidden, near_two], [weight_block(weight_two, b) for b in (0, 1)], False, "half_two")
-    far_two, tokens = after(far_two, token)
-    beyond_two = across(far_two, "col", 1)
-    slices_two, (far_two,) = after(slices_two, far_two)
+    rest, token = with_coefs(rest, stats, norm_one, (far_lead,))
+    far_rest = across(rest, "col", 2)
+    hidden, _ = rows_call(result_kernel, big, [lin_one], [val], norm_one, BF, [], "hidden", (token,))
+    near_two = across(hidden, "col", 1)
+    early, token = half(
+        ids, big, [hidden, near_two], [weight_block(weight_two, b) for b in (0, 1)], False, "half_two"
+    )
+    far_rest, tokens = after(far_rest, token)
+    beyond_two = [across(x, "col", 1) for x in (far_lead, far_rest)]
+    early, far_two = far_half(
+        ids, big, (far_lead, far_rest), weight_block(weight_two, 2), val, early, "far_half_two", tokens
+    )
+    lin_two, stats, beyond_two, token = forward(ids, big, lead, early, beyond_two, weight_two, tiles, "forward_two")
+    norm_two = (small_gather(stats, "row"), g2, b2)
+    slices_two, tokens = after(slices_two, token)
     rows_two, crossing = weight_rows(slices_two)
-    early, _ = half(ids, big, [far_two], [weight_block(weight_two, 2)], False, "far_half_two", tokens, early)
-    lin_two, stats = forward(ids, big, early, beyond_two, weight_two, tiles, "forward_two", tokens)
-    norm_two = (small_gather(stats, "row"), g2, b2)
 
     sums = rows_call(
-        sums_kernel, big, [lin_two, cotangent], [val], norm_two, None, [pltpu.VMEM((2, 8, columns), F32)], "sums_two"
+        sums_kernel, big, [lin_two, cotangent], [val], norm_two, None, [pltpu.VMEM((2, 8, columns), F32)], "sums_two", tokens
     )
     grads_two = small_gather(sums, "row")
     turned, _ = turn_call(True, big, lin_two, cotangent, tiles, norm_two, grads_two, "turn_two", crossing)

time: 331 us -> 321 us (0.970)
  waiting for transfers between devices: 129 us -> 107 us
  blocking collectives: 23 us -> 36.5 us
    ppermute x40 -> x42, waiting for transfers between devices: 122 us -> 106 us  [across(): return lax.ppermute(value, axis, [(i, i ^ distance) for i in range(size)])]
    all_to_all x2 -> x3, blocking collectives: 23 us -> 36.5 us  [small_gather(): return lax.all_to_all(copies, axis, split_axis=0, concat_axis=0, tiled=True)]
    all_to_all x2 -> x1, waiting for transfers between devices: 7.08 us -> 0.92 us  [small_gather(): return lax.all_to_all(copies, axis, split_axis=0, concat_axis=0, tiled=True)]
    all_to_all x2 -> x1, starting transfers between devices: 8.1 us -> 4.07 us  [small_gather(): return lax.all_to_all(copies, axis, split_axis=0, concat_axis=0, tiled=True)]
    ppermute x40 -> x42, starting transfers between devices: 30.6 us -> 34 us  [across(): return lax.ppermute(value, axis, [(i, i ^ distance) for i in range(size)])]
  transfers between devices with their start and end apart: 42 -> 43, of which waited for: 19 -> 23; matrix products, arithmetic and copies ran while one was open for 1% -> 1% of each run, Pallas kernels for 28% -> 28%
where the time goes in v6:
time: 321 us; the launch traced here: 320 us
  Pallas kernels  116 us (36%)
  waiting for transfers between devices  107 us (33%)
  starting transfers between devices  38.1 us (12%)
  blocking collectives  36.5 us (11%)
  local copies, waits for them, and re-layouts  21.8 us (7%)
    pallas_call x41, Pallas kernels, launch(): pl.pallas_call(body, grid_spec=pltpu.PrefetchScalarGridSpec(num_scalar_pr...  115 us
    ppermute x42, waiting for transfers between devices, across(): return lax.ppermute(value, axis, [(i, i ^ distance) for i in range(size)])  106 us
    all_to_all x3, blocking collectives, small_gather(): return lax.all_to_all(copies, axis, split_axis=0, concat_axis=0, tiled=True)  36.5 us
    ppermute x42, starting transfers between devices, across(): return lax.ppermute(value, axis, [(i, i ^ distance) for i in range(size)])  34 us
    unnamed x128, local copies, waits for them, and re-layouts  19.9 us
  transfers between devices with their start and end apart: 43, of which 23 were waited for; matrix products, arithmetic and copies ran while one was open for 1% of the time, Pallas kernels for 28%

profile of v6, /device:TPU:0, one launch (start us, length us, event | category | flops | bytes accessed | tf_op | source)
XLA Modules:
  0.0 320.2 jit_solution(4620265483962098711)
XLA Ops:
  1.2 2.6 collective-permute-start
  4.6 5.0 %tiles.1 = (bf16[14,128,256]{2,1,0:T(8,128)(2,1)S(1)}, bf16[14,128,256]{2,1,0:T(8,128)(2,1)S(1)}, f32[14,128,128]{2,1,0:T(8,128)S(1)}, f32[14,128,128]{2,1,0:T(8,128)S(1)}, f32[8,128]{1,0:T(8,128)S(1)}) custom-call(s32[14,32,128]{2,1,0:T(8,128)S(1)} %bitcast_bitcast_fusion.refs_0_, s32[14,1,128]{2,1,0:T(1,128)S(1)} %reshape.35.refs_1_), custom_call_target="tpu_custom_call" | custom-call | flops 1000000 | bytes 1000 | tf_op jit(solution)/shard_map/tiles/pallas_call | solution.py:45
  17.0 4.0 %half_one.1 = (f32[1792,512]{1,0:T(8,128)S(1)}, f32[8,128]{1,0:T(8,128)S(1)}) custom-call(s32[7]{0:T(128)S(1)} %stack.31.refs_0_, bf16[1792,512]{1,0:T(8,128)(2,1)S(1)} %copy-done.12, bf16[1792,512]{1,0:T(8,128)(2,1)} %collective-permute-done.1.refs_2_, bf16[2048,512]{1,0:T(8,128)(2,1)S(1)} %copy-done.5, bf16[2048,512]{1,0:T(8,128)(2,1)S(1)} %copy-done.5), custom_call_target="tpu_custom_call" | custom-call | flops 1000000 | bytes 1000 | tf_op jit(solution)/shard_map/half_one/pallas_call | solution.py:45
  20.9 23.7 %collective-permute-done.refs_1_.refs_3_ = bf16[1792,512]{1,0:T(8,128)(2,1)} collective-permute-done((bf16[1792,512]{1,0:T(8,128)(2,1)}, bf16[1792,512]{1,0:T(8,128)(2,1)}, u32[]{:S(2)}, u32[]{:S(2)}) %collective-permute-start) | collective-permute-done | bytes 1835040 | tf_op jit(solution)/shard_map/ppermute | solution.py:631
  44.7 3.5 %far_half_one.1 = (f32[1792,512]{1,0:T(8,128)S(1)}, f32[8,128]{1,0:T(8,128)}) custom-call(s32[7]{0:T(128)S(1)} %stack.31.refs_0_, bf16[1792,512]{1,0:T(8,128)(2,1)} %collective-permute-done.refs_1_.refs_3_, bf16[2048,512]{1,0:T(8,128)(2,1)S(1)} %copy-done.5, f32[1792,512]{1,0:T(8,128)S(1)} %get-tuple-element.124.refs_3_, ...), custom_call_target="tpu_custom_call" | custom-call | flops 1000000 | bytes 1000 | tf_op jit(solution)/shard_map/far_half_one/pallas_call | solution.py:45
  48.7 4.5 %forward_one.1 = (f32[1792,512]{1,0:T(8,128)S(1)}, f32[8,8,512]{2,1,0:T(8,128)S(1)}, f32[8,128]{1,0:T(8,128)}, bf16[640,512]{1,0:T(8,128)(2,1)S(1)}, bf16[1168,512]{1,0:T(8,128)(2,1)S(1)}) custom-call(s32[7]{0:T(128)S(1)} %stack.31.refs_0_, f32[1792,512]{1,0:T(8,128)S(1)} %get-tuple-element.128.refs_1_, ...), custom_call_target="tpu_custom_call" | custom-call | flops 1000000 | bytes 1000 | tf_op jit(solution)/shard_map/forward_one/pallas_call | solution.py:45
  53.1 1.8 collective-permute-start.3
  54.9 12.9 %all_to_all.20.refs_1_.refs_2_.refs_4_ = f32[8,8,512]{2,1,0:T(8,128)S(1)} all-to-all(f32[8,8,512]{2,1,0:T(8,128)S(1)} %get-tuple-element.133.refs_0_), channel_id=1, replica_groups=mesh['row'=8,'col'=4] {'row'}, dimensions={0} | all-to-all | bytes 262144 | tf_op jit(solution)/shard_map/all_to_all | solution.py:121
  67.8 2.1 collective-permute-done.3.refs_5_.refs_1_
  71.2 1.8 collective-permute-start.4
  73.0 2.0 collective-permute-done.5.refs_2_
  75.0 2.8 half_two.1
  77.8 22.1 %collective-permute-done.4.refs_2_ = bf16[1168,512]{1,0:T(8,128)(2,1)S(1)} collective-permute-done((bf16[1168,512]{1,0:T(8,128)(2,1)S(1)}, bf16[1168,512]{1,0:T(8,128)(2,1)S(1)}, u32[]{:S(2)}, u32[]{:S(2)}) %collective-permute-start.4) | collective-permute-done | bytes 1196064 | tf_op jit(solution)/shard_map/ppermute | solution.py:631
  100.4 2.1 far_half_two.1
  103.9 3.8 %forward_two.1 = (f32[1792,512]{1,0:T(8,128)S(1)}, f32[8,8,512]{2,1,0:T(8,128)S(1)}, bf16[1792,512]{1,0:T(8,128)(2,1)S(1)}, f32[8,128]{1,0:T(8,128)S(1)}) custom-call(s32[7]{0:T(128)S(1)} %stack.31.refs_0_, f32[1792,512]{1,0:T(8,128)S(1)} %get-tuple-element.143.refs_1_, bf16[640,512]{1,0:T(8,128)(2,1)S(1)} %collective-permute-done.6.refs_2_, ...), custom_call_target="tpu_custom_call" | custom-call | flops 1000000 | bytes 1000 | tf_op jit(solution)/shard_map/forward_two/pallas_call | solution.py:45
  107.8 1.8 collective-permute-start.8
  109.9 13.2 %all_to_all.21.refs_3_.refs_4_.refs_2_ = f32[8,8,512]{2,1,0:T(8,128)S(1)} all-to-all(f32[8,8,512]{2,1,0:T(8,128)S(1)} %get-tuple-element.145), channel_id=1, replica_groups=mesh['row'=8,'col'=4] {'row'}, dimensions={0} | all-to-all | bytes 262144 | tf_op jit(solution)/shard_map/all_to_all | solution.py:121
  123.0 2.1 sums_two.1
  125.1 10.4 %all_to_all.22.refs_5_ = f32[8,8,512]{2,1,0:T(8,128)} all-to-all(f32[8,8,512]{2,1,0:T(8,128)S(1)} %sums_two.1), channel_id=1, replica_groups=mesh['row'=8,'col'=4] {'row'}, dimensions={0} | all-to-all | bytes 262144 | tf_op jit(solution)/shard_map/all_to_all | solution.py:121
  136.5 6.4 %turn_two.1 = (bf16[1792,512]{1,0:T(8,128)(2,1)}, f32[8,128]{1,0:T(8,128)}) custom-call(f32[1792,512]{1,0:T(8,128)} %copy-done.7, bf16[1792,512]{1,0:T(8,128)(2,1)} %refs_1_.9, f32[14,128,128]{2,1,0:T(8,128)} %copy-done.17, bf16[14,128,256]{2,1,0:T(8,128)(2,1)} %copy-done.24, f32[8,8,512]{2,1,0:T(8,128)} %copy-done.26, f32[8,8,512]{2,1,0:T(8,128)} %all_to_all.22.refs_5_, ...), custom_call_target="tpu_custom_call" | custom-call | flops 1000000 | bytes 1000 | tf_op jit(solution)/shard_map/turn_two/pallas_call | solution.py:45
  144.7 6.2 %terms_two.2 = (bf16[512,512]{1,0:T(8,128)(2,1)}, bf16[512,512]{1,0:T(8,128)(2,1)}, f32[8,128]{1,0:T(8,128)}) custom-call(s32[7]{0:T(128)} %copy-done.32, bf16[1792,512]{1,0:T(8,128)(2,1)} %copy-done.15, bf16[1792,512]{1,0:T(8,128)(2,1)} %copy-done.16, bf16[1792,512]{1,0:T(8,128)(2,1)} %copy-done.18, bf16[1792,512]{1,0:T(8,128)(2,1)} %copy-done.19, ...), custom_call_target="tpu_custom_call" | custom-call | flops 1000000 | bytes 1000 | tf_op jit(solution)/shard_map/terms_two/pallas_call | solution.py:45
  152.3 6.3 %terms_two.3 = (bf16[512,512]{1,0:T(8,128)(2,1)}, bf16[512,512]{1,0:T(8,128)(2,1)}, f32[8,128]{1,0:T(8,128)}) custom-call(s32[7]{0:T(128)} %copy-done.32, bf16[1792,512]{1,0:T(8,128)(2,1)} %copy-done.15, bf16[1792,512]{1,0:T(8,128)(2,1)} %copy-done.16, bf16[1792,512]{1,0:T(8,128)(2,1)} %copy-done.18, bf16[1792,512]{1,0:T(8,128)(2,1)} %copy-done.19, ...), custom_call_target="tpu_custom_call" | custom-call | flops 1000000 | bytes 1000 | tf_op jit(solution)/shard_map/terms_two/pallas_call | solution.py:45
  160.8 4.0 %half_back_two.1 = (f32[1792,512]{1,0:T(8,128)S(1)}, f32[8,128]{1,0:T(8,128)S(1)}) custom-call(s32[7]{0:T(128)S(1)} %copy-done.33, bf16[1792,512]{1,0:T(8,128)(2,1)S(1)} %copy-done.14, bf16[1792,512]{1,0:T(8,128)(2,1)} %collective-permute-done.12.refs_2_, bf16[2048,512]{1,0:T(8,128)(2,1)S(1)} %copy-done.3, ...), custom_call_target="tpu_custom_call" | custom-call | flops 1000000 | bytes 1000 | tf_op jit(solution)/shard_map/half_back_two/pallas_call | solution.py:45
  170.7 10.9 %collective-permute-done.16.refs_2_ = bf16[256,512]{1,0:T(8,128)(2,1)S(1)} collective-permute-done((bf16[256,512]{1,0:T(8,128)(2,1)S(1)}, bf16[256,512]{1,0:T(8,128)(2,1)S(1)}, u32[]{:S(2)}, u32[]{:S(2)}) %collective-permute-start.16) | collective-permute-done | bytes 262176 | tf_op jit(solution)/shard_map/ppermute | solution.py:631
  183.9 1.8 collective-permute-done.10.refs_1_
  191.4 3.9 %far_half_back_two.1 = (f32[1792,512]{1,0:T(8,128)S(1)}, f32[8,128]{1,0:T(8,128)}) custom-call(s32[7]{0:T(128)S(1)} %copy-done.33, bf16[1792,512]{1,0:T(8,128)(2,1)} %collective-permute-done.10.refs_1_, bf16[512,512]{1,0:T(8,128)(2,1)S(1)} %copy-done.31, f32[1792,512]{1,0:T(8,128)S(1)} %get-tuple-element.178.refs_3_, ...), custom_call_target="tpu_custom_call" | custom-call | flops 1000000 | bytes 1000 | tf_op jit(solution)/shard_map/far_half_back_two/pallas_call | solution.py:45
  195.3 3.8 %backward_two.1 = (f32[1792,512]{1,0:T(8,128)S(1)}, f32[8,8,512]{2,1,0:T(8,128)}) custom-call(f32[1792,512]{1,0:T(8,128)S(1)} %get-tuple-element.181.refs_0_, bf16[1792,512]{1,0:T(8,128)(2,1)S(1)} %collective-permute-done.17.refs_1_, bf16[512,512]{1,0:T(8,128)(2,1)S(1)} %collective-permute-done.18.refs_2_, f32[1792,512]{1,0:T(8,128)S(1)} %copy-done.10, ...), custom_call_target="tpu_custom_call" | custom-call | flops 1000000 | bytes 1000 | tf_op jit(solution)/shard_map/backward_two/pallas_call | solution.py:45
  199.1 1.8 copy-done.23
  203.9 4.1 %all-to-all-start.3 = ((f32[8,8,512]{2,1,0:T(8,128)}), f32[8,8,512]{2,1,0:T(8,128)S(1)}, u32[]{:S(2)}, u32[]{:S(2)}) async-start(f32[8,8,512]{2,1,0:T(8,128)} %get-tuple-element.183.refs_3_), calls=%async_computation.3 | async-start | bytes 262144 | tf_op jit(solution)/shard_map/all_to_all | solution.py:121
  208.0 8.2 %collective-permute-done.24.refs_2_ = bf16[256,512]{1,0:T(8,128)(2,1)S(1)} collective-permute-done((bf16[256,512]{1,0:T(8,128)(2,1)S(1)}, bf16[256,512]{1,0:T(8,128)(2,1)S(1)}, u32[]{:S(2)}, u32[]{:S(2)}) %collective-permute-start.24) | collective-permute-done | bytes 262176 | tf_op jit(solution)/shard_map/ppermute | solution.py:631
  219.2 5.7 %turn_one.1 = (bf16[1792,512]{1,0:T(8,128)(2,1)}, f32[8,128]{1,0:T(8,128)}) custom-call(f32[1792,512]{1,0:T(8,128)} %copy-done.9, f32[1792,512]{1,0:T(8,128)} %copy-done.23, f32[14,128,128]{2,1,0:T(8,128)} %copy-done.17, bf16[14,128,256]{2,1,0:T(8,128)(2,1)} %copy-done.24, f32[8,8,512]{2,1,0:T(8,128)} %copy-done.25, f32[8,8,512]{2,1,0:T(8,128)} %copy-done.60, ...), custom_call_target="tpu_custom_call" | custom-call | flops 1000000 | bytes 1000 | tf_op jit(solution)/shard_map/turn_one/pallas_call | solution.py:45
  226.8 6.2 %terms_one.2 = (bf16[512,512]{1,0:T(8,128)(2,1)}, bf16[512,512]{1,0:T(8,128)(2,1)}, f32[8,128]{1,0:T(8,128)}) custom-call(s32[7]{0:T(128)} %copy-done.32, bf16[1792,512]{1,0:T(8,128)(2,1)} %refs_1_.11, bf16[1792,512]{1,0:T(8,128)(2,1)} %collective-permute-done.1.refs_2_, bf16[1792,512]{1,0:T(8,128)(2,1)} %collective-permute-done.refs_1_.refs_3_, ...), custom_call_target="tpu_custom_call" | custom-call | flops 1000000 | bytes 1000 | tf_op jit(solution)/shard_map/terms_one/pallas_call | solution.py:45
  233.0 2.0 collective-permute-start.30
  234.9 4.5 %collective-permute-done.27.refs_7_.refs_2_ = bf16[512,512]{1,0:T(8,128)(2,1)S(1)} collective-permute-done((bf16[512,512]{1,0:T(8,128)(2,1)S(1)}, bf16[512,512]{1,0:T(8,128)(2,1)S(1)}, u32[]{:S(2)}, u32[]{:S(2)}) %collective-permute-start.27) | collective-permute-done | bytes 524320 | tf_op jit(solution)/shard_map/ppermute | solution.py:631
  242.3 6.3 %terms_one.3 = (bf16[512,512]{1,0:T(8,128)(2,1)}, bf16[512,512]{1,0:T(8,128)(2,1)}, f32[8,128]{1,0:T(8,128)}) custom-call(s32[7]{0:T(128)} %copy-done.32, bf16[1792,512]{1,0:T(8,128)(2,1)} %refs_1_.11, bf16[1792,512]{1,0:T(8,128)(2,1)} %collective-permute-done.1.refs_2_, bf16[1792,512]{1,0:T(8,128)(2,1)} %collective-permute-done.refs_1_.refs_3_, ...), custom_call_target="tpu_custom_call" | custom-call | flops 1000000 | bytes 1000 | tf_op jit(solution)/shard_map/terms_one/pallas_call | solution.py:45
  248.6 3.1 collective-permute-done.30.refs_2_
  258.3 1.8 collective-permute-start.32
  260.1 4.3 %half_back_one.1 = (f32[1792,512]{1,0:T(8,128)S(1)}, f32[8,128]{1,0:T(8,128)S(1)}) custom-call(s32[7]{0:T(128)S(1)} %copy-done.34, bf16[1792,512]{1,0:T(8,128)(2,1)S(1)} %copy-done.11, bf16[1792,512]{1,0:T(8,128)(2,1)} %collective-permute-done.25.refs_2_, bf16[2048,512]{1,0:T(8,128)(2,1)S(1)} %copy-done.6, ...), custom_call_target="tpu_custom_call" | custom-call | flops 1000000 | bytes 1000 | tf_op jit(solution)/shard_map/half_back_one/pallas_call | solution.py:45
  264.5 2.6 output.1
  273.3 4.7 %place_two.1 = (f32[2048,512]{1,0:T(8,128)}, f32[8,128]{1,0:T(8,128)}) custom-call(s32[7]{0:T(128)} %copy-done.32, bf16[512,512]{1,0:T(8,128)(2,1)} %copy-done.37, bf16[512,512]{1,0:T(8,128)(2,1)} %copy-done.57, bf16[512,512]{1,0:T(8,128)(2,1)} %copy-done.36, bf16[512,512]{1,0:T(8,128)(2,1)} %copy-done.58, f32[8,128]{1,0:T(8,128)} %copy-done.44, ...), custom_call_target="tpu_custom_call" | custom-call | flops 1000000 | bytes 1000 | tf_op jit(solution)/shard_map/place_two/pallas_call | solution.py:45
  278.0 8.1 %collective-permute-done.34.refs_2_ = bf16[256,512]{1,0:T(8,128)(2,1)S(1)} collective-permute-done((bf16[256,512]{1,0:T(8,128)(2,1)S(1)}, bf16[256,512]{1,0:T(8,128)(2,1)S(1)}, u32[]{:S(2)}, u32[]{:S(2)}) %collective-permute-start.34) | collective-permute-done | bytes 262176 | tf_op jit(solution)/shard_map/ppermute | solution.py:631
  288.1 2.8 collective-permute-start.40
  290.9 2.0 copy-done.22
  293.6 3.6 %far_half_back_one.1 = (f32[1792,512]{1,0:T(8,128)S(1)}, f32[8,128]{1,0:T(8,128)}) custom-call(s32[7]{0:T(128)S(1)} %copy-done.35, bf16[1792,512]{1,0:T(8,128)(2,1)} %collective-permute-done.31.refs_1_, bf16[512,512]{1,0:T(8,128)(2,1)S(1)} %copy-done.29, f32[1792,512]{1,0:T(8,128)S(1)} %copy-done.22, f32[8,128]{1,0:T(8,128)S(1)} %copy-done.45, ...), custom_call_target="tpu_custom_call" | custom-call | flops 1000000 | bytes 1000 | tf_op jit(solution)/shard_map/far_half_back_one/pallas_call | solution.py:45
  297.3 2.6 backward_one.1
  305.3 9.1 %collective-permute-done.39.refs_2_ = bf16[512,512]{1,0:T(8,128)(2,1)S(1)} collective-permute-done((bf16[512,512]{1,0:T(8,128)(2,1)S(1)}, bf16[512,512]{1,0:T(8,128)(2,1)S(1)}, u32[]{:S(2)}, u32[]{:S(2)}) %collective-permute-start.39) | collective-permute-done | bytes 524320 | tf_op jit(solution)/shard_map/ppermute | solution.py:631
  314.4 2.7 collective-permute-done.41.refs_4_
  317.1 3.1 place_one.1
  (218 shorter events, 64.0 us)
Async XLA Ops:
  0.6 14.9 %collective-permute-start.1 = (bf16[1792,512]{1,0:T(8,128)(2,1)}, bf16[1792,512]{1,0:T(8,128)(2,1)}, u32[]{:S(2)}, u32[]{:S(2)}) collective-permute-start(bf16[1792,512]{1,0:T(8,128)(2,1)} %refs_1_.11), channel_id=1, source_target_pairs={{0,1},{1,0},{2,3},{3,2},{4,5},{5,4},{6,7},{7,6},{8,9},{9,8},{10,11... | collective-permute-start | bytes 5505032 | tf_op jit(solution)/shard_map/ppermute | solution.py:631
  1.2 43.5 %collective-permute-start = (bf16[1792,512]{1,0:T(8,128)(2,1)}, bf16[1792,512]{1,0:T(8,128)(2,1)}, u32[]{:S(2)}, u32[]{:S(2)}) collective-permute-start(bf16[1792,512]{1,0:T(8,128)(2,1)} %refs_1_.11), channel_id=1, source_target_pairs={{0,2},{1,3},{2,0},{3,1},{4,6},{5,7},{6,4},{7,5},{8,10},{9,11},{10,... | collective-permute-start | bytes 5505032 | tf_op jit(solution)/shard_map/ppermute | solution.py:631
  4.6 99.3 %copy-start.32 = (s32[7]{0:T(128)}, s32[7]{0:T(128)S(1)}, u32[]{:S(2)}) copy-start(s32[7]{0:T(128)S(1)} %stack.31.refs_0_) | copy-start | bytes 88
  13.7 90.1 %copy-start.17 = (f32[14,128,128]{2,1,0:T(8,128)}, f32[14,128,128]{2,1,0:T(8,128)S(1)}, u32[]{:S(2)}) copy-start(f32[14,128,128]{2,1,0:T(8,128)S(1)} %get-tuple-element.130.refs_5_.refs_6_.refs_2_) | copy-start | bytes 2752516
  15.5 29.2 %copy-start.56 = (bf16[512,512]{1,0:T(8,128)(2,1)}, bf16[512,512]{1,0:T(8,128)(2,1)S(1)}, u32[]{:S(2)}) copy-start(bf16[512,512]{1,0:T(8,128)(2,1)S(1)} %get-tuple-element.163) | copy-start | bytes 1572868
  44.7 4.0 %collective-permute-start.2 = (bf16[1792,512]{1,0:T(8,128)(2,1)}, bf16[1792,512]{1,0:T(8,128)(2,1)S(1)}, u32[]{:S(2)}, u32[]{:S(2)}) collective-permute-start(bf16[1792,512]{1,0:T(8,128)(2,1)} %collective-permute-done.refs_1_.refs_3_), channel_id=1, source_target_pairs={{0,1},{1,0},{2,3},{3,2},{4,5},{5,4},{6,7},{7,6},{8,9},{9,8},{10,11... | collective-permute-start | bytes 5505032 | tf_op jit(solution)/shard_map/ppermute | solution.py:631
  53.1 16.8 %collective-permute-start.3 = (bf16[640,512]{1,0:T(8,128)(2,1)S(1)}, bf16[640,512]{1,0:T(8,128)(2,1)S(1)}, u32[]{:S(2)}, u32[]{:S(2)}) collective-permute-start(bf16[640,512]{1,0:T(8,128)(2,1)S(1)} %get-tuple-element.132), channel_id=1, source_target_pairs={{0,2},{1,3},{2,0},{3,1},{4,6},{5,7},{6,4},{7,5},{8,10},{9,11},{10,... | collective-permute-start | bytes 1966088 | tf_op jit(solution)/shard_map/ppermute | solution.py:631
  67.8 127.4 %copy-start.25 = (f32[8,8,512]{2,1,0:T(8,128)}, f32[8,8,512]{2,1,0:T(8,128)S(1)}, u32[]{:S(2)}) copy-start(f32[8,8,512]{2,1,0:T(8,128)S(1)} %all_to_all.20.refs_1_.refs_2_.refs_4_) | copy-start | bytes 393220
  71.2 3.8 %collective-permute-start.5 = (bf16[1792,512]{1,0:T(8,128)(2,1)S(1)}, bf16[1792,512]{1,0:T(8,128)(2,1)S(1)}, u32[]{:S(2)}, u32[]{:S(2)}) collective-permute-start(bf16[1792,512]{1,0:T(8,128)(2,1)S(1)} %get-tuple-element.138.refs_1_), channel_id=1, source_target_pairs={{0,1},{1,0},{2,3},{3,2},{4,5},{5,4},{6,7},{7,6},{8,9},{9,8},{10,11... | collective-permute-start | bytes 5505032 | tf_op jit(solution)/shard_map/ppermute | solution.py:631
  71.2 28.7 %collective-permute-start.4 = (bf16[1168,512]{1,0:T(8,128)(2,1)S(1)}, bf16[1168,512]{1,0:T(8,128)(2,1)S(1)}, u32[]{:S(2)}, u32[]{:S(2)}) collective-permute-start(bf16[1168,512]{1,0:T(8,128)(2,1)S(1)} %get-tuple-element.135), channel_id=1, source_target_pairs={{0,2},{1,3},{2,0},{3,1},{4,6},{5,7},{6,4},{7,5},{8,10},{9,11},{10,... | collective-permute-start | bytes 3588104 | tf_op jit(solution)/shard_map/ppermute | solution.py:631
  99.9 3.9 %collective-permute-start.7 = (bf16[1168,512]{1,0:T(8,128)(2,1)S(1)}, bf16[1168,512]{1,0:T(8,128)(2,1)S(1)}, u32[]{:S(2)}, u32[]{:S(2)}) collective-permute-start(bf16[1168,512]{1,0:T(8,128)(2,1)S(1)} %collective-permute-done.4.refs_2_), channel_id=1, source_target_pairs={{0,1},{1,0},{2,3},{3,2},{4,5},{5,4},{6,7},{7,6},{8,9},{9,8},{10,11... | collective-permute-start | bytes 3588104 | tf_op jit(solution)/shard_map/ppermute | solution.py:631
  99.9 3.9 %collective-permute-start.6 = (bf16[640,512]{1,0:T(8,128)(2,1)S(1)}, bf16[640,512]{1,0:T(8,128)(2,1)S(1)}, u32[]{:S(2)}, u32[]{:S(2)}) collective-permute-start(bf16[640,512]{1,0:T(8,128)(2,1)S(1)} %collective-permute-done.3.refs_5_.refs_1_), channel_id=1, source_target_pairs={{0,1},{1,0},{2,3},{3,2},{4,5},{5,4},{6,7},{7,6},{8,9},{9,8},{10,11... | collective-permute-start | bytes 1966088 | tf_op jit(solution)/shard_map/ppermute | solution.py:631
  107.8 27.8 %collective-permute-start.8 = (bf16[512,512]{1,0:T(8,128)(2,1)S(1)}, bf16[512,512]{1,0:T(8,128)(2,1)S(1)}, u32[]{:S(2)}, u32[]{:S(2)}) collective-permute-start(bf16[512,512]{1,0:T(8,128)(2,1)S(1)} %get-tuple-element.155), channel_id=1, source_target_pairs={{0,2},{1,3},{2,0},{3,1},{4,6},{5,7},{6,4},{7,5},{8,10},{9,11},{10,... | collective-permute-start | bytes 1572872 | tf_op jit(solution)/shard_map/ppermute | solution.py:631
  109.6 26.0 %collective-permute-start.9 = (bf16[512,512]{1,0:T(8,128)(2,1)S(1)}, bf16[512,512]{1,0:T(8,128)(2,1)S(1)}, u32[]{:S(2)}, u32[]{:S(2)}) collective-permute-start(bf16[512,512]{1,0:T(8,128)(2,1)S(1)} %get-tuple-element.156), channel_id=1, source_target_pairs={{0,2},{1,3},{2,0},{3,1},{4,6},{5,7},{6,4},{7,5},{8,10},{9,11},{10,... | collective-permute-start | bytes 1572872 | tf_op jit(solution)/shard_map/ppermute | solution.py:631
  142.9 15.7 %collective-permute-start.12 = (bf16[1792,512]{1,0:T(8,128)(2,1)}, bf16[1792,512]{1,0:T(8,128)(2,1)}, u32[]{:S(2)}, u32[]{:S(2)}) collective-permute-start(bf16[1792,512]{1,0:T(8,128)(2,1)} %get-tuple-element.157.refs_5_.refs_1_), channel_id=1, source_target_pairs={{0,1},{1,0},{2,3},{3,2},{4,5},{5,4},{6,7},{7,6},{8,9},{9,8},{10,11... | collective-permute-start | bytes 5505032 | tf_op jit(solution)/shard_map/ppermute | solution.py:631
  142.9 42.7 %collective-permute-start.10 = (bf16[1792,512]{1,0:T(8,128)(2,1)}, bf16[1792,512]{1,0:T(8,128)(2,1)}, u32[]{:S(2)}, u32[]{:S(2)}) collective-permute-start(bf16[1792,512]{1,0:T(8,128)(2,1)} %get-tuple-element.157.refs_5_.refs_1_), channel_id=1, source_target_pairs={{0,2},{1,3},{2,0},{3,1},{4,6},{5,7},{6,4},{7,5},{8,10},{9,11},{10,... | collective-permute-start | bytes 5505032 | tf_op jit(solution)/shard_map/ppermute | solution.py:631
  144.5 14.1 %collective-permute-start.13 = (bf16[512,512]{1,0:T(8,128)(2,1)}, bf16[512,512]{1,0:T(8,128)(2,1)S(1)}, u32[]{:S(2)}, u32[]{:S(2)}) collective-permute-start(bf16[512,512]{1,0:T(8,128)(2,1)} %copy-done.56), channel_id=1, source_target_pairs={{0,1},{1,0},{2,3},{3,2},{4,5},{5,4},{6,7},{7,6},{8,9},{9,8},{10,11... | collective-permute-start | bytes 1572872 | tf_op jit(solution)/shard_map/ppermute | solution.py:631
  150.9 14.6 %collective-permute-start.15 = (bf16[512,512]{1,0:T(8,128)(2,1)}, bf16[512,512]{1,0:T(8,128)(2,1)}, u32[]{:S(2)}, u32[]{:S(2)}) collective-permute-start(bf16[512,512]{1,0:T(8,128)(2,1)} %get-tuple-element.170), channel_id=1, source_target_pairs={{0,8},{4,12},{8,0},{12,4},{16,24},{20,28},{24,16},{28,20},{1,9},{5... | collective-permute-start | bytes 1572872 | tf_op jit(solution)/shard_map/ppermute | solution.py:631
  151.0 17.5 %collective-permute-start.11 = (bf16[512,512]{1,0:T(8,128)(2,1)}, bf16[512,512]{1,0:T(8,128)(2,1)}, u32[]{:S(2)}, u32[]{:S(2)}) collective-permute-start(bf16[512,512]{1,0:T(8,128)(2,1)} %get-tuple-element.162), channel_id=1, source_target_pairs={{0,4},{4,0},{8,12},{12,8},{16,20},{20,16},{24,28},{28,24},{1,5},{5... | collective-permute-start | bytes 1572872 | tf_op jit(solution)/shard_map/ppermute | solution.py:631
  164.9 26.5 %copy-start.31 = (bf16[512,512]{1,0:T(8,128)(2,1)S(1)}, bf16[512,512]{1,0:T(8,128)(2,1)}, u32[]{:S(2)}) copy-start(bf16[512,512]{1,0:T(8,128)(2,1)} %copy-done.30) | copy-start | bytes 1572868
  167.2 14.4 %collective-permute-start.16 = (bf16[256,512]{1,0:T(8,128)(2,1)S(1)}, bf16[256,512]{1,0:T(8,128)(2,1)S(1)}, u32[]{:S(2)}, u32[]{:S(2)}) collective-permute-start(bf16[256,512]{1,0:T(8,128)(2,1)S(1)} %get-tuple-element.174), channel_id=1, source_target_pairs={{0,16},{4,20},{8,24},{12,28},{16,0},{20,4},{24,8},{28,12},{1,17},{... | collective-permute-start | bytes 786440 | tf_op jit(solution)/shard_map/ppermute | solution.py:631
  170.1 13.2 %collective-permute-start.14 = (bf16[256,512]{1,0:T(8,128)(2,1)S(1)}, bf16[256,512]{1,0:T(8,128)(2,1)S(1)}, u32[]{:S(2)}, u32[]{:S(2)}) collective-permute-start(bf16[256,512]{1,0:T(8,128)(2,1)S(1)} %get-tuple-element.167), channel_id=1, source_target_pairs={{0,8},{4,12},{8,0},{12,4},{16,24},{20,28},{24,16},{28,20},{1,9},{5... | collective-permute-start | bytes 786440 | tf_op jit(solution)/shard_map/ppermute | solution.py:631
  185.7 9.6 %collective-permute-start.17 = (bf16[1792,512]{1,0:T(8,128)(2,1)}, bf16[1792,512]{1,0:T(8,128)(2,1)S(1)}, u32[]{:S(2)}, u32[]{:S(2)}) collective-permute-start(bf16[1792,512]{1,0:T(8,128)(2,1)} %collective-permute-done.10.refs_1_), channel_id=1, source_target_pairs={{0,1},{1,0},{2,3},{3,2},{4,5},{5,4},{6,7},{7,6},{8,9},{9,8},{10,11... | collective-permute-start | bytes 5505032 | tf_op jit(solution)/shard_map/ppermute | solution.py:631
  185.7 4.2 %collective-permute-start.18 = (bf16[512,512]{1,0:T(8,128)(2,1)S(1)}, bf16[512,512]{1,0:T(8,128)(2,1)S(1)}, u32[]{:S(2)}, u32[]{:S(2)}) collective-permute-start(bf16[512,512]{1,0:T(8,128)(2,1)S(1)} %copy-done.63), channel_id=1, source_target_pairs={{0,1},{1,0},{2,3},{3,2},{4,5},{5,4},{6,7},{7,6},{8,9},{9,8},{10,11... | collective-permute-start | bytes 1572872 | tf_op jit(solution)/shard_map/ppermute | solution.py:631
  186.2 14.7 %collective-permute-start.23 = (bf16[256,512]{1,0:T(8,128)(2,1)S(1)}, bf16[256,512]{1,0:T(8,128)(2,1)S(1)}, u32[]{:S(2)}, u32[]{:S(2)}) collective-permute-start(bf16[256,512]{1,0:T(8,128)(2,1)S(1)} %get-tuple-element.189.refs_1_), channel_id=1, source_target_pairs={{0,4},{4,0},{8,12},{12,8},{16,20},{20,16},{24,28},{28,24},{1,5},{5... | collective-permute-start | bytes 786440 | tf_op jit(solution)/shard_map/ppermute | solution.py:631
  186.4 15.6 %collective-permute-start.21 = (bf16[256,512]{1,0:T(8,128)(2,1)S(1)}, bf16[256,512]{1,0:T(8,128)(2,1)S(1)}, u32[]{:S(2)}, u32[]{:S(2)}) collective-permute-start(bf16[256,512]{1,0:T(8,128)(2,1)S(1)} %get-tuple-element.186.refs_1_), channel_id=1, source_target_pairs={{0,16},{4,20},{8,24},{12,28},{16,0},{20,4},{24,8},{28,12},{1,17},{... | collective-permute-start | bytes 786440 | tf_op jit(solution)/shard_map/ppermute | solution.py:631
  187.7 29.9 %collective-permute-start.19 = (bf16[512,512]{1,0:T(8,128)(2,1)}, bf16[512,512]{1,0:T(8,128)(2,1)S(1)}, u32[]{:S(2)}, u32[]{:S(2)}) collective-permute-start(bf16[512,512]{1,0:T(8,128)(2,1)} %get-tuple-element.184), channel_id=1, source_target_pairs={{0,2},{1,3},{2,0},{3,1},{4,6},{5,7},{6,4},{7,5},{8,10},{9,11},{10,... | collective-permute-start | bytes 1572872 | tf_op jit(solution)/shard_map/ppermute | solution.py:631
  189.9 27.8 %collective-permute-start.20 = (bf16[512,512]{1,0:T(8,128)(2,1)}, bf16[512,512]{1,0:T(8,128)(2,1)}, u32[]{:S(2)}, u32[]{:S(2)}) collective-permute-start(bf16[512,512]{1,0:T(8,128)(2,1)} %get-tuple-element.185), channel_id=1, source_target_pairs={{0,2},{1,3},{2,0},{3,1},{4,6},{5,7},{6,4},{7,5},{8,10},{9,11},{10,... | collective-permute-start | bytes 1572872 | tf_op jit(solution)/shard_map/ppermute | solution.py:631
  201.5 14.6 %collective-permute-start.24 = (bf16[256,512]{1,0:T(8,128)(2,1)S(1)}, bf16[256,512]{1,0:T(8,128)(2,1)S(1)}, u32[]{:S(2)}, u32[]{:S(2)}) collective-permute-start(bf16[256,512]{1,0:T(8,128)(2,1)S(1)} %get-tuple-element.192.refs_1_), channel_id=1, source_target_pairs={{0,16},{4,20},{8,24},{12,28},{16,0},{20,4},{24,8},{28,12},{1,17},{... | collective-permute-start | bytes 786440 | tf_op jit(solution)/shard_map/ppermute | solution.py:631
  202.6 14.4 %collective-permute-start.22 = (bf16[256,512]{1,0:T(8,128)(2,1)S(1)}, bf16[256,512]{1,0:T(8,128)(2,1)S(1)}, u32[]{:S(2)}, u32[]{:S(2)}) collective-permute-start(bf16[256,512]{1,0:T(8,128)(2,1)S(1)} %get-tuple-element.187.refs_1_), channel_id=1, source_target_pairs={{0,8},{4,12},{8,0},{12,4},{16,24},{20,28},{24,16},{28,20},{1,9},{5... | collective-permute-start | bytes 786440 | tf_op jit(solution)/shard_map/ppermute | solution.py:631
  203.9 14.7 %all-to-all-start.3 = ((f32[8,8,512]{2,1,0:T(8,128)}), f32[8,8,512]{2,1,0:T(8,128)S(1)}, u32[]{:S(2)}, u32[]{:S(2)}) async-start(f32[8,8,512]{2,1,0:T(8,128)} %get-tuple-element.183.refs_3_), calls=%async_computation.3 | async-start | bytes 262144 | tf_op jit(solution)/shard_map/all_to_all | solution.py:121
  224.9 35.2 %collective-permute-start.25 = (bf16[1792,512]{1,0:T(8,128)(2,1)}, bf16[1792,512]{1,0:T(8,128)(2,1)}, u32[]{:S(2)}, u32[]{:S(2)}) collective-permute-start(bf16[1792,512]{1,0:T(8,128)(2,1)} %get-tuple-element.194.refs_5_.refs_1_), channel_id=1, source_target_pairs={{0,1},{1,0},{2,3},{3,2},{4,5},{5,4},{6,7},{7,6},{8,9},{9,8},{10,11... | collective-permute-start | bytes 5505032 | tf_op jit(solution)/shard_map/ppermute | solution.py:631
  224.9 46.8 %collective-permute-start.31 = (bf16[1792,512]{1,0:T(8,128)(2,1)}, bf16[1792,512]{1,0:T(8,128)(2,1)}, u32[]{:S(2)}, u32[]{:S(2)}) collective-permute-start(bf16[1792,512]{1,0:T(8,128)(2,1)} %get-tuple-element.194.refs_5_.refs_1_), channel_id=1, source_target_pairs={{0,2},{1,3},{2,0},{3,1},{4,6},{5,7},{6,4},{7,5},{8,10},{9,11},{10,... | collective-permute-start | bytes 5505032 | tf_op jit(solution)/shard_map/ppermute | solution.py:631
  225.5 14.0 %collective-permute-start.27 = (bf16[512,512]{1,0:T(8,128)(2,1)S(1)}, bf16[512,512]{1,0:T(8,128)(2,1)S(1)}, u32[]{:S(2)}, u32[]{:S(2)}) collective-permute-start(bf16[512,512]{1,0:T(8,128)(2,1)S(1)} %get-tuple-element.197.refs_1_), channel_id=1, source_target_pairs={{0,4},{4,0},{8,12},{12,8},{16,20},{20,16},{24,28},{28,24},{1,5},{5... | collective-permute-start | bytes 1572872 | tf_op jit(solution)/shard_map/ppermute | solution.py:631
  226.7 14.8 %collective-permute-start.28 = (bf16[512,512]{1,0:T(8,128)(2,1)S(1)}, bf16[512,512]{1,0:T(8,128)(2,1)S(1)}, u32[]{:S(2)}, u32[]{:S(2)}) collective-permute-start(bf16[512,512]{1,0:T(8,128)(2,1)S(1)} %get-tuple-element.198.refs_3_), channel_id=1, source_target_pairs={{0,8},{4,12},{8,0},{12,4},{16,24},{20,28},{24,16},{28,20},{1,9},{5... | collective-permute-start | bytes 1572872 | tf_op jit(solution)/shard_map/ppermute | solution.py:631
  233.0 18.7 %collective-permute-start.30 = (bf16[512,512]{1,0:T(8,128)(2,1)}, bf16[512,512]{1,0:T(8,128)(2,1)}, u32[]{:S(2)}, u32[]{:S(2)}) collective-permute-start(bf16[512,512]{1,0:T(8,128)(2,1)} %get-tuple-element.203), channel_id=1, source_target_pairs={{0,8},{4,12},{8,0},{12,4},{16,24},{20,28},{24,16},{28,20},{1,9},{5... | collective-permute-start | bytes 1572872 | tf_op jit(solution)/shard_map/ppermute | solution.py:631
  239.4 16.1 %collective-permute-start.29 = (bf16[512,512]{1,0:T(8,128)(2,1)}, bf16[512,512]{1,0:T(8,128)(2,1)}, u32[]{:S(2)}, u32[]{:S(2)}) collective-permute-start(bf16[512,512]{1,0:T(8,128)(2,1)} %get-tuple-element.200), channel_id=1, source_target_pairs={{0,4},{4,0},{8,12},{12,8},{16,20},{20,16},{24,28},{28,24},{1,5},{5... | collective-permute-start | bytes 1572872 | tf_op jit(solution)/shard_map/ppermute | solution.py:631
  241.5 18.6 %collective-permute-start.26 = (bf16[512,512]{1,0:T(8,128)(2,1)}, bf16[512,512]{1,0:T(8,128)(2,1)S(1)}, u32[]{:S(2)}, u32[]{:S(2)}) collective-permute-start(bf16[512,512]{1,0:T(8,128)(2,1)} %get-tuple-element.195), channel_id=1, source_target_pairs={{0,1},{1,0},{2,3},{3,2},{4,5},{5,4},{6,7},{7,6},{8,9},{9,8},{10,11... | collective-permute-start | bytes 1572872 | tf_op jit(solution)/shard_map/ppermute | solution.py:631
  254.5 13.8 %collective-permute-start.33 = (bf16[256,512]{1,0:T(8,128)(2,1)S(1)}, bf16[256,512]{1,0:T(8,128)(2,1)S(1)}, u32[]{:S(2)}, u32[]{:S(2)}) collective-permute-start(bf16[256,512]{1,0:T(8,128)(2,1)S(1)} %get-tuple-element.212), channel_id=1, source_target_pairs={{0,16},{4,20},{8,24},{12,28},{16,0},{20,4},{24,8},{28,12},{1,17},{... | collective-permute-start | bytes 786440 | tf_op jit(solution)/shard_map/ppermute | solution.py:631
  258.3 12.8 %collective-permute-start.32 = (bf16[256,512]{1,0:T(8,128)(2,1)S(1)}, bf16[256,512]{1,0:T(8,128)(2,1)S(1)}, u32[]{:S(2)}, u32[]{:S(2)}) collective-permute-start(bf16[256,512]{1,0:T(8,128)(2,1)S(1)} %get-tuple-element.208), channel_id=1, source_target_pairs={{0,8},{4,12},{8,0},{12,4},{16,24},{20,28},{24,16},{28,20},{1,9},{5... | collective-permute-start | bytes 786440 | tf_op jit(solution)/shard_map/ppermute | solution.py:631
  271.7 25.5 %collective-permute-start.36 = (bf16[1792,512]{1,0:T(8,128)(2,1)}, bf16[1792,512]{1,0:T(8,128)(2,1)S(1)}, u32[]{:S(2)}, u32[]{:S(2)}) collective-permute-start(bf16[1792,512]{1,0:T(8,128)(2,1)} %collective-permute-done.31.refs_1_), channel_id=1, source_target_pairs={{0,1},{1,0},{2,3},{3,2},{4,5},{5,4},{6,7},{7,6},{8,9},{9,8},{10,11... | collective-permute-start | bytes 5505032 | tf_op jit(solution)/shard_map/ppermute | solution.py:631
  271.8 25.4 %collective-permute-start.37 = (bf16[512,512]{1,0:T(8,128)(2,1)}, bf16[512,512]{1,0:T(8,128)(2,1)S(1)}, u32[]{:S(2)}, u32[]{:S(2)}) collective-permute-start(bf16[512,512]{1,0:T(8,128)(2,1)} %collective-permute-done.20.refs_9_), channel_id=1, source_target_pairs={{0,1},{1,0},{2,3},{3,2},{4,5},{5,4},{6,7},{7,6},{8,9},{9,8},{10,11... | collective-permute-start | bytes 1572872 | tf_op jit(solution)/shard_map/ppermute | solution.py:631
  272.3 13.8 %collective-permute-start.34 = (bf16[256,512]{1,0:T(8,128)(2,1)S(1)}, bf16[256,512]{1,0:T(8,128)(2,1)S(1)}, u32[]{:S(2)}, u32[]{:S(2)}) collective-permute-start(bf16[256,512]{1,0:T(8,128)(2,1)S(1)} %get-tuple-element.218.refs_1_), channel_id=1, source_target_pairs={{0,16},{4,20},{8,24},{12,28},{16,0},{20,4},{24,8},{28,12},{1,17},{... | collective-permute-start | bytes 786440 | tf_op jit(solution)/shard_map/ppermute | solution.py:631
  272.3 15.2 %collective-permute-start.35 = (bf16[256,512]{1,0:T(8,128)(2,1)S(1)}, bf16[256,512]{1,0:T(8,128)(2,1)S(1)}, u32[]{:S(2)}, u32[]{:S(2)}) collective-permute-start(bf16[256,512]{1,0:T(8,128)(2,1)S(1)} %get-tuple-element.221.refs_1_), channel_id=1, source_target_pairs={{0,4},{4,0},{8,12},{12,8},{16,20},{20,16},{24,28},{28,24},{1,5},{5... | collective-permute-start | bytes 786440 | tf_op jit(solution)/shard_map/ppermute | solution.py:631
  287.4 12.8 %collective-permute-start.38 = (bf16[256,512]{1,0:T(8,128)(2,1)S(1)}, bf16[256,512]{1,0:T(8,128)(2,1)S(1)}, u32[]{:S(2)}, u32[]{:S(2)}) collective-permute-start(bf16[256,512]{1,0:T(8,128)(2,1)S(1)} %get-tuple-element.225.refs_1_), channel_id=1, source_target_pairs={{0,8},{4,12},{8,0},{12,4},{16,24},{20,28},{24,16},{28,20},{1,9},{5... | collective-permute-start | bytes 786440 | tf_op jit(solution)/shard_map/ppermute | solution.py:631
  288.1 14.9 %collective-permute-start.40 = (bf16[256,512]{1,0:T(8,128)(2,1)S(1)}, bf16[256,512]{1,0:T(8,128)(2,1)S(1)}, u32[]{:S(2)}, u32[]{:S(2)}) collective-permute-start(bf16[256,512]{1,0:T(8,128)(2,1)S(1)} %get-tuple-element.228.refs_1_), channel_id=1, source_target_pairs={{0,16},{4,20},{8,24},{12,28},{16,0},{20,4},{24,8},{28,12},{1,17},{... | collective-permute-start | bytes 786440 | tf_op jit(solution)/shard_map/ppermute | solution.py:631
  301.4 13.0 %collective-permute-start.39 = (bf16[512,512]{1,0:T(8,128)(2,1)S(1)}, bf16[512,512]{1,0:T(8,128)(2,1)S(1)}, u32[]{:S(2)}, u32[]{:S(2)}) collective-permute-start(bf16[512,512]{1,0:T(8,128)(2,1)S(1)} %get-tuple-element.227.refs_1_), channel_id=1, source_target_pairs={{0,4},{4,0},{8,12},{12,8},{16,20},{20,16},{24,28},{28,24},{1,5},{5... | collective-permute-start | bytes 1572872 | tf_op jit(solution)/shard_map/ppermute | solution.py:631
  304.1 13.0 %collective-permute-start.41 = (bf16[512,512]{1,0:T(8,128)(2,1)S(1)}, bf16[512,512]{1,0:T(8,128)(2,1)S(1)}, u32[]{:S(2)}, u32[]{:S(2)}) collective-permute-start(bf16[512,512]{1,0:T(8,128)(2,1)S(1)} %get-tuple-element.229.refs_3_), channel_id=1, source_target_pairs={{0,8},{4,12},{8,0},{12,4},{16,24},{20,28},{24,16},{28,20},{1,9},{5... | collective-permute-start | bytes 1572872 | tf_op jit(solution)/shard_map/ppermute | solution.py:631
  (59 other events, 433.0 us)

commit v7 on v6

--- a/solution.py
+++ b/solution.py
@@ -84,7 +84,7 @@
     eye = (rows == cols).astype(F32)
     joined = hits + eye
     counts = joined + joined * eye
-    ht_ref[0] = wide(counts.astype(BF), 2 * SLOT)
+    ht_ref[0] = counts.astype(BF)
     h_ref[0] = wide(counts.T.astype(BF), 2 * SLOT)
     valid = valid_ref[0].astype(F32)
     inv_ref[0] = jnp.broadcast_to(valid / (degree + 1.0), (SLOT, SLOT)).T
@@ -99,8 +99,12 @@
     return launch(
         tiles_kernel, (slots,),
         [pl.BlockSpec((1, NBR, SLOT), lambda i: (i, 0, 0)), pl.BlockSpec((1, 1, SLOT), lambda i: (i, 0, 0))],
-        [double, double, square, square, token_spec()],
-        [jax.ShapeDtypeStruct((slots, SLOT, 2 * SLOT), BF)] * 2 + [jax.ShapeDtypeStruct((slots, SLOT, SLOT), F32)] * 2 + [TOKEN],
+        [double, square, square, square, token_spec()],
+        [
+            jax.ShapeDtypeStruct((slots, SLOT, w), t)
+            for w, t in ((2 * SLOT, BF), (SLOT, BF), (SLOT, F32), (SLOT, F32))
+        ]
+        + [TOKEN],
         [turned, node_valid.reshape(slots, 1, SLOT)], "tiles",
     )
 
@@ -461,9 +465,7 @@
             else:
                 grad = grad_ref[rows, :]
             weight = wide(inv_ref[s, inner, :], columns)
-            high, low = split(weight * (grad - (at(co_ref, 5) + away * at(co_ref, 6))))
-            lg_ref[s, inner, :] = high
-            lg_ref[s, SLOT + r * PART : SLOT + (r + 1) * PART, :] = low
+            lg_ref[s, inner, :] = (weight * (grad - (at(co_ref, 5) + away * at(co_ref, 6)))).astype(BF)
         out_ref[s * SLOT : (s + 1) * SLOT, :] = (dot(ht_ref[s], lg_ref[s]) * at(co_ref, 1)).astype(BF)
 
 
@@ -490,7 +492,7 @@
     _, ht, inv, _ = tiles
     return rows_call(
         functools.partial(turn_kernel, from_cot), big, [lin, grad], [inv, ht], [norm[0], sums, *norm[1:]], BF,
-        [pltpu.VMEM((big, 2 * SLOT, lin.shape[1]), BF)], name, tokens, 60,
+        [pltpu.VMEM((big, SLOT, lin.shape[1]), BF)], name, tokens, 60,
     )
 
 
@@ -815,20 +817,20 @@
     def terms_one(other, tokens, h=turned):
         return weight_terms(ids, other, ((features, near_one), (far_one, beyond_one)), h, "terms_one", tokens)
 
-    sum_one = RowSum("row", ids, terms_one, "one", lambda: tuple(sum_two.got))
+    sum_one = RowSum("row", ids, terms_one, "one", lambda: (sum_two.got[1],))
     weights = [weight_block(weight_one, 0), whole_block(rows_one[0])]
     early, token = half(ids, big, [turned, near], weights, True, "half_back_one", sum_one.next())
     output, token = rows_call(result_kernel, big, [lin_two], [val], norm_two, F32, [], "output", (token,))
     started = sum_one.next(token)
     far, tokens = after(far, *started)
     beyond = across(far, "col", 1)
-    grad_weight_two, token = sum_two.placed(60, started)
-    tokens = (*tokens, *sum_one.next(token))
+    tokens = (*tokens, *sum_one.next())
     early, _ = half(ids, big, [far], [whole_block(rows_one[1])], True, "far_half_back_one", tokens, early)
     grad_features, token = backward(big, early, beyond, rows_one[2], None, None, "backward_one", tokens)
     while sum_one.stage < sum_one.stages - 1:
         sum_one.next()
-    sum_one.next(token)
+    tokens = sum_one.next(token)
+    grad_weight_two, _ = sum_two.placed(60, tokens)
     grad_weight_one, _ = sum_one.placed(24)
 
     sums_one, sums_two = jnp.sum(grads_one, axis=0), jnp.sum(grads_two, axis=0)

time: 321 us -> 317 us (0.988)
  Pallas kernels: 116 us -> 111 us
  local copies, waits for them, and re-layouts: 21.8 us -> 18.2 us
    pallas_call x41, Pallas kernels: 115 us -> 111 us  [launch(): pl.pallas_call(body, grid_spec=pltpu.PrefetchScalarGridSpec(num_scalar_pr...]
    unnamed x128 -> x120, local copies, waits for them, and re-layouts: 19.9 us -> 16.2 us
where the time goes in v7:
time: 317 us; the launch traced here: 316 us
  Pallas kernels  111 us (35%)
  waiting for transfers between devices  109 us (34%)
  starting transfers between devices  40.6 us (13%)
  blocking collectives  36.5 us (12%)
  local copies, waits for them, and re-layouts  18.2 us (6%)
    pallas_call x41, Pallas kernels, launch(): pl.pallas_call(body, grid_spec=pltpu.PrefetchScalarGridSpec(num_scalar_pr...  111 us
    ppermute x42, waiting for transfers between devices, across(): return lax.ppermute(value, axis, [(i, i ^ distance) for i in range(size)])  109 us
    ppermute x42, starting transfers between devices, across(): return lax.ppermute(value, axis, [(i, i ^ distance) for i in range(size)])  36.6 us
    all_to_all x3, blocking collectives, small_gather(): return lax.all_to_all(copies, axis, split_axis=0, concat_axis=0, tiled=True)  36.5 us
    unnamed x120, local copies, waits for them, and re-layouts  16.2 us
  transfers between devices with their start and end apart: 43, of which 23 were waited for; matrix products, arithmetic and copies ran while one was open for 1% of the time, Pallas kernels for 28%

profile of v7, /device:TPU:0, one launch (start us, length us, event | category | flops | bytes accessed | tf_op | source)
XLA Modules:
  0.0 316.4 jit_solution(12463366786153138931)
XLA Ops:
  1.2 2.6 collective-permute-start
  4.6 4.9 %tiles.1 = (bf16[14,128,256]{2,1,0:T(8,128)(2,1)S(1)}, bf16[14,128,128]{2,1,0:T(8,128)(2,1)S(1)}, f32[14,128,128]{2,1,0:T(8,128)S(1)}, f32[14,128,128]{2,1,0:T(8,128)S(1)}, f32[8,128]{1,0:T(8,128)S(1)}) custom-call(s32[14,32,128]{2,1,0:T(8,128)S(1)} %bitcast_bitcast_fusion.refs_0_, s32[14,1,128]{2,1,0:T(1,128)S(1)} %reshape.35.refs_1_), custom_call_target="tpu_custom_call" | custom-call | flops 1000000 | bytes 1000 | tf_op jit(solution)/shard_map/tiles/pallas_call | solution.py:45
  13.5 1.7 weight_slices.1
  16.7 2.8 half_one.1
  19.5 25.2 %collective-permute-done.refs_1_.refs_3_ = bf16[1792,512]{1,0:T(8,128)(2,1)} collective-permute-done((bf16[1792,512]{1,0:T(8,128)(2,1)}, bf16[1792,512]{1,0:T(8,128)(2,1)}, u32[]{:S(2)}, u32[]{:S(2)}) %collective-permute-start) | collective-permute-done | bytes 1835040 | tf_op jit(solution)/shard_map/ppermute | solution.py:633
  44.7 3.5 %far_half_one.1 = (f32[1792,512]{1,0:T(8,128)S(1)}, f32[8,128]{1,0:T(8,128)}) custom-call(s32[7]{0:T(128)S(1)} %stack.31.refs_0_, bf16[1792,512]{1,0:T(8,128)(2,1)} %collective-permute-done.refs_1_.refs_3_, bf16[2048,512]{1,0:T(8,128)(2,1)S(1)} %copy-done.5, f32[1792,512]{1,0:T(8,128)S(1)} %get-tuple-element.125.refs_3_, ...), custom_call_target="tpu_custom_call" | custom-call | flops 1000000 | bytes 1000 | tf_op jit(solution)/shard_map/far_half_one/pallas_call | solution.py:45
  48.7 4.4 %forward_one.1 = (f32[1792,512]{1,0:T(8,128)S(1)}, f32[8,8,512]{2,1,0:T(8,128)S(1)}, f32[8,128]{1,0:T(8,128)}, bf16[640,512]{1,0:T(8,128)(2,1)S(1)}, bf16[1168,512]{1,0:T(8,128)(2,1)S(1)}) custom-call(s32[7]{0:T(128)S(1)} %stack.31.refs_0_, f32[1792,512]{1,0:T(8,128)S(1)} %get-tuple-element.129.refs_1_, ...), custom_call_target="tpu_custom_call" | custom-call | flops 1000000 | bytes 1000 | tf_op jit(solution)/shard_map/forward_one/pallas_call | solution.py:45
  53.1 1.8 collective-permute-start.3
  54.8 12.9 %all_to_all.20.refs_1_.refs_2_.refs_4_ = f32[8,8,512]{2,1,0:T(8,128)S(1)} all-to-all(f32[8,8,512]{2,1,0:T(8,128)S(1)} %get-tuple-element.134.refs_0_), channel_id=1, replica_groups=mesh['row'=8,'col'=4] {'row'}, dimensions={0} | all-to-all | bytes 262144 | tf_op jit(solution)/shard_map/all_to_all | solution.py:125
  67.8 2.1 collective-permute-done.3.refs_5_.refs_1_
  71.1 1.8 collective-permute-start.4
  72.9 2.0 collective-permute-done.5.refs_2_
  74.9 2.8 half_two.1
  77.7 22.1 %collective-permute-done.4.refs_2_ = bf16[1168,512]{1,0:T(8,128)(2,1)S(1)} collective-permute-done((bf16[1168,512]{1,0:T(8,128)(2,1)S(1)}, bf16[1168,512]{1,0:T(8,128)(2,1)S(1)}, u32[]{:S(2)}, u32[]{:S(2)}) %collective-permute-start.4) | collective-permute-done | bytes 1196064 | tf_op jit(solution)/shard_map/ppermute | solution.py:633
  100.4 2.1 far_half_two.1
  103.8 3.8 %forward_two.1 = (f32[1792,512]{1,0:T(8,128)S(1)}, f32[8,8,512]{2,1,0:T(8,128)S(1)}, bf16[1792,512]{1,0:T(8,128)(2,1)S(1)}, f32[8,128]{1,0:T(8,128)S(1)}) custom-call(s32[7]{0:T(128)S(1)} %stack.31.refs_0_, f32[1792,512]{1,0:T(8,128)S(1)} %get-tuple-element.144.refs_1_, bf16[640,512]{1,0:T(8,128)(2,1)S(1)} %collective-permute-done.6.refs_2_, ...), custom_call_target="tpu_custom_call" | custom-call | flops 1000000 | bytes 1000 | tf_op jit(solution)/shard_map/forward_two/pallas_call | solution.py:45
  107.6 1.8 collective-permute-start.8
  109.7 13.2 %all_to_all.21.refs_3_.refs_4_.refs_2_ = f32[8,8,512]{2,1,0:T(8,128)S(1)} all-to-all(f32[8,8,512]{2,1,0:T(8,128)S(1)} %get-tuple-element.146), channel_id=1, replica_groups=mesh['row'=8,'col'=4] {'row'}, dimensions={0} | all-to-all | bytes 262144 | tf_op jit(solution)/shard_map/all_to_all | solution.py:125
  122.9 2.0 sums_two.1
  125.0 10.4 %all_to_all.22.refs_5_ = f32[8,8,512]{2,1,0:T(8,128)} all-to-all(f32[8,8,512]{2,1,0:T(8,128)S(1)} %sums_two.1), channel_id=1, replica_groups=mesh['row'=8,'col'=4] {'row'}, dimensions={0} | all-to-all | bytes 262144 | tf_op jit(solution)/shard_map/all_to_all | solution.py:125
  136.3 5.9 %turn_two.1 = (bf16[1792,512]{1,0:T(8,128)(2,1)}, f32[8,128]{1,0:T(8,128)}) custom-call(f32[1792,512]{1,0:T(8,128)} %copy-done.7, bf16[1792,512]{1,0:T(8,128)(2,1)} %refs_1_.9, f32[14,128,128]{2,1,0:T(8,128)} %copy-done.18, bf16[14,128,128]{2,1,0:T(8,128)(2,1)} %copy-done.30, f32[8,8,512]{2,1,0:T(8,128)} %copy-done.24, f32[8,8,512]{2,1,0:T(8,128)} %all_to_all.22.refs_5_, ...), custom_call_target="tpu_custom_call" | custom-call | flops 1000000 | bytes 1000 | tf_op jit(solution)/shard_map/turn_two/pallas_call | solution.py:45
  143.9 6.2 %terms_two.2 = (bf16[512,512]{1,0:T(8,128)(2,1)}, bf16[512,512]{1,0:T(8,128)(2,1)}, f32[8,128]{1,0:T(8,128)}) custom-call(s32[7]{0:T(128)} %copy-done.31, bf16[1792,512]{1,0:T(8,128)(2,1)} %copy-done.16, bf16[1792,512]{1,0:T(8,128)(2,1)} %copy-done.17, bf16[1792,512]{1,0:T(8,128)(2,1)} %copy-done.20, bf16[1792,512]{1,0:T(8,128)(2,1)} %copy-done.21, ...), custom_call_target="tpu_custom_call" | custom-call | flops 1000000 | bytes 1000 | tf_op jit(solution)/shard_map/terms_two/pallas_call | solution.py:45
  151.5 6.3 %terms_two.3 = (bf16[512,512]{1,0:T(8,128)(2,1)}, bf16[512,512]{1,0:T(8,128)(2,1)}, f32[8,128]{1,0:T(8,128)}) custom-call(s32[7]{0:T(128)} %copy-done.31, bf16[1792,512]{1,0:T(8,128)(2,1)} %copy-done.16, bf16[1792,512]{1,0:T(8,128)(2,1)} %copy-done.17, bf16[1792,512]{1,0:T(8,128)(2,1)} %copy-done.20, bf16[1792,512]{1,0:T(8,128)(2,1)} %copy-done.21, ...), custom_call_target="tpu_custom_call" | custom-call | flops 1000000 | bytes 1000 | tf_op jit(solution)/shard_map/terms_two/pallas_call | solution.py:45
  160.1 4.0 %half_back_two.1 = (f32[1792,512]{1,0:T(8,128)S(1)}, f32[8,128]{1,0:T(8,128)S(1)}) custom-call(s32[7]{0:T(128)S(1)} %copy-done.32, bf16[1792,512]{1,0:T(8,128)(2,1)S(1)} %copy-done.12, bf16[1792,512]{1,0:T(8,128)(2,1)} %collective-permute-done.12.refs_2_, bf16[2048,512]{1,0:T(8,128)(2,1)S(1)} %copy-done.3, ...), custom_call_target="tpu_custom_call" | custom-call | flops 1000000 | bytes 1000 | tf_op jit(solution)/shard_map/half_back_two/pallas_call | solution.py:45
  167.8 1.7 two_0_1.1
  170.0 10.9 %collective-permute-done.16.refs_2_ = bf16[256,512]{1,0:T(8,128)(2,1)S(1)} collective-permute-done((bf16[256,512]{1,0:T(8,128)(2,1)S(1)}, bf16[256,512]{1,0:T(8,128)(2,1)S(1)}, u32[]{:S(2)}, u32[]{:S(2)}) %collective-permute-start.16) | collective-permute-done | bytes 262176 | tf_op jit(solution)/shard_map/ppermute | solution.py:633
  190.6 3.9 %far_half_back_two.1 = (f32[1792,512]{1,0:T(8,128)S(1)}, f32[8,128]{1,0:T(8,128)}) custom-call(s32[7]{0:T(128)S(1)} %copy-done.32, bf16[1792,512]{1,0:T(8,128)(2,1)} %collective-permute-done.10.refs_1_, bf16[512,512]{1,0:T(8,128)(2,1)S(1)} %copy-done.27, f32[1792,512]{1,0:T(8,128)S(1)} %get-tuple-element.179.refs_3_, ...), custom_call_target="tpu_custom_call" | custom-call | flops 1000000 | bytes 1000 | tf_op jit(solution)/shard_map/far_half_back_two/pallas_call | solution.py:45
  194.5 3.8 %backward_two.1 = (f32[1792,512]{1,0:T(8,128)S(1)}, f32[8,8,512]{2,1,0:T(8,128)}) custom-call(f32[1792,512]{1,0:T(8,128)S(1)} %get-tuple-element.182.refs_0_, bf16[1792,512]{1,0:T(8,128)(2,1)S(1)} %collective-permute-done.17.refs_1_, bf16[512,512]{1,0:T(8,128)(2,1)S(1)} %collective-permute-done.18.refs_2_, f32[1792,512]{1,0:T(8,128)S(1)} %copy-done.10, ...), custom_call_target="tpu_custom_call" | custom-call | flops 1000000 | bytes 1000 | tf_op jit(solution)/shard_map/backward_two/pallas_call | solution.py:45
  198.4 1.8 copy-done.22
  203.2 4.0 %all-to-all-start.3 = ((f32[8,8,512]{2,1,0:T(8,128)}), f32[8,8,512]{2,1,0:T(8,128)S(1)}, u32[]{:S(2)}, u32[]{:S(2)}) async-start(f32[8,8,512]{2,1,0:T(8,128)} %get-tuple-element.184.refs_3_), calls=%async_computation.3 | async-start | bytes 262144 | tf_op jit(solution)/shard_map/all_to_all | solution.py:125
  207.2 8.3 %collective-permute-done.24.refs_2_ = bf16[256,512]{1,0:T(8,128)(2,1)S(1)} collective-permute-done((bf16[256,512]{1,0:T(8,128)(2,1)S(1)}, bf16[256,512]{1,0:T(8,128)(2,1)S(1)}, u32[]{:S(2)}, u32[]{:S(2)}) %collective-permute-start.24) | collective-permute-done | bytes 262176 | tf_op jit(solution)/shard_map/ppermute | solution.py:633
  218.5 5.2 %turn_one.1 = (bf16[1792,512]{1,0:T(8,128)(2,1)}, f32[8,128]{1,0:T(8,128)}) custom-call(f32[1792,512]{1,0:T(8,128)} %copy-done.9, f32[1792,512]{1,0:T(8,128)} %copy-done.22, f32[14,128,128]{2,1,0:T(8,128)} %copy-done.18, bf16[14,128,128]{2,1,0:T(8,128)(2,1)} %copy-done.30, f32[8,8,512]{2,1,0:T(8,128)} %copy-done.23, f32[8,8,512]{2,1,0:T(8,128)} %copy-done.56, ...), custom_call_target="tpu_custom_call" | custom-call | flops 1000000 | bytes 1000 | tf_op jit(solution)/shard_map/turn_one/pallas_call | solution.py:45
  224.7 6.2 %terms_one.2 = (bf16[512,512]{1,0:T(8,128)(2,1)}, bf16[512,512]{1,0:T(8,128)(2,1)}, f32[8,128]{1,0:T(8,128)}) custom-call(s32[7]{0:T(128)} %copy-done.31, bf16[1792,512]{1,0:T(8,128)(2,1)} %refs_1_.11, bf16[1792,512]{1,0:T(8,128)(2,1)} %copy-done.14, bf16[1792,512]{1,0:T(8,128)(2,1)} %collective-permute-done.refs_1_.refs_3_, bf16[1792,512]{1,0:T(8,128)(2,1)} %copy-done.15, ...), custom_call_target="tpu_custom_call" | custom-call | flops 1000000 | bytes 1000 | tf_op jit(solution)/shard_map/terms_one/pallas_call | solution.py:45
  230.9 1.9 collective-permute-start.29
  234.0 5.3 %collective-permute-done.27.refs_7_.refs_4_ = bf16[512,512]{1,0:T(8,128)(2,1)S(1)} collective-permute-done((bf16[512,512]{1,0:T(8,128)(2,1)S(1)}, bf16[512,512]{1,0:T(8,128)(2,1)S(1)}, u32[]{:S(2)}, u32[]{:S(2)}) %collective-permute-start.27) | collective-permute-done | bytes 524320 | tf_op jit(solution)/shard_map/ppermute | solution.py:633
  240.1 6.3 %terms_one.3 = (bf16[512,512]{1,0:T(8,128)(2,1)}, bf16[512,512]{1,0:T(8,128)(2,1)}, f32[8,128]{1,0:T(8,128)}) custom-call(s32[7]{0:T(128)} %copy-done.31, bf16[1792,512]{1,0:T(8,128)(2,1)} %refs_1_.11, bf16[1792,512]{1,0:T(8,128)(2,1)} %copy-done.14, bf16[1792,512]{1,0:T(8,128)(2,1)} %collective-permute-done.refs_1_.refs_3_, bf16[1792,512]{1,0:T(8,128)(2,1)} %copy-done.15, ...), custom_call_target="tpu_custom_call" | custom-call | flops 1000000 | bytes 1000 | tf_op jit(solution)/shard_map/terms_one/pallas_call | solution.py:45
  246.4 3.4 %collective-permute-done.29.refs_2_ = bf16[512,512]{1,0:T(8,128)(2,1)} collective-permute-done((bf16[512,512]{1,0:T(8,128)(2,1)}, bf16[512,512]{1,0:T(8,128)(2,1)}, u32[]{:S(2)}, u32[]{:S(2)}) %collective-permute-start.29) | collective-permute-done | bytes 524320 | tf_op jit(solution)/shard_map/ppermute | solution.py:633
  255.7 1.8 collective-permute-start.31
  257.5 4.3 %half_back_one.1 = (f32[1792,512]{1,0:T(8,128)S(1)}, f32[8,128]{1,0:T(8,128)S(1)}) custom-call(s32[7]{0:T(128)S(1)} %copy-done.33, bf16[1792,512]{1,0:T(8,128)(2,1)S(1)} %copy-done.11, bf16[1792,512]{1,0:T(8,128)(2,1)} %collective-permute-done.25.refs_2_, bf16[2048,512]{1,0:T(8,128)(2,1)S(1)} %copy-done.6, ...), custom_call_target="tpu_custom_call" | custom-call | flops 1000000 | bytes 1000 | tf_op jit(solution)/shard_map/half_back_one/pallas_call | solution.py:45
  261.9 2.3 output.1
  264.2 2.4 collective-permute-done.32.refs_2_
  271.3 12.2 %collective-permute-done.33.refs_2_ = bf16[256,512]{1,0:T(8,128)(2,1)S(1)} collective-permute-done((bf16[256,512]{1,0:T(8,128)(2,1)S(1)}, bf16[256,512]{1,0:T(8,128)(2,1)S(1)}, u32[]{:S(2)}, u32[]{:S(2)}) %collective-permute-start.33) | collective-permute-done | bytes 262176 | tf_op jit(solution)/shard_map/ppermute | solution.py:633
  284.8 2.8 collective-permute-start.39
  289.2 3.6 %far_half_back_one.1 = (f32[1792,512]{1,0:T(8,128)S(1)}, f32[8,128]{1,0:T(8,128)}) custom-call(s32[7]{0:T(128)S(1)} %copy-done.33, bf16[1792,512]{1,0:T(8,128)(2,1)} %collective-permute-done.30.refs_1_, bf16[512,512]{1,0:T(8,128)(2,1)S(1)} %copy-done.29, f32[1792,512]{1,0:T(8,128)S(1)} %get-tuple-element.215.refs_3_, ...), custom_call_target="tpu_custom_call" | custom-call | flops 1000000 | bytes 1000 | tf_op jit(solution)/shard_map/far_half_back_one/pallas_call | solution.py:45
  292.8 2.6 backward_one.1
  302.4 4.8 %place_two.1 = (f32[2048,512]{1,0:T(8,128)}, f32[8,128]{1,0:T(8,128)}) custom-call(s32[7]{0:T(128)} %copy-done.31, bf16[512,512]{1,0:T(8,128)(2,1)} %copy-done.36, bf16[512,512]{1,0:T(8,128)(2,1)} %collective-permute-done.41.refs_2_, bf16[512,512]{1,0:T(8,128)(2,1)} %copy-done.35, bf16[512,512]{1,0:T(8,128)(2,1)} %copy-done.54, f32[8,128]{1,0:T(8,128)} %copy-done.48, ...), custom_call_target="tpu_custom_call" | custom-call | flops 1000000 | bytes 1000 | tf_op jit(solution)/shard_map/place_two/pallas_call | solution.py:45
  307.2 4.9 %collective-permute-done.38.refs_2_ = bf16[512,512]{1,0:T(8,128)(2,1)S(1)} collective-permute-done((bf16[512,512]{1,0:T(8,128)(2,1)S(1)}, bf16[512,512]{1,0:T(8,128)(2,1)S(1)}, u32[]{:S(2)}, u32[]{:S(2)}) %collective-permute-start.38) | collective-permute-done | bytes 524320 | tf_op jit(solution)/shard_map/ppermute | solution.py:633
  313.3 3.1 place_one.1
  (210 shorter events, 61.1 us)
Async XLA Ops:
  0.6 14.6 %collective-permute-start.1 = (bf16[1792,512]{1,0:T(8,128)(2,1)}, bf16[1792,512]{1,0:T(8,128)(2,1)S(1)}, u32[]{:S(2)}, u32[]{:S(2)}) collective-permute-start(bf16[1792,512]{1,0:T(8,128)(2,1)} %refs_1_.11), channel_id=1, source_target_pairs={{0,1},{1,0},{2,3},{3,2},{4,5},{5,4},{6,7},{7,6},{8,9},{9,8},{10,11... | collective-permute-start | bytes 5505032 | tf_op jit(solution)/shard_map/ppermute | solution.py:633
  1.2 43.5 %collective-permute-start = (bf16[1792,512]{1,0:T(8,128)(2,1)}, bf16[1792,512]{1,0:T(8,128)(2,1)}, u32[]{:S(2)}, u32[]{:S(2)}) collective-permute-start(bf16[1792,512]{1,0:T(8,128)(2,1)} %refs_1_.11), channel_id=1, source_target_pairs={{0,2},{1,3},{2,0},{3,1},{4,6},{5,7},{6,4},{7,5},{8,10},{9,11},{10,... | collective-permute-start | bytes 5505032 | tf_op jit(solution)/shard_map/ppermute | solution.py:633
  4.6 99.2 %copy-start.31 = (s32[7]{0:T(128)}, s32[7]{0:T(128)S(1)}, u32[]{:S(2)}) copy-start(s32[7]{0:T(128)S(1)} %stack.31.refs_0_) | copy-start | bytes 88
  13.5 90.3 %copy-start.18 = (f32[14,128,128]{2,1,0:T(8,128)}, f32[14,128,128]{2,1,0:T(8,128)S(1)}, u32[]{:S(2)}) copy-start(f32[14,128,128]{2,1,0:T(8,128)S(1)} %get-tuple-element.131.refs_5_.refs_6_.refs_2_) | copy-start | bytes 2752516
  44.7 4.0 %collective-permute-start.2 = (bf16[1792,512]{1,0:T(8,128)(2,1)}, bf16[1792,512]{1,0:T(8,128)(2,1)S(1)}, u32[]{:S(2)}, u32[]{:S(2)}) collective-permute-start(bf16[1792,512]{1,0:T(8,128)(2,1)} %collective-permute-done.refs_1_.refs_3_), channel_id=1, source_target_pairs={{0,1},{1,0},{2,3},{3,2},{4,5},{5,4},{6,7},{7,6},{8,9},{9,8},{10,11... | collective-permute-start | bytes 5505032 | tf_op jit(solution)/shard_map/ppermute | solution.py:633
  53.1 16.8 %collective-permute-start.3 = (bf16[640,512]{1,0:T(8,128)(2,1)S(1)}, bf16[640,512]{1,0:T(8,128)(2,1)S(1)}, u32[]{:S(2)}, u32[]{:S(2)}) collective-permute-start(bf16[640,512]{1,0:T(8,128)(2,1)S(1)} %get-tuple-element.133), channel_id=1, source_target_pairs={{0,2},{1,3},{2,0},{3,1},{4,6},{5,7},{6,4},{7,5},{8,10},{9,11},{10,... | collective-permute-start | bytes 1966088 | tf_op jit(solution)/shard_map/ppermute | solution.py:633
  67.8 126.8 %copy-start.23 = (f32[8,8,512]{2,1,0:T(8,128)}, f32[8,8,512]{2,1,0:T(8,128)S(1)}, u32[]{:S(2)}) copy-start(f32[8,8,512]{2,1,0:T(8,128)S(1)} %all_to_all.20.refs_1_.refs_2_.refs_4_) | copy-start | bytes 393220
  71.1 3.8 %collective-permute-start.5 = (bf16[1792,512]{1,0:T(8,128)(2,1)S(1)}, bf16[1792,512]{1,0:T(8,128)(2,1)S(1)}, u32[]{:S(2)}, u32[]{:S(2)}) collective-permute-start(bf16[1792,512]{1,0:T(8,128)(2,1)S(1)} %get-tuple-element.139.refs_1_), channel_id=1, source_target_pairs={{0,1},{1,0},{2,3},{3,2},{4,5},{5,4},{6,7},{7,6},{8,9},{9,8},{10,11... | collective-permute-start | bytes 5505032 | tf_op jit(solution)/shard_map/ppermute | solution.py:633
  71.1 28.7 %collective-permute-start.4 = (bf16[1168,512]{1,0:T(8,128)(2,1)S(1)}, bf16[1168,512]{1,0:T(8,128)(2,1)S(1)}, u32[]{:S(2)}, u32[]{:S(2)}) collective-permute-start(bf16[1168,512]{1,0:T(8,128)(2,1)S(1)} %get-tuple-element.136), channel_id=1, source_target_pairs={{0,2},{1,3},{2,0},{3,1},{4,6},{5,7},{6,4},{7,5},{8,10},{9,11},{10,... | collective-permute-start | bytes 3588104 | tf_op jit(solution)/shard_map/ppermute | solution.py:633
  99.9 3.9 %collective-permute-start.7 = (bf16[1168,512]{1,0:T(8,128)(2,1)S(1)}, bf16[1168,512]{1,0:T(8,128)(2,1)S(1)}, u32[]{:S(2)}, u32[]{:S(2)}) collective-permute-start(bf16[1168,512]{1,0:T(8,128)(2,1)S(1)} %collective-permute-done.4.refs_2_), channel_id=1, source_target_pairs={{0,1},{1,0},{2,3},{3,2},{4,5},{5,4},{6,7},{7,6},{8,9},{9,8},{10,11... | collective-permute-start | bytes 3588104 | tf_op jit(solution)/shard_map/ppermute | solution.py:633
  99.9 3.9 %collective-permute-start.6 = (bf16[640,512]{1,0:T(8,128)(2,1)S(1)}, bf16[640,512]{1,0:T(8,128)(2,1)S(1)}, u32[]{:S(2)}, u32[]{:S(2)}) collective-permute-start(bf16[640,512]{1,0:T(8,128)(2,1)S(1)} %collective-permute-done.3.refs_5_.refs_1_), channel_id=1, source_target_pairs={{0,1},{1,0},{2,3},{3,2},{4,5},{5,4},{6,7},{7,6},{8,9},{9,8},{10,11... | collective-permute-start | bytes 1966088 | tf_op jit(solution)/shard_map/ppermute | solution.py:633
  107.6 27.7 %collective-permute-start.8 = (bf16[512,512]{1,0:T(8,128)(2,1)S(1)}, bf16[512,512]{1,0:T(8,128)(2,1)S(1)}, u32[]{:S(2)}, u32[]{:S(2)}) collective-permute-start(bf16[512,512]{1,0:T(8,128)(2,1)S(1)} %get-tuple-element.156), channel_id=1, source_target_pairs={{0,2},{1,3},{2,0},{3,1},{4,6},{5,7},{6,4},{7,5},{8,10},{9,11},{10,... | collective-permute-start | bytes 1572872 | tf_op jit(solution)/shard_map/ppermute | solution.py:633
  109.4 25.9 %collective-permute-start.9 = (bf16[512,512]{1,0:T(8,128)(2,1)S(1)}, bf16[512,512]{1,0:T(8,128)(2,1)S(1)}, u32[]{:S(2)}, u32[]{:S(2)}) collective-permute-start(bf16[512,512]{1,0:T(8,128)(2,1)S(1)} %get-tuple-element.157), channel_id=1, source_target_pairs={{0,2},{1,3},{2,0},{3,1},{4,6},{5,7},{6,4},{7,5},{8,10},{9,11},{10,... | collective-permute-start | bytes 1572872 | tf_op jit(solution)/shard_map/ppermute | solution.py:633
  142.2 15.7 %collective-permute-start.12 = (bf16[1792,512]{1,0:T(8,128)(2,1)}, bf16[1792,512]{1,0:T(8,128)(2,1)}, u32[]{:S(2)}, u32[]{:S(2)}) collective-permute-start(bf16[1792,512]{1,0:T(8,128)(2,1)} %get-tuple-element.158.refs_5_.refs_1_), channel_id=1, source_target_pairs={{0,1},{1,0},{2,3},{3,2},{4,5},{5,4},{6,7},{7,6},{8,9},{9,8},{10,11... | collective-permute-start | bytes 5505032 | tf_op jit(solution)/shard_map/ppermute | solution.py:633
  142.2 42.7 %collective-permute-start.10 = (bf16[1792,512]{1,0:T(8,128)(2,1)}, bf16[1792,512]{1,0:T(8,128)(2,1)}, u32[]{:S(2)}, u32[]{:S(2)}) collective-permute-start(bf16[1792,512]{1,0:T(8,128)(2,1)} %get-tuple-element.158.refs_5_.refs_1_), channel_id=1, source_target_pairs={{0,2},{1,3},{2,0},{3,1},{4,6},{5,7},{6,4},{7,5},{8,10},{9,11},{10,... | collective-permute-start | bytes 5505032 | tf_op jit(solution)/shard_map/ppermute | solution.py:633
  143.8 14.1 %collective-permute-start.13 = (bf16[512,512]{1,0:T(8,128)(2,1)}, bf16[512,512]{1,0:T(8,128)(2,1)S(1)}, u32[]{:S(2)}, u32[]{:S(2)}) collective-permute-start(bf16[512,512]{1,0:T(8,128)(2,1)} %copy-done.53), channel_id=1, source_target_pairs={{0,1},{1,0},{2,3},{3,2},{4,5},{5,4},{6,7},{7,6},{8,9},{9,8},{10,11... | collective-permute-start | bytes 1572872 | tf_op jit(solution)/shard_map/ppermute | solution.py:633
  150.2 14.6 %collective-permute-start.15 = (bf16[512,512]{1,0:T(8,128)(2,1)}, bf16[512,512]{1,0:T(8,128)(2,1)}, u32[]{:S(2)}, u32[]{:S(2)}) collective-permute-start(bf16[512,512]{1,0:T(8,128)(2,1)} %get-tuple-element.171), channel_id=1, source_target_pairs={{0,8},{4,12},{8,0},{12,4},{16,24},{20,28},{24,16},{28,20},{1,9},{5... | collective-permute-start | bytes 1572872 | tf_op jit(solution)/shard_map/ppermute | solution.py:633
  150.3 17.5 %collective-permute-start.11 = (bf16[512,512]{1,0:T(8,128)(2,1)}, bf16[512,512]{1,0:T(8,128)(2,1)}, u32[]{:S(2)}, u32[]{:S(2)}) collective-permute-start(bf16[512,512]{1,0:T(8,128)(2,1)} %get-tuple-element.163), channel_id=1, source_target_pairs={{0,4},{4,0},{8,12},{12,8},{16,20},{20,16},{24,28},{28,24},{1,5},{5... | collective-permute-start | bytes 1572872 | tf_op jit(solution)/shard_map/ppermute | solution.py:633
  164.1 26.5 %copy-start.27 = (bf16[512,512]{1,0:T(8,128)(2,1)S(1)}, bf16[512,512]{1,0:T(8,128)(2,1)}, u32[]{:S(2)}) copy-start(bf16[512,512]{1,0:T(8,128)(2,1)} %copy-done.26) | copy-start | bytes 1572868
  166.4 14.4 %collective-permute-start.16 = (bf16[256,512]{1,0:T(8,128)(2,1)S(1)}, bf16[256,512]{1,0:T(8,128)(2,1)S(1)}, u32[]{:S(2)}, u32[]{:S(2)}) collective-permute-start(bf16[256,512]{1,0:T(8,128)(2,1)S(1)} %get-tuple-element.175), channel_id=1, source_target_pairs={{0,16},{4,20},{8,24},{12,28},{16,0},{20,4},{24,8},{28,12},{1,17},{... | collective-permute-start | bytes 786440 | tf_op jit(solution)/shard_map/ppermute | solution.py:633
  169.5 13.2 %collective-permute-start.14 = (bf16[256,512]{1,0:T(8,128)(2,1)S(1)}, bf16[256,512]{1,0:T(8,128)(2,1)S(1)}, u32[]{:S(2)}, u32[]{:S(2)}) collective-permute-start(bf16[256,512]{1,0:T(8,128)(2,1)S(1)} %get-tuple-element.168), channel_id=1, source_target_pairs={{0,8},{4,12},{8,0},{12,4},{16,24},{20,28},{24,16},{28,20},{1,9},{5... | collective-permute-start | bytes 786440 | tf_op jit(solution)/shard_map/ppermute | solution.py:633
  184.9 9.6 %collective-permute-start.17 = (bf16[1792,512]{1,0:T(8,128)(2,1)}, bf16[1792,512]{1,0:T(8,128)(2,1)S(1)}, u32[]{:S(2)}, u32[]{:S(2)}) collective-permute-start(bf16[1792,512]{1,0:T(8,128)(2,1)} %collective-permute-done.10.refs_1_), channel_id=1, source_target_pairs={{0,1},{1,0},{2,3},{3,2},{4,5},{5,4},{6,7},{7,6},{8,9},{9,8},{10,11... | collective-permute-start | bytes 5505032 | tf_op jit(solution)/shard_map/ppermute | solution.py:633
  184.9 4.2 %collective-permute-start.18 = (bf16[512,512]{1,0:T(8,128)(2,1)S(1)}, bf16[512,512]{1,0:T(8,128)(2,1)S(1)}, u32[]{:S(2)}, u32[]{:S(2)}) collective-permute-start(bf16[512,512]{1,0:T(8,128)(2,1)S(1)} %copy-done.59), channel_id=1, source_target_pairs={{0,1},{1,0},{2,3},{3,2},{4,5},{5,4},{6,7},{7,6},{8,9},{9,8},{10,11... | collective-permute-start | bytes 1572872 | tf_op jit(solution)/shard_map/ppermute | solution.py:633
  185.5 14.7 %collective-permute-start.23 = (bf16[256,512]{1,0:T(8,128)(2,1)S(1)}, bf16[256,512]{1,0:T(8,128)(2,1)S(1)}, u32[]{:S(2)}, u32[]{:S(2)}) collective-permute-start(bf16[256,512]{1,0:T(8,128)(2,1)S(1)} %get-tuple-element.190.refs_1_), channel_id=1, source_target_pairs={{0,4},{4,0},{8,12},{12,8},{16,20},{20,16},{24,28},{28,24},{1,5},{5... | collective-permute-start | bytes 786440 | tf_op jit(solution)/shard_map/ppermute | solution.py:633
  185.7 15.6 %collective-permute-start.21 = (bf16[256,512]{1,0:T(8,128)(2,1)S(1)}, bf16[256,512]{1,0:T(8,128)(2,1)S(1)}, u32[]{:S(2)}, u32[]{:S(2)}) collective-permute-start(bf16[256,512]{1,0:T(8,128)(2,1)S(1)} %get-tuple-element.187.refs_1_), channel_id=1, source_target_pairs={{0,16},{4,20},{8,24},{12,28},{16,0},{20,4},{24,8},{28,12},{1,17},{... | collective-permute-start | bytes 786440 | tf_op jit(solution)/shard_map/ppermute | solution.py:633
  187.0 30.7 %collective-permute-start.19 = (bf16[512,512]{1,0:T(8,128)(2,1)}, bf16[512,512]{1,0:T(8,128)(2,1)S(1)}, u32[]{:S(2)}, u32[]{:S(2)}) collective-permute-start(bf16[512,512]{1,0:T(8,128)(2,1)} %get-tuple-element.185), channel_id=1, source_target_pairs={{0,2},{1,3},{2,0},{3,1},{4,6},{5,7},{6,4},{7,5},{8,10},{9,11},{10,... | collective-permute-start | bytes 1572872 | tf_op jit(solution)/shard_map/ppermute | solution.py:633
  189.1 28.6 %collective-permute-start.20 = (bf16[512,512]{1,0:T(8,128)(2,1)}, bf16[512,512]{1,0:T(8,128)(2,1)}, u32[]{:S(2)}, u32[]{:S(2)}) collective-permute-start(bf16[512,512]{1,0:T(8,128)(2,1)} %get-tuple-element.186), channel_id=1, source_target_pairs={{0,2},{1,3},{2,0},{3,1},{4,6},{5,7},{6,4},{7,5},{8,10},{9,11},{10,... | collective-permute-start | bytes 1572872 | tf_op jit(solution)/shard_map/ppermute | solution.py:633
  200.8 14.7 %collective-permute-start.24 = (bf16[256,512]{1,0:T(8,128)(2,1)S(1)}, bf16[256,512]{1,0:T(8,128)(2,1)S(1)}, u32[]{:S(2)}, u32[]{:S(2)}) collective-permute-start(bf16[256,512]{1,0:T(8,128)(2,1)S(1)} %get-tuple-element.193.refs_1_), channel_id=1, source_target_pairs={{0,16},{4,20},{8,24},{12,28},{16,0},{20,4},{24,8},{28,12},{1,17},{... | collective-permute-start | bytes 786440 | tf_op jit(solution)/shard_map/ppermute | solution.py:633
  201.9 14.4 %collective-permute-start.22 = (bf16[256,512]{1,0:T(8,128)(2,1)S(1)}, bf16[256,512]{1,0:T(8,128)(2,1)S(1)}, u32[]{:S(2)}, u32[]{:S(2)}) collective-permute-start(bf16[256,512]{1,0:T(8,128)(2,1)S(1)} %get-tuple-element.188.refs_1_), channel_id=1, source_target_pairs={{0,8},{4,12},{8,0},{12,4},{16,24},{20,28},{24,16},{28,20},{1,9},{5... | collective-permute-start | bytes 786440 | tf_op jit(solution)/shard_map/ppermute | solution.py:633
  203.2 14.7 %all-to-all-start.3 = ((f32[8,8,512]{2,1,0:T(8,128)}), f32[8,8,512]{2,1,0:T(8,128)S(1)}, u32[]{:S(2)}, u32[]{:S(2)}) async-start(f32[8,8,512]{2,1,0:T(8,128)} %get-tuple-element.184.refs_3_), calls=%async_computation.3 | async-start | bytes 262144 | tf_op jit(solution)/shard_map/all_to_all | solution.py:125
  223.8 33.7 %collective-permute-start.25 = (bf16[1792,512]{1,0:T(8,128)(2,1)}, bf16[1792,512]{1,0:T(8,128)(2,1)}, u32[]{:S(2)}, u32[]{:S(2)}) collective-permute-start(bf16[1792,512]{1,0:T(8,128)(2,1)} %get-tuple-element.195.refs_5_.refs_1_), channel_id=1, source_target_pairs={{0,1},{1,0},{2,3},{3,2},{4,5},{5,4},{6,7},{7,6},{8,9},{9,8},{10,11... | collective-permute-start | bytes 5505032 | tf_op jit(solution)/shard_map/ppermute | solution.py:633
  223.8 45.4 %collective-permute-start.30 = (bf16[1792,512]{1,0:T(8,128)(2,1)}, bf16[1792,512]{1,0:T(8,128)(2,1)}, u32[]{:S(2)}, u32[]{:S(2)}) collective-permute-start(bf16[1792,512]{1,0:T(8,128)(2,1)} %get-tuple-element.195.refs_5_.refs_1_), channel_id=1, source_target_pairs={{0,2},{1,3},{2,0},{3,1},{4,6},{5,7},{6,4},{7,5},{8,10},{9,11},{10,... | collective-permute-start | bytes 5505032 | tf_op jit(solution)/shard_map/ppermute | solution.py:633
  224.5 14.8 %collective-permute-start.27 = (bf16[512,512]{1,0:T(8,128)(2,1)S(1)}, bf16[512,512]{1,0:T(8,128)(2,1)S(1)}, u32[]{:S(2)}, u32[]{:S(2)}) collective-permute-start(bf16[512,512]{1,0:T(8,128)(2,1)S(1)} %get-tuple-element.198.refs_3_), channel_id=1, source_target_pairs={{0,8},{4,12},{8,0},{12,4},{16,24},{20,28},{24,16},{28,20},{1,9},{5... | collective-permute-start | bytes 1572872 | tf_op jit(solution)/shard_map/ppermute | solution.py:633
  230.9 18.9 %collective-permute-start.29 = (bf16[512,512]{1,0:T(8,128)(2,1)}, bf16[512,512]{1,0:T(8,128)(2,1)}, u32[]{:S(2)}, u32[]{:S(2)}) collective-permute-start(bf16[512,512]{1,0:T(8,128)(2,1)} %get-tuple-element.203), channel_id=1, source_target_pairs={{0,8},{4,12},{8,0},{12,4},{16,24},{20,28},{24,16},{28,20},{1,9},{5... | collective-permute-start | bytes 1572872 | tf_op jit(solution)/shard_map/ppermute | solution.py:633
  232.8 21.2 %collective-permute-start.28 = (bf16[512,512]{1,0:T(8,128)(2,1)}, bf16[512,512]{1,0:T(8,128)(2,1)S(1)}, u32[]{:S(2)}, u32[]{:S(2)}) collective-permute-start(bf16[512,512]{1,0:T(8,128)(2,1)} %get-tuple-element.200), channel_id=1, source_target_pairs={{0,4},{4,0},{8,12},{12,8},{16,20},{20,16},{24,28},{28,24},{1,5},{5... | collective-permute-start | bytes 1572872 | tf_op jit(solution)/shard_map/ppermute | solution.py:633
  239.3 18.2 %collective-permute-start.26 = (bf16[512,512]{1,0:T(8,128)(2,1)}, bf16[512,512]{1,0:T(8,128)(2,1)S(1)}, u32[]{:S(2)}, u32[]{:S(2)}) collective-permute-start(bf16[512,512]{1,0:T(8,128)(2,1)} %get-tuple-element.196), channel_id=1, source_target_pairs={{0,1},{1,0},{2,3},{3,2},{4,5},{5,4},{6,7},{7,6},{8,9},{9,8},{10,11... | collective-permute-start | bytes 1572872 | tf_op jit(solution)/shard_map/ppermute | solution.py:633
  252.6 14.0 %collective-permute-start.32 = (bf16[256,512]{1,0:T(8,128)(2,1)S(1)}, bf16[256,512]{1,0:T(8,128)(2,1)S(1)}, u32[]{:S(2)}, u32[]{:S(2)}) collective-permute-start(bf16[256,512]{1,0:T(8,128)(2,1)S(1)} %get-tuple-element.212), channel_id=1, source_target_pairs={{0,16},{4,20},{8,24},{12,28},{16,0},{20,4},{24,8},{28,12},{1,17},{... | collective-permute-start | bytes 786440 | tf_op jit(solution)/shard_map/ppermute | solution.py:633
  255.7 12.8 %collective-permute-start.31 = (bf16[256,512]{1,0:T(8,128)(2,1)S(1)}, bf16[256,512]{1,0:T(8,128)(2,1)S(1)}, u32[]{:S(2)}, u32[]{:S(2)}) collective-permute-start(bf16[256,512]{1,0:T(8,128)(2,1)S(1)} %get-tuple-element.208), channel_id=1, source_target_pairs={{0,8},{4,12},{8,0},{12,4},{16,24},{20,28},{24,16},{28,20},{1,9},{5... | collective-permute-start | bytes 786440 | tf_op jit(solution)/shard_map/ppermute | solution.py:633
  264.2 25.0 %copy-start.29 = (bf16[512,512]{1,0:T(8,128)(2,1)S(1)}, bf16[512,512]{1,0:T(8,128)(2,1)}, u32[]{:S(2)}) copy-start(bf16[512,512]{1,0:T(8,128)(2,1)} %copy-done.28) | copy-start | bytes 1572868
  269.1 23.7 %collective-permute-start.35 = (bf16[1792,512]{1,0:T(8,128)(2,1)}, bf16[1792,512]{1,0:T(8,128)(2,1)S(1)}, u32[]{:S(2)}, u32[]{:S(2)}) collective-permute-start(bf16[1792,512]{1,0:T(8,128)(2,1)} %collective-permute-done.30.refs_1_), channel_id=1, source_target_pairs={{0,1},{1,0},{2,3},{3,2},{4,5},{5,4},{6,7},{7,6},{8,9},{9,8},{10,11... | collective-permute-start | bytes 5505032 | tf_op jit(solution)/shard_map/ppermute | solution.py:633
  269.2 23.6 %collective-permute-start.36 = (bf16[512,512]{1,0:T(8,128)(2,1)}, bf16[512,512]{1,0:T(8,128)(2,1)S(1)}, u32[]{:S(2)}, u32[]{:S(2)}) collective-permute-start(bf16[512,512]{1,0:T(8,128)(2,1)} %collective-permute-done.20.refs_9_), channel_id=1, source_target_pairs={{0,1},{1,0},{2,3},{3,2},{4,5},{5,4},{6,7},{7,6},{8,9},{9,8},{10,11... | collective-permute-start | bytes 1572872 | tf_op jit(solution)/shard_map/ppermute | solution.py:633
  269.7 13.8 %collective-permute-start.33 = (bf16[256,512]{1,0:T(8,128)(2,1)S(1)}, bf16[256,512]{1,0:T(8,128)(2,1)S(1)}, u32[]{:S(2)}, u32[]{:S(2)}) collective-permute-start(bf16[256,512]{1,0:T(8,128)(2,1)S(1)} %get-tuple-element.218.refs_1_), channel_id=1, source_target_pairs={{0,16},{4,20},{8,24},{12,28},{16,0},{20,4},{24,8},{28,12},{1,17},{... | collective-permute-start | bytes 786440 | tf_op jit(solution)/shard_map/ppermute | solution.py:633
  269.7 14.5 %collective-permute-start.34 = (bf16[256,512]{1,0:T(8,128)(2,1)S(1)}, bf16[256,512]{1,0:T(8,128)(2,1)S(1)}, u32[]{:S(2)}, u32[]{:S(2)}) collective-permute-start(bf16[256,512]{1,0:T(8,128)(2,1)S(1)} %get-tuple-element.220.refs_1_), channel_id=1, source_target_pairs={{0,4},{4,0},{8,12},{12,8},{16,20},{20,16},{24,28},{28,24},{1,5},{5... | collective-permute-start | bytes 786440 | tf_op jit(solution)/shard_map/ppermute | solution.py:633
  284.1 12.8 %collective-permute-start.37 = (bf16[256,512]{1,0:T(8,128)(2,1)S(1)}, bf16[256,512]{1,0:T(8,128)(2,1)S(1)}, u32[]{:S(2)}, u32[]{:S(2)}) collective-permute-start(bf16[256,512]{1,0:T(8,128)(2,1)S(1)} %get-tuple-element.224.refs_1_), channel_id=1, source_target_pairs={{0,8},{4,12},{8,0},{12,4},{16,24},{20,28},{24,16},{28,20},{1,9},{5... | collective-permute-start | bytes 786440 | tf_op jit(solution)/shard_map/ppermute | solution.py:633
  284.8 14.9 %collective-permute-start.39 = (bf16[256,512]{1,0:T(8,128)(2,1)S(1)}, bf16[256,512]{1,0:T(8,128)(2,1)S(1)}, u32[]{:S(2)}, u32[]{:S(2)}) collective-permute-start(bf16[256,512]{1,0:T(8,128)(2,1)S(1)} %get-tuple-element.227.refs_1_), channel_id=1, source_target_pairs={{0,16},{4,20},{8,24},{12,28},{16,0},{20,4},{24,8},{28,12},{1,17},{... | collective-permute-start | bytes 786440 | tf_op jit(solution)/shard_map/ppermute | solution.py:633
  287.6 14.8 %collective-permute-start.41 = (bf16[512,512]{1,0:T(8,128)(2,1)S(1)}, bf16[512,512]{1,0:T(8,128)(2,1)}, u32[]{:S(2)}, u32[]{:S(2)}) collective-permute-start(bf16[512,512]{1,0:T(8,128)(2,1)S(1)} %copy-done.37), channel_id=1, source_target_pairs={{0,4},{4,0},{8,12},{12,8},{16,20},{20,16},{24,28},{28,24},{1,5},{5... | collective-permute-start | bytes 1572872 | tf_op jit(solution)/shard_map/ppermute | solution.py:633
  297.5 14.6 %collective-permute-start.38 = (bf16[512,512]{1,0:T(8,128)(2,1)S(1)}, bf16[512,512]{1,0:T(8,128)(2,1)S(1)}, u32[]{:S(2)}, u32[]{:S(2)}) collective-permute-start(bf16[512,512]{1,0:T(8,128)(2,1)S(1)} %get-tuple-element.226.refs_1_), channel_id=1, source_target_pairs={{0,4},{4,0},{8,12},{12,8},{16,20},{20,16},{24,28},{28,24},{1,5},{5... | collective-permute-start | bytes 1572872 | tf_op jit(solution)/shard_map/ppermute | solution.py:633
  300.3 13.1 %collective-permute-start.40 = (bf16[512,512]{1,0:T(8,128)(2,1)S(1)}, bf16[512,512]{1,0:T(8,128)(2,1)S(1)}, u32[]{:S(2)}, u32[]{:S(2)}) collective-permute-start(bf16[512,512]{1,0:T(8,128)(2,1)S(1)} %get-tuple-element.228.refs_3_), channel_id=1, source_target_pairs={{0,8},{4,12},{8,0},{12,4},{16,24},{20,28},{24,16},{28,20},{1,9},{5... | collective-permute-start | bytes 1572872 | tf_op jit(solution)/shard_map/ppermute | solution.py:633
  (55 other events, 394.1 us)

commit v8 on v7

--- a/solution.py
+++ b/solution.py
@@ -109,8 +109,8 @@
     )
 
 
-def combine(g_ref):
-    mref, first, second, count = (g_ref[:, k, :] for k in range(4))
+def combine(g_ref, columns):
+    mref, first, second, count = (unpacked(g_ref, k, columns) for k in range(4))
     shift = first / count
     mean_each = mref + shift
     spread_each = second - first * shift
@@ -125,18 +125,27 @@
     return lax.all_to_all(copies, axis, split_axis=0, concat_axis=0, tiled=True)
 
 
-def copies_shape(columns):
-    return (lax.axis_size("row"), 8, columns)
+def copies_shape(columns, count):
+    rows = count * columns // LANES
+    return (lax.axis_size("row"), rows + -rows % 8, LANES)
 
 
 def spread_rows(out_ref, rows):
-    block = jnp.concatenate([*rows, jnp.zeros((8 - len(rows), out_ref.shape[2]), F32)], axis=0)
+    pieces = [row[:, j : j + LANES] for row in rows for j in range(0, row.shape[1], LANES)]
+    if len(pieces) < out_ref.shape[1]:
+        pieces.append(jnp.zeros((out_ref.shape[1] - len(pieces), LANES), F32))
+    block = jnp.concatenate(pieces, axis=0)
 
     def one(n, carry):
         out_ref[n] = block
         return carry
 
     lax.fori_loop(0, out_ref.shape[0], one, 0)
+
+
+def unpacked(ref, k, columns):
+    per = columns // LANES
+    return jnp.concatenate([ref[:, k * per + j, :] for j in range(per)], axis=1)
 
 
 def split(value):
@@ -334,8 +343,8 @@
     tile = pl.BlockSpec((big, SLOT, SLOT), lambda i, ids: (i, 0, 0))
     double = pl.BlockSpec((big, SLOT, 2 * SLOT), lambda i, ids: (i, 0, 0))
     _, block = weight_block(weight, 3)
-    outs = [flat, pl.BlockSpec(copies_shape(columns), lambda i, ids: (0, 0, 0))]
-    shapes = [jax.ShapeDtypeStruct((nodes, columns), F32), jax.ShapeDtypeStruct(copies_shape(columns), F32)]
+    outs = [flat, pl.BlockSpec(copies_shape(columns, 4), lambda i, ids: (0, 0, 0))]
+    shapes = [jax.ShapeDtypeStruct((nodes, columns), F32), jax.ShapeDtypeStruct(copies_shape(columns, 4), F32)]
     if got:
         outs.append(to)
         shapes.append(jax.ShapeDtypeStruct((nodes, depth), BF))
@@ -355,7 +364,7 @@
 
 
 def columns_of(g_ref, gamma_ref, beta_ref, co_ref):
-    total, mean, inv_std = combine(g_ref)
+    total, mean, inv_std = combine(g_ref, gamma_ref.shape[1])
     put(co_ref, 0, mean)
     put(co_ref, 1, 0.5 * gamma_ref[...] * inv_std)
     put(co_ref, 2, 0.5 * beta_ref[...])
@@ -378,7 +387,8 @@
     mark(token_ref)
     columns_of(g_ref, gamma_ref, beta_ref, co_ref)
     scale = at(co_ref, 1)
-    shift = (st_ref[0, 0:1, :] - at(co_ref, 0)) * scale + at(co_ref, 2)
+    reference = unpacked(st_ref, 0, scale.shape[1])
+    shift = (reference - at(co_ref, 0)) * scale + at(co_ref, 2)
     rows = [*split_three(scale), *split_three(shift)]
     rows.append(jnp.zeros((TAIL - len(rows), scale.shape[1]), BF))
     out_ref[...] = jnp.concatenate([r.astype(F32) for r in rows], axis=0).astype(BF)
@@ -390,7 +400,7 @@
     return pl.pallas_call(
         lambda *refs: coefs_kernel(*refs[: len(args)], *refs[len(args) + len(tokens) :]),
         grid=(1,),
-        in_specs=[pl.BlockSpec((1, 8, columns), lambda i: (0, 0, 0))]
+        in_specs=[pl.BlockSpec((1,) + stats.shape[1:], lambda i: (0, 0, 0))]
         + [pl.BlockSpec(v.shape, lambda i, n=v.ndim: (0,) * n) for v in norm]
         + [pl.BlockSpec(memory_space=pl.ANY)] * (1 + len(tokens)),
         out_specs=[pl.BlockSpec((TAIL, columns), lambda i: (nodes // TAIL - 1, 0)), token_spec()],
@@ -448,10 +458,9 @@
     @pl.when(pl.program_id(0) == 0)
     def _():
         columns_of(g_ref, gamma_ref, beta_ref, co_ref)
-        sg = sg_ref[...]
         twice = 2.0 / at(co_ref, 4)
-        put(co_ref, 5, twice * jnp.sum(sg[:, 0, :], axis=0, keepdims=True))
-        put(co_ref, 6, twice * at(co_ref, 3) * jnp.sum(sg[:, 1, :], axis=0, keepdims=True))
+        put(co_ref, 5, twice * jnp.sum(unpacked(sg_ref, 0, lin_ref.shape[1]), axis=0, keepdims=True))
+        put(co_ref, 6, twice * at(co_ref, 3) * jnp.sum(unpacked(sg_ref, 1, lin_ref.shape[1]), axis=0, keepdims=True))
 
     columns = lin_ref.shape[1]
 
@@ -477,8 +486,8 @@
     ins += [pl.BlockSpec((big,) + t.shape[1:], lambda i: (i, 0, 0)) for t in tiles]
     ins += [pl.BlockSpec(s.shape, lambda i, n=s.ndim: (0,) * n) for s in smalls]
     if out_dtype is None:
-        out_spec = pl.BlockSpec(copies_shape(columns), lambda i: (0, 0, 0))
-        out_shape = jax.ShapeDtypeStruct(copies_shape(columns), F32)
+        out_spec = pl.BlockSpec(copies_shape(columns, 2), lambda i: (0, 0, 0))
+        out_shape = jax.ShapeDtypeStruct(copies_shape(columns, 2), F32)
     else:
         out_spec = [flat, token_spec()]
         out_shape = [jax.ShapeDtypeStruct((nodes, columns), out_dtype), TOKEN]
@@ -538,8 +547,8 @@
     else:
         ins += [flat, *map(fixed, norm)]
         args += [lin, *norm]
-        out_specs.append(pl.BlockSpec(copies_shape(columns), lambda i: (0, 0, 0)))
-        out_shape.append(jax.ShapeDtypeStruct(copies_shape(columns), F32))
+        out_specs.append(pl.BlockSpec(copies_shape(columns, 2), lambda i: (0, 0, 0)))
+        out_shape.append(jax.ShapeDtypeStruct(copies_shape(columns, 2), F32))
         scratch = [pltpu.VMEM((8, columns), F32), pltpu.VMEM((2, 8, columns), F32)]
     return launch(
         functools.partial(backward_kernel, big, last), (nodes // rows,), ins, out_specs, out_shape, args, name,
@@ -701,37 +710,40 @@
         self.orders = [list(range(self.bits)), list(range(1, self.bits)) + [0]]
         *self.send, self.sent = terms(1, ())
         *self.keep, self.kept = terms(0, (self.sent, *between()))
-        self.stage = 0
+        self.done = [0, 0]
+        self.got = [None, None]
         self.step(())
 
-    def step(self, tokens):
-        s, last = self.stage, self.bits - 1
-        self.stage += 1
-        started = []
-        for n in range(2):
-            rows = self.keep[n].shape[0]
-            call = lambda kernel, sizes: small_call(
-                kernel, self.meta, self.keep[n], self.got[n], sizes, f"{self.name}_{n}_{s}", tokens
-            )
-            if 0 < s < last:
-                fold = functools.partial(fold_kernel, False, self.orders[n][s])
-                self.send[n], self.keep[n], token = call(fold, [rows // 2] * 2)
-            elif s == last or s == last + 1:
-                self.keep[n], token = call(functools.partial(fold_kernel, True, 0), [rows])
-            elif s > last + 1:
-                self.keep[n], token = call(join_kernel, [2 * rows])
-            if s > 0:
-                started.append(token)
+    def advance(self, n, *tokens):
+        s, last = self.done[n], self.bits - 1
+        if s == self.stages:
+            return tokens
+        self.done[n] += 1
+        started = ()
+        rows = self.keep[n].shape[0]
+        call = lambda kernel, sizes: small_call(
+            kernel, self.meta, self.keep[n], self.got[n], sizes, f"{self.name}_{n}_{s}", tokens
+        )
+        if 0 < s < last:
+            fold = functools.partial(fold_kernel, False, self.orders[n][s])
+            self.send[n], self.keep[n], *started = call(fold, [rows // 2] * 2)
+        elif s == last or s == last + 1:
+            self.keep[n], *started = call(functools.partial(fold_kernel, True, 0), [rows])
+        elif s > last + 1:
+            self.keep[n], *started = call(join_kernel, [2 * rows])
         level = s if s <= last else 2 * last - s
         moved = self.send if s < last else self.keep
-        self.got = [across(moved[n], self.axis, 1 << self.orders[n][level]) for n in range(2)]
+        self.got[n] = across(moved[n], self.axis, 1 << self.orders[n][level])
         return tuple(started)
 
+    def step(self, tokens):
+        return (*self.advance(0, *tokens), *self.advance(1, *tokens))
+
     def next(self, *tokens):
-        return self.step(tokens) if self.stage < self.stages else tokens
+        return self.step(tokens) if min(self.done) < self.stages else tokens
 
     def placed(self, limit, tokens=()):
-        while self.stage < self.stages:
+        while min(self.done) < self.stages:
             self.step(())
         blocks = [v for n in range(2) for v in (self.keep[n], self.got[n])]
         return place_blocks(self.meta, blocks, self.orders, f"place_{self.name}", limit, tokens)
@@ -808,7 +820,7 @@
     rows_one, crossing = weight_rows(slices_one)
     early, _ = half(ids, big, [far], [whole_block(rows_two[1])], True, "far_half_back_two", tokens, early)
     grad_one, sums = backward(big, early, beyond, rows_two[2], lin_one, norm_one, "backward_two", tokens)
-    tokens = (*crossing, *sum_two.next(*sum_two.next(sums)))
+    tokens = (*crossing, *sum_two.next(sums))
     grads_one = small_gather(sums, "row")
 
     turned, _ = turn_call(False, big, lin_one, grad_one, tiles, norm_one, grads_one, "turn_one", tokens)
@@ -817,7 +829,7 @@
     def terms_one(other, tokens, h=turned):
         return weight_terms(ids, other, ((features, near_one), (far_one, beyond_one)), h, "terms_one", tokens)
 
-    sum_one = RowSum("row", ids, terms_one, "one", lambda: (sum_two.got[1],))
+    sum_one = RowSum("row", ids, terms_one, "one", lambda: sum_two.next())
     weights = [weight_block(weight_one, 0), whole_block(rows_one[0])]
     early, token = half(ids, big, [turned, near], weights, True, "half_back_one", sum_one.next())
     output, token = rows_call(result_kernel, big, [lin_two], [val], norm_two, F32, [], "output", (token,))
@@ -825,15 +837,16 @@
     far, tokens = after(far, *started)
     beyond = across(far, "col", 1)
     tokens = (*tokens, *sum_one.next())
-    early, _ = half(ids, big, [far], [whole_block(rows_one[1])], True, "far_half_back_one", tokens, early)
+    early, _ = half(ids, big, [far], [whole_block(rows_one[1])], True, "far_half_back_one", (*tokens, sum_two.got[1]), early)
     grad_features, token = backward(big, early, beyond, rows_one[2], None, None, "backward_one", tokens)
-    while sum_one.stage < sum_one.stages - 1:
+    while min(sum_one.done) < sum_one.stages - 1:
         sum_one.next()
     tokens = sum_one.next(token)
     grad_weight_two, _ = sum_two.placed(60, tokens)
     grad_weight_one, _ = sum_one.placed(24)
 
-    sums_one, sums_two = jnp.sum(grads_one, axis=0), jnp.sum(grads_two, axis=0)
+    per = columns // LANES
+    sums_one, sums_two = (jnp.sum(g, axis=0)[: 2 * per].reshape(2, columns) for g in (grads_one, grads_two))
     return (
         output,
         grad_features,

time: 317 us -> 316 us (level)
  waiting for transfers between devices: 109 us -> 101 us
  Pallas kernels: 111 us -> 117 us
    ppermute x42, waiting for transfers between devices: 109 us -> 101 us  [across(): return lax.ppermute(value, axis, [(i, i ^ distance) for i in range(size)])]
    pallas_call x41, Pallas kernels: 111 us -> 117 us  [launch(): pl.pallas_call(body, grid_spec=pltpu.PrefetchScalarGridSpec(num_scalar_pr...]
    unnamed x120 -> x126, local copies, waits for them, and re-layouts: 16.2 us -> 17.3 us
  transfers between devices with their start and end apart: 43 -> 43, of which waited for: 23 -> 20; matrix products, arithmetic and copies ran while one was open for 1% -> 1% of each run, Pallas kernels for 28% -> 30%
where the time goes in v8:
time: 316 us; the launch traced here: 315 us
  Pallas kernels  117 us (37%)
  waiting for transfers between devices  101 us (32%)
  starting transfers between devices  41.4 us (13%)
  blocking collectives  35 us (11%)
  local copies, waits for them, and re-layouts  19.3 us (6%)
    pallas_call x41, Pallas kernels, launch(): pl.pallas_call(body, grid_spec=pltpu.PrefetchScalarGridSpec(num_scalar_pr...  117 us
    ppermute x42, waiting for transfers between devices, across(): return lax.ppermute(value, axis, [(i, i ^ distance) for i in range(size)])  101 us
    ppermute x42, starting transfers between devices, across(): return lax.ppermute(value, axis, [(i, i ^ distance) for i in range(size)])  37.6 us
    all_to_all x3, blocking collectives, small_gather(): return lax.all_to_all(copies, axis, split_axis=0, concat_axis=0, tiled=True)  35 us
    unnamed x126, local copies, waits for them, and re-layouts  17.3 us
  transfers between devices with their start and end apart: 43, of which 20 were waited for; matrix products, arithmetic and copies ran while one was open for 1% of the time, Pallas kernels for 30%

profile of v8, /device:TPU:0, one launch (start us, length us, event | category | flops | bytes accessed | tf_op | source)
XLA Modules:
  0.0 315.1 jit_solution(606601629515506461)
XLA Ops:
  1.2 2.6 collective-permute-start
  4.6 4.9 %tiles.1 = (bf16[14,128,256]{2,1,0:T(8,128)(2,1)S(1)}, bf16[14,128,128]{2,1,0:T(8,128)(2,1)S(1)}, f32[14,128,128]{2,1,0:T(8,128)S(1)}, f32[14,128,128]{2,1,0:T(8,128)S(1)}, f32[8,128]{1,0:T(8,128)S(1)}) custom-call(s32[14,32,128]{2,1,0:T(8,128)S(1)} %bitcast_bitcast_fusion.refs_0_, s32[14,1,128]{2,1,0:T(1,128)S(1)} %reshape.45.refs_1_), custom_call_target="tpu_custom_call" | custom-call | flops 1000000 | bytes 1000 | tf_op jit(solution)/shard_map/tiles/pallas_call | solution.py:45
  16.7 4.0 %half_one.1 = (f32[1792,512]{1,0:T(8,128)S(1)}, f32[8,128]{1,0:T(8,128)S(1)}) custom-call(s32[7]{0:T(128)S(1)} %stack.31.refs_0_, bf16[1792,512]{1,0:T(8,128)(2,1)S(1)} %copy-done.12, bf16[1792,512]{1,0:T(8,128)(2,1)} %collective-permute-done.1.refs_2_, bf16[2048,512]{1,0:T(8,128)(2,1)S(1)} %copy-done.5, bf16[2048,512]{1,0:T(8,128)(2,1)S(1)} %copy-done.5), custom_call_target="tpu_custom_call" | custom-call | flops 1000000 | bytes 1000 | tf_op jit(solution)/shard_map/half_one/pallas_call | solution.py:45
  20.7 24.0 %collective-permute-done.refs_1_.refs_3_ = bf16[1792,512]{1,0:T(8,128)(2,1)} collective-permute-done((bf16[1792,512]{1,0:T(8,128)(2,1)}, bf16[1792,512]{1,0:T(8,128)(2,1)}, u32[]{:S(2)}, u32[]{:S(2)}) %collective-permute-start) | collective-permute-done | bytes 1835040 | tf_op jit(solution)/shard_map/ppermute | solution.py:642
  44.7 3.5 %far_half_one.1 = (f32[1792,512]{1,0:T(8,128)S(1)}, f32[8,128]{1,0:T(8,128)}) custom-call(s32[7]{0:T(128)S(1)} %stack.31.refs_0_, bf16[1792,512]{1,0:T(8,128)(2,1)} %collective-permute-done.refs_1_.refs_3_, bf16[2048,512]{1,0:T(8,128)(2,1)S(1)} %copy-done.5, f32[1792,512]{1,0:T(8,128)S(1)} %get-tuple-element.125.refs_3_, ...), custom_call_target="tpu_custom_call" | custom-call | flops 1000000 | bytes 1000 | tf_op jit(solution)/shard_map/far_half_one/pallas_call | solution.py:45
  48.7 4.4 %forward_one.1 = (f32[1792,512]{1,0:T(8,128)S(1)}, f32[8,16,128]{2,1,0:T(8,128)S(1)}, f32[8,128]{1,0:T(8,128)}, bf16[640,512]{1,0:T(8,128)(2,1)S(1)}, bf16[1168,512]{1,0:T(8,128)(2,1)S(1)}) custom-call(s32[7]{0:T(128)S(1)} %stack.31.refs_0_, f32[1792,512]{1,0:T(8,128)S(1)} %get-tuple-element.129.refs_1_, ...), custom_call_target="tpu_custom_call" | custom-call | flops 1000000 | bytes 1000 | tf_op jit(solution)/shard_map/forward_one/pallas_call | solution.py:45
  54.8 12.5 %all_to_all.20.refs_1_.refs_2_.refs_4_ = f32[8,16,128]{2,1,0:T(8,128)S(1)} all-to-all(f32[8,16,128]{2,1,0:T(8,128)S(1)} %get-tuple-element.134.refs_0_), channel_id=1, replica_groups=mesh['row'=8,'col'=4] {'row'}, dimensions={0} | all-to-all | bytes 131072 | tf_op jit(solution)/shard_map/all_to_all | solution.py:125
  67.3 2.5 collective-permute-done.3.refs_5_.refs_1_
  71.2 1.8 collective-permute-start.4
  73.0 2.0 collective-permute-done.5.refs_2_
  75.0 2.8 half_two.1
  77.8 22.1 %collective-permute-done.4.refs_2_ = bf16[1168,512]{1,0:T(8,128)(2,1)S(1)} collective-permute-done((bf16[1168,512]{1,0:T(8,128)(2,1)S(1)}, bf16[1168,512]{1,0:T(8,128)(2,1)S(1)}, u32[]{:S(2)}, u32[]{:S(2)}) %collective-permute-start.4) | collective-permute-done | bytes 1196064 | tf_op jit(solution)/shard_map/ppermute | solution.py:642
  100.4 2.1 far_half_two.1
  103.9 3.8 %forward_two.1 = (f32[1792,512]{1,0:T(8,128)S(1)}, f32[8,16,128]{2,1,0:T(8,128)S(1)}, bf16[1792,512]{1,0:T(8,128)(2,1)S(1)}, f32[8,128]{1,0:T(8,128)S(1)}) custom-call(s32[7]{0:T(128)S(1)} %stack.31.refs_0_, f32[1792,512]{1,0:T(8,128)S(1)} %get-tuple-element.144.refs_1_, bf16[640,512]{1,0:T(8,128)(2,1)S(1)} %collective-permute-done.6.refs_2_, ...), custom_call_target="tpu_custom_call" | custom-call | flops 1000000 | bytes 1000 | tf_op jit(solution)/shard_map/forward_two/pallas_call | solution.py:45
  107.7 1.8 collective-permute-start.8
  109.8 12.7 %all_to_all.21.refs_3_.refs_4_.refs_2_ = f32[8,16,128]{2,1,0:T(8,128)S(1)} all-to-all(f32[8,16,128]{2,1,0:T(8,128)S(1)} %get-tuple-element.146), channel_id=1, replica_groups=mesh['row'=8,'col'=4] {'row'}, dimensions={0} | all-to-all | bytes 131072 | tf_op jit(solution)/shard_map/all_to_all | solution.py:125
  122.5 2.0 sums_two.1
  124.6 9.7 %all_to_all.22.refs_5_ = f32[8,8,128]{2,1,0:T(8,128)} all-to-all(f32[8,8,128]{2,1,0:T(8,128)S(1)} %sums_two.1), channel_id=1, replica_groups=mesh['row'=8,'col'=4] {'row'}, dimensions={0} | all-to-all | bytes 65536 | tf_op jit(solution)/shard_map/all_to_all | solution.py:125
  135.3 5.8 %turn_two.1 = (bf16[1792,512]{1,0:T(8,128)(2,1)}, f32[8,128]{1,0:T(8,128)}) custom-call(f32[1792,512]{1,0:T(8,128)} %copy-done.7, bf16[1792,512]{1,0:T(8,128)(2,1)} %refs_1_.9, f32[14,128,128]{2,1,0:T(8,128)} %copy-done.17, bf16[14,128,128]{2,1,0:T(8,128)(2,1)} %copy-done.27, f32[8,16,128]{2,1,0:T(8,128)} %copy-done.29, f32[8,8,128]{2,1,0:T(8,128)} %all_to_all.22.refs_5_, ...), custom_call_target="tpu_custom_call" | custom-call | flops 1000000 | bytes 1000 | tf_op jit(solution)/shard_map/turn_two/pallas_call | solution.py:45
  142.9 6.2 %terms_two.2 = (bf16[512,512]{1,0:T(8,128)(2,1)}, bf16[512,512]{1,0:T(8,128)(2,1)}, f32[8,128]{1,0:T(8,128)}) custom-call(s32[7]{0:T(128)} %copy-done.31, bf16[1792,512]{1,0:T(8,128)(2,1)} %copy-done.15, bf16[1792,512]{1,0:T(8,128)(2,1)} %copy-done.16, bf16[1792,512]{1,0:T(8,128)(2,1)} %copy-done.19, bf16[1792,512]{1,0:T(8,128)(2,1)} %copy-done.20, ...), custom_call_target="tpu_custom_call" | custom-call | flops 1000000 | bytes 1000 | tf_op jit(solution)/shard_map/terms_two/pallas_call | solution.py:45
  150.8 6.3 %terms_two.3 = (bf16[512,512]{1,0:T(8,128)(2,1)}, bf16[512,512]{1,0:T(8,128)(2,1)}, f32[8,128]{1,0:T(8,128)}) custom-call(s32[7]{0:T(128)} %copy-done.31, bf16[1792,512]{1,0:T(8,128)(2,1)} %copy-done.15, bf16[1792,512]{1,0:T(8,128)(2,1)} %copy-done.16, bf16[1792,512]{1,0:T(8,128)(2,1)} %copy-done.19, bf16[1792,512]{1,0:T(8,128)(2,1)} %copy-done.20, ...), custom_call_target="tpu_custom_call" | custom-call | flops 1000000 | bytes 1000 | tf_op jit(solution)/shard_map/terms_two/pallas_call | solution.py:45
  159.3 4.0 %half_back_two.1 = (f32[1792,512]{1,0:T(8,128)S(1)}, f32[8,128]{1,0:T(8,128)S(1)}) custom-call(s32[7]{0:T(128)S(1)} %copy-done.32, bf16[1792,512]{1,0:T(8,128)(2,1)S(1)} %copy-done.14, bf16[1792,512]{1,0:T(8,128)(2,1)} %collective-permute-done.12.refs_2_, bf16[2048,512]{1,0:T(8,128)(2,1)S(1)} %copy-done.3, ...), custom_call_target="tpu_custom_call" | custom-call | flops 1000000 | bytes 1000 | tf_op jit(solution)/shard_map/half_back_two/pallas_call | solution.py:45
  165.3 2.4 collective-permute-start.16
  170.0 9.8 %collective-permute-done.16.refs_2_ = bf16[256,512]{1,0:T(8,128)(2,1)S(1)} collective-permute-done((bf16[256,512]{1,0:T(8,128)(2,1)S(1)}, bf16[256,512]{1,0:T(8,128)(2,1)S(1)}, u32[]{:S(2)}, u32[]{:S(2)}) %collective-permute-start.16) | collective-permute-done | bytes 262176 | tf_op jit(solution)/shard_map/ppermute | solution.py:642
  189.2 3.9 %far_half_back_two.1 = (f32[1792,512]{1,0:T(8,128)S(1)}, f32[8,128]{1,0:T(8,128)}) custom-call(s32[7]{0:T(128)S(1)} %copy-done.32, bf16[1792,512]{1,0:T(8,128)(2,1)} %collective-permute-done.10.refs_1_, bf16[512,512]{1,0:T(8,128)(2,1)S(1)} %copy-done.23, f32[1792,512]{1,0:T(8,128)S(1)} %get-tuple-element.179.refs_3_, ...), custom_call_target="tpu_custom_call" | custom-call | flops 1000000 | bytes 1000 | tf_op jit(solution)/shard_map/far_half_back_two/pallas_call | solution.py:45
  193.1 3.8 %backward_two.1 = (f32[1792,512]{1,0:T(8,128)S(1)}, f32[8,8,128]{2,1,0:T(8,128)}) custom-call(f32[1792,512]{1,0:T(8,128)S(1)} %get-tuple-element.182.refs_0_, bf16[1792,512]{1,0:T(8,128)(2,1)S(1)} %collective-permute-done.17.refs_1_, bf16[512,512]{1,0:T(8,128)(2,1)S(1)} %collective-permute-done.18.refs_2_, f32[1792,512]{1,0:T(8,128)S(1)} %copy-done.10, ...), custom_call_target="tpu_custom_call" | custom-call | flops 1000000 | bytes 1000 | tf_op jit(solution)/shard_map/backward_two/pallas_call | solution.py:45
  196.9 1.8 copy-done.21
  198.7 3.8 %all-to-all-start.3 = ((f32[8,8,128]{2,1,0:T(8,128)}), f32[8,8,128]{2,1,0:T(8,128)S(1)}, u32[]{:S(2)}, u32[]{:S(2)}) async-start(f32[8,8,128]{2,1,0:T(8,128)} %get-tuple-element.184.refs_3_), calls=%async_computation.3 | async-start | bytes 65536 | tf_op jit(solution)/shard_map/all_to_all | solution.py:125
  206.4 3.3 %collective-permute-done.20.refs_9_ = bf16[512,512]{1,0:T(8,128)(2,1)S(1)} collective-permute-done((bf16[512,512]{1,0:T(8,128)(2,1)}, bf16[512,512]{1,0:T(8,128)(2,1)S(1)}, u32[]{:S(2)}, u32[]{:S(2)}) %collective-permute-start.20) | collective-permute-done | bytes 524320 | tf_op jit(solution)/shard_map/ppermute | solution.py:642
  210.5 5.1 %turn_one.1 = (bf16[1792,512]{1,0:T(8,128)(2,1)}, f32[8,128]{1,0:T(8,128)}) custom-call(f32[1792,512]{1,0:T(8,128)} %copy-done.9, f32[1792,512]{1,0:T(8,128)} %copy-done.21, f32[14,128,128]{2,1,0:T(8,128)} %copy-done.17, bf16[14,128,128]{2,1,0:T(8,128)(2,1)} %copy-done.27, f32[8,16,128]{2,1,0:T(8,128)} %copy-done.28, f32[8,8,128]{2,1,0:T(8,128)} %copy-done.61, ...), custom_call_target="tpu_custom_call" | custom-call | flops 1000000 | bytes 1000 | tf_op jit(solution)/shard_map/turn_one/pallas_call | solution.py:45
  219.9 6.2 %terms_one.2 = (bf16[512,512]{1,0:T(8,128)(2,1)}, bf16[512,512]{1,0:T(8,128)(2,1)}, f32[8,128]{1,0:T(8,128)}) custom-call(s32[7]{0:T(128)} %copy-done.31, bf16[1792,512]{1,0:T(8,128)(2,1)} %refs_1_.11, bf16[1792,512]{1,0:T(8,128)(2,1)} %collective-permute-done.1.refs_2_, bf16[1792,512]{1,0:T(8,128)(2,1)} %collective-permute-done.refs_1_.refs_3_, ...), custom_call_target="tpu_custom_call" | custom-call | flops 1000000 | bytes 1000 | tf_op jit(solution)/shard_map/terms_one/pallas_call | solution.py:45
  226.6 5.4 %collective-permute-done.26.refs_2_ = bf16[256,512]{1,0:T(8,128)(2,1)S(1)} collective-permute-done((bf16[256,512]{1,0:T(8,128)(2,1)S(1)}, bf16[256,512]{1,0:T(8,128)(2,1)S(1)}, u32[]{:S(2)}, u32[]{:S(2)}) %collective-permute-start.26) | collective-permute-done | bytes 262176 | tf_op jit(solution)/shard_map/ppermute | solution.py:642
  235.3 6.3 %terms_one.3 = (bf16[512,512]{1,0:T(8,128)(2,1)}, bf16[512,512]{1,0:T(8,128)(2,1)}, f32[8,128]{1,0:T(8,128)}) custom-call(s32[7]{0:T(128)} %copy-done.31, bf16[1792,512]{1,0:T(8,128)(2,1)} %refs_1_.11, bf16[1792,512]{1,0:T(8,128)(2,1)} %collective-permute-done.1.refs_2_, bf16[1792,512]{1,0:T(8,128)(2,1)} %collective-permute-done.refs_1_.refs_3_, ...), custom_call_target="tpu_custom_call" | custom-call | flops 1000000 | bytes 1000 | tf_op jit(solution)/shard_map/terms_one/pallas_call | solution.py:45
  249.4 2.2 collective-permute-start.30
  251.7 4.3 %half_back_one.1 = (f32[1792,512]{1,0:T(8,128)S(1)}, f32[8,128]{1,0:T(8,128)S(1)}) custom-call(s32[7]{0:T(128)S(1)} %copy-done.34, bf16[1792,512]{1,0:T(8,128)(2,1)S(1)} %copy-done.11, bf16[1792,512]{1,0:T(8,128)(2,1)} %collective-permute-done.23.refs_2_, bf16[2048,512]{1,0:T(8,128)(2,1)S(1)} %copy-done.6, ...), custom_call_target="tpu_custom_call" | custom-call | flops 1000000 | bytes 1000 | tf_op jit(solution)/shard_map/half_back_one/pallas_call | solution.py:45
  256.1 2.4 output.1
  258.5 2.2 collective-permute-done.31.refs_2_
  261.2 2.3 collective-permute-done.30.refs_2_
  264.8 1.9 collective-permute-start.32
  267.8 14.2 %collective-permute-done.32.refs_2_ = bf16[256,512]{1,0:T(8,128)(2,1)S(1)} collective-permute-done((bf16[256,512]{1,0:T(8,128)(2,1)S(1)}, bf16[256,512]{1,0:T(8,128)(2,1)S(1)}, u32[]{:S(2)}, u32[]{:S(2)}) %collective-permute-start.32) | collective-permute-done | bytes 262176 | tf_op jit(solution)/shard_map/ppermute | solution.py:642
  282.6 2.8 collective-permute-start.37
  287.9 3.6 %far_half_back_one.1 = (f32[1792,512]{1,0:T(8,128)S(1)}, f32[8,128]{1,0:T(8,128)}) custom-call(s32[7]{0:T(128)S(1)} %copy-done.34, bf16[1792,512]{1,0:T(8,128)(2,1)} %collective-permute-done.29.refs_1_, bf16[512,512]{1,0:T(8,128)(2,1)S(1)} %copy-done.26, f32[1792,512]{1,0:T(8,128)S(1)} %get-tuple-element.214.refs_3_, ...), custom_call_target="tpu_custom_call" | custom-call | flops 1000000 | bytes 1000 | tf_op jit(solution)/shard_map/far_half_back_one/pallas_call | solution.py:45
  291.6 2.6 backward_one.1
  294.2 2.0 collective-permute-done.37.refs_2_
  298.0 2.4 collective-permute-done.39.refs_2_
  303.6 4.7 %place_two.1 = (f32[2048,512]{1,0:T(8,128)}, f32[8,128]{1,0:T(8,128)}) custom-call(s32[7]{0:T(128)} %copy-done.31, bf16[512,512]{1,0:T(8,128)(2,1)} %get-tuple-element.230.refs_1_, bf16[512,512]{1,0:T(8,128)(2,1)} %copy-done.57, bf16[512,512]{1,0:T(8,128)(2,1)} %copy-done.36, bf16[512,512]{1,0:T(8,128)(2,1)} %copy-done.24, f32[8,128]{1,0:T(8,128)} %copy-done.49, ...), custom_call_target="tpu_custom_call" | custom-call | flops 1000000 | bytes 1000 | tf_op jit(solution)/shard_map/place_two/pallas_call | solution.py:45
  308.3 3.3 %collective-permute-done.38.refs_2_ = bf16[512,512]{1,0:T(8,128)(2,1)S(1)} collective-permute-done((bf16[512,512]{1,0:T(8,128)(2,1)S(1)}, bf16[512,512]{1,0:T(8,128)(2,1)S(1)}, u32[]{:S(2)}, u32[]{:S(2)}) %collective-permute-start.38) | collective-permute-done | bytes 524320 | tf_op jit(solution)/shard_map/ppermute | solution.py:642
  312.0 3.1 place_one.1
  (216 shorter events, 66.2 us)
Async XLA Ops:
  0.6 14.6 %collective-permute-start.1 = (bf16[1792,512]{1,0:T(8,128)(2,1)}, bf16[1792,512]{1,0:T(8,128)(2,1)}, u32[]{:S(2)}, u32[]{:S(2)}) collective-permute-start(bf16[1792,512]{1,0:T(8,128)(2,1)} %refs_1_.11), channel_id=1, source_target_pairs={{0,1},{1,0},{2,3},{3,2},{4,5},{5,4},{6,7},{7,6},{8,9},{9,8},{10,11... | collective-permute-start | bytes 5505032 | tf_op jit(solution)/shard_map/ppermute | solution.py:642
  1.2 43.5 %collective-permute-start = (bf16[1792,512]{1,0:T(8,128)(2,1)}, bf16[1792,512]{1,0:T(8,128)(2,1)}, u32[]{:S(2)}, u32[]{:S(2)}) collective-permute-start(bf16[1792,512]{1,0:T(8,128)(2,1)} %refs_1_.11), channel_id=1, source_target_pairs={{0,2},{1,3},{2,0},{3,1},{4,6},{5,7},{6,4},{7,5},{8,10},{9,11},{10,... | collective-permute-start | bytes 5505032 | tf_op jit(solution)/shard_map/ppermute | solution.py:642
  4.6 99.3 %copy-start.31 = (s32[7]{0:T(128)}, s32[7]{0:T(128)S(1)}, u32[]{:S(2)}) copy-start(s32[7]{0:T(128)S(1)} %stack.31.refs_0_) | copy-start | bytes 88
  13.5 90.4 %copy-start.17 = (f32[14,128,128]{2,1,0:T(8,128)}, f32[14,128,128]{2,1,0:T(8,128)S(1)}, u32[]{:S(2)}) copy-start(f32[14,128,128]{2,1,0:T(8,128)S(1)} %get-tuple-element.131.refs_5_.refs_6_.refs_2_) | copy-start | bytes 2752516
  44.7 4.0 %collective-permute-start.2 = (bf16[1792,512]{1,0:T(8,128)(2,1)}, bf16[1792,512]{1,0:T(8,128)(2,1)S(1)}, u32[]{:S(2)}, u32[]{:S(2)}) collective-permute-start(bf16[1792,512]{1,0:T(8,128)(2,1)} %collective-permute-done.refs_1_.refs_3_), channel_id=1, source_target_pairs={{0,1},{1,0},{2,3},{3,2},{4,5},{5,4},{6,7},{7,6},{8,9},{9,8},{10,11... | collective-permute-start | bytes 5505032 | tf_op jit(solution)/shard_map/ppermute | solution.py:642
  53.1 16.8 %collective-permute-start.3 = (bf16[640,512]{1,0:T(8,128)(2,1)S(1)}, bf16[640,512]{1,0:T(8,128)(2,1)S(1)}, u32[]{:S(2)}, u32[]{:S(2)}) collective-permute-start(bf16[640,512]{1,0:T(8,128)(2,1)S(1)} %get-tuple-element.133), channel_id=1, source_target_pairs={{0,2},{1,3},{2,0},{3,1},{4,6},{5,7},{6,4},{7,5},{8,10},{9,11},{10,... | collective-permute-start | bytes 1966088 | tf_op jit(solution)/shard_map/ppermute | solution.py:642
  67.3 125.7 %copy-start.28 = (f32[8,16,128]{2,1,0:T(8,128)}, f32[8,16,128]{2,1,0:T(8,128)S(1)}, u32[]{:S(2)}) copy-start(f32[8,16,128]{2,1,0:T(8,128)S(1)} %all_to_all.20.refs_1_.refs_2_.refs_4_) | copy-start | bytes 196612
  71.2 3.8 %collective-permute-start.5 = (bf16[1792,512]{1,0:T(8,128)(2,1)S(1)}, bf16[1792,512]{1,0:T(8,128)(2,1)S(1)}, u32[]{:S(2)}, u32[]{:S(2)}) collective-permute-start(bf16[1792,512]{1,0:T(8,128)(2,1)S(1)} %get-tuple-element.139.refs_1_), channel_id=1, source_target_pairs={{0,1},{1,0},{2,3},{3,2},{4,5},{5,4},{6,7},{7,6},{8,9},{9,8},{10,11... | collective-permute-start | bytes 5505032 | tf_op jit(solution)/shard_map/ppermute | solution.py:642
  71.2 28.7 %collective-permute-start.4 = (bf16[1168,512]{1,0:T(8,128)(2,1)S(1)}, bf16[1168,512]{1,0:T(8,128)(2,1)S(1)}, u32[]{:S(2)}, u32[]{:S(2)}) collective-permute-start(bf16[1168,512]{1,0:T(8,128)(2,1)S(1)} %get-tuple-element.136), channel_id=1, source_target_pairs={{0,2},{1,3},{2,0},{3,1},{4,6},{5,7},{6,4},{7,5},{8,10},{9,11},{10,... | collective-permute-start | bytes 3588104 | tf_op jit(solution)/shard_map/ppermute | solution.py:642
  99.9 3.9 %collective-permute-start.7 = (bf16[1168,512]{1,0:T(8,128)(2,1)S(1)}, bf16[1168,512]{1,0:T(8,128)(2,1)S(1)}, u32[]{:S(2)}, u32[]{:S(2)}) collective-permute-start(bf16[1168,512]{1,0:T(8,128)(2,1)S(1)} %collective-permute-done.4.refs_2_), channel_id=1, source_target_pairs={{0,1},{1,0},{2,3},{3,2},{4,5},{5,4},{6,7},{7,6},{8,9},{9,8},{10,11... | collective-permute-start | bytes 3588104 | tf_op jit(solution)/shard_map/ppermute | solution.py:642
  99.9 3.9 %collective-permute-start.6 = (bf16[640,512]{1,0:T(8,128)(2,1)S(1)}, bf16[640,512]{1,0:T(8,128)(2,1)S(1)}, u32[]{:S(2)}, u32[]{:S(2)}) collective-permute-start(bf16[640,512]{1,0:T(8,128)(2,1)S(1)} %collective-permute-done.3.refs_5_.refs_1_), channel_id=1, source_target_pairs={{0,1},{1,0},{2,3},{3,2},{4,5},{5,4},{6,7},{7,6},{8,9},{9,8},{10,11... | collective-permute-start | bytes 1966088 | tf_op jit(solution)/shard_map/ppermute | solution.py:642
  107.7 26.7 %collective-permute-start.8 = (bf16[512,512]{1,0:T(8,128)(2,1)S(1)}, bf16[512,512]{1,0:T(8,128)(2,1)S(1)}, u32[]{:S(2)}, u32[]{:S(2)}) collective-permute-start(bf16[512,512]{1,0:T(8,128)(2,1)S(1)} %get-tuple-element.156), channel_id=1, source_target_pairs={{0,2},{1,3},{2,0},{3,1},{4,6},{5,7},{6,4},{7,5},{8,10},{9,11},{10,... | collective-permute-start | bytes 1572872 | tf_op jit(solution)/shard_map/ppermute | solution.py:642
  109.5 24.9 %collective-permute-start.9 = (bf16[512,512]{1,0:T(8,128)(2,1)S(1)}, bf16[512,512]{1,0:T(8,128)(2,1)S(1)}, u32[]{:S(2)}, u32[]{:S(2)}) collective-permute-start(bf16[512,512]{1,0:T(8,128)(2,1)S(1)} %get-tuple-element.157), channel_id=1, source_target_pairs={{0,2},{1,3},{2,0},{3,1},{4,6},{5,7},{6,4},{7,5},{8,10},{9,11},{10,... | collective-permute-start | bytes 1572872 | tf_op jit(solution)/shard_map/ppermute | solution.py:642
  141.1 16.0 %collective-permute-start.12 = (bf16[1792,512]{1,0:T(8,128)(2,1)}, bf16[1792,512]{1,0:T(8,128)(2,1)}, u32[]{:S(2)}, u32[]{:S(2)}) collective-permute-start(bf16[1792,512]{1,0:T(8,128)(2,1)} %get-tuple-element.158.refs_5_.refs_1_), channel_id=1, source_target_pairs={{0,1},{1,0},{2,3},{3,2},{4,5},{5,4},{6,7},{7,6},{8,9},{9,8},{10,11... | collective-permute-start | bytes 5505032 | tf_op jit(solution)/shard_map/ppermute | solution.py:642
  141.1 42.7 %collective-permute-start.10 = (bf16[1792,512]{1,0:T(8,128)(2,1)}, bf16[1792,512]{1,0:T(8,128)(2,1)}, u32[]{:S(2)}, u32[]{:S(2)}) collective-permute-start(bf16[1792,512]{1,0:T(8,128)(2,1)} %get-tuple-element.158.refs_5_.refs_1_), channel_id=1, source_target_pairs={{0,2},{1,3},{2,0},{3,1},{4,6},{5,7},{6,4},{7,5},{8,10},{9,11},{10,... | collective-permute-start | bytes 5505032 | tf_op jit(solution)/shard_map/ppermute | solution.py:642
  142.7 14.4 %collective-permute-start.13 = (bf16[512,512]{1,0:T(8,128)(2,1)}, bf16[512,512]{1,0:T(8,128)(2,1)S(1)}, u32[]{:S(2)}, u32[]{:S(2)}) collective-permute-start(bf16[512,512]{1,0:T(8,128)(2,1)} %copy-done.54), channel_id=1, source_target_pairs={{0,1},{1,0},{2,3},{3,2},{4,5},{5,4},{6,7},{7,6},{8,9},{9,8},{10,11... | collective-permute-start | bytes 1572872 | tf_op jit(solution)/shard_map/ppermute | solution.py:642
  149.1 14.6 %collective-permute-start.15 = (bf16[512,512]{1,0:T(8,128)(2,1)}, bf16[512,512]{1,0:T(8,128)(2,1)}, u32[]{:S(2)}, u32[]{:S(2)}) collective-permute-start(bf16[512,512]{1,0:T(8,128)(2,1)} %get-tuple-element.171), channel_id=1, source_target_pairs={{0,8},{4,12},{8,0},{12,4},{16,24},{20,28},{24,16},{28,20},{1,9},{5... | collective-permute-start | bytes 1572872 | tf_op jit(solution)/shard_map/ppermute | solution.py:642
  149.5 18.2 %collective-permute-start.11 = (bf16[512,512]{1,0:T(8,128)(2,1)}, bf16[512,512]{1,0:T(8,128)(2,1)}, u32[]{:S(2)}, u32[]{:S(2)}) collective-permute-start(bf16[512,512]{1,0:T(8,128)(2,1)} %get-tuple-element.163), channel_id=1, source_target_pairs={{0,4},{4,0},{8,12},{12,8},{16,20},{20,16},{24,28},{28,24},{1,5},{5... | collective-permute-start | bytes 1572872 | tf_op jit(solution)/shard_map/ppermute | solution.py:642
  165.3 14.5 %collective-permute-start.16 = (bf16[256,512]{1,0:T(8,128)(2,1)S(1)}, bf16[256,512]{1,0:T(8,128)(2,1)S(1)}, u32[]{:S(2)}, u32[]{:S(2)}) collective-permute-start(bf16[256,512]{1,0:T(8,128)(2,1)S(1)} %get-tuple-element.175), channel_id=1, source_target_pairs={{0,16},{4,20},{8,24},{12,28},{16,0},{20,4},{24,8},{28,12},{1,17},{... | collective-permute-start | bytes 786440 | tf_op jit(solution)/shard_map/ppermute | solution.py:642
  169.5 13.0 %collective-permute-start.14 = (bf16[256,512]{1,0:T(8,128)(2,1)S(1)}, bf16[256,512]{1,0:T(8,128)(2,1)S(1)}, u32[]{:S(2)}, u32[]{:S(2)}) collective-permute-start(bf16[256,512]{1,0:T(8,128)(2,1)S(1)} %get-tuple-element.168), channel_id=1, source_target_pairs={{0,8},{4,12},{8,0},{12,4},{16,24},{20,28},{24,16},{28,20},{1,9},{5... | collective-permute-start | bytes 786440 | tf_op jit(solution)/shard_map/ppermute | solution.py:642
  183.9 9.2 %collective-permute-start.17 = (bf16[1792,512]{1,0:T(8,128)(2,1)}, bf16[1792,512]{1,0:T(8,128)(2,1)S(1)}, u32[]{:S(2)}, u32[]{:S(2)}) collective-permute-start(bf16[1792,512]{1,0:T(8,128)(2,1)} %collective-permute-done.10.refs_1_), channel_id=1, source_target_pairs={{0,1},{1,0},{2,3},{3,2},{4,5},{5,4},{6,7},{7,6},{8,9},{9,8},{10,11... | collective-permute-start | bytes 5505032 | tf_op jit(solution)/shard_map/ppermute | solution.py:642
  183.9 4.2 %collective-permute-start.18 = (bf16[512,512]{1,0:T(8,128)(2,1)S(1)}, bf16[512,512]{1,0:T(8,128)(2,1)S(1)}, u32[]{:S(2)}, u32[]{:S(2)}) collective-permute-start(bf16[512,512]{1,0:T(8,128)(2,1)S(1)} %copy-done.56), channel_id=1, source_target_pairs={{0,1},{1,0},{2,3},{3,2},{4,5},{5,4},{6,7},{7,6},{8,9},{9,8},{10,11... | collective-permute-start | bytes 1572872 | tf_op jit(solution)/shard_map/ppermute | solution.py:642
  184.4 22.0 %collective-permute-start.19 = (bf16[512,512]{1,0:T(8,128)(2,1)}, bf16[512,512]{1,0:T(8,128)(2,1)S(1)}, u32[]{:S(2)}, u32[]{:S(2)}) collective-permute-start(bf16[512,512]{1,0:T(8,128)(2,1)} %get-tuple-element.185), channel_id=1, source_target_pairs={{0,2},{1,3},{2,0},{3,1},{4,6},{5,7},{6,4},{7,5},{8,10},{9,11},{10,... | collective-permute-start | bytes 1572872 | tf_op jit(solution)/shard_map/ppermute | solution.py:642
  185.9 23.8 %collective-permute-start.20 = (bf16[512,512]{1,0:T(8,128)(2,1)}, bf16[512,512]{1,0:T(8,128)(2,1)S(1)}, u32[]{:S(2)}, u32[]{:S(2)}) collective-permute-start(bf16[512,512]{1,0:T(8,128)(2,1)} %get-tuple-element.186), channel_id=1, source_target_pairs={{0,2},{1,3},{2,0},{3,1},{4,6},{5,7},{6,4},{7,5},{8,10},{9,11},{10,... | collective-permute-start | bytes 1572872 | tf_op jit(solution)/shard_map/ppermute | solution.py:642
  186.4 16.1 %collective-permute-start.22 = (bf16[256,512]{1,0:T(8,128)(2,1)}, bf16[256,512]{1,0:T(8,128)(2,1)}, u32[]{:S(2)}, u32[]{:S(2)}) collective-permute-start(bf16[256,512]{1,0:T(8,128)(2,1)} %get-tuple-element.189.refs_1_), channel_id=1, source_target_pairs={{0,4},{4,0},{8,12},{12,8},{16,20},{20,16},{24,28},{28,24},{1,5},{5... | collective-permute-start | bytes 786440 | tf_op jit(solution)/shard_map/ppermute | solution.py:642
  188.0 16.7 %collective-permute-start.21 = (bf16[256,512]{1,0:T(8,128)(2,1)}, bf16[256,512]{1,0:T(8,128)(2,1)}, u32[]{:S(2)}, u32[]{:S(2)}) collective-permute-start(bf16[256,512]{1,0:T(8,128)(2,1)} %get-tuple-element.187.refs_1_), channel_id=1, source_target_pairs={{0,16},{4,20},{8,24},{12,28},{16,0},{20,4},{24,8},{28,12},{1,17},{... | collective-permute-start | bytes 786440 | tf_op jit(solution)/shard_map/ppermute | solution.py:642
  198.7 10.9 %all-to-all-start.3 = ((f32[8,8,128]{2,1,0:T(8,128)}), f32[8,8,128]{2,1,0:T(8,128)S(1)}, u32[]{:S(2)}, u32[]{:S(2)}) async-start(f32[8,8,128]{2,1,0:T(8,128)} %get-tuple-element.184.refs_3_), calls=%async_computation.3 | async-start | bytes 65536 | tf_op jit(solution)/shard_map/all_to_all | solution.py:125
  215.6 36.0 %collective-permute-start.23 = (bf16[1792,512]{1,0:T(8,128)(2,1)}, bf16[1792,512]{1,0:T(8,128)(2,1)}, u32[]{:S(2)}, u32[]{:S(2)}) collective-permute-start(bf16[1792,512]{1,0:T(8,128)(2,1)} %get-tuple-element.191.refs_5_.refs_1_), channel_id=1, source_target_pairs={{0,1},{1,0},{2,3},{3,2},{4,5},{5,4},{6,7},{7,6},{8,9},{9,8},{10,11... | collective-permute-start | bytes 5505032 | tf_op jit(solution)/shard_map/ppermute | solution.py:642
  215.6 48.5 %collective-permute-start.29 = (bf16[1792,512]{1,0:T(8,128)(2,1)}, bf16[1792,512]{1,0:T(8,128)(2,1)}, u32[]{:S(2)}, u32[]{:S(2)}) collective-permute-start(bf16[1792,512]{1,0:T(8,128)(2,1)} %get-tuple-element.191.refs_5_.refs_1_), channel_id=1, source_target_pairs={{0,2},{1,3},{2,0},{3,1},{4,6},{5,7},{6,4},{7,5},{8,10},{9,11},{10,... | collective-permute-start | bytes 5505032 | tf_op jit(solution)/shard_map/ppermute | solution.py:642
  217.2 14.8 %collective-permute-start.26 = (bf16[256,512]{1,0:T(8,128)(2,1)S(1)}, bf16[256,512]{1,0:T(8,128)(2,1)S(1)}, u32[]{:S(2)}, u32[]{:S(2)}) collective-permute-start(bf16[256,512]{1,0:T(8,128)(2,1)S(1)} %get-tuple-element.196.refs_1_), channel_id=1, source_target_pairs={{0,16},{4,20},{8,24},{12,28},{16,0},{20,4},{24,8},{28,12},{1,17},{... | collective-permute-start | bytes 786440 | tf_op jit(solution)/shard_map/ppermute | solution.py:642
  218.3 14.3 %collective-permute-start.25 = (bf16[256,512]{1,0:T(8,128)(2,1)S(1)}, bf16[256,512]{1,0:T(8,128)(2,1)S(1)}, u32[]{:S(2)}, u32[]{:S(2)}) collective-permute-start(bf16[256,512]{1,0:T(8,128)(2,1)S(1)} %get-tuple-element.194.refs_1_), channel_id=1, source_target_pairs={{0,8},{4,12},{8,0},{12,4},{16,24},{20,28},{24,16},{28,20},{1,9},{5... | collective-permute-start | bytes 786440 | tf_op jit(solution)/shard_map/ppermute | solution.py:642
  226.1 17.3 %collective-permute-start.28 = (bf16[512,512]{1,0:T(8,128)(2,1)}, bf16[512,512]{1,0:T(8,128)(2,1)}, u32[]{:S(2)}, u32[]{:S(2)}) collective-permute-start(bf16[512,512]{1,0:T(8,128)(2,1)} %get-tuple-element.202), channel_id=1, source_target_pairs={{0,8},{4,12},{8,0},{12,4},{16,24},{20,28},{24,16},{28,20},{1,9},{5... | collective-permute-start | bytes 1572872 | tf_op jit(solution)/shard_map/ppermute | solution.py:642
  232.0 14.7 %collective-permute-start.27 = (bf16[512,512]{1,0:T(8,128)(2,1)}, bf16[512,512]{1,0:T(8,128)(2,1)}, u32[]{:S(2)}, u32[]{:S(2)}) collective-permute-start(bf16[512,512]{1,0:T(8,128)(2,1)} %get-tuple-element.199), channel_id=1, source_target_pairs={{0,4},{4,0},{8,12},{12,8},{16,20},{20,16},{24,28},{28,24},{1,5},{5... | collective-permute-start | bytes 1572872 | tf_op jit(solution)/shard_map/ppermute | solution.py:642
  232.7 19.0 %collective-permute-start.24 = (bf16[512,512]{1,0:T(8,128)(2,1)}, bf16[512,512]{1,0:T(8,128)(2,1)S(1)}, u32[]{:S(2)}, u32[]{:S(2)}) collective-permute-start(bf16[512,512]{1,0:T(8,128)(2,1)} %get-tuple-element.192), channel_id=1, source_target_pairs={{0,1},{1,0},{2,3},{3,2},{4,5},{5,4},{6,7},{7,6},{8,9},{9,8},{10,11... | collective-permute-start | bytes 1572872 | tf_op jit(solution)/shard_map/ppermute | solution.py:642
  233.3 31.0 %copy-start.36 = (bf16[512,512]{1,0:T(8,128)(2,1)}, bf16[512,512]{1,0:T(8,128)(2,1)S(1)}, u32[]{:S(2)}) copy-start(bf16[512,512]{1,0:T(8,128)(2,1)S(1)} %get-tuple-element.221.refs_3_) | copy-start | bytes 1572868
  246.1 14.5 %collective-permute-start.31 = (bf16[256,512]{1,0:T(8,128)(2,1)S(1)}, bf16[256,512]{1,0:T(8,128)(2,1)S(1)}, u32[]{:S(2)}, u32[]{:S(2)}) collective-permute-start(bf16[256,512]{1,0:T(8,128)(2,1)S(1)} %get-tuple-element.211), channel_id=1, source_target_pairs={{0,16},{4,20},{8,24},{12,28},{16,0},{20,4},{24,8},{28,12},{1,17},{... | collective-permute-start | bytes 786440 | tf_op jit(solution)/shard_map/ppermute | solution.py:642
  249.4 14.1 %collective-permute-start.30 = (bf16[256,512]{1,0:T(8,128)(2,1)S(1)}, bf16[256,512]{1,0:T(8,128)(2,1)S(1)}, u32[]{:S(2)}, u32[]{:S(2)}) collective-permute-start(bf16[256,512]{1,0:T(8,128)(2,1)S(1)} %get-tuple-element.207), channel_id=1, source_target_pairs={{0,8},{4,12},{8,0},{12,4},{16,24},{20,28},{24,16},{28,20},{1,9},{5... | collective-permute-start | bytes 786440 | tf_op jit(solution)/shard_map/ppermute | solution.py:642
  258.5 29.4 %copy-start.26 = (bf16[512,512]{1,0:T(8,128)(2,1)S(1)}, bf16[512,512]{1,0:T(8,128)(2,1)}, u32[]{:S(2)}) copy-start(bf16[512,512]{1,0:T(8,128)(2,1)} %copy-done.25) | copy-start | bytes 1572868
  264.2 27.4 %collective-permute-start.35 = (bf16[1792,512]{1,0:T(8,128)(2,1)}, bf16[1792,512]{1,0:T(8,128)(2,1)S(1)}, u32[]{:S(2)}, u32[]{:S(2)}) collective-permute-start(bf16[1792,512]{1,0:T(8,128)(2,1)} %collective-permute-done.29.refs_1_), channel_id=1, source_target_pairs={{0,1},{1,0},{2,3},{3,2},{4,5},{5,4},{6,7},{7,6},{8,9},{9,8},{10,11... | collective-permute-start | bytes 5505032 | tf_op jit(solution)/shard_map/ppermute | solution.py:642
  264.2 22.5 %collective-permute-start.34 = (bf16[512,512]{1,0:T(8,128)(2,1)S(1)}, bf16[512,512]{1,0:T(8,128)(2,1)S(1)}, u32[]{:S(2)}, u32[]{:S(2)}) collective-permute-start(bf16[512,512]{1,0:T(8,128)(2,1)S(1)} %get-tuple-element.221.refs_3_), channel_id=1, source_target_pairs={{0,8},{4,12},{8,0},{12,4},{16,24},{20,28},{24,16},{28,20},{1,9},{5... | collective-permute-start | bytes 1572872 | tf_op jit(solution)/shard_map/ppermute | solution.py:642
  264.3 27.2 %collective-permute-start.36 = (bf16[512,512]{1,0:T(8,128)(2,1)S(1)}, bf16[512,512]{1,0:T(8,128)(2,1)S(1)}, u32[]{:S(2)}, u32[]{:S(2)}) collective-permute-start(bf16[512,512]{1,0:T(8,128)(2,1)S(1)} %copy-done.59), channel_id=1, source_target_pairs={{0,1},{1,0},{2,3},{3,2},{4,5},{5,4},{6,7},{7,6},{8,9},{9,8},{10,11... | collective-permute-start | bytes 1572872 | tf_op jit(solution)/shard_map/ppermute | solution.py:642
  264.8 17.2 %collective-permute-start.32 = (bf16[256,512]{1,0:T(8,128)(2,1)S(1)}, bf16[256,512]{1,0:T(8,128)(2,1)S(1)}, u32[]{:S(2)}, u32[]{:S(2)}) collective-permute-start(bf16[256,512]{1,0:T(8,128)(2,1)S(1)} %get-tuple-element.217.refs_1_), channel_id=1, source_target_pairs={{0,16},{4,20},{8,24},{12,28},{16,0},{20,4},{24,8},{28,12},{1,17},{... | collective-permute-start | bytes 786440 | tf_op jit(solution)/shard_map/ppermute | solution.py:642
  266.7 18.6 %collective-permute-start.33 = (bf16[256,512]{1,0:T(8,128)(2,1)S(1)}, bf16[256,512]{1,0:T(8,128)(2,1)S(1)}, u32[]{:S(2)}, u32[]{:S(2)}) collective-permute-start(bf16[256,512]{1,0:T(8,128)(2,1)S(1)} %get-tuple-element.219.refs_1_), channel_id=1, source_target_pairs={{0,4},{4,0},{8,12},{12,8},{16,20},{20,16},{24,28},{28,24},{1,5},{5... | collective-permute-start | bytes 786440 | tf_op jit(solution)/shard_map/ppermute | solution.py:642
  282.6 13.6 %collective-permute-start.37 = (bf16[256,512]{1,0:T(8,128)(2,1)S(1)}, bf16[256,512]{1,0:T(8,128)(2,1)S(1)}, u32[]{:S(2)}, u32[]{:S(2)}) collective-permute-start(bf16[256,512]{1,0:T(8,128)(2,1)S(1)} %get-tuple-element.224.refs_1_), channel_id=1, source_target_pairs={{0,8},{4,12},{8,0},{12,4},{16,24},{20,28},{24,16},{28,20},{1,9},{5... | collective-permute-start | bytes 786440 | tf_op jit(solution)/shard_map/ppermute | solution.py:642
  286.0 14.4 %collective-permute-start.39 = (bf16[256,512]{1,0:T(8,128)(2,1)S(1)}, bf16[256,512]{1,0:T(8,128)(2,1)S(1)}, u32[]{:S(2)}, u32[]{:S(2)}) collective-permute-start(bf16[256,512]{1,0:T(8,128)(2,1)S(1)} %get-tuple-element.227.refs_1_), channel_id=1, source_target_pairs={{0,16},{4,20},{8,24},{12,28},{16,0},{20,4},{24,8},{28,12},{1,17},{... | collective-permute-start | bytes 786440 | tf_op jit(solution)/shard_map/ppermute | solution.py:642
  286.7 16.0 %collective-permute-start.41 = (bf16[512,512]{1,0:T(8,128)(2,1)}, bf16[512,512]{1,0:T(8,128)(2,1)S(1)}, u32[]{:S(2)}, u32[]{:S(2)}) collective-permute-start(bf16[512,512]{1,0:T(8,128)(2,1)} %get-tuple-element.230.refs_1_), channel_id=1, source_target_pairs={{0,4},{4,0},{8,12},{12,8},{16,20},{20,16},{24,28},{28,24},{1,5},{5... | collective-permute-start | bytes 1572872 | tf_op jit(solution)/shard_map/ppermute | solution.py:642
  296.8 14.8 %collective-permute-start.38 = (bf16[512,512]{1,0:T(8,128)(2,1)S(1)}, bf16[512,512]{1,0:T(8,128)(2,1)S(1)}, u32[]{:S(2)}, u32[]{:S(2)}) collective-permute-start(bf16[512,512]{1,0:T(8,128)(2,1)S(1)} %get-tuple-element.226.refs_1_), channel_id=1, source_target_pairs={{0,4},{4,0},{8,12},{12,8},{16,20},{20,16},{24,28},{28,24},{1,5},{5... | collective-permute-start | bytes 1572872 | tf_op jit(solution)/shard_map/ppermute | solution.py:642
  301.6 10.5 %collective-permute-start.40 = (bf16[512,512]{1,0:T(8,128)(2,1)S(1)}, bf16[512,512]{1,0:T(8,128)(2,1)S(1)}, u32[]{:S(2)}, u32[]{:S(2)}) collective-permute-start(bf16[512,512]{1,0:T(8,128)(2,1)S(1)} %get-tuple-element.228.refs_3_), channel_id=1, source_target_pairs={{0,8},{4,12},{8,0},{12,4},{16,24},{20,28},{24,16},{28,20},{1,9},{5... | collective-permute-start | bytes 1572872 | tf_op jit(solution)/shard_map/ppermute | solution.py:642
  (58 other events, 415.9 us)

commit v9 on v8

--- a/solution.py
+++ b/solution.py
@@ -820,7 +820,7 @@
     rows_one, crossing = weight_rows(slices_one)
     early, _ = half(ids, big, [far], [whole_block(rows_two[1])], True, "far_half_back_two", tokens, early)
     grad_one, sums = backward(big, early, beyond, rows_two[2], lin_one, norm_one, "backward_two", tokens)
-    tokens = (*crossing, *sum_two.next(sums))
+    tokens = (crossing[1], *sum_two.next(sums))
     grads_one = small_gather(sums, "row")
 
     turned, _ = turn_call(False, big, lin_one, grad_one, tiles, norm_one, grads_one, "turn_one", tokens)

time: 316 us -> 314 us (level)
  waiting for transfers between devices: 101 us -> 106 us
  Pallas kernels: 117 us -> 113 us
  starting transfers between devices: 41.4 us -> 38.2 us
    all_to_all x1, waiting for transfers between devices: 0.01 us -> 4.55 us  [small_gather(): return lax.all_to_all(copies, axis, split_axis=0, concat_axis=0, tiled=True)]
    pallas_call x41, Pallas kernels: 117 us -> 113 us  [launch(): pl.pallas_call(body, grid_spec=pltpu.PrefetchScalarGridSpec(num_scalar_pr...]
    unnamed x126 -> x130, local copies, waits for them, and re-layouts: 17.3 us -> 17.3 us
  transfers between devices with their start and end apart: 43 -> 43, of which waited for: 20 -> 20; matrix products, arithmetic and copies ran while one was open for 1% -> 1% of each run, Pallas kernels for 30% -> 29%
where the time goes in v9:
time: 314 us; the launch traced here: 313 us
  Pallas kernels  113 us (36%)
  waiting for transfers between devices  106 us (34%)
  starting transfers between devices  38.2 us (12%)
  blocking collectives  35 us (11%)
  local copies, waits for them, and re-layouts  19.3 us (6%)
    pallas_call x41, Pallas kernels, launch(): pl.pallas_call(body, grid_spec=pltpu.PrefetchScalarGridSpec(num_scalar_pr...  113 us
    ppermute x42, waiting for transfers between devices, across(): return lax.ppermute(value, axis, [(i, i ^ distance) for i in range(size)])  102 us
    all_to_all x3, blocking collectives, small_gather(): return lax.all_to_all(copies, axis, split_axis=0, concat_axis=0, tiled=True)  35 us
    ppermute x42, starting transfers between devices, across(): return lax.ppermute(value, axis, [(i, i ^ distance) for i in range(size)])  34.7 us
    unnamed x130, local copies, waits for them, and re-layouts  17.3 us
  transfers between devices with their start and end apart: 43, of which 20 were waited for; matrix products, arithmetic and copies ran while one was open for 1% of the time, Pallas kernels for 29%

profile of v9, /device:TPU:0, one launch (start us, length us, event | category | flops | bytes accessed | tf_op | source)
XLA Modules:
  0.0 313.3 jit_solution(3830181073738771675)
XLA Ops:
  1.2 2.6 collective-permute-start
  4.6 4.9 %tiles.1 = (bf16[14,128,256]{2,1,0:T(8,128)(2,1)S(1)}, bf16[14,128,128]{2,1,0:T(8,128)(2,1)S(1)}, f32[14,128,128]{2,1,0:T(8,128)S(1)}, f32[14,128,128]{2,1,0:T(8,128)S(1)}, f32[8,128]{1,0:T(8,128)S(1)}) custom-call(s32[14,32,128]{2,1,0:T(8,128)S(1)} %bitcast_bitcast_fusion.refs_0_, s32[14,1,128]{2,1,0:T(1,128)S(1)} %reshape.45.refs_1_), custom_call_target="tpu_custom_call" | custom-call | flops 1000000 | bytes 1000 | tf_op jit(solution)/shard_map/tiles/pallas_call | solution.py:45
  16.5 4.0 %half_one.1 = (f32[1792,512]{1,0:T(8,128)S(1)}, f32[8,128]{1,0:T(8,128)S(1)}) custom-call(s32[7]{0:T(128)S(1)} %stack.31.refs_0_, bf16[1792,512]{1,0:T(8,128)(2,1)S(1)} %copy-done.12, bf16[1792,512]{1,0:T(8,128)(2,1)} %collective-permute-done.1.refs_2_, bf16[2048,512]{1,0:T(8,128)(2,1)S(1)} %copy-done.5, bf16[2048,512]{1,0:T(8,128)(2,1)S(1)} %copy-done.5), custom_call_target="tpu_custom_call" | custom-call | flops 1000000 | bytes 1000 | tf_op jit(solution)/shard_map/half_one/pallas_call | solution.py:45
  20.5 24.2 %collective-permute-done.refs_1_.refs_3_ = bf16[1792,512]{1,0:T(8,128)(2,1)} collective-permute-done((bf16[1792,512]{1,0:T(8,128)(2,1)}, bf16[1792,512]{1,0:T(8,128)(2,1)}, u32[]{:S(2)}, u32[]{:S(2)}) %collective-permute-start) | collective-permute-done | bytes 1835040 | tf_op jit(solution)/shard_map/ppermute | solution.py:642
  44.7 3.5 %far_half_one.1 = (f32[1792,512]{1,0:T(8,128)S(1)}, f32[8,128]{1,0:T(8,128)}) custom-call(s32[7]{0:T(128)S(1)} %stack.31.refs_0_, bf16[1792,512]{1,0:T(8,128)(2,1)} %collective-permute-done.refs_1_.refs_3_, bf16[2048,512]{1,0:T(8,128)(2,1)S(1)} %copy-done.5, f32[1792,512]{1,0:T(8,128)S(1)} %get-tuple-element.125.refs_3_, ...), custom_call_target="tpu_custom_call" | custom-call | flops 1000000 | bytes 1000 | tf_op jit(solution)/shard_map/far_half_one/pallas_call | solution.py:45
  48.7 4.4 %forward_one.1 = (f32[1792,512]{1,0:T(8,128)S(1)}, f32[8,16,128]{2,1,0:T(8,128)S(1)}, f32[8,128]{1,0:T(8,128)}, bf16[640,512]{1,0:T(8,128)(2,1)S(1)}, bf16[1168,512]{1,0:T(8,128)(2,1)S(1)}) custom-call(s32[7]{0:T(128)S(1)} %stack.31.refs_0_, f32[1792,512]{1,0:T(8,128)S(1)} %get-tuple-element.129.refs_1_, ...), custom_call_target="tpu_custom_call" | custom-call | flops 1000000 | bytes 1000 | tf_op jit(solution)/shard_map/forward_one/pallas_call | solution.py:45
  54.8 12.5 %all_to_all.20.refs_1_.refs_2_.refs_4_ = f32[8,16,128]{2,1,0:T(8,128)S(1)} all-to-all(f32[8,16,128]{2,1,0:T(8,128)S(1)} %get-tuple-element.134.refs_0_), channel_id=1, replica_groups=mesh['row'=8,'col'=4] {'row'}, dimensions={0} | all-to-all | bytes 131072 | tf_op jit(solution)/shard_map/all_to_all | solution.py:125
  67.3 2.5 collective-permute-done.3.refs_5_.refs_1_
  71.2 1.8 collective-permute-start.4
  73.0 2.0 collective-permute-done.5.refs_2_
  75.0 2.8 half_two.1
  77.8 22.1 %collective-permute-done.4.refs_2_ = bf16[1168,512]{1,0:T(8,128)(2,1)S(1)} collective-permute-done((bf16[1168,512]{1,0:T(8,128)(2,1)S(1)}, bf16[1168,512]{1,0:T(8,128)(2,1)S(1)}, u32[]{:S(2)}, u32[]{:S(2)}) %collective-permute-start.4) | collective-permute-done | bytes 1196064 | tf_op jit(solution)/shard_map/ppermute | solution.py:642
  100.4 2.1 far_half_two.1
  103.9 3.8 %forward_two.1 = (f32[1792,512]{1,0:T(8,128)S(1)}, f32[8,16,128]{2,1,0:T(8,128)S(1)}, bf16[1792,512]{1,0:T(8,128)(2,1)S(1)}, f32[8,128]{1,0:T(8,128)S(1)}) custom-call(s32[7]{0:T(128)S(1)} %stack.31.refs_0_, f32[1792,512]{1,0:T(8,128)S(1)} %get-tuple-element.144.refs_1_, bf16[640,512]{1,0:T(8,128)(2,1)S(1)} %collective-permute-done.6.refs_2_, ...), custom_call_target="tpu_custom_call" | custom-call | flops 1000000 | bytes 1000 | tf_op jit(solution)/shard_map/forward_two/pallas_call | solution.py:45
  107.7 1.8 collective-permute-start.8
  109.8 12.7 %all_to_all.21.refs_3_.refs_4_.refs_2_ = f32[8,16,128]{2,1,0:T(8,128)S(1)} all-to-all(f32[8,16,128]{2,1,0:T(8,128)S(1)} %get-tuple-element.146), channel_id=1, replica_groups=mesh['row'=8,'col'=4] {'row'}, dimensions={0} | all-to-all | bytes 131072 | tf_op jit(solution)/shard_map/all_to_all | solution.py:125
  122.5 2.0 sums_two.1
  124.6 9.7 %all_to_all.22.refs_5_ = f32[8,8,128]{2,1,0:T(8,128)} all-to-all(f32[8,8,128]{2,1,0:T(8,128)S(1)} %sums_two.1), channel_id=1, replica_groups=mesh['row'=8,'col'=4] {'row'}, dimensions={0} | all-to-all | bytes 65536 | tf_op jit(solution)/shard_map/all_to_all | solution.py:125
  135.3 5.8 %turn_two.1 = (bf16[1792,512]{1,0:T(8,128)(2,1)}, f32[8,128]{1,0:T(8,128)}) custom-call(f32[1792,512]{1,0:T(8,128)} %copy-done.7, bf16[1792,512]{1,0:T(8,128)(2,1)} %refs_1_.9, f32[14,128,128]{2,1,0:T(8,128)} %copy-done.17, bf16[14,128,128]{2,1,0:T(8,128)(2,1)} %copy-done.25, f32[8,16,128]{2,1,0:T(8,128)} %copy-done.27, f32[8,8,128]{2,1,0:T(8,128)} %all_to_all.22.refs_5_, ...), custom_call_target="tpu_custom_call" | custom-call | flops 1000000 | bytes 1000 | tf_op jit(solution)/shard_map/turn_two/pallas_call | solution.py:45
  142.9 6.2 %terms_two.2 = (bf16[512,512]{1,0:T(8,128)(2,1)}, bf16[512,512]{1,0:T(8,128)(2,1)}, f32[8,128]{1,0:T(8,128)}) custom-call(s32[7]{0:T(128)} %copy-done.29, bf16[1792,512]{1,0:T(8,128)(2,1)} %copy-done.15, bf16[1792,512]{1,0:T(8,128)(2,1)} %copy-done.16, bf16[1792,512]{1,0:T(8,128)(2,1)} %copy-done.19, bf16[1792,512]{1,0:T(8,128)(2,1)} %copy-done.20, ...), custom_call_target="tpu_custom_call" | custom-call | flops 1000000 | bytes 1000 | tf_op jit(solution)/shard_map/terms_two/pallas_call | solution.py:45
  150.8 6.3 %terms_two.3 = (bf16[512,512]{1,0:T(8,128)(2,1)}, bf16[512,512]{1,0:T(8,128)(2,1)}, f32[8,128]{1,0:T(8,128)}) custom-call(s32[7]{0:T(128)} %copy-done.29, bf16[1792,512]{1,0:T(8,128)(2,1)} %copy-done.15, bf16[1792,512]{1,0:T(8,128)(2,1)} %copy-done.16, bf16[1792,512]{1,0:T(8,128)(2,1)} %copy-done.19, bf16[1792,512]{1,0:T(8,128)(2,1)} %copy-done.20, ...), custom_call_target="tpu_custom_call" | custom-call | flops 1000000 | bytes 1000 | tf_op jit(solution)/shard_map/terms_two/pallas_call | solution.py:45
  159.3 4.0 %half_back_two.1 = (f32[1792,512]{1,0:T(8,128)S(1)}, f32[8,128]{1,0:T(8,128)S(1)}) custom-call(s32[7]{0:T(128)S(1)} %copy-done.30, bf16[1792,512]{1,0:T(8,128)(2,1)S(1)} %copy-done.14, bf16[1792,512]{1,0:T(8,128)(2,1)} %collective-permute-done.12.refs_2_, bf16[2048,512]{1,0:T(8,128)(2,1)S(1)} %copy-done.3, ...), custom_call_target="tpu_custom_call" | custom-call | flops 1000000 | bytes 1000 | tf_op jit(solution)/shard_map/half_back_two/pallas_call | solution.py:45
  165.4 2.4 collective-permute-start.16
  170.0 9.8 %collective-permute-done.16.refs_2_ = bf16[256,512]{1,0:T(8,128)(2,1)S(1)} collective-permute-done((bf16[256,512]{1,0:T(8,128)(2,1)S(1)}, bf16[256,512]{1,0:T(8,128)(2,1)S(1)}, u32[]{:S(2)}, u32[]{:S(2)}) %collective-permute-start.16) | collective-permute-done | bytes 262176 | tf_op jit(solution)/shard_map/ppermute | solution.py:642
  180.4 2.0 collective-permute-done.14.refs_2_
  186.4 2.1 collective-permute-start.20
  188.5 3.9 %far_half_back_two.1 = (f32[1792,512]{1,0:T(8,128)S(1)}, f32[8,128]{1,0:T(8,128)}) custom-call(s32[7]{0:T(128)S(1)} %copy-done.30, bf16[1792,512]{1,0:T(8,128)(2,1)} %collective-permute-done.10.refs_1_, bf16[512,512]{1,0:T(8,128)(2,1)S(1)} %copy-done.23, f32[1792,512]{1,0:T(8,128)S(1)} %get-tuple-element.179.refs_3_, ...), custom_call_target="tpu_custom_call" | custom-call | flops 1000000 | bytes 1000 | tf_op jit(solution)/shard_map/far_half_back_two/pallas_call | solution.py:45
  192.4 3.8 %backward_two.1 = (f32[1792,512]{1,0:T(8,128)S(1)}, f32[8,8,128]{2,1,0:T(8,128)}) custom-call(f32[1792,512]{1,0:T(8,128)S(1)} %get-tuple-element.182.refs_0_, bf16[1792,512]{1,0:T(8,128)(2,1)S(1)} %collective-permute-done.17.refs_1_, bf16[512,512]{1,0:T(8,128)(2,1)S(1)} %collective-permute-done.18.refs_2_, f32[1792,512]{1,0:T(8,128)S(1)} %copy-done.10, ...), custom_call_target="tpu_custom_call" | custom-call | flops 1000000 | bytes 1000 | tf_op jit(solution)/shard_map/backward_two/pallas_call | solution.py:45
  196.2 1.8 copy-done.21
  198.1 3.6 %all-to-all-start.3 = ((f32[8,8,128]{2,1,0:T(8,128)}), f32[8,8,128]{2,1,0:T(8,128)S(1)}, u32[]{:S(2)}, u32[]{:S(2)}) async-start(f32[8,8,128]{2,1,0:T(8,128)} %get-tuple-element.184.refs_3_), calls=%async_computation.3 | async-start | bytes 65536 | tf_op jit(solution)/shard_map/all_to_all | solution.py:125
  203.5 4.5 %all-to-all-done.3.refs_5_ = f32[8,8,128]{2,1,0:T(8,128)S(1)} async-done(((f32[8,8,128]{2,1,0:T(8,128)}), f32[8,8,128]{2,1,0:T(8,128)S(1)}, u32[]{:S(2)}, u32[]{:S(2)}) %all-to-all-start.3) | async-done | bytes 32800 | tf_op jit(solution)/shard_map/all_to_all | solution.py:125
  208.7 5.2 %turn_one.1 = (bf16[1792,512]{1,0:T(8,128)(2,1)}, f32[8,128]{1,0:T(8,128)}) custom-call(f32[1792,512]{1,0:T(8,128)} %copy-done.9, f32[1792,512]{1,0:T(8,128)} %copy-done.21, f32[14,128,128]{2,1,0:T(8,128)} %copy-done.17, bf16[14,128,128]{2,1,0:T(8,128)(2,1)} %copy-done.25, f32[8,16,128]{2,1,0:T(8,128)} %copy-done.26, f32[8,8,128]{2,1,0:T(8,128)} %copy-done.63, ...), custom_call_target="tpu_custom_call" | custom-call | flops 1000000 | bytes 1000 | tf_op jit(solution)/shard_map/turn_one/pallas_call | solution.py:45
  215.5 6.2 %terms_one.2 = (bf16[512,512]{1,0:T(8,128)(2,1)}, bf16[512,512]{1,0:T(8,128)(2,1)}, f32[8,128]{1,0:T(8,128)}) custom-call(s32[7]{0:T(128)} %copy-done.29, bf16[1792,512]{1,0:T(8,128)(2,1)} %refs_1_.11, bf16[1792,512]{1,0:T(8,128)(2,1)} %collective-permute-done.1.refs_2_, bf16[1792,512]{1,0:T(8,128)(2,1)} %collective-permute-done.refs_1_.refs_3_, ...), custom_call_target="tpu_custom_call" | custom-call | flops 1000000 | bytes 1000 | tf_op jit(solution)/shard_map/terms_one/pallas_call | solution.py:45
  223.2 6.0 %collective-permute-done.25.refs_2_ = bf16[256,512]{1,0:T(8,128)(2,1)S(1)} collective-permute-done((bf16[256,512]{1,0:T(8,128)(2,1)S(1)}, bf16[256,512]{1,0:T(8,128)(2,1)S(1)}, u32[]{:S(2)}, u32[]{:S(2)}) %collective-permute-start.25) | collective-permute-done | bytes 262176 | tf_op jit(solution)/shard_map/ppermute | solution.py:642
  232.5 6.4 %terms_one.3 = (bf16[512,512]{1,0:T(8,128)(2,1)}, bf16[512,512]{1,0:T(8,128)(2,1)}, f32[8,128]{1,0:T(8,128)}) custom-call(s32[7]{0:T(128)} %copy-done.29, bf16[1792,512]{1,0:T(8,128)(2,1)} %refs_1_.11, bf16[1792,512]{1,0:T(8,128)(2,1)} %collective-permute-done.1.refs_2_, bf16[1792,512]{1,0:T(8,128)(2,1)} %collective-permute-done.refs_1_.refs_3_, ...), custom_call_target="tpu_custom_call" | custom-call | flops 1000000 | bytes 1000 | tf_op jit(solution)/shard_map/terms_one/pallas_call | solution.py:45
  247.5 4.3 %half_back_one.1 = (f32[1792,512]{1,0:T(8,128)S(1)}, f32[8,128]{1,0:T(8,128)S(1)}) custom-call(s32[7]{0:T(128)S(1)} %copy-done.32, bf16[1792,512]{1,0:T(8,128)(2,1)S(1)} %copy-done.11, bf16[1792,512]{1,0:T(8,128)(2,1)} %collective-permute-done.22.refs_2_, bf16[2048,512]{1,0:T(8,128)(2,1)S(1)} %copy-done.6, ...), custom_call_target="tpu_custom_call" | custom-call | flops 1000000 | bytes 1000 | tf_op jit(solution)/shard_map/half_back_one/pallas_call | solution.py:45
  251.9 2.4 output.1
  254.3 2.7 collective-permute-done.30.refs_2_
  257.6 2.1 collective-permute-done.29.refs_2_
  262.2 2.5 collective-permute-start.34
  264.7 10.5 %collective-permute-done.32.refs_2_ = bf16[256,512]{1,0:T(8,128)(2,1)S(1)} collective-permute-done((bf16[256,512]{1,0:T(8,128)(2,1)S(1)}, bf16[256,512]{1,0:T(8,128)(2,1)S(1)}, u32[]{:S(2)}, u32[]{:S(2)}) %collective-permute-start.32) | collective-permute-done | bytes 262176 | tf_op jit(solution)/shard_map/ppermute | solution.py:642
  276.6 6.8 %collective-permute-done.33.refs_2_ = bf16[256,512]{1,0:T(8,128)(2,1)S(1)} collective-permute-done((bf16[256,512]{1,0:T(8,128)(2,1)S(1)}, bf16[256,512]{1,0:T(8,128)(2,1)S(1)}, u32[]{:S(2)}, u32[]{:S(2)}) %collective-permute-start.33) | collective-permute-done | bytes 262176 | tf_op jit(solution)/shard_map/ppermute | solution.py:642
  284.1 2.3 collective-permute-start.39
  287.1 3.6 %far_half_back_one.1 = (f32[1792,512]{1,0:T(8,128)S(1)}, f32[8,128]{1,0:T(8,128)}) custom-call(s32[7]{0:T(128)S(1)} %copy-done.32, bf16[1792,512]{1,0:T(8,128)(2,1)} %collective-permute-done.28.refs_1_, bf16[512,512]{1,0:T(8,128)(2,1)S(1)} %collective-permute-done.31.refs_2_, f32[1792,512]{1,0:T(8,128)S(1)} %get-tuple-element.214.refs_3_, ...), custom_call_target="tpu_custom_call" | custom-call | flops 1000000 | bytes 1000 | tf_op jit(solution)/shard_map/far_half_back_one/pallas_call | solution.py:45
  290.8 2.6 backward_one.1
  302.3 4.7 %place_two.1 = (f32[2048,512]{1,0:T(8,128)}, f32[8,128]{1,0:T(8,128)}) custom-call(s32[7]{0:T(128)} %copy-done.29, bf16[512,512]{1,0:T(8,128)(2,1)} %get-tuple-element.230.refs_1_, bf16[512,512]{1,0:T(8,128)(2,1)} %copy-done.61, bf16[512,512]{1,0:T(8,128)(2,1)} %copy-done.34, bf16[512,512]{1,0:T(8,128)(2,1)} %copy-done.24, f32[8,128]{1,0:T(8,128)} %copy-done.49, ...), custom_call_target="tpu_custom_call" | custom-call | flops 1000000 | bytes 1000 | tf_op jit(solution)/shard_map/place_two/pallas_call | solution.py:45
  307.0 3.3 %collective-permute-done.38.refs_2_ = bf16[512,512]{1,0:T(8,128)(2,1)S(1)} collective-permute-done((bf16[512,512]{1,0:T(8,128)(2,1)S(1)}, bf16[512,512]{1,0:T(8,128)(2,1)S(1)}, u32[]{:S(2)}, u32[]{:S(2)}) %collective-permute-start.38) | collective-permute-done | bytes 524320 | tf_op jit(solution)/shard_map/ppermute | solution.py:642
  310.3 3.1 place_one.1
  (220 shorter events, 61.4 us)
Async XLA Ops:
  0.6 15.9 %collective-permute-start.1 = (bf16[1792,512]{1,0:T(8,128)(2,1)}, bf16[1792,512]{1,0:T(8,128)(2,1)}, u32[]{:S(2)}, u32[]{:S(2)}) collective-permute-start(bf16[1792,512]{1,0:T(8,128)(2,1)} %refs_1_.11), channel_id=1, source_target_pairs={{0,1},{1,0},{2,3},{3,2},{4,5},{5,4},{6,7},{7,6},{8,9},{9,8},{10,11... | collective-permute-start | bytes 5505032 | tf_op jit(solution)/shard_map/ppermute | solution.py:642
  1.2 43.5 %collective-permute-start = (bf16[1792,512]{1,0:T(8,128)(2,1)}, bf16[1792,512]{1,0:T(8,128)(2,1)}, u32[]{:S(2)}, u32[]{:S(2)}) collective-permute-start(bf16[1792,512]{1,0:T(8,128)(2,1)} %refs_1_.11), channel_id=1, source_target_pairs={{0,2},{1,3},{2,0},{3,1},{4,6},{5,7},{6,4},{7,5},{8,10},{9,11},{10,... | collective-permute-start | bytes 5505032 | tf_op jit(solution)/shard_map/ppermute | solution.py:642
  4.6 99.3 %copy-start.29 = (s32[7]{0:T(128)}, s32[7]{0:T(128)S(1)}, u32[]{:S(2)}) copy-start(s32[7]{0:T(128)S(1)} %stack.31.refs_0_) | copy-start | bytes 88
  13.5 90.4 %copy-start.17 = (f32[14,128,128]{2,1,0:T(8,128)}, f32[14,128,128]{2,1,0:T(8,128)S(1)}, u32[]{:S(2)}) copy-start(f32[14,128,128]{2,1,0:T(8,128)S(1)} %get-tuple-element.131.refs_5_.refs_6_.refs_2_) | copy-start | bytes 2752516
  44.7 4.0 %collective-permute-start.2 = (bf16[1792,512]{1,0:T(8,128)(2,1)}, bf16[1792,512]{1,0:T(8,128)(2,1)S(1)}, u32[]{:S(2)}, u32[]{:S(2)}) collective-permute-start(bf16[1792,512]{1,0:T(8,128)(2,1)} %collective-permute-done.refs_1_.refs_3_), channel_id=1, source_target_pairs={{0,1},{1,0},{2,3},{3,2},{4,5},{5,4},{6,7},{7,6},{8,9},{9,8},{10,11... | collective-permute-start | bytes 5505032 | tf_op jit(solution)/shard_map/ppermute | solution.py:642
  53.1 16.8 %collective-permute-start.3 = (bf16[640,512]{1,0:T(8,128)(2,1)S(1)}, bf16[640,512]{1,0:T(8,128)(2,1)S(1)}, u32[]{:S(2)}, u32[]{:S(2)}) collective-permute-start(bf16[640,512]{1,0:T(8,128)(2,1)S(1)} %get-tuple-element.133), channel_id=1, source_target_pairs={{0,2},{1,3},{2,0},{3,1},{4,6},{5,7},{6,4},{7,5},{8,10},{9,11},{10,... | collective-permute-start | bytes 1966088 | tf_op jit(solution)/shard_map/ppermute | solution.py:642
  67.3 125.1 %copy-start.26 = (f32[8,16,128]{2,1,0:T(8,128)}, f32[8,16,128]{2,1,0:T(8,128)S(1)}, u32[]{:S(2)}) copy-start(f32[8,16,128]{2,1,0:T(8,128)S(1)} %all_to_all.20.refs_1_.refs_2_.refs_4_) | copy-start | bytes 196612
  71.2 3.8 %collective-permute-start.5 = (bf16[1792,512]{1,0:T(8,128)(2,1)S(1)}, bf16[1792,512]{1,0:T(8,128)(2,1)S(1)}, u32[]{:S(2)}, u32[]{:S(2)}) collective-permute-start(bf16[1792,512]{1,0:T(8,128)(2,1)S(1)} %get-tuple-element.139.refs_1_), channel_id=1, source_target_pairs={{0,1},{1,0},{2,3},{3,2},{4,5},{5,4},{6,7},{7,6},{8,9},{9,8},{10,11... | collective-permute-start | bytes 5505032 | tf_op jit(solution)/shard_map/ppermute | solution.py:642
  71.2 28.7 %collective-permute-start.4 = (bf16[1168,512]{1,0:T(8,128)(2,1)S(1)}, bf16[1168,512]{1,0:T(8,128)(2,1)S(1)}, u32[]{:S(2)}, u32[]{:S(2)}) collective-permute-start(bf16[1168,512]{1,0:T(8,128)(2,1)S(1)} %get-tuple-element.136), channel_id=1, source_target_pairs={{0,2},{1,3},{2,0},{3,1},{4,6},{5,7},{6,4},{7,5},{8,10},{9,11},{10,... | collective-permute-start | bytes 3588104 | tf_op jit(solution)/shard_map/ppermute | solution.py:642
  99.9 3.9 %collective-permute-start.7 = (bf16[1168,512]{1,0:T(8,128)(2,1)S(1)}, bf16[1168,512]{1,0:T(8,128)(2,1)S(1)}, u32[]{:S(2)}, u32[]{:S(2)}) collective-permute-start(bf16[1168,512]{1,0:T(8,128)(2,1)S(1)} %collective-permute-done.4.refs_2_), channel_id=1, source_target_pairs={{0,1},{1,0},{2,3},{3,2},{4,5},{5,4},{6,7},{7,6},{8,9},{9,8},{10,11... | collective-permute-start | bytes 3588104 | tf_op jit(solution)/shard_map/ppermute | solution.py:642
  99.9 3.9 %collective-permute-start.6 = (bf16[640,512]{1,0:T(8,128)(2,1)S(1)}, bf16[640,512]{1,0:T(8,128)(2,1)S(1)}, u32[]{:S(2)}, u32[]{:S(2)}) collective-permute-start(bf16[640,512]{1,0:T(8,128)(2,1)S(1)} %collective-permute-done.3.refs_5_.refs_1_), channel_id=1, source_target_pairs={{0,1},{1,0},{2,3},{3,2},{4,5},{5,4},{6,7},{7,6},{8,9},{9,8},{10,11... | collective-permute-start | bytes 1966088 | tf_op jit(solution)/shard_map/ppermute | solution.py:642
  107.7 26.7 %collective-permute-start.8 = (bf16[512,512]{1,0:T(8,128)(2,1)S(1)}, bf16[512,512]{1,0:T(8,128)(2,1)S(1)}, u32[]{:S(2)}, u32[]{:S(2)}) collective-permute-start(bf16[512,512]{1,0:T(8,128)(2,1)S(1)} %get-tuple-element.156), channel_id=1, source_target_pairs={{0,2},{1,3},{2,0},{3,1},{4,6},{5,7},{6,4},{7,5},{8,10},{9,11},{10,... | collective-permute-start | bytes 1572872 | tf_op jit(solution)/shard_map/ppermute | solution.py:642
  109.5 24.9 %collective-permute-start.9 = (bf16[512,512]{1,0:T(8,128)(2,1)S(1)}, bf16[512,512]{1,0:T(8,128)(2,1)S(1)}, u32[]{:S(2)}, u32[]{:S(2)}) collective-permute-start(bf16[512,512]{1,0:T(8,128)(2,1)S(1)} %get-tuple-element.157), channel_id=1, source_target_pairs={{0,2},{1,3},{2,0},{3,1},{4,6},{5,7},{6,4},{7,5},{8,10},{9,11},{10,... | collective-permute-start | bytes 1572872 | tf_op jit(solution)/shard_map/ppermute | solution.py:642
  141.1 16.0 %collective-permute-start.12 = (bf16[1792,512]{1,0:T(8,128)(2,1)}, bf16[1792,512]{1,0:T(8,128)(2,1)}, u32[]{:S(2)}, u32[]{:S(2)}) collective-permute-start(bf16[1792,512]{1,0:T(8,128)(2,1)} %get-tuple-element.158.refs_5_.refs_1_), channel_id=1, source_target_pairs={{0,1},{1,0},{2,3},{3,2},{4,5},{5,4},{6,7},{7,6},{8,9},{9,8},{10,11... | collective-permute-start | bytes 5505032 | tf_op jit(solution)/shard_map/ppermute | solution.py:642
  141.2 42.7 %collective-permute-start.10 = (bf16[1792,512]{1,0:T(8,128)(2,1)}, bf16[1792,512]{1,0:T(8,128)(2,1)}, u32[]{:S(2)}, u32[]{:S(2)}) collective-permute-start(bf16[1792,512]{1,0:T(8,128)(2,1)} %get-tuple-element.158.refs_5_.refs_1_), channel_id=1, source_target_pairs={{0,2},{1,3},{2,0},{3,1},{4,6},{5,7},{6,4},{7,5},{8,10},{9,11},{10,... | collective-permute-start | bytes 5505032 | tf_op jit(solution)/shard_map/ppermute | solution.py:642
  142.7 14.4 %collective-permute-start.13 = (bf16[512,512]{1,0:T(8,128)(2,1)}, bf16[512,512]{1,0:T(8,128)(2,1)S(1)}, u32[]{:S(2)}, u32[]{:S(2)}) collective-permute-start(bf16[512,512]{1,0:T(8,128)(2,1)} %copy-done.56), channel_id=1, source_target_pairs={{0,1},{1,0},{2,3},{3,2},{4,5},{5,4},{6,7},{7,6},{8,9},{9,8},{10,11... | collective-permute-start | bytes 1572872 | tf_op jit(solution)/shard_map/ppermute | solution.py:642
  149.1 14.6 %collective-permute-start.15 = (bf16[512,512]{1,0:T(8,128)(2,1)}, bf16[512,512]{1,0:T(8,128)(2,1)}, u32[]{:S(2)}, u32[]{:S(2)}) collective-permute-start(bf16[512,512]{1,0:T(8,128)(2,1)} %get-tuple-element.171), channel_id=1, source_target_pairs={{0,8},{4,12},{8,0},{12,4},{16,24},{20,28},{24,16},{28,20},{1,9},{5... | collective-permute-start | bytes 1572872 | tf_op jit(solution)/shard_map/ppermute | solution.py:642
  149.6 18.2 %collective-permute-start.11 = (bf16[512,512]{1,0:T(8,128)(2,1)}, bf16[512,512]{1,0:T(8,128)(2,1)}, u32[]{:S(2)}, u32[]{:S(2)}) collective-permute-start(bf16[512,512]{1,0:T(8,128)(2,1)} %get-tuple-element.163), channel_id=1, source_target_pairs={{0,4},{4,0},{8,12},{12,8},{16,20},{20,16},{24,28},{28,24},{1,5},{5... | collective-permute-start | bytes 1572872 | tf_op jit(solution)/shard_map/ppermute | solution.py:642
  163.4 25.1 %copy-start.23 = (bf16[512,512]{1,0:T(8,128)(2,1)S(1)}, bf16[512,512]{1,0:T(8,128)(2,1)}, u32[]{:S(2)}) copy-start(bf16[512,512]{1,0:T(8,128)(2,1)} %copy-done.22) | copy-start | bytes 1572868
  165.4 14.4 %collective-permute-start.16 = (bf16[256,512]{1,0:T(8,128)(2,1)S(1)}, bf16[256,512]{1,0:T(8,128)(2,1)S(1)}, u32[]{:S(2)}, u32[]{:S(2)}) collective-permute-start(bf16[256,512]{1,0:T(8,128)(2,1)S(1)} %get-tuple-element.175), channel_id=1, source_target_pairs={{0,16},{4,20},{8,24},{12,28},{16,0},{20,4},{24,8},{28,12},{1,17},{... | collective-permute-start | bytes 786440 | tf_op jit(solution)/shard_map/ppermute | solution.py:642
  169.5 13.0 %collective-permute-start.14 = (bf16[256,512]{1,0:T(8,128)(2,1)S(1)}, bf16[256,512]{1,0:T(8,128)(2,1)S(1)}, u32[]{:S(2)}, u32[]{:S(2)}) collective-permute-start(bf16[256,512]{1,0:T(8,128)(2,1)S(1)} %get-tuple-element.168), channel_id=1, source_target_pairs={{0,8},{4,12},{8,0},{12,4},{16,24},{20,28},{24,16},{28,20},{1,9},{5... | collective-permute-start | bytes 786440 | tf_op jit(solution)/shard_map/ppermute | solution.py:642
  183.9 8.5 %collective-permute-start.17 = (bf16[1792,512]{1,0:T(8,128)(2,1)}, bf16[1792,512]{1,0:T(8,128)(2,1)S(1)}, u32[]{:S(2)}, u32[]{:S(2)}) collective-permute-start(bf16[1792,512]{1,0:T(8,128)(2,1)} %collective-permute-done.10.refs_1_), channel_id=1, source_target_pairs={{0,1},{1,0},{2,3},{3,2},{4,5},{5,4},{6,7},{7,6},{8,9},{9,8},{10,11... | collective-permute-start | bytes 5505032 | tf_op jit(solution)/shard_map/ppermute | solution.py:642
  183.9 8.5 %collective-permute-start.18 = (bf16[512,512]{1,0:T(8,128)(2,1)S(1)}, bf16[512,512]{1,0:T(8,128)(2,1)S(1)}, u32[]{:S(2)}, u32[]{:S(2)}) collective-permute-start(bf16[512,512]{1,0:T(8,128)(2,1)S(1)} %copy-done.60), channel_id=1, source_target_pairs={{0,1},{1,0},{2,3},{3,2},{4,5},{5,4},{6,7},{7,6},{8,9},{9,8},{10,11... | collective-permute-start | bytes 1572872 | tf_op jit(solution)/shard_map/ppermute | solution.py:642
  184.4 19.1 %collective-permute-start.19 = (bf16[512,512]{1,0:T(8,128)(2,1)S(1)}, bf16[512,512]{1,0:T(8,128)(2,1)S(1)}, u32[]{:S(2)}, u32[]{:S(2)}) collective-permute-start(bf16[512,512]{1,0:T(8,128)(2,1)S(1)} %copy-done.55), channel_id=1, source_target_pairs={{0,2},{1,3},{2,0},{3,1},{4,6},{5,7},{6,4},{7,5},{8,10},{9,11},{10,... | collective-permute-start | bytes 1572872 | tf_op jit(solution)/shard_map/ppermute | solution.py:642
  185.9 15.7 %collective-permute-start.21 = (bf16[256,512]{1,0:T(8,128)(2,1)S(1)}, bf16[256,512]{1,0:T(8,128)(2,1)S(1)}, u32[]{:S(2)}, u32[]{:S(2)}) collective-permute-start(bf16[256,512]{1,0:T(8,128)(2,1)S(1)} %get-tuple-element.188.refs_1_), channel_id=1, source_target_pairs={{0,4},{4,0},{8,12},{12,8},{16,20},{20,16},{24,28},{28,24},{1,5},{5... | collective-permute-start | bytes 786440 | tf_op jit(solution)/shard_map/ppermute | solution.py:642
  186.4 16.5 %collective-permute-start.20 = (bf16[256,512]{1,0:T(8,128)(2,1)S(1)}, bf16[256,512]{1,0:T(8,128)(2,1)S(1)}, u32[]{:S(2)}, u32[]{:S(2)}) collective-permute-start(bf16[256,512]{1,0:T(8,128)(2,1)S(1)} %get-tuple-element.186.refs_1_), channel_id=1, source_target_pairs={{0,16},{4,20},{8,24},{12,28},{16,0},{20,4},{24,8},{28,12},{1,17},{... | collective-permute-start | bytes 786440 | tf_op jit(solution)/shard_map/ppermute | solution.py:642
  198.1 10.0 %all-to-all-start.3 = ((f32[8,8,128]{2,1,0:T(8,128)}), f32[8,8,128]{2,1,0:T(8,128)S(1)}, u32[]{:S(2)}, u32[]{:S(2)}) async-start(f32[8,8,128]{2,1,0:T(8,128)} %get-tuple-element.184.refs_3_), calls=%async_computation.3 | async-start | bytes 65536 | tf_op jit(solution)/shard_map/all_to_all | solution.py:125
  213.8 33.6 %collective-permute-start.22 = (bf16[1792,512]{1,0:T(8,128)(2,1)}, bf16[1792,512]{1,0:T(8,128)(2,1)}, u32[]{:S(2)}, u32[]{:S(2)}) collective-permute-start(bf16[1792,512]{1,0:T(8,128)(2,1)} %get-tuple-element.190.refs_5_.refs_1_), channel_id=1, source_target_pairs={{0,1},{1,0},{2,3},{3,2},{4,5},{5,4},{6,7},{7,6},{8,9},{9,8},{10,11... | collective-permute-start | bytes 5505032 | tf_op jit(solution)/shard_map/ppermute | solution.py:642
  213.8 46.5 %collective-permute-start.28 = (bf16[1792,512]{1,0:T(8,128)(2,1)}, bf16[1792,512]{1,0:T(8,128)(2,1)}, u32[]{:S(2)}, u32[]{:S(2)}) collective-permute-start(bf16[1792,512]{1,0:T(8,128)(2,1)} %get-tuple-element.190.refs_5_.refs_1_), channel_id=1, source_target_pairs={{0,2},{1,3},{2,0},{3,1},{4,6},{5,7},{6,4},{7,5},{8,10},{9,11},{10,... | collective-permute-start | bytes 5505032 | tf_op jit(solution)/shard_map/ppermute | solution.py:642
  214.4 14.8 %collective-permute-start.25 = (bf16[256,512]{1,0:T(8,128)(2,1)S(1)}, bf16[256,512]{1,0:T(8,128)(2,1)S(1)}, u32[]{:S(2)}, u32[]{:S(2)}) collective-permute-start(bf16[256,512]{1,0:T(8,128)(2,1)S(1)} %get-tuple-element.195.refs_1_), channel_id=1, source_target_pairs={{0,16},{4,20},{8,24},{12,28},{16,0},{20,4},{24,8},{28,12},{1,17},{... | collective-permute-start | bytes 786440 | tf_op jit(solution)/shard_map/ppermute | solution.py:642
  215.0 14.9 %collective-permute-start.24 = (bf16[256,512]{1,0:T(8,128)(2,1)S(1)}, bf16[256,512]{1,0:T(8,128)(2,1)S(1)}, u32[]{:S(2)}, u32[]{:S(2)}) collective-permute-start(bf16[256,512]{1,0:T(8,128)(2,1)S(1)} %get-tuple-element.193.refs_1_), channel_id=1, source_target_pairs={{0,8},{4,12},{8,0},{12,4},{16,24},{20,28},{24,16},{28,20},{1,9},{5... | collective-permute-start | bytes 786440 | tf_op jit(solution)/shard_map/ppermute | solution.py:642
  221.7 18.7 %collective-permute-start.27 = (bf16[512,512]{1,0:T(8,128)(2,1)}, bf16[512,512]{1,0:T(8,128)(2,1)}, u32[]{:S(2)}, u32[]{:S(2)}) collective-permute-start(bf16[512,512]{1,0:T(8,128)(2,1)} %get-tuple-element.201), channel_id=1, source_target_pairs={{0,8},{4,12},{8,0},{12,4},{16,24},{20,28},{24,16},{28,20},{1,9},{5... | collective-permute-start | bytes 1572872 | tf_op jit(solution)/shard_map/ppermute | solution.py:642
  229.2 14.7 %collective-permute-start.26 = (bf16[512,512]{1,0:T(8,128)(2,1)}, bf16[512,512]{1,0:T(8,128)(2,1)}, u32[]{:S(2)}, u32[]{:S(2)}) collective-permute-start(bf16[512,512]{1,0:T(8,128)(2,1)} %get-tuple-element.198), channel_id=1, source_target_pairs={{0,4},{4,0},{8,12},{12,8},{16,20},{20,16},{24,28},{28,24},{1,5},{5... | collective-permute-start | bytes 1572872 | tf_op jit(solution)/shard_map/ppermute | solution.py:642
  229.9 17.5 %collective-permute-start.23 = (bf16[512,512]{1,0:T(8,128)(2,1)}, bf16[512,512]{1,0:T(8,128)(2,1)S(1)}, u32[]{:S(2)}, u32[]{:S(2)}) collective-permute-start(bf16[512,512]{1,0:T(8,128)(2,1)} %get-tuple-element.191), channel_id=1, source_target_pairs={{0,1},{1,0},{2,3},{3,2},{4,5},{5,4},{6,7},{7,6},{8,9},{9,8},{10,11... | collective-permute-start | bytes 1572872 | tf_op jit(solution)/shard_map/ppermute | solution.py:642
  230.5 31.7 %copy-start.34 = (bf16[512,512]{1,0:T(8,128)(2,1)}, bf16[512,512]{1,0:T(8,128)(2,1)S(1)}, u32[]{:S(2)}) copy-start(bf16[512,512]{1,0:T(8,128)(2,1)S(1)} %get-tuple-element.221.refs_3_) | copy-start | bytes 1572868
  243.1 13.8 %collective-permute-start.30 = (bf16[256,512]{1,0:T(8,128)(2,1)S(1)}, bf16[256,512]{1,0:T(8,128)(2,1)S(1)}, u32[]{:S(2)}, u32[]{:S(2)}) collective-permute-start(bf16[256,512]{1,0:T(8,128)(2,1)S(1)} %get-tuple-element.210), channel_id=1, source_target_pairs={{0,16},{4,20},{8,24},{12,28},{16,0},{20,4},{24,8},{28,12},{1,17},{... | collective-permute-start | bytes 786440 | tf_op jit(solution)/shard_map/ppermute | solution.py:642
  246.6 13.1 %collective-permute-start.29 = (bf16[256,512]{1,0:T(8,128)(2,1)S(1)}, bf16[256,512]{1,0:T(8,128)(2,1)S(1)}, u32[]{:S(2)}, u32[]{:S(2)}) collective-permute-start(bf16[256,512]{1,0:T(8,128)(2,1)S(1)} %get-tuple-element.206), channel_id=1, source_target_pairs={{0,8},{4,12},{8,0},{12,4},{16,24},{20,28},{24,16},{28,20},{1,9},{5... | collective-permute-start | bytes 786440 | tf_op jit(solution)/shard_map/ppermute | solution.py:642
  260.3 30.4 %collective-permute-start.35 = (bf16[1792,512]{1,0:T(8,128)(2,1)}, bf16[1792,512]{1,0:T(8,128)(2,1)S(1)}, u32[]{:S(2)}, u32[]{:S(2)}) collective-permute-start(bf16[1792,512]{1,0:T(8,128)(2,1)} %collective-permute-done.28.refs_1_), channel_id=1, source_target_pairs={{0,1},{1,0},{2,3},{3,2},{4,5},{5,4},{6,7},{7,6},{8,9},{9,8},{10,11... | collective-permute-start | bytes 5505032 | tf_op jit(solution)/shard_map/ppermute | solution.py:642
  260.4 14.8 %collective-permute-start.32 = (bf16[256,512]{1,0:T(8,128)(2,1)S(1)}, bf16[256,512]{1,0:T(8,128)(2,1)S(1)}, u32[]{:S(2)}, u32[]{:S(2)}) collective-permute-start(bf16[256,512]{1,0:T(8,128)(2,1)S(1)} %get-tuple-element.217.refs_1_), channel_id=1, source_target_pairs={{0,16},{4,20},{8,24},{12,28},{16,0},{20,4},{24,8},{28,12},{1,17},{... | collective-permute-start | bytes 786440 | tf_op jit(solution)/shard_map/ppermute | solution.py:642
  260.7 23.4 %collective-permute-start.31 = (bf16[512,512]{1,0:T(8,128)(2,1)S(1)}, bf16[512,512]{1,0:T(8,128)(2,1)S(1)}, u32[]{:S(2)}, u32[]{:S(2)}) collective-permute-start(bf16[512,512]{1,0:T(8,128)(2,1)S(1)} %copy-done.53), channel_id=1, source_target_pairs={{0,2},{1,3},{2,0},{3,1},{4,6},{5,7},{6,4},{7,5},{8,10},{9,11},{10,... | collective-permute-start | bytes 1572872 | tf_op jit(solution)/shard_map/ppermute | solution.py:642
  262.2 24.2 %collective-permute-start.34 = (bf16[512,512]{1,0:T(8,128)(2,1)S(1)}, bf16[512,512]{1,0:T(8,128)(2,1)S(1)}, u32[]{:S(2)}, u32[]{:S(2)}) collective-permute-start(bf16[512,512]{1,0:T(8,128)(2,1)S(1)} %get-tuple-element.221.refs_3_), channel_id=1, source_target_pairs={{0,8},{4,12},{8,0},{12,4},{16,24},{20,28},{24,16},{28,20},{1,9},{5... | collective-permute-start | bytes 1572872 | tf_op jit(solution)/shard_map/ppermute | solution.py:642
  264.7 26.0 %collective-permute-start.36 = (bf16[512,512]{1,0:T(8,128)(2,1)S(1)}, bf16[512,512]{1,0:T(8,128)(2,1)S(1)}, u32[]{:S(2)}, u32[]{:S(2)}) collective-permute-start(bf16[512,512]{1,0:T(8,128)(2,1)S(1)} %copy-done.58), channel_id=1, source_target_pairs={{0,1},{1,0},{2,3},{3,2},{4,5},{5,4},{6,7},{7,6},{8,9},{9,8},{10,11... | collective-permute-start | bytes 1572872 | tf_op jit(solution)/shard_map/ppermute | solution.py:642
  275.2 8.2 %collective-permute-start.33 = (bf16[256,512]{1,0:T(8,128)(2,1)S(1)}, bf16[256,512]{1,0:T(8,128)(2,1)S(1)}, u32[]{:S(2)}, u32[]{:S(2)}) collective-permute-start(bf16[256,512]{1,0:T(8,128)(2,1)S(1)} %get-tuple-element.219.refs_1_), channel_id=1, source_target_pairs={{0,4},{4,0},{8,12},{12,8},{16,20},{20,16},{24,28},{28,24},{1,5},{5... | collective-permute-start | bytes 786440 | tf_op jit(solution)/shard_map/ppermute | solution.py:642
  283.4 11.4 %collective-permute-start.37 = (bf16[256,512]{1,0:T(8,128)(2,1)S(1)}, bf16[256,512]{1,0:T(8,128)(2,1)S(1)}, u32[]{:S(2)}, u32[]{:S(2)}) collective-permute-start(bf16[256,512]{1,0:T(8,128)(2,1)S(1)} %get-tuple-element.224.refs_1_), channel_id=1, source_target_pairs={{0,8},{4,12},{8,0},{12,4},{16,24},{20,28},{24,16},{28,20},{1,9},{5... | collective-permute-start | bytes 786440 | tf_op jit(solution)/shard_map/ppermute | solution.py:642
  284.1 14.0 %collective-permute-start.39 = (bf16[256,512]{1,0:T(8,128)(2,1)S(1)}, bf16[256,512]{1,0:T(8,128)(2,1)S(1)}, u32[]{:S(2)}, u32[]{:S(2)}) collective-permute-start(bf16[256,512]{1,0:T(8,128)(2,1)S(1)} %get-tuple-element.227.refs_1_), channel_id=1, source_target_pairs={{0,16},{4,20},{8,24},{12,28},{16,0},{20,4},{24,8},{28,12},{1,17},{... | collective-permute-start | bytes 786440 | tf_op jit(solution)/shard_map/ppermute | solution.py:642
  286.4 15.1 %collective-permute-start.41 = (bf16[512,512]{1,0:T(8,128)(2,1)}, bf16[512,512]{1,0:T(8,128)(2,1)S(1)}, u32[]{:S(2)}, u32[]{:S(2)}) collective-permute-start(bf16[512,512]{1,0:T(8,128)(2,1)} %get-tuple-element.230.refs_1_), channel_id=1, source_target_pairs={{0,4},{4,0},{8,12},{12,8},{16,20},{20,16},{24,28},{28,24},{1,5},{5... | collective-permute-start | bytes 1572872 | tf_op jit(solution)/shard_map/ppermute | solution.py:642
  295.4 14.8 %collective-permute-start.38 = (bf16[512,512]{1,0:T(8,128)(2,1)S(1)}, bf16[512,512]{1,0:T(8,128)(2,1)S(1)}, u32[]{:S(2)}, u32[]{:S(2)}) collective-permute-start(bf16[512,512]{1,0:T(8,128)(2,1)S(1)} %get-tuple-element.226.refs_1_), channel_id=1, source_target_pairs={{0,4},{4,0},{8,12},{12,8},{16,20},{20,16},{24,28},{28,24},{1,5},{5... | collective-permute-start | bytes 1572872 | tf_op jit(solution)/shard_map/ppermute | solution.py:642
  299.2 11.0 %collective-permute-start.40 = (bf16[512,512]{1,0:T(8,128)(2,1)S(1)}, bf16[512,512]{1,0:T(8,128)(2,1)S(1)}, u32[]{:S(2)}, u32[]{:S(2)}) collective-permute-start(bf16[512,512]{1,0:T(8,128)(2,1)S(1)} %get-tuple-element.228.refs_3_), channel_id=1, source_target_pairs={{0,8},{4,12},{8,0},{12,4},{16,24},{20,28},{24,16},{28,20},{1,9},{5... | collective-permute-start | bytes 1572872 | tf_op jit(solution)/shard_map/ppermute | solution.py:642
  (60 other events, 418.3 us)
